TPU v7x, 32 devices: a whole 2x2x4 slice. The times are simulated.
32 devices in a mesh: shard: 4 (over y, x), expert: 8 (over z, core).
Axes of the slice: x: 2, y: 2, z: 4, core: 2. Of those that a mesh axis runs over, the one named last changes fastest.
Arguments:
- block_input: bfloat16 [8, 512, 2048], P('expert', 'shard'), may hold values from -6 to 6
- segment_ids: int32 [8, 512], P('expert'), may hold values from 0 to 1, never falling along the last dimension, each value on 1 to 384 neighbouring positions
- expert_routes: int32 [8, 512, 8], P('expert', 'shard'), may hold values from 0 to 15, all different within a row; in each aligned block of 128 rows (0 to 127, 128 to 255, ..., all dimensions but the last counted through in order) at most 96 rows name the same one
- attn_gain: bfloat16 [2048], P('shard'), may hold values from 0.5 to 1.5
- w_query: bfloat16 [2048, 2048], P('shard'), may hold values from -0.125 to 0.125
- w_key: bfloat16 [2048, 2048], P('shard'), may hold values from -0.125 to 0.125
- w_value: bfloat16 [2048, 2048], P('shard'), may hold values from -0.125 to 0.125
- query_gain: bfloat16 [2048], P('shard'), may hold values from 0.5 to 1.5
- key_gain: bfloat16 [2048], P('shard'), may hold values from 0.5 to 1.5
- w_output: bfloat16 [2048, 2048], P('shard'), may hold values from -0.75 to 0.75
- moe_gain: bfloat16 [2048], P('shard'), may hold values from 0.5 to 1.5
- w_router: bfloat16 [2048, 16], P('shard'), may hold values from -0.0625 to 0.0625
- w_gate: bfloat16 [16, 2048, 1024], P('expert', None, 'shard'), may hold values from -0.125 to 0.125
- w_up: bfloat16 [16, 2048, 1024], P('expert', None, 'shard'), may hold values from -0.125 to 0.125
- w_down: bfloat16 [16, 1024, 2048], P('expert', 'shard'), may hold values from -3 to 3
- out_cotangent: float32 [8, 512, 2048], P('expert', 'shard'), may hold values from -6 to 6
Outputs:
- block_output: float32 [8, 512, 2048], P('expert', 'shard')
- grad_input: float32 [8, 512, 2048], P('expert', 'shard')
- grad_attn_gain: float32 [2048], P('shard')
- grad_w_query: float32 [2048, 2048], P('shard')
- grad_w_key: float32 [2048, 2048], P('shard')
- grad_w_value: float32 [2048, 2048], P('shard')
- grad_query_gain: float32 [2048], P('shard')
- grad_key_gain: float32 [2048], P('shard')
- grad_w_output: float32 [2048, 2048], P('shard')
- grad_moe_gain: float32 [2048], P('shard')
- grad_w_router: float32 [2048, 16], P('shard')
- grad_w_gate: float32 [16, 2048, 1024], P('expert', None, 'shard')
- grad_w_up: float32 [16, 2048, 1024], P('expert', None, 'shard')
- grad_w_down: float32 [16, 1024, 2048], P('expert', 'shard')
Inputs may be any that keep to these rules, and one draw needn't show every extreme that they name: `expert_routes`: each row names 8 different experts. The rows of one device name any one expert at most 96 times, and in some device's rows some expert is named exactly 96 times. `segment_ids`: segment ids never fall along a group; each sequence has 128 to 384 tokens.
All inputs are finite; a program needn't handle non-finite values.
Results may differ from a plain program's by a relative error of at most 0.025.
Values may be sent and summed in bfloat16 or wider, within the bound.
No kernel may reach another device: no remote copies, remote signals or barrier semaphores. Data moves between devices by JAX's collectives and lax.ppermute only.
A program may use at most 448 MiB of HBM per device.

v0:
```python
import jax
import jax.numpy as jnp
from jax import lax
from jax.sharding import PartitionSpec as P

HEADS = 16
HEAD_DIM = 128
TOP = 8


epsilon = 1e-05


def rms_scale(values):
    return lax.rsqrt(jnp.mean(values * values, axis=-1, keepdims=True) + epsilon)


def rope_tables(positions):
    half_dim = HEAD_DIM // 2
    inverse = 10000.0 ** (-(jnp.arange(half_dim).astype(jnp.float32) * 2.0) / HEAD_DIM)
    angles = positions[:, None] * inverse[None, :]
    cosine = jnp.concatenate([jnp.cos(angles), jnp.cos(angles)], axis=-1)[:, None, :]
    sine_part = jnp.concatenate([jnp.sin(angles), jnp.sin(angles)], axis=-1)[:, None, :]
    return (cosine, sine_part)


def rope_apply(values, cosine, sine_part):
    half_dim = values.shape[-1] // 2
    turned = jnp.concatenate([-values[..., half_dim:], values[..., :half_dim]], axis=-1)
    return values * cosine + turned * sine_part


def rope_back(grad_values, cosine, sine_part):
    half_dim = grad_values.shape[-1] // 2
    scaled = grad_values * sine_part
    turned = jnp.concatenate([scaled[..., half_dim:], -scaled[..., :half_dim]], axis=-1)
    return grad_values * cosine + turned


def norm_back(grad_out, source, scale_now, gain_now):
    weighted = grad_out * gain_now
    inner_mean = jnp.mean(weighted * source, axis=-1, keepdims=True)
    grad_source = scale_now * (weighted - source * scale_now * scale_now * inner_mean)
    grad_gain = jnp.sum(grad_out * source * scale_now, axis=0)
    return (grad_source, grad_gain)


def masked_scores(q_heads, k_heads, allowed):
    raw_scores = jnp.einsum(
        "qhd,khd->hqk", q_heads, k_heads, preferred_element_type=jnp.float32
    ) * HEAD_DIM ** (-0.5)
    return jnp.where(allowed[None], raw_scores, -1e30)


def expert_front(arrived, gate_w, up_w, down_w):
    gate_pre = jnp.einsum("erd,edf->erf", arrived, gate_w, preferred_element_type=jnp.float32)
    up_pre = jnp.einsum("erd,edf->erf", arrived, up_w, preferred_element_type=jnp.float32)
    sigmoid_gate = jax.nn.sigmoid(gate_pre)
    silu_gate = gate_pre * sigmoid_gate
    hidden_b = (silu_gate * up_pre).astype(jnp.bfloat16)
    partial_out = jnp.einsum("erf,efd->erd", hidden_b, down_w, preferred_element_type=jnp.float32)
    return ((gate_pre, up_pre, sigmoid_gate, silu_gate, hidden_b), partial_out)


def expert_back(arrived, grad_arrived, kept, gate_w, up_w, down_w):
    gate_pre, up_pre, sigmoid_gate, silu_gate, hidden_b = kept
    grad_down = jnp.einsum(
        "erf,erd->efd", hidden_b, grad_arrived, preferred_element_type=jnp.float32
    )
    grad_hidden = jnp.einsum(
        "erd,efd->erf", grad_arrived, down_w, preferred_element_type=jnp.float32
    )
    gate_grad_b = (
        grad_hidden * up_pre * sigmoid_gate * (1.0 + gate_pre * (1.0 - sigmoid_gate))
    ).astype(jnp.bfloat16)
    up_grad_b = (grad_hidden * silu_gate).astype(jnp.bfloat16)
    grad_gate = jnp.einsum("erd,erf->edf", arrived, gate_grad_b, preferred_element_type=jnp.float32)
    grad_up = jnp.einsum("erd,erf->edf", arrived, up_grad_b, preferred_element_type=jnp.float32)
    back_part = jnp.einsum(
        "erf,edf->erd", gate_grad_b, gate_w, preferred_element_type=jnp.float32
    ) + jnp.einsum("erf,edf->erd", up_grad_b, up_w, preferred_element_type=jnp.float32)
    return (grad_gate, grad_up, grad_down, back_part)


def on_device(
    block_input,
    segment_ids,
    expert_routes,
    attn_gain,
    w_query,
    w_key,
    w_value,
    query_gain,
    key_gain,
    w_output,
    moe_gain,
    w_router,
    w_gate,
    w_up,
    w_down,
    out_cotangent,
):
    expert_count = lax.axis_size("expert")
    tok_count = block_input.shape[1]
    group_count = segment_ids.shape[1]
    model_width = block_input.shape[2]
    local_experts = w_gate.shape[0]
    experts_all = local_experts * expert_count
    capacity = max(2, 3 * TOP * tok_count // (2 * experts_all))
    slot_total = experts_all * capacity
    assignments = tok_count * TOP
    gathered = (
        lax.all_gather(w_query, "shard", axis=0, tiled=True),
        lax.all_gather(w_key, "shard", axis=0, tiled=True),
        lax.all_gather(w_value, "shard", axis=0, tiled=True),
        lax.all_gather(w_output, "shard", axis=0, tiled=True),
        lax.all_gather(w_router, "shard", axis=0, tiled=True),
        lax.all_gather(attn_gain, "shard", axis=0, tiled=True),
        lax.all_gather(query_gain, "shard", axis=0, tiled=True),
        lax.all_gather(key_gain, "shard", axis=0, tiled=True),
        lax.all_gather(moe_gain, "shard", axis=0, tiled=True),
    )
    (
        query_all,
        key_all,
        value_all,
        output_all,
        router_all,
        gain_one,
        gain_query,
        gain_key,
        gain_two,
    ) = gathered
    gain_one = gain_one.astype(jnp.float32)
    gain_query = gain_query.astype(jnp.float32)
    gain_key = gain_key.astype(jnp.float32)
    gain_two = gain_two.astype(jnp.float32)
    first_row = lax.axis_index("shard") * tok_count
    query_index = first_row + jnp.arange(tok_count)
    cosine, sine_part = rope_tables(query_index.astype(jnp.float32))
    source = block_input[0].astype(jnp.float32)
    scale_one = rms_scale(source)
    normed = (source * scale_one * gain_one).astype(jnp.bfloat16)
    q_proj = jnp.dot(normed, query_all, preferred_element_type=jnp.float32)
    k_proj = jnp.dot(normed, key_all, preferred_element_type=jnp.float32)
    v_local = jnp.dot(normed, value_all, preferred_element_type=jnp.float32).astype(jnp.bfloat16)
    q_scale = rms_scale(q_proj)
    k_scale = rms_scale(k_proj)
    q_heads = rope_apply(
        (q_proj * q_scale * gain_query).reshape(tok_count, HEADS, HEAD_DIM), cosine, sine_part
    ).astype(jnp.bfloat16)
    k_local = rope_apply(
        (k_proj * k_scale * gain_key).reshape(tok_count, HEADS, HEAD_DIM), cosine, sine_part
    ).astype(jnp.bfloat16)
    k_group, v_group = (
        lax.all_gather(k_local.reshape(tok_count, model_width), "shard", axis=0, tiled=True),
        lax.all_gather(v_local, "shard", axis=0, tiled=True),
    )
    k_group = k_group.reshape(group_count, HEADS, HEAD_DIM)
    v_group = v_group.reshape(group_count, HEADS, HEAD_DIM)
    seg_all = segment_ids[0]
    seg_query = lax.dynamic_slice_in_dim(seg_all, first_row, tok_count)
    key_index = jnp.arange(group_count)
    allowed = (seg_query[:, None] == seg_all[None, :]) & (
        key_index[None, :] <= query_index[:, None]
    )
    scores = masked_scores(q_heads, k_group, allowed)
    top_score = jnp.max(scores, axis=-1, keepdims=True)
    log_total = top_score + jnp.log(jnp.sum(jnp.exp(scores - top_score), axis=-1, keepdims=True))
    probs_b = jnp.exp(scores - log_total).astype(jnp.bfloat16)
    attended = (
        jnp.einsum("hqk,khd->qhd", probs_b, v_group, preferred_element_type=jnp.float32)
        .astype(jnp.bfloat16)
        .reshape(tok_count, model_width)
    )
    residual = source + jnp.dot(attended, output_all, preferred_element_type=jnp.float32)
    scale_two = rms_scale(residual)
    mixed_in = (residual * scale_two * gain_two).astype(jnp.bfloat16)
    logits = jnp.dot(mixed_in, router_all, preferred_element_type=jnp.float32)
    powers = jnp.exp(logits)
    router_probs = powers / jnp.sum(powers, axis=-1, keepdims=True)
    routes = expert_routes[0]
    one_hot = (routes[:, :, None] == jnp.arange(experts_all)[None, None, :]).astype(jnp.float32)
    chosen = jnp.sum(router_probs[:, None, :] * one_hot, axis=-1)
    flat_routes = routes.reshape(assignments)
    route_hits = (flat_routes[:, None] == jnp.arange(experts_all)[None, :]).astype(jnp.int32)
    earlier = jnp.cumsum(route_hits, axis=0) - route_hits
    slot_within = jnp.sum(earlier * route_hits, axis=1)
    owner_major = (
        flat_routes % local_experts * expert_count + flat_routes // local_experts
    ) * capacity + slot_within
    repeated = jnp.repeat(mixed_in, TOP, axis=0)
    gate_use, up_use, down_use = (
        lax.all_gather(w_gate, "shard", axis=2, tiled=True),
        lax.all_gather(w_up, "shard", axis=2, tiled=True),
        lax.all_gather(w_down, "shard", axis=1, tiled=True),
    )
    outgoing = (
        jnp.zeros((slot_total, model_width), jnp.bfloat16)
        .at[owner_major]
        .set(repeated)
        .reshape(local_experts, expert_count * capacity, model_width)
    )
    arrived = lax.all_to_all(outgoing, "expert", split_axis=1, concat_axis=1, tiled=True)
    kept, partial_out = expert_front(arrived, gate_use, up_use, down_use)
    returned = lax.all_to_all(
        partial_out.astype(jnp.bfloat16), "expert", split_axis=1, concat_axis=1, tiled=True
    )
    y_float = (
        returned.reshape(slot_total, model_width)[owner_major]
        .reshape(tok_count, TOP, model_width)
        .astype(jnp.float32)
    )
    block_output = residual + jnp.sum(chosen[:, :, None] * y_float, axis=1)
    cotangent = out_cotangent[0]
    chosen_grad = jnp.sum(cotangent[:, None, :] * y_float, axis=-1)
    grad_rows = (
        (chosen[:, :, None] * cotangent[:, None, :])
        .astype(jnp.bfloat16)
        .reshape(assignments, model_width)
    )
    grad_outgoing = (
        jnp.zeros((slot_total, model_width), jnp.bfloat16)
        .at[owner_major]
        .set(grad_rows)
        .reshape(local_experts, expert_count * capacity, model_width)
    )
    grad_arrived = lax.all_to_all(grad_outgoing, "expert", split_axis=1, concat_axis=1, tiled=True)
    whole_gate, whole_up, whole_down, back_part = expert_back(
        arrived, grad_arrived, kept, gate_use, up_use, down_use
    )
    back_returned = lax.all_to_all(
        back_part.astype(jnp.bfloat16), "expert", split_axis=1, concat_axis=1, tiled=True
    )
    back_rows = (
        back_returned.reshape(slot_total, model_width)[owner_major]
        .reshape(tok_count, TOP, model_width)
        .astype(jnp.float32)
    )
    grad_w_gate, grad_w_up, grad_w_down = (
        lax.psum_scatter(
            whole_gate.astype(jnp.bfloat16), "shard", scatter_dimension=2, tiled=True
        ).astype(jnp.float32),
        lax.psum_scatter(
            whole_up.astype(jnp.bfloat16), "shard", scatter_dimension=2, tiled=True
        ).astype(jnp.float32),
        lax.psum_scatter(
            whole_down.astype(jnp.bfloat16), "shard", scatter_dimension=1, tiled=True
        ).astype(jnp.float32),
    )
    prob_grad = jnp.sum(chosen_grad[:, :, None] * one_hot, axis=1)
    logit_grad = (
        router_probs * (prob_grad - jnp.sum(router_probs * prob_grad, axis=-1, keepdims=True))
    ).astype(jnp.bfloat16)
    grad_router = jnp.dot(mixed_in.T, logit_grad, preferred_element_type=jnp.float32)
    mixed_grad = jnp.sum(back_rows, axis=1) + jnp.dot(
        logit_grad, router_all.T, preferred_element_type=jnp.float32
    )
    residual_norm_grad, grad_gain_two = norm_back(mixed_grad, residual, scale_two, gain_two)
    residual_grad = cotangent + residual_norm_grad
    residual_grad_b = residual_grad.astype(jnp.bfloat16)
    grad_output_w = jnp.dot(attended.T, residual_grad_b, preferred_element_type=jnp.float32)
    attended_grad = (
        jnp.dot(residual_grad_b, output_all.T, preferred_element_type=jnp.float32)
        .astype(jnp.bfloat16)
        .reshape(tok_count, HEADS, HEAD_DIM)
    )
    probs_full = jnp.exp(masked_scores(q_heads, k_group, allowed) - log_total)
    delta_rows = jnp.einsum(
        "qhd,qhd->hq",
        attended_grad,
        attended.reshape(tok_count, HEADS, HEAD_DIM),
        preferred_element_type=jnp.float32,
    )
    prob_value = jnp.einsum(
        "qhd,khd->hqk", attended_grad, v_group, preferred_element_type=jnp.float32
    )
    score_grad = (probs_full * (prob_value - delta_rows[:, :, None])).astype(jnp.bfloat16)
    query_grad = jnp.einsum(
        "hqk,khd->qhd", score_grad, k_group, preferred_element_type=jnp.float32
    ) * HEAD_DIM ** (-0.5)
    key_part = jnp.einsum(
        "hqk,qhd->khd", score_grad, q_heads, preferred_element_type=jnp.float32
    ) * HEAD_DIM ** (-0.5)
    value_part = jnp.einsum(
        "hqk,qhd->khd", probs_b, attended_grad, preferred_element_type=jnp.float32
    )
    key_grad, value_grad = (
        lax.psum_scatter(
            key_part.reshape(group_count, model_width).astype(jnp.bfloat16),
            "shard",
            scatter_dimension=0,
            tiled=True,
        ).astype(jnp.float32),
        lax.psum_scatter(
            value_part.reshape(group_count, model_width).astype(jnp.bfloat16),
            "shard",
            scatter_dimension=0,
            tiled=True,
        ).astype(jnp.float32),
    )
    query_pre = rope_back(query_grad, cosine, sine_part).reshape(tok_count, model_width)
    key_pre = rope_back(key_grad.reshape(tok_count, HEADS, HEAD_DIM), cosine, sine_part).reshape(
        tok_count, model_width
    )
    q_proj_grad, grad_gain_query = norm_back(query_pre, q_proj, q_scale, gain_query)
    k_proj_grad, grad_gain_key = norm_back(key_pre, k_proj, k_scale, gain_key)
    q_grad_b = q_proj_grad.astype(jnp.bfloat16)
    k_grad_b = k_proj_grad.astype(jnp.bfloat16)
    v_grad_b = value_grad.astype(jnp.bfloat16)
    grad_query_w = jnp.dot(normed.T, q_grad_b, preferred_element_type=jnp.float32)
    grad_key_w = jnp.dot(normed.T, k_grad_b, preferred_element_type=jnp.float32)
    grad_value_w = jnp.dot(normed.T, v_grad_b, preferred_element_type=jnp.float32)
    normed_grad = (
        jnp.dot(q_grad_b, query_all.T, preferred_element_type=jnp.float32)
        + jnp.dot(k_grad_b, key_all.T, preferred_element_type=jnp.float32)
        + jnp.dot(v_grad_b, value_all.T, preferred_element_type=jnp.float32)
    )
    input_norm_grad, grad_gain_one = norm_back(normed_grad, source, scale_one, gain_one)
    grad_input = residual_grad + input_norm_grad
    shared_grads = (
        lax.psum_scatter(
            grad_gain_one.astype(jnp.bfloat16), "shard", scatter_dimension=0, tiled=True
        ).astype(jnp.float32),
        lax.psum_scatter(
            grad_query_w.astype(jnp.bfloat16), "shard", scatter_dimension=0, tiled=True
        ).astype(jnp.float32),
        lax.psum_scatter(
            grad_key_w.astype(jnp.bfloat16), "shard", scatter_dimension=0, tiled=True
        ).astype(jnp.float32),
        lax.psum_scatter(
            grad_value_w.astype(jnp.bfloat16), "shard", scatter_dimension=0, tiled=True
        ).astype(jnp.float32),
        lax.psum_scatter(
            grad_gain_query.astype(jnp.bfloat16), "shard", scatter_dimension=0, tiled=True
        ).astype(jnp.float32),
        lax.psum_scatter(
            grad_gain_key.astype(jnp.bfloat16), "shard", scatter_dimension=0, tiled=True
        ).astype(jnp.float32),
        lax.psum_scatter(
            grad_output_w.astype(jnp.bfloat16), "shard", scatter_dimension=0, tiled=True
        ).astype(jnp.float32),
        lax.psum_scatter(
            grad_gain_two.astype(jnp.bfloat16), "shard", scatter_dimension=0, tiled=True
        ).astype(jnp.float32),
        lax.psum_scatter(
            grad_router.astype(jnp.bfloat16), "shard", scatter_dimension=0, tiled=True
        ).astype(jnp.float32),
    )
    shared_grads = (
        lax.psum(shared_grads[0].astype(jnp.bfloat16), "expert").astype(jnp.float32),
        lax.psum(shared_grads[1].astype(jnp.bfloat16), "expert").astype(jnp.float32),
        lax.psum(shared_grads[2].astype(jnp.bfloat16), "expert").astype(jnp.float32),
        lax.psum(shared_grads[3].astype(jnp.bfloat16), "expert").astype(jnp.float32),
        lax.psum(shared_grads[4].astype(jnp.bfloat16), "expert").astype(jnp.float32),
        lax.psum(shared_grads[5].astype(jnp.bfloat16), "expert").astype(jnp.float32),
        lax.psum(shared_grads[6].astype(jnp.bfloat16), "expert").astype(jnp.float32),
        lax.psum(shared_grads[7].astype(jnp.bfloat16), "expert").astype(jnp.float32),
        lax.psum(shared_grads[8].astype(jnp.bfloat16), "expert").astype(jnp.float32),
    )
    return (
        (block_output[None], grad_input[None])
        + tuple(shared_grads)
        + (grad_w_gate, grad_w_up, grad_w_down)
    )


def solution(mesh):
    placed = (
        P("expert", "shard", None),
        P("expert", None),
        P("expert", "shard", None),
        P("shard"),
        P("shard", None),
        P("shard", None),
        P("shard", None),
        P("shard"),
        P("shard"),
        P("shard", None),
        P("shard"),
        P("shard", None),
        P("expert", None, "shard"),
        P("expert", None, "shard"),
        P("expert", "shard", None),
        P("expert", "shard", None),
    )
    return jax.shard_map(
        on_device,
        mesh=mesh,
        in_specs=placed,
        out_specs=(
            P("expert", "shard", None),
            P("expert", "shard", None),
            P("shard"),
            P("shard", None),
            P("shard", None),
            P("shard", None),
            P("shard"),
            P("shard"),
            P("shard", None),
            P("shard"),
            P("shard", None),
            P("expert", None, "shard"),
            P("expert", None, "shard"),
            P("expert", "shard", None),
        ),
        check_vma=False,
    )
```

profile of v0, /device:TPU:0, one launch (start us, length us, event | category | flops | bytes accessed | tf_op | source)
XLA Modules:
  0.0 2066.4 jit_solution(11814601134856175152)
XLA Ops:
  9.5 9.5 all-gather
  19.1 8.1 all-gather.2
  27.2 7.1 all-gather.1
  37.5 62.9 %all-gather.20.cloned.1.call-done = bf16[2048,2048]{1,0:T(8,128)(2,1)} async-done(((bf16[512,2048]{1,0:T(8,128)(2,1)}), bf16[2048,2048]{1,0:T(8,128)(2,1)}) %all-gather.20.cloned.1.call-update) | async-done | bytes 8388624 | tf_op jit(solution)/shard_map/all_gather | solution.py:114
  106.6 83.2 %all-gather.18.cloned.1.call-done = bf16[2048,2048]{1,0:T(8,128)(2,1)} async-done(((bf16[512,2048]{1,0:T(8,128)(2,1)}), bf16[2048,2048]{1,0:T(8,128)(2,1)}) %all-gather.18.cloned.1.call-update) | async-done | bytes 8388624 | tf_op jit(solution)/shard_map/all_gather | solution.py:113
  205.3 74.0 %all-gather.14.cloned.1.call-done = bf16[2048,2048]{1,0:T(8,128)(2,1)} async-done(((bf16[512,2048]{1,0:T(8,128)(2,1)}), bf16[2048,2048]{1,0:T(8,128)(2,1)}) %all-gather.14.cloned.1.call-update) | async-done | bytes 8388624 | tf_op jit(solution)/shard_map/all_gather | solution.py:115
  292.4 8.2 all-gather.3
  300.8 16.2 all-gather.22.cloned.1.call-done
  324.2 30.4 %all-gather.16.cloned.1.call-done = bf16[512,2048]{1,0:T(8,128)(2,1)} async-done(((bf16[128,2048]{1,0:T(8,128)(2,1)}), bf16[512,2048]{1,0:T(8,128)(2,1)}) %all-gather.16.cloned.1.call-update) | async-done | bytes 2097168 | tf_op jit(solution)/shard_map/all_gather | solution.py:157
  359.0 84.9 %all-gather.24.cloned.1.call-done = bf16[2048,2048]{1,0:T(8,128)(2,1)} async-done(((bf16[512,2048]{1,0:T(8,128)(2,1)}), bf16[2048,2048]{1,0:T(8,128)(2,1)}) %all-gather.24.cloned.1.call-update) | async-done | bytes 8388624 | tf_op jit(solution)/shard_map/all_gather | solution.py:116
  449.8 10.6 scatter_custom_fusion
  460.4 12.7 copy.211
  478.7 8.2 all_gather.52
  487.5 10.6 scatter_custom_fusion.1
  498.1 12.6 copy.217
  510.7 106.2 %all-to-all-done = bf16[2,768,2048]{2,0,1:T(2,128)(2,1)} async-done(((bf16[2,768,2048]{2,0,1:T(2,128)(2,1)}), bf16[2,768,2048]{2,0,1:T(2,128)(2,1)}, u32[]{:S(2)}, u32[]{:S(2)}) %all-to-all-start) | async-done | bytes 6291488 | tf_op jit(solution)/shard_map/all_to_all | solution.py:204
  621.7 16.4 copy.230
  638.1 13.0 fusion.72
  651.1 13.0 fusion.73
  664.1 48.0 %all-gather.30.cloned.1.call-done = bf16[2,1024,2048]{2,1,0:T(8,128)(2,1)} async-done(((bf16[2,256,2048]{2,1,0:T(8,128)(2,1)}), bf16[2,1024,2048]{2,1,0:T(8,128)(2,1)}) %all-gather.30.cloned.1.call-update) | async-done | bytes 8388624 | tf_op jit(solution)/shard_map/all_gather | solution.py:196
  712.1 48.6 %all-to-all-done.2 = bf16[2,768,2048]{2,0,1:T(2,128)(2,1)} async-done(((bf16[2,768,2048]{2,0,1:T(2,128)(2,1)}), bf16[2,768,2048]{2,0,1:T(2,128)(2,1)}, u32[]{:S(2)}, u32[]{:S(2)}) %all-to-all-start.2) | async-done | bytes 6291488 | tf_op jit(solution)/shard_map/all_to_all | solution.py:228
  760.7 20.4 multiply_convert_fusion
  781.1 10.7 convolution_convert_fusion.6
  791.8 18.8 copy.214
  815.6 13.5 fusion.74
  829.0 14.3 add_convert_fusion
  843.3 12.6 copy.219
  855.9 98.6 %all-to-all-done.1 = bf16[2,768,2048]{2,0,1:T(2,128)(2,1)} async-done(((bf16[2,768,2048]{2,0,1:T(2,128)(2,1)}), bf16[2,768,2048]{2,0,1:T(2,128)(2,1)}, u32[]{:S(2)}, u32[]{:S(2)}) %all-to-all-start.1) | async-done | bytes 6291488 | tf_op jit(solution)/shard_map/all_to_all | solution.py:206
  959.4 8.3 copy.215
  967.7 12.8 gather_fusion
  985.5 112.8 %all-to-all-done.3 = bf16[2,768,2048]{2,0,1:T(2,128)(2,1)} async-done(((bf16[2,768,2048]{2,0,1:T(2,128)(2,1)}), bf16[2,768,2048]{2,0,1:T(2,128)(2,1)}, u32[]{:S(2)}, u32[]{:S(2)}) %all-to-all-start.3) | async-done | bytes 6291488 | tf_op jit(solution)/shard_map/all_to_all | solution.py:232
  1098.2 8.3 copy.220
  1106.6 12.6 gather_fusion.1
  1180.2 6.8 convolution_convert_fusion.1
  1187.5 27.2 %reduce-scatter.13.cloned.1.call-done = bf16[128,2048]{1,0:T(8,128)(2,1)} async-done(((bf16[512,2048]{1,0:T(8,128)(2,1)}), bf16[128,2048]{1,0:T(8,128)(2,1)}) %reduce-scatter.13.cloned.1.call-update) | async-done | bytes 524304 | tf_op jit(solution)/shard_map/reduce_scatter | solution.py:289
  1232.8 15.4 fusion.8
  1248.3 12.0 convolution_convert_fusion.5
  1260.5 12.0 convolution_convert_fusion.4
  1272.6 31.4 %reduce-scatter.21.cloned.1.call-done = bf16[512,2048]{1,0:T(8,128)(2,1)} async-done(((bf16[2048,2048]{1,0:T(8,128)(2,1)}), bf16[512,2048]{1,0:T(8,128)(2,1)}) %reduce-scatter.21.cloned.1.call-update) | async-done | bytes 2097168 | tf_op jit(solution)/shard_map/reduce_scatter | solution.py:340
  1304.0 89.8 %reduce-scatter.15.cloned.1.call-done = bf16[512,2048]{1,0:T(8,128)(2,1)} async-done(((bf16[2048,2048]{1,0:T(8,128)(2,1)}), bf16[512,2048]{1,0:T(8,128)(2,1)}) %reduce-scatter.15.cloned.1.call-update) | async-done | bytes 2097168 | tf_op jit(solution)/shard_map/reduce_scatter | solution.py:325
  1393.8 89.4 %reduce-scatter.19.cloned.1.call-done = bf16[512,2048]{1,0:T(8,128)(2,1)} async-done(((bf16[2048,2048]{1,0:T(8,128)(2,1)}), bf16[512,2048]{1,0:T(8,128)(2,1)}) %reduce-scatter.19.cloned.1.call-update) | async-done | bytes 2097168 | tf_op jit(solution)/shard_map/reduce_scatter | solution.py:331
  1483.2 89.6 %reduce-scatter.17.cloned.1.call-done = bf16[512,2048]{1,0:T(8,128)(2,1)} async-done(((bf16[2048,2048]{1,0:T(8,128)(2,1)}), bf16[512,2048]{1,0:T(8,128)(2,1)}) %reduce-scatter.17.cloned.1.call-update) | async-done | bytes 2097168 | tf_op jit(solution)/shard_map/reduce_scatter | solution.py:328
  1590.7 15.0 all-reduce.6
  1606.0 26.5 %all-reduce.4 = (bf16[512]{0:T(512)(128)(2,1)S(1)}, bf16[512]{0:T(512)(128)(2,1)S(1)}, bf16[512]{0:T(512)(128)(2,1)S(1)}, bf16[512]{0:T(512)(128)(2,1)S(1)}, bf16[512,16]{0,1:T(8,128)(2,1)S(1)}) all-reduce(bf16[512]{0:T(512)(128)(2,1)S(1)} %dynamic-slice.2, ...), channel_id=1, replica_groups=mesh['shard'=4,'expert'=8] {'expert'}, use_global_device_ids=true, to_apply=%region_26.27 | all-reduce | flops 10240 | bytes 40960 | tf_op jit(solution)/shard_map/psum | solution.py:351
  1636.8 52.5 %reduce-scatter.29.cloned.1.call-done = bf16[2,256,2048]{2,1,0:T(8,128)(2,1)} async-done(((bf16[2,1024,2048]{2,1,0:T(8,128)(2,1)}), bf16[2,256,2048]{2,1,0:T(8,128)(2,1)}) %reduce-scatter.29.cloned.1.call-update) | async-done | bytes 2097168 | tf_op jit(solution)/shard_map/reduce_scatter | solution.py:247
  1693.4 85.2 %reduce-scatter.25.cloned.1.call-done = bf16[2,2048,256]{2,1,0:T(8,128)(2,1)} async-done(((bf16[2,2048,1024]{2,1,0:T(8,128)(2,1)}), bf16[2,2048,256]{2,1,0:T(8,128)(2,1)}) %reduce-scatter.25.cloned.1.call-update) | async-done | bytes 2097168 | tf_op jit(solution)/shard_map/reduce_scatter | solution.py:241
  1782.5 85.8 %reduce-scatter.27.cloned.1.call-done = bf16[2,2048,256]{2,1,0:T(8,128)(2,1)} async-done(((bf16[2,2048,1024]{2,1,0:T(8,128)(2,1)}), bf16[2,2048,256]{2,1,0:T(8,128)(2,1)}) %reduce-scatter.27.cloned.1.call-update) | async-done | bytes 2097168 | tf_op jit(solution)/shard_map/reduce_scatter | solution.py:244
  1872.3 175.2 %all-reduce.9.cloned.1.call-done = (bf16[512,2048]{1,0:T(8,128)(2,1)}, bf16[512,2048]{1,0:T(8,128)(2,1)}, bf16[512,2048]{1,0:T(8,128)(2,1)}, bf16[512,2048]{1,0:T(8,128)(2,1)}) async-done(((bf16[512,2048]{1,0:T(8,128)(2,1)}, bf16[512,2048]{1,0:T(8,128)(2,1)}, bf16[512,2048]{1,0:T(8,128)(2,1)}, bf16[512,2048]{1,0:T(8,128)(2,1)}), (bf16[512,2048]{1,0:T(8,128)(2,1)}, bf16[512,2048]{1,0:T(8,128)(2,1)}, ...) | async-done | bytes 8388624 | tf_op jit(solution)/shard_map/psum | solution.py:352
  (291 shorter events, 208.5 us)
Async XLA Ops:
  7.2 11.9 copy-start.54
  7.2 20.0 copy-start.55
  7.2 93.1 %all-gather.20.cloned.1.call-start = ((), (), s32[]{:S(2)}) async-start(), calls=%async_computation.17 | async-start | bytes 10485760 | tf_op jit(solution)/shard_map/all_gather | solution.py:114
  7.9 29.3 %copy-start = (bf16[1,128,2048]{2,1,0:T(8,128)(2,1)S(1)}, bf16[1,128,2048]{2,1,0:T(8,128)(2,1)}, u32[]{:S(2)}) copy-start(bf16[1,128,2048]{2,1,0:T(8,128)(2,1)} %param.16) | copy-start | bytes 1572868
  8.0 181.9 %all-gather.18.cloned.1.call-start = ((), (), s32[]{:S(2)}) async-start(), calls=%async_computation.16 | async-start | bytes 10485760 | tf_op jit(solution)/shard_map/all_gather | solution.py:113
  8.7 270.6 %all-gather.14.cloned.1.call-start = ((), (), s32[]{:S(2)}) async-start(), calls=%async_computation.14 | async-start | bytes 10485760 | tf_op jit(solution)/shard_map/all_gather | solution.py:115
  9.4 307.5 %all-gather.22.cloned.1.call-start = ((), (), s32[]{:S(2)}) async-start(), calls=%async_computation.18 | async-start | bytes 2621440 | tf_op jit(solution)/shard_map/all_gather | solution.py:156
  19.1 260.2 %copy-start.21 = (f32[4,1,512]{2,1,0:T(1,128)}, f32[4,1,512]{2,1,0:T(1,128)S(1)}, u32[]{:S(2)}) copy-start(f32[4,1,512]{2,1,0:T(1,128)S(1)} %convert_element_type.299) | copy-start | bytes 24580
  27.2 175.7 %copy-start.34 = (f32[4,1,512]{2,1,0:T(1,128)}, f32[4,1,512]{2,1,0:T(1,128)S(1)}, u32[]{:S(2)}) copy-start(f32[4,1,512]{2,1,0:T(1,128)S(1)} %convert_element_type.301) | copy-start | bytes 24580
  34.3 160.3 %copy-start.36 = (f32[4,1,512]{2,1,0:T(1,128)}, f32[4,1,512]{2,1,0:T(1,128)S(1)}, u32[]{:S(2)}) copy-start(f32[4,1,512]{2,1,0:T(1,128)S(1)} %convert_element_type.300) | copy-start | bytes 24580
  37.3 162.6 %copy-start.30 = (f32[128,128]{0,1:T(8,128)}, f32[128,128]{0,1:T(8,128)S(1)}, u32[]{:S(2)}) copy-start(f32[128,128]{0,1:T(8,128)S(1)} %get-tuple-element.56) | copy-start | bytes 196612
  37.5 241.8 %copy-start.40 = (f32[128]{0:T(128)}, f32[128]{0:T(128)S(1)}, u32[]{:S(2)}) copy-start(f32[128]{0:T(128)S(1)} %add_rsqrt_fusion.3) | copy-start | bytes 1540
  105.1 97.8 %copy-start.3 = (f32[128,2048]{1,0:T(8,128)}, f32[128,2048]{1,0:T(8,128)S(1)}, u32[]{:S(2)}) copy-start(f32[128,2048]{1,0:T(8,128)S(1)} %get-tuple-element.60) | copy-start | bytes 3145732
  105.1 97.8 %copy-start.46 = (f32[128]{0:T(128)}, f32[128]{0:T(128)S(1)}, u32[]{:S(2)}) copy-start(f32[128]{0:T(128)S(1)} %add_rsqrt_fusion.1) | copy-start | bytes 1540
  201.1 118.8 %copy-start.17 = (bf16[128,16,128]{0,2,1:T(8,128)(2,1)}, bf16[128,16,128]{0,2,1:T(8,128)(2,1)S(1)}, u32[]{:S(2)}) copy-start(bf16[128,16,128]{0,2,1:T(8,128)(2,1)S(1)} %get-tuple-element.52) | copy-start | bytes 1572868
  205.3 149.3 %all-gather.16.cloned.1.call-start = ((), (), s32[]{:S(2)}) async-start(), calls=%async_computation.15 | async-start | bytes 2621440 | tf_op jit(solution)/shard_map/all_gather | solution.py:157
  284.8 7.5 copy-start.56
  284.8 15.8 copy-start.52
  284.8 159.1 %all-gather.24.cloned.1.call-start = ((), (), s32[]{:S(2)}) async-start(), calls=%async_computation.19 | async-start | bytes 10485760 | tf_op jit(solution)/shard_map/all_gather | solution.py:116
  285.4 352.7 %all-gather.26.cloned.1.call-start = ((), (), s32[]{:S(2)}) async-start(), calls=%async_computation.20 | async-start | bytes 10485760 | tf_op jit(solution)/shard_map/all_gather | solution.py:194
  286.2 365.0 %all-gather.28.cloned.1.call-start = ((), (), s32[]{:S(2)}) async-start(), calls=%async_computation.21 | async-start | bytes 10485760 | tf_op jit(solution)/shard_map/all_gather | solution.py:195
  300.6 148.1 %copy-start.38 = (f32[4,1,512]{2,1,0:T(1,128)}, f32[4,1,512]{2,1,0:T(1,128)S(1)}, u32[]{:S(2)}) copy-start(f32[4,1,512]{2,1,0:T(1,128)S(1)} %convert_element_type.302) | copy-start | bytes 24580
  300.8 53.8 %copy-start.28 = (pred[128,512]{1,0:T(8,128)(4,1)}, pred[128,512]{1,0:T(8,128)(4,1)S(1)}, u32[]{:S(2)}) copy-start(pred[128,512]{1,0:T(8,128)(4,1)S(1)} %fusion.47) | copy-start | bytes 196612
  324.2 34.8 %copy-start.43 = (f32[16,128]{1,0:T(8,128)}, f32[16,128]{1,0:T(8,128)S(1)}, u32[]{:S(2)}) copy-start(f32[16,128]{1,0:T(8,128)S(1)} %log_add_fusion) | copy-start | bytes 24580
  359.0 89.7 %copy-start.11 = (bf16[16,128,128]{2,1,0:T(8,128)(2,1)}, bf16[16,128,128]{2,1,0:T(8,128)(2,1)S(1)}, u32[]{:S(2)}) copy-start(bf16[16,128,128]{2,1,0:T(8,128)(2,1)S(1)} %fusion.27) | copy-start | bytes 1572868
  448.7 11.8 copy-start.50
  449.8 37.2 %copy-start.15 = (bf16[128,2048]{1,0:T(8,128)(2,1)}, bf16[128,2048]{1,0:T(8,128)(2,1)S(1)}, u32[]{:S(2)}) copy-start(bf16[128,2048]{1,0:T(8,128)(2,1)S(1)} %multiply_convert_fusion.7) | copy-start | bytes 1572868
  473.1 14.4 copy-start.13
  473.1 143.8 %all-to-all-start = ((bf16[2,768,2048]{2,0,1:T(2,128)(2,1)}), bf16[2,768,2048]{2,0,1:T(2,128)(2,1)}, u32[]{:S(2)}, u32[]{:S(2)}) async-start(bf16[2,768,2048]{2,0,1:T(2,128)(2,1)} %copy.211), calls=%async_computation | async-start | bytes 12582912 | tf_op jit(solution)/shard_map/all_to_all | solution.py:204
  478.0 234.1 %all-gather.30.cloned.1.call-start = ((), (), s32[]{:S(2)}) async-start(), calls=%async_computation.22 | async-start | bytes 10485760 | tf_op jit(solution)/shard_map/all_gather | solution.py:196
  616.9 143.7 %all-to-all-start.2 = ((bf16[2,768,2048]{2,0,1:T(2,128)(2,1)}), bf16[2,768,2048]{2,0,1:T(2,128)(2,1)}, u32[]{:S(2)}, u32[]{:S(2)}) async-start(bf16[2,768,2048]{2,0,1:T(2,128)(2,1)} %copy.217), calls=%async_computation.2 | async-start | bytes 12582912 | tf_op jit(solution)/shard_map/all_to_all | solution.py:228
  810.6 143.9 %all-to-all-start.1 = ((bf16[2,768,2048]{2,0,1:T(2,128)(2,1)}), bf16[2,768,2048]{2,0,1:T(2,128)(2,1)}, u32[]{:S(2)}, u32[]{:S(2)}) async-start(bf16[2,768,2048]{2,0,1:T(2,128)(2,1)} %copy.214), calls=%async_computation.1 | async-start | bytes 12582912 | tf_op jit(solution)/shard_map/all_to_all | solution.py:206
  954.5 143.7 %all-to-all-start.3 = ((bf16[2,768,2048]{2,0,1:T(2,128)(2,1)}), bf16[2,768,2048]{2,0,1:T(2,128)(2,1)}, u32[]{:S(2)}, u32[]{:S(2)}) async-start(bf16[2,768,2048]{2,0,1:T(2,128)(2,1)} %copy.219), calls=%async_computation.3 | async-start | bytes 12582912 | tf_op jit(solution)/shard_map/all_to_all | solution.py:232
  959.3 220.9 %reduce-scatter.31.cloned.1.call-start = ((), (), s32[]{:S(2)}) async-start(), calls=%async_computation.32 | async-start | bytes 2621440
  1126.2 6.9 copy-start.29
  1126.2 6.9 copy-start.44
  1142.3 72.4 %reduce-scatter.13.cloned.1.call-start = ((), (), s32[]{:S(2)}) async-start(), calls=%async_computation.23 | async-start | bytes 2621440 | tf_op jit(solution)/shard_map/reduce_scatter | solution.py:289
  1157.7 146.3 %reduce-scatter.21.cloned.1.call-start = ((), (), s32[]{:S(2)}) async-start(), calls=%async_computation.27 | async-start | bytes 10485760 | tf_op jit(solution)/shard_map/reduce_scatter | solution.py:340
  1163.6 230.2 %reduce-scatter.15.cloned.1.call-start = ((), (), s32[]{:S(2)}) async-start(), calls=%async_computation.24 | async-start | bytes 10485760 | tf_op jit(solution)/shard_map/reduce_scatter | solution.py:325
  1180.1 303.0 %reduce-scatter.19.cloned.1.call-start = ((), (), s32[]{:S(2)}) async-start(), calls=%async_computation.26 | async-start | bytes 10485760 | tf_op jit(solution)/shard_map/reduce_scatter | solution.py:331
  1187.0 29.9 %copy-start.31 = (f32[128,128]{0,1:T(8,128)S(1)}, f32[128,128]{0,1:T(8,128)}, u32[]{:S(2)}) copy-start(f32[128,128]{0,1:T(8,128)} %copy-done.30) | copy-start | bytes 196612
  1187.0 385.8 %reduce-scatter.17.cloned.1.call-start = ((), (), s32[]{:S(2)}) async-start(), calls=%async_computation.25 | async-start | bytes 10485760 | tf_op jit(solution)/shard_map/reduce_scatter | solution.py:328
  1230.9 375.1 %reduce-scatter.23.cloned.1.call-start = ((), (), s32[]{:S(2)}) async-start(), calls=%async_computation.28 | async-start | bytes 81920 | tf_op jit(solution)/shard_map/reduce_scatter | solution.py:346
  1232.8 456.5 %reduce-scatter.29.cloned.1.call-start = ((), (), s32[]{:S(2)}) async-start(), calls=%async_computation.31 | async-start | bytes 10485760 | tf_op jit(solution)/shard_map/reduce_scatter | solution.py:247
  1248.2 530.4 %reduce-scatter.25.cloned.1.call-start = ((), (), s32[]{:S(2)}) async-start(), calls=%async_computation.29 | async-start | bytes 10485760 | tf_op jit(solution)/shard_map/reduce_scatter | solution.py:241
  1260.3 608.1 %reduce-scatter.27.cloned.1.call-start = ((), (), s32[]{:S(2)}) async-start(), calls=%async_computation.30 | async-start | bytes 10485760 | tf_op jit(solution)/shard_map/reduce_scatter | solution.py:244
  1272.6 774.9 %all-reduce.9.cloned.1.call-start = ((), (), s32[]{:S(2)}) async-start(), calls=%async_computation.33 | async-start | bytes 16777216 | tf_op jit(solution)/shard_map/psum | solution.py:352
  1574.7 12.9 slice-start
  (36 other events, 138.3 us)
Sparse Core Ops, SparseCore 0:
  9.9 90.3 all-gather.19
  102.2 87.5 all-gather.17
  191.7 87.5 all-gather.13
  281.6 35.3 all-gather.21
  319.2 35.2 all-gather.15
  356.3 87.5 all-gather.23
  445.7 87.4 all-gather.25
  535.0 87.4 all-gather.27
  624.4 87.6 all-gather.29
  1142.4 33.1 reduce-scatter.30
  1179.4 35.1 reduce-scatter.12
  1217.6 86.3 reduce-scatter.20
  1307.4 86.3 reduce-scatter.14
  1396.7 86.4 reduce-scatter.18
  1486.4 86.3 reduce-scatter.16
  1575.9 23.6 reduce-scatter.22
  1602.8 86.4 reduce-scatter.28
  1692.2 86.3 reduce-scatter.24
  1782.0 86.3 reduce-scatter.26
  1870.8 176.6 all-reduce.8
where the time goes:
time: 2070 us
  waiting for transfers between devices  1500 us (72%)
  matrix products  212 us (10%)
  local copies, waits for them, and re-layouts  163 us (8%)
  blocking collectives  82.6 us (4%)
  other arithmetic  75.2 us (4%)
  starting transfers between devices  21 us (1%)
    psum x1, waiting for transfers between devices, on_device(): lax.psum(shared_grads[1].astype(jnp.bfloat16), 'expert').astype(jnp.float32)  175 us
    all_to_all x1, waiting for transfers between devices, on_device(): lax.all_to_all(back_part.astype(jnp.bfloat16), 'expert', split_axis=1, co...  113 us
    all_to_all x1, waiting for transfers between devices, on_device(): lax.all_to_all(outgoing, 'expert', split_axis=1, concat_axis=1, tiled=True)  106 us
    all_to_all x1, waiting for transfers between devices, on_device(): lax.all_to_all(partial_out.astype(jnp.bfloat16), 'expert', split_axis=1,...  98.6 us
    reduce_scatter x1, waiting for transfers between devices, on_device(): lax.psum_scatter(grad_query_w.astype(jnp.bfloat16), 'shard', scatter_dime...  89.8 us
    reduce_scatter x1, waiting for transfers between devices, on_device(): lax.psum_scatter(grad_key_w.astype(jnp.bfloat16), 'shard', scatter_dimens...  89.6 us
    reduce_scatter x1, waiting for transfers between devices, on_device(): lax.psum_scatter(grad_value_w.astype(jnp.bfloat16), 'shard', scatter_dime...  89.4 us
    reduce_scatter x1, waiting for transfers between devices, on_device(): lax.psum_scatter(whole_up.astype(jnp.bfloat16), 'shard', scatter_dimensio...  85.8 us
  transfers between devices with their start and end apart: 24, of which 20 were waited for; matrix products, arithmetic and copies ran while one was open for 16% of the time, Pallas kernels for 0%

commit v1 on v0

v1 whole, which is shorter than its diff:
```python
import jax
import jax.numpy as jnp
from jax import lax
from jax.experimental import pallas as pl
from jax.experimental.pallas import tpu as pltpu
from jax.sharding import PartitionSpec as P

HEAD_DIM = 128
LANES = 128
EPSILON = 1e-05
SCORE_SCALE = HEAD_DIM ** (-0.5)
F32 = jnp.float32
BF16 = jnp.bfloat16
ORDER = (((0, 0), (0, 1)), ((0, 2), (0, 3)), ((1, 0), (1, 2)), ((1, 1), (1, 3)))


def dot(a, b):
    return jnp.dot(a, b, preferred_element_type=F32)


def dot_t(a, b):
    return lax.dot_general(a, b, (((1,), (1,)), ((), ())), preferred_element_type=F32)


def t_dot(a, b):
    return lax.dot_general(a, b, (((0,), (0,)), ((), ())), preferred_element_type=F32)


def flip_shard(values, bit):
    count = lax.axis_size("shard")
    return lax.ppermute(values, "shard", [(i, i ^ bit) for i in range(count)])


def swap_x(values):
    return flip_shard(values, 1)


def swap_y(values):
    return flip_shard(values, 2)


def swap_far(values):
    return flip_shard(values, 3)


def flip_expert(values, bit):
    count = lax.axis_size("expert")
    return lax.ppermute(values, "expert", [(i, i ^ bit) for i in range(count)])


def swap_core(values):
    return flip_expert(values, 1)


def ring_up(values):
    count = lax.axis_size("expert")
    return lax.ppermute(values, "expert", [(i, (i + 2) % count) for i in range(count)])


def after(values, *others):
    return lax.optimization_barrier((values, others))[0]


def spread_xy(first, second):
    pair_a = jnp.stack([first, swap_x(first)])
    pair_b = jnp.stack([second, swap_y(second)])
    return [pair_a, swap_y(pair_a), pair_b, swap_x(pair_b)]


def reduce_xy(blocks):
    keep_a, send_a, keep_b, send_b = blocks
    got_a, got_b = swap_y(send_a), swap_x(send_b)
    far_a = swap_x((keep_a[1].astype(F32) + got_a[1].astype(F32)).astype(BF16))
    far_b = swap_y((keep_b[1].astype(F32) + got_b[1].astype(F32)).astype(BF16))
    return (keep_a[0], got_a[0], far_a), (keep_b[0], got_b[0], far_b)


def total_of(terms):
    total = terms[0].astype(F32)
    for term in terms[1:]:
        total = total + term.astype(F32)
    return total


def exchange_blocks(for_x, for_y):
    got_x, got_y = swap_x(for_x), swap_y(for_y)
    depth = 2 * for_x.shape[0] // 3
    far = jnp.concatenate([swap_y(got_x[depth:]), swap_x(got_y[depth:])], axis=0)
    return [got_x[:depth], got_y[:depth], far]


def gather_parts(part):
    return [part, swap_x(part), swap_y(part), swap_far(part)]


def ring_gather(piece):
    pieces = [piece]
    for _ in range(lax.axis_size("expert") // 2 - 1):
        pieces.append(ring_up(pieces[-1]))
    return pieces


def ring_sum(pieces):
    chips = lax.axis_size("expert") // 2
    total = pieces(1).astype(BF16)
    for j in range(2, chips):
        total = (ring_up(total).astype(F32) + pieces(j).astype(F32)).astype(BF16)
    return ring_up(total), pieces(0)


def expert_sum(own, chip):
    chips = lax.axis_size("expert") // 2
    parts, rows, columns = own.shape
    split = own.reshape(parts, chips, rows // chips, columns)

    def piece(j):
        at = lax.rem(chip + chips - j, chips)
        return lax.dynamic_index_in_dim(split, at, 1, keepdims=False)

    total, mine = ring_sum(piece)
    return (total.astype(F32) + mine).astype(BF16)


def expert_spread(piece, core, chip):
    chips = lax.axis_size("expert") // 2
    parts, rows, columns = piece.shape
    spread = jnp.zeros((parts, chips, rows, columns), piece.dtype)
    for j, got in enumerate(ring_gather(piece)):
        spread = lax.dynamic_update_slice_in_dim(
            spread, got[:, None], lax.rem(chip + chips - j, chips), 1
        )
    half = spread.reshape(parts, 1, chips * rows, columns)
    other = swap_core(half)
    first = jnp.where(core == 0, half, other)
    second = jnp.where(core == 0, other, half)
    return jnp.concatenate([first, second], axis=1).reshape(parts, 2 * chips * rows, columns)


def rms_scale(values):
    return lax.rsqrt(jnp.mean(values * values, axis=-1, keepdims=True) + EPSILON)


def norm_back(grad_out, source, scale_now, gain_now):
    weighted = grad_out * gain_now
    inner_mean = jnp.mean(weighted * source, axis=-1, keepdims=True)
    grad_source = scale_now * (weighted - source * scale_now * scale_now * inner_mean)
    grad_gain = jnp.sum(grad_out * source * scale_now, axis=0, keepdims=True)
    return (grad_source, grad_gain)


def whole(shape):
    return pl.BlockSpec(shape, lambda *_: (0,) * len(shape))


def scalars():
    return pl.BlockSpec(memory_space=pltpu.SMEM)


def call(kernel, name, args, outs, flops, smem=(), transcendentals=0):
    moved = sum(a.size * a.dtype.itemsize for a in args) + sum(
        o.size * o.dtype.itemsize for o in outs
    )
    return pl.pallas_call(
        kernel,
        in_specs=[scalars() if n in smem else whole(a.shape) for n, a in enumerate(args)],
        out_specs=[whole(o.shape) for o in outs],
        out_shape=outs,
        cost_estimate=pl.CostEstimate(
            flops=flops, bytes_accessed=moved, transcendentals=transcendentals
        ),
        name=name,
    )(*args)


def out(shape, dtype):
    return jax.ShapeDtypeStruct(shape, dtype)


def pack_stats(first, second):
    rows = first.shape[0]
    lane = lax.broadcasted_iota(jnp.int32, (rows, LANES), 1)
    spread = jnp.where(lane == 0, first, jnp.where(lane == 1, second, 0.0))
    return [spread[n : n + LANES].T[:8] for n in range(0, rows, LANES)]


def sum_stats(mine, from_x, from_y, far):
    def turn(values):
        return pltpu.roll(values, LANES // 2, 1)

    totals = [
        mine[0] + turn(from_x[0]) + from_y[1] + turn(far[1]),
        mine[1] + turn(from_x[1]) + from_y[0] + turn(far[0]),
        mine[2] + from_x[3] + turn(from_y[2]) + turn(far[3]),
        mine[3] + from_x[2] + turn(from_y[3]) + turn(far[2]),
    ]
    pad = jnp.zeros((LANES - 8, LANES), F32)
    return jnp.concatenate([jnp.concatenate([t, pad], axis=0).T for t in totals], axis=0)


def project_kernel(
    at_ref, r0, r1, r2, r3, gain_ref, *refs
):
    weight_refs, (normed_ref, proj_ref, stats_ref, scale_ref) = refs[:8], refs[8:]
    part = proj_ref.shape[1] // 3
    for n, ref in enumerate((r0, r1, r2, r3)):
        source = ref[...].reshape(LANES, ref.shape[2]).astype(F32)
        scale = rms_scale(source)
        rows = slice(n * LANES, (n + 1) * LANES)
        normed_ref[rows, :] = (source * scale * gain_ref[...]).astype(BF16)
        scale_ref[rows, :] = jnp.broadcast_to(scale, (LANES, LANES))
    depth = weight_refs[0].shape[0]
    for third in range(3):
        cols = slice(third * part, (third + 1) * part)
        total = None
        for n, ref in enumerate(weight_refs):
            rows = pl.ds(pl.multiple_of(at_ref[n] * depth, depth), depth)
            more = dot(normed_ref[:, rows], ref[:, cols])
            total = more if total is None else total + more
        proj_ref[:, cols] = total
    q_proj, k_proj = proj_ref[:, :part], proj_ref[:, part : 2 * part]
    packed = pack_stats(
        jnp.sum(q_proj * q_proj, axis=-1, keepdims=True),
        jnp.sum(k_proj * k_proj, axis=-1, keepdims=True),
    )
    for n, stats in enumerate(packed):
        stats_ref[n] = stats


def attend_kernel(
    width, proj_ref, s0, s1, s2, s3, gain_q_ref, gain_k_ref, cos_ref, sin_ref, bias_ref, w_ref, *refs
):
    q_ref, k_ref, v_ref, lse_ref, scales_ref, attended_ref = refs[:6]
    part_refs = refs[6:]
    part = w_ref.shape[0]
    rows = proj_ref.shape[0]
    sums = sum_stats(s0, s1, s2, s3)
    scales = lax.rsqrt(sums / width + EPSILON)
    scales_ref[...] = scales
    lane = lax.broadcasted_iota(jnp.int32, (rows, LANES), 1)
    q_scale, k_scale = scales[:, 0:1], scales[:, 1:2]
    cosine, sine_part = cos_ref[...], sin_ref[...]
    lse_all = jnp.zeros((rows, LANES), F32)
    for h in range(part // HEAD_DIM):
        cols = slice(h * HEAD_DIM, (h + 1) * HEAD_DIM)
        k_cols = slice(part + h * HEAD_DIM, part + (h + 1) * HEAD_DIM)
        v_cols = slice(2 * part + h * HEAD_DIM, 2 * part + (h + 1) * HEAD_DIM)
        query = proj_ref[:, cols] * q_scale * gain_q_ref[:, cols]
        key = proj_ref[:, k_cols] * k_scale * gain_k_ref[:, cols]
        query = (query * cosine + pltpu.roll(query, HEAD_DIM // 2, 1) * sine_part).astype(BF16)
        key = (key * cosine + pltpu.roll(key, HEAD_DIM // 2, 1) * sine_part).astype(BF16)
        value = proj_ref[:, v_cols].astype(BF16)
        q_ref[:, cols] = query
        k_ref[:, cols] = key
        v_ref[:, cols] = value
        scores = dot_t(query, key) * SCORE_SCALE + bias_ref[...]
        top = jnp.max(scores, axis=-1, keepdims=True)
        powers = jnp.exp(scores - top)
        total = jnp.sum(powers, axis=-1, keepdims=True)
        lse_all = jnp.where(lane == h, top + jnp.log(total), lse_all)
        attended_ref[:, cols] = dot((powers / total).astype(BF16), value).astype(BF16)
    lse_ref[...] = lse_all
    step = 512
    for c in range(w_ref.shape[1] // step):
        cols = slice(c * step, (c + 1) * step)
        for n, ref in enumerate(part_refs):
            got = dot(attended_ref[n * LANES : (n + 1) * LANES, :], w_ref[:, cols])
            ref[:, :, cols] = got.astype(BF16).reshape(2, LANES // 2, step)


def settle_kernel(x_ref, a0, a1, a2, b0, b1, b2, gain_ref, residual_ref, mixed_ref):
    for n, refs in enumerate(((a0, a1, a2), (b0, b1, b2))):
        residual = x_ref[n].astype(F32) + total_of([r[...] for r in refs])
        residual_ref[n] = residual
        mixed_ref[n] = (residual * rms_scale(residual) * gain_ref[...]).astype(BF16)


def flip_kernel(gate_ref, up_ref, down_ref, gate_up_t_ref, down_t_ref):
    unit_part = gate_ref.shape[2]
    for e in range(2):
        low = e * unit_part
        gate_up_t_ref[low : low + unit_part, :] = gate_ref[e].T
        gate_up_t_ref[2 * unit_part + low : 2 * unit_part + low + unit_part, :] = up_ref[e].T
        down_t_ref[:, low : low + unit_part] = down_ref[e].T


def flip_call(w_gate, w_up, w_down):
    two, width, unit_part = w_gate.shape
    step = 512
    tall = pl.BlockSpec((two, step, unit_part), lambda i: (0, i, 0))
    return pl.pallas_call(
        flip_kernel,
        grid=(width // step,),
        in_specs=[tall, tall, pl.BlockSpec((two, unit_part, step), lambda i: (0, 0, i))],
        out_specs=[
            pl.BlockSpec((4 * unit_part, step), lambda i: (0, i)),
            pl.BlockSpec((step, 2 * unit_part), lambda i: (i, 0)),
        ],
        out_shape=[out((4 * unit_part, width), BF16), out((width, 2 * unit_part), BF16)],
        cost_estimate=pl.CostEstimate(flops=0, bytes_accessed=12 * w_gate.size, transcendentals=0),
        name="flip",
    )(w_gate, w_up, w_down)


def lead_kernel(cot_ref, down_t_ref, lead_ref):
    width = down_t_ref.shape[0]
    count = lead_ref.shape[1]
    cot = cot_ref[...].reshape(count, cot_ref.shape[4])[:, :width]
    lead_ref[0] = dot(cot, down_t_ref[...])


def lead_call(cot, down_t):
    shards, chips, two, rows, columns = cot.shape
    width, units = down_t.shape
    count = shards * two * rows
    return pl.pallas_call(
        lead_kernel,
        grid=(chips,),
        in_specs=[
            pl.BlockSpec((shards, 1, two, rows, columns), lambda i: (0, i, 0, 0, 0)),
            whole(down_t.shape),
        ],
        out_specs=pl.BlockSpec((1, count, units), lambda i: (i, 0, 0)),
        out_shape=out((chips, count, units), F32),
        cost_estimate=pl.CostEstimate(
            flops=2 * chips * count * down_t.size,
            bytes_accessed=2 * cot.size + 4 * chips * count * units + 2 * down_t.size,
            transcendentals=0,
        ),
        name="lead",
    )(cot, down_t)


def expert_kernel(m, experts_all, at_ref, *refs):
    row_refs = refs[: 8 * m]
    routed_refs, lead_refs = refs[8 * m : 8 * m + 2], refs[8 * m + 2 : 8 * m + 4]
    gate_ref, up_ref, gate_up_t_ref, router_ref = refs[8 * m + 4 : 8 * m + 8]
    own_refs, other_ref, grads_ref, scaled_out = (
        refs[8 * m + 8 : 8 * m + 12],
        refs[8 * m + 12],
        refs[8 * m + 13],
        refs[8 * m + 14],
    )
    rows_ref, routed_ref, lead_ref, scaled_ref = refs[8 * m + 15 :]
    width = router_ref.shape[0]
    units = lead_ref.shape[1]
    unit_part = units // 2
    half = LANES // 2
    me = at_ref[1]
    now = pl.program_id(0)
    blocks = [block for pair in ORDER for block in pair]
    for side in range(2):
        for j in range(m):

            @pl.when(now == side * m + j)
            def _():
                for n in range(4):
                    ref = row_refs[(side * m + j) * 4 + n]
                    rows_ref[n * LANES : (n + 1) * LANES, :] = ref[...].reshape(LANES, width)

        @pl.when(now // m == side)
        def _():
            for n, (part, d) in enumerate(blocks):
                to = slice(n * half, (n + 1) * half)
                routed_ref[to, :] = routed_refs[side][me ^ d, 0, part]
                lead_ref[to, :] = lead_refs[side][0, 2 * (me ^ d) + part]

    rows = rows_ref[...]
    count = rows.shape[0]
    lane = lax.broadcasted_iota(jnp.int32, (count, LANES), 1)
    routed = routed_ref[...].astype(F32)
    powers = jnp.where(lane < experts_all, jnp.exp(dot(rows, router_ref[...])), 0.0)
    weights = powers * routed / jnp.sum(powers, axis=-1, keepdims=True)
    spot = jnp.zeros((count, LANES), F32)
    for e in range(2):
        here = (lane == at_ref[0] * 2 + e).astype(F32)
        chosen = jnp.sum(weights * here, axis=-1, keepdims=True)
        low = e * unit_part
        gate_pre = dot(rows, gate_ref[e])
        up_pre = dot(rows, up_ref[e])
        lead = lead_ref[:, low : low + unit_part]
        sigmoid_gate = 1.0 / (1.0 + jnp.exp(-gate_pre))
        silu_gate = gate_pre * sigmoid_gate
        hidden = (silu_gate * up_pre).astype(BF16).astype(F32)
        spot = spot + jnp.sum(hidden * lead, axis=-1, keepdims=True) * (here * routed)
        grad_hidden = lead * chosen
        gate_grad = grad_hidden * up_pre * sigmoid_gate * (1.0 + gate_pre * (1.0 - sigmoid_gate))
        grads_ref[0, :, low : low + unit_part] = gate_grad.astype(BF16)
        grads_ref[0, :, units + low : units + low + unit_part] = (grad_hidden * silu_gate).astype(
            BF16
        )
        scaled_ref[:, low : low + unit_part] = (hidden * chosen).astype(BF16)
    for n, (part, d) in enumerate(blocks):
        scaled_out[0, 2 * (me ^ d) + part] = scaled_ref[n * half : (n + 1) * half, :]
    spot = spot.astype(BF16)
    step = 512
    parts = [
        dot(grads_ref[0], gate_up_t_ref[:, c * step : (c + 1) * step]).astype(BF16)
        for c in range(width // step)
    ]

    @pl.when(now < m)
    def _():
        for n, ref in enumerate(own_refs):
            at = slice(n * LANES, (n + 1) * LANES)
            ref[:, 0, :, width:] = spot[at].reshape(2, half, LANES)
            for c in range(width // step):
                ref[:, 0, :, c * step : (c + 1) * step] = parts[c][at].reshape(2, half, step)

    @pl.when(now >= m)
    def _():
        for n in range(4):
            at = slice(n * LANES, (n + 1) * LANES)
            other_ref[n, :, 0, :, width:] = spot[at].reshape(2, half, LANES)
            for c in range(width // step):
                other_ref[n, :, 0, :, c * step : (c + 1) * step] = parts[c][at].reshape(
                    2, half, step
                )


def expert_call(at, rows, cots, first, leads, w_gate, w_up, gate_up_t, router, experts_all):
    m = len(rows[0])
    two, half, width = rows[0][0][0].shape
    shards, _, _, _, columns = cots[0].shape
    units = leads[0].shape[2]
    count = 8 * half
    leads = [v.reshape(v.shape[0], 8, half, units) for v in leads]
    own_shape = (two, m, half, width + LANES)
    flat = [array for side in rows for chip_rows in side for array in chip_rows]

    def where(side, i):
        return jnp.minimum(i, m - 1) if side == 0 else jnp.maximum(i - m, 0)

    def routed_spec(side):
        return pl.BlockSpec(
            (shards, 1, two, half, LANES),
            lambda i, _: (0, where(side, i) + first, 0, 0, width // LANES),
        )

    def lead_spec(side):
        return pl.BlockSpec((1, 8, half, units), lambda i, _: (where(side, i) + first, 0, 0, 0))

    return pl.pallas_call(
        lambda *refs: expert_kernel(m, experts_all, *refs),
        grid_spec=pltpu.PrefetchScalarGridSpec(
            num_scalar_prefetch=1,
            grid=(2 * m,),
            in_specs=[
                pl.BlockSpec(a.shape, lambda i, _: (0, 0, 0), pipeline_mode=pl.Buffered(1))
                for a in flat
            ]
            + [routed_spec(0), routed_spec(1), lead_spec(0), lead_spec(1)]
            + [whole(w_gate.shape), whole(w_up.shape), whole(gate_up_t.shape), whole(router.shape)],
            out_specs=[
                pl.BlockSpec(
                    (two, 1, half, width + LANES), lambda i, _: (0, where(0, i), 0, 0)
                )
                for _ in range(4)
            ]
            + [
                pl.BlockSpec(
                    (4, two, 1, half, width + LANES), lambda i, _: (0, 0, where(1, i), 0, 0)
                ),
                pl.BlockSpec((1, count, 2 * units), lambda i, _: (i, 0, 0)),
                pl.BlockSpec((1, 8, half, units), lambda i, _: (i, 0, 0, 0)),
            ],
            scratch_shapes=[
                pltpu.VMEM((count, width), BF16),
                pltpu.VMEM((count, LANES), BF16),
                pltpu.VMEM((count, units), F32),
                pltpu.VMEM((count, units), BF16),
            ],
        ),
        out_shape=[out(own_shape, BF16)] * 4
        + [
            out((4,) + own_shape, BF16),
            out((2 * m, count, 2 * units), BF16),
            out((2 * m, 8, half, units), BF16),
        ],
        compiler_params=pltpu.CompilerParams(vmem_limit_bytes=48 << 20),
        cost_estimate=pl.CostEstimate(
            flops=8 * m * count * gate_up_t.size,
            bytes_accessed=8 * m * count * width + 4 * gate_up_t.size + 20 * m * count * units,
            transcendentals=2 * m * count * units,
        ),
        name="experts",
    )(at, *flat, *cots, *leads, w_gate, w_up, gate_up_t, router)


def mix_kernel(scaled_ref, down_ref, *refs):
    out_ref = refs[-1]
    width = down_ref.shape[1]
    shards, _, rows, _ = out_ref.shape
    step = 512
    for c in range(width // step):
        cols = slice(c * step, (c + 1) * step)
        part = dot(scaled_ref[0], down_ref[:, cols]).reshape(shards, rows, step)
        if len(refs) == 2:
            part = part + refs[0][:, 0, :, cols].astype(F32)
        out_ref[:, 0, :, cols] = part.astype(BF16)


def mix_call(scaled, down, shards, *others):
    chips, count, units = scaled.shape
    width = down.shape[1]
    rows = count // shards
    result = pl.BlockSpec((shards, 1, rows, width), lambda i: (0, i, 0, 0))
    return pl.pallas_call(
        mix_kernel,
        grid=(chips,),
        in_specs=[pl.BlockSpec((1, count, units), lambda i: (i, 0, 0)), whole(down.shape)]
        + [result] * len(others),
        out_specs=result,
        out_shape=out((shards, chips, rows, width), BF16),
        cost_estimate=pl.CostEstimate(
            flops=2 * scaled.size * width,
            bytes_accessed=2 * scaled.size + 2 * down.size + 4 * chips * count * width,
            transcendentals=0,
        ),
        name="mix",
    )(scaled, down, *others)


def row_grad_kernel(plan, grad_columns, *refs):
    out_ref = refs[-1]
    _, step, unit_part = out_ref.shape
    total = jnp.zeros((step, 2 * unit_part), F32)
    for row_at, grads_at, k in plan:
        rows = jnp.concatenate([refs[n][...].reshape(LANES, step) for n in row_at], axis=0)
        total = total + t_dot(rows, refs[grads_at][k])
    for e in range(2):
        out_ref[e] = total[:, e * unit_part : (e + 1) * unit_part]


def row_grad_call(groups, which):
    step = 256
    half, width = groups[0][0][0][0][0].shape[1:]
    count, four = groups[0][2].shape[1:]
    units = four // 2
    args, specs, plan = [], [], []

    def add(array, spec):
        args.append(array)
        specs.append(spec)
        return len(args) - 1

    for rows, _, grads, _ in groups:
        m = len(rows[0])
        held = add(
            grads,
            pl.BlockSpec(
                (2 * m, count, units), lambda i: (0, 0, which), pipeline_mode=pl.Buffered(1)
            ),
        )
        for side in range(2):
            for j in range(m):
                tiles = [
                    add(r, pl.BlockSpec((2, half, step), lambda i: (0, 0, i)))
                    for r in rows[side][j]
                ]
                plan.append((tiles, held, side * m + j))
    return pl.pallas_call(
        lambda *refs: row_grad_kernel(plan, which, *refs),
        grid=(width // step,),
        in_specs=specs,
        out_specs=pl.BlockSpec((2, step, units // 2), lambda i: (0, i, 0)),
        out_shape=out((2, width, units // 2), F32),
        cost_estimate=pl.CostEstimate(
            flops=2 * len(plan) * count * width * units,
            bytes_accessed=2 * len(plan) * count * (width + units) + 4 * width * units,
            transcendentals=0,
        ),
        name="row_grads",
    )(*args)


def down_grad_kernel(scaled_a, scaled_b, cot_a, cot_b, out_ref):
    _, unit_part, step = out_ref.shape
    shards, chips, two, half, _ = cot_a.shape
    count = shards * two * half
    total = jnp.zeros((2 * unit_part, step), F32)
    for scaled_ref, cot_ref in ((scaled_a, cot_a), (scaled_b, cot_b)):
        for j in range(chips):
            total = total + t_dot(scaled_ref[j], cot_ref[:, j].reshape(count, step))
    for e in range(2):
        out_ref[e] = total[e * unit_part : (e + 1) * unit_part]


def down_grad_call(scaled, cots, first, chips_now):
    step = 256
    shards, _, two, half, _ = cots[0].shape
    _, count, units = scaled[0].shape
    width = (cots[0].shape[4] // step) * step
    held = pl.BlockSpec(
        (chips_now, count, units),
        lambda i: (first // chips_now, 0, 0),
        pipeline_mode=pl.Buffered(1),
    )
    tile = pl.BlockSpec(
        (shards, chips_now, two, half, step), lambda i: (0, first // chips_now, 0, 0, i)
    )
    return pl.pallas_call(
        down_grad_kernel,
        grid=(width // step,),
        in_specs=[held, held, tile, tile],
        out_specs=pl.BlockSpec((2, units // 2, step), lambda i: (0, 0, i)),
        out_shape=out((2, units // 2, width), F32),
        cost_estimate=pl.CostEstimate(
            flops=4 * chips_now * count * width * units,
            bytes_accessed=4 * chips_now * count * (width + units) + 4 * width * units,
            transcendentals=0,
        ),
        name="down_grads",
    )(*scaled, *cots)


def add_up(parts):
    total = parts[0]
    for part in parts[1:]:
        total = total + part
    return total


def turn_kernel(
    experts_all,
    ring_ref,
    a0,
    a1,
    a2,
    b0,
    b1,
    b2,
    residual_ref,
    cot_ref,
    mixed_ref,
    router_ref,
    router_rows_ref,
    gain_ref,
    grad_ref,
    grad_b_ref,
    gain_grad_ref,
    router_grad_ref,
):
    width = residual_ref.shape[2]
    half = residual_ref.shape[1]
    lane = lax.broadcasted_iota(jnp.int32, (half, LANES), 1)
    gain_grad, router_grad = None, None
    for n, refs in enumerate(((a0, a1, a2), (b0, b1, b2))):
        back = ring_ref[n].astype(F32) + total_of([r[...] for r in refs])
        mixed = mixed_ref[n]
        powers = jnp.where(lane < experts_all, jnp.exp(dot(mixed, router_ref[...])), 0.0)
        probs = powers / jnp.sum(powers, axis=-1, keepdims=True)
        prob_grad = back[:, width:]
        logit_grad = (
            probs * (prob_grad - jnp.sum(probs * prob_grad, axis=-1, keepdims=True))
        ).astype(BF16)
        mixed_grad = back[:, :width] + dot(logit_grad, router_rows_ref[...])
        residual = residual_ref[n]
        norm_grad, gain_now = norm_back(mixed_grad, residual, rms_scale(residual), gain_ref[...])
        total = cot_ref[n] + norm_grad
        grad_ref[n] = total
        grad_b_ref[n] = total.astype(BF16)
        router_now = t_dot(logit_grad, mixed)
        gain_grad = gain_now if gain_grad is None else gain_grad + gain_now
        router_grad = router_now if router_grad is None else router_grad + router_now
    gain_grad_ref[...] = jnp.broadcast_to(gain_grad, gain_grad_ref.shape)
    router_grad_ref[...] = router_grad[: router_grad_ref.shape[0]]


def output_grad_kernel(core_ref, g0, g1, g2, g3, attended_ref, own_ref, other_ref):
    part, width = attended_ref.shape[1], g0.shape[2]
    half = part // 2
    step = 512
    own_cols = pl.ds(pl.multiple_of(core_ref[0] * half, half), half)
    other_cols = pl.ds(pl.multiple_of((1 - core_ref[0]) * half, half), half)
    for c in range(width // step):
        cols = slice(c * step, (c + 1) * step)
        grads = jnp.concatenate(
            [g[:, :, cols].reshape(LANES, step) for g in (g0, g1, g2, g3)], axis=0
        )
        own_ref[0, :, cols] = t_dot(attended_ref[:, own_cols], grads)
        other_ref[0, :, cols] = t_dot(attended_ref[:, other_cols], grads).astype(BF16)


def attend_back_kernel(
    g0,
    g1,
    g2,
    g3,
    w_ref,
    attended_ref,
    q_ref,
    k_ref,
    v_ref,
    lse_ref,
    scales_ref,
    bias_ref,
    cos_ref,
    sin_ref,
    gain_q_ref,
    gain_k_ref,
    proj_ref,
    query_ref,
    key_ref,
    value_ref,
    stats_ref,
    gains_ref,
    grad_ref,
):
    part, width = w_ref.shape
    rows = proj_ref.shape[0]
    grad_ref[...] = jnp.concatenate(
        [g[...].reshape(LANES, width) for g in (g0, g1, g2, g3)], axis=0
    )
    q_scale, k_scale = scales_ref[:, 0:1], scales_ref[:, 1:2]
    cosine, sine_part = cos_ref[...], sin_ref[...]
    q_inner = jnp.zeros((rows, 1), F32)
    k_inner = jnp.zeros((rows, 1), F32)
    for h in range(part // HEAD_DIM):
        cols = slice(h * HEAD_DIM, (h + 1) * HEAD_DIM)
        k_cols = slice(part + h * HEAD_DIM, part + (h + 1) * HEAD_DIM)
        attended_grad = dot_t(grad_ref[...], w_ref[cols, :]).astype(BF16)
        query, key, value = q_ref[:, cols], k_ref[:, cols], v_ref[:, cols]
        probs = jnp.exp(
            dot_t(query, key) * SCORE_SCALE + bias_ref[...] - lse_ref[:, h : h + 1]
        )
        delta = jnp.sum(
            attended_grad.astype(F32) * attended_ref[:, cols].astype(F32), axis=-1, keepdims=True
        )
        score_grad = (probs * (dot_t(attended_grad, value) - delta)).astype(BF16)
        value_ref[:, cols] = t_dot(probs.astype(BF16), attended_grad).astype(BF16)
        query_grad = dot(score_grad, key) * SCORE_SCALE
        key_grad = t_dot(score_grad, query) * SCORE_SCALE
        query_pre = query_grad * cosine + pltpu.roll(query_grad * sine_part, HEAD_DIM // 2, 1)
        key_pre = key_grad * cosine + pltpu.roll(key_grad * sine_part, HEAD_DIM // 2, 1)
        q_proj, k_proj = proj_ref[:, cols], proj_ref[:, k_cols]
        gains_ref[0:1, cols] = jnp.sum(query_pre * q_proj * q_scale, axis=0, keepdims=True)
        gains_ref[1:2, cols] = jnp.sum(key_pre * k_proj * k_scale, axis=0, keepdims=True)
        query_pre = query_pre * gain_q_ref[:, cols]
        key_pre = key_pre * gain_k_ref[:, cols]
        query_ref[:, cols] = query_pre
        key_ref[:, cols] = key_pre
        q_inner = q_inner + jnp.sum(query_pre * q_proj, axis=-1, keepdims=True)
        k_inner = k_inner + jnp.sum(key_pre * k_proj, axis=-1, keepdims=True)
    for n, stats in enumerate(pack_stats(q_inner, k_inner)):
        stats_ref[n] = stats


def project_back_kernel(
    at_ref, core_ref, s0, s1, s2, s3, query_ref, key_ref, value_ref, proj_ref, scales_ref, normed_ref, *refs
):
    weight_refs = refs[:8]
    part_refs, own_ref, other_ref, all_ref = refs[8:12], refs[12], refs[13], refs[14]
    width = normed_ref.shape[1]
    part = query_ref.shape[1]
    inner = sum_stats(s0, s1, s2, s3) / width
    for n, (grad_ref, low) in enumerate(((query_ref, 0), (key_ref, part))):
        scale = scales_ref[:, n : n + 1]
        factor = scale * scale * inner[:, n : n + 1]
        all_ref[:, low : low + part] = (
            scale * (grad_ref[...] - proj_ref[:, low : low + part] * factor)
        ).astype(BF16)
    all_ref[:, 2 * part :] = value_ref[...]
    depth = weight_refs[0].shape[0]
    for n, ref in enumerate(weight_refs):
        at = pl.ds(pl.multiple_of(at_ref[n] * depth, depth), depth)
        got = dot_t(all_ref[...], ref[...]).astype(BF16)
        for k, part_ref in enumerate(part_refs):
            part_ref[:, :, at] = got[k * LANES : (k + 1) * LANES].reshape(2, LANES // 2, depth)
    for p in range(width // (2 * depth)):
        for ref, side in ((own_ref, core_ref[0]), (other_ref, 1 - core_ref[0])):
            at = pl.ds(pl.multiple_of((2 * p + side) * depth, depth), depth)
            for third in range(3):
                cols = slice(third * part, (third + 1) * part)
                ref[p, :, cols] = t_dot(normed_ref[:, at], all_ref[:, cols]).astype(ref.dtype)


def finish_kernel(a0, a1, a2, b0, b1, b2, x_ref, grad_ref, gain_ref, out_ref, gain_grad_ref):
    gain_grad = None
    for n, refs in enumerate(((a0, a1, a2), (b0, b1, b2))):
        source = x_ref[n].astype(F32)
        normed_grad = total_of([r[...] for r in refs])
        norm_grad, gain_now = norm_back(normed_grad, source, rms_scale(source), gain_ref[...])
        out_ref[n] = grad_ref[n] + norm_grad
        gain_grad = gain_now if gain_grad is None else gain_grad + gain_now
    gain_grad_ref[...] = jnp.broadcast_to(gain_grad, gain_grad_ref.shape)


def cut_kernel(at_ref, *refs):
    sources, (own_ref, spare_ref, x_ref, y_ref) = refs[:15], refs[15:]
    depth, part = sources[0].shape
    rows = depth // 2
    for w in range(3):
        cols = slice(w * part, (w + 1) * part)
        own_ref[:, cols] = sources[w][...]
        x_ref[:depth, cols] = sources[3 + w][...]
        y_ref[:depth, cols] = sources[6 + w][...]
        x_ref[depth:, cols] = sources[9 + w][:rows, :]
        y_ref[depth:, cols] = sources[9 + w][rows:, :]
        spare_ref[:, cols] = sources[12 + w][...]


def cut_call(at, w_query, w_key, w_value):
    rows, width = w_query.shape
    part = width // 4
    depth = rows // 2

    def block(member, core):
        return pl.BlockSpec((depth, part), lambda i, at: (at[core], at[member]))

    full, more = (depth, 3 * part), (3 * depth // 2, 3 * part)
    fulls = [full, full, more, more]
    return pl.pallas_call(
        cut_kernel,
        grid_spec=pltpu.PrefetchScalarGridSpec(
            num_scalar_prefetch=1,
            grid=(1,),
            in_specs=[block(d, 4) for d in range(4) for _ in range(3)]
            + [block(0, 5) for _ in range(3)],
            out_specs=[whole(s) for s in fulls],
        ),
        out_shape=[out(s, BF16) for s in fulls],
        name="cut",
    )(at, *([w_query, w_key, w_value] * 5))


def on_device(
    block_input,
    segment_ids,
    expert_routes,
    attn_gain,
    w_query,
    w_key,
    w_value,
    query_gain,
    key_gain,
    w_output,
    moe_gain,
    w_router,
    w_gate,
    w_up,
    w_down,
    out_cotangent,
):
    expert_count = lax.axis_size("expert")
    shard_count = lax.axis_size("shard")
    chips = expert_count // 2
    me = lax.axis_index("shard")
    place = lax.axis_index("expert")
    core = lax.rem(place, 2)
    chip = place // 2
    tok_count = block_input.shape[1]
    half = tok_count // 2
    group_count = segment_ids.shape[1]
    width = block_input.shape[2]
    part = width // shard_count
    local_experts = w_gate.shape[0]
    experts_all = local_experts * expert_count
    unit_part = w_gate.shape[2]
    units = local_experts * unit_part
    core_at = jnp.reshape(core, (1,))

    own_input = block_input.reshape(2, half, width)
    group_input = [b.reshape(2, half, width) for b in spread_xy(own_input[:1], own_input[1:])]

    small = jnp.concatenate([attn_gain[None], moe_gain[None], w_router.T], axis=0)
    small = jnp.pad(small, ((0, (-small.shape[0]) % 32), (0, 0)))
    small_all = jnp.zeros((small.shape[0], width), BF16)
    small_parts = gather_parts(small)
    for d, got in enumerate(small_parts):
        small_all = lax.dynamic_update_slice_in_dim(small_all, got, (me ^ d) * part, 1)
    gain_one = small_all[0:1].astype(F32)
    gain_two = small_all[1:2].astype(F32)
    router = small_all[2 : 2 + experts_all]
    router = jnp.pad(router, ((0, LANES - experts_all), (0, 0)))
    router_t = router.T

    depth = part // 2
    at = jnp.stack([me, me ^ 1, me ^ 2, me ^ 3, core, 1 - core])
    cuts = cut_call(at, w_query, w_key, w_value)
    direct = exchange_blocks(*after(cuts[2:], group_input[0], group_input[2], small_parts))
    passed = [swap_core(block) for block in direct]
    weight_blocks = list(cuts[:2]) + direct + passed
    weight_at = jnp.stack(
        [2 * me + core, 2 * me + 1 - core]
        + [2 * (me ^ d) + core for d in (1, 2, 3)]
        + [2 * (me ^ d) + 1 - core for d in (1, 2, 3)]
    )

    routes = expert_routes[0]
    routed = jnp.sum(
        (routes[:, :, None] == jnp.arange(experts_all)[None, None, :]).astype(F32), axis=1
    )
    cotangent = out_cotangent[0]
    cot_block = (
        jnp.concatenate(
            [cotangent, routed, jnp.zeros((tok_count, LANES - experts_all), F32)], axis=1
        )
        .astype(BF16)
        .reshape(2, half, width + LANES)
    )
    cot_block = after(cot_block, group_input[0], group_input[2])
    cot_pieces = jnp.concatenate(ring_gather(cot_block), axis=0)
    cot = lax.all_gather(after(cot_pieces, direct), "shard", axis=0, tiled=True)

    down_w = w_down.reshape(units, width)
    gate_up_t, down_t = flip_call(w_gate, w_up, w_down)

    starts = [(me ^ d) * tok_count + side * half for pair in ORDER for side, d in pair]
    position = jnp.concatenate([p + jnp.arange(half) for p in starts])
    seg_all = segment_ids[0]
    seg_here = jnp.concatenate([lax.dynamic_slice_in_dim(seg_all, p, half) for p in starts])
    allowed = (seg_here[:, None] == seg_here[None, :]) & (position[None, :] <= position[:, None])
    bias = jnp.where(allowed, 0.0, -1e30).astype(F32)
    half_dim = HEAD_DIM // 2
    inverse = 10000.0 ** (-(jnp.arange(half_dim).astype(F32) * 2.0) / HEAD_DIM)
    angles = position.astype(F32)[:, None] * inverse[None, :]
    cosine = jnp.concatenate([jnp.cos(angles), jnp.cos(angles)], axis=-1)
    sine_part = jnp.concatenate([-jnp.sin(angles), jnp.sin(angles)], axis=-1)
    gain_query = query_gain.astype(F32)[None]
    gain_key = key_gain.astype(F32)[None]
    normed, proj, squares, scale_one = call(
        project_kernel,
        "project",
        [weight_at] + group_input + [after(gain_one, gate_up_t)] + weight_blocks,
        [
            out((group_count, width), BF16),
            out((group_count, 3 * part), F32),
            out((4, 8, LANES), F32),
            out((group_count, LANES), F32),
        ],
        2 * group_count * width * 3 * part,
        smem=(0,),
    )
    quad = out((2, half, width), BF16)
    square_parts = out((group_count, part), BF16)
    heads = call(
        lambda *refs: attend_kernel(width, *refs),
        "attend",
        [proj] + gather_parts(squares) + [gain_query, gain_key, cosine, sine_part, bias, w_output],
        [square_parts] * 3
        + [out((group_count, LANES), F32)] * 2
        + [square_parts]
        + [quad] * 4,
        4 * group_count * group_count * part + 2 * group_count * part * width,
    )
    q_heads, k_heads, v_heads, log_total, scales, attended = heads[:6]
    terms_a, terms_b = reduce_xy([b.reshape(2, 1, half, width) for b in heads[6:]])
    residual, mixed_in = call(
        settle_kernel,
        "settle",
        [own_input]
        + [t.reshape(half, width) for t in terms_a + terms_b]
        + [gain_two],
        [out((2, half, width), F32), out((2, half, width), BF16)],
        tok_count * width,
    )

    pieces = ring_gather(mixed_in)
    cot = after(cot, mixed_in).reshape(shard_count, chips, 2, half, width + LANES)
    cots = (cot, swap_core(cot))
    leads = [lead_call(c, down_t) for c in cots]
    size = 1
    at = jnp.stack([place, me])
    all_rows = []
    for piece in pieces:
        own = [b.reshape(2, half, width) for b in spread_xy(piece[:1], piece[1:])]
        all_rows.append((own, [swap_core(r) for r in own]))
    groups, back_terms, scaled_all, totals_all = [], [None] * chips, ([], []), []
    for low in range(0, chips, size):
        rows = [[all_rows[j][side] for j in range(low, low + size)] for side in range(2)]
        at_now = after(at, totals_all[low - 2]) if low > 1 else at
        got = expert_call(
            at_now, rows, cots, low, leads, w_gate, w_up, gate_up_t, router_t, experts_all
        )
        groups.append((rows, low, got[5], got[6]))
        for side in range(2):
            scaled_all[side].append(got[6][side * size : (side + 1) * size])
        passed_back = swap_core(got[4])
        totals_all.append(
            [
                (a.astype(F32) + passed_back[n].astype(F32)).astype(BF16)
                for n, a in enumerate(got[:4])
            ]
        )
    for n, low in enumerate(range(0, chips, size)):
        terms_a, terms_b = reduce_xy(after(totals_all[n], [r[0] for r in all_rows]))
        for j in range(low, low + size):
            back_terms[j] = [[t[j - low] for t in terms] for terms in (terms_a, terms_b)]

    def back_piece(j):
        return jnp.stack([total_of(terms) for terms in back_terms[j]])

    ring_total = back_piece(1).astype(BF16)
    for j in range(2, chips):
        ring_total = (ring_up(ring_total).astype(F32) + back_piece(j)).astype(BF16)
    ring_total = ring_up(ring_total)
    grad_res, grad_res_b, grad_gain_two, grad_router = call(
        lambda *refs: turn_kernel(experts_all, *refs),
        "turn",
        [ring_total]
        + back_terms[0][0]
        + back_terms[0][1]
        + [residual, cotangent.reshape(2, half, width), mixed_in, router_t, router]
        + [gain_two],
        [
            out((2, half, width), F32),
            out((2, half, width), BF16),
            out((8, width), F32),
            out((experts_all, width), F32),
        ],
        8 * tok_count * width * LANES,
    )

    scaled_all = [
        jnp.concatenate(s, axis=0).reshape(chips, group_count, units) for s in scaled_all
    ]
    mix_other = mix_call(after(scaled_all[1], grad_res_b), down_w, shard_count)
    mix_passed = swap_core(mix_other)

    group_grad = [b.reshape(2, half, width) for b in spread_xy(grad_res_b[:1], grad_res_b[1:])]
    output_own, output_other = call(
        output_grad_kernel,
        "output_grad",
        [core_at] + after(group_grad, mix_other) + [attended],
        [out((1, part // 2, width), F32), out((1, part // 2, width), BF16)],
        2 * group_count * part * width,
        smem=(0,),
    )
    query_pre, key_pre, value_grad, inner, gain_grads, _ = call(
        attend_back_kernel,
        "attend_back",
        after(group_grad, output_other)
        + [w_output, attended, q_heads, k_heads, v_heads, log_total, scales, bias]
        + [cosine, sine_part, gain_query, gain_key, proj],
        [
            out((group_count, part), F32),
            out((group_count, part), F32),
            square_parts,
            out((4, 8, LANES), F32),
            out((8, part), F32),
            out((group_count, width), BF16),
        ],
        10 * group_count * group_count * part + 2 * group_count * part * width,
    )
    output_total = output_own + swap_core(output_other).astype(F32)
    out_total = mix_call(
        after(scaled_all[0], query_pre), down_w, shard_count, mix_passed
    ).reshape(-1, width)
    out_sums = lax.psum_scatter(out_total, "shard", scatter_dimension=0, tiled=True)
    got = call(
        project_back_kernel,
        "project_back",
        [weight_at, core_at]
        + gather_parts(inner)
        + [query_pre, key_pre, value_grad, proj, scales, normed]
        + weight_blocks,
        [quad] * 4
        + [
            out((4, depth, 3 * part), F32),
            out((4, depth, 3 * part), BF16),
            out((group_count, 3 * part), BF16),
        ],
        4 * group_count * width * 3 * part,
        smem=(0, 1),
    )
    terms_a, terms_b = reduce_xy([b.reshape(2, 1, half, width) for b in got[:4]])
    grad_input, grad_gain_one = call(
        finish_kernel,
        "finish",
        [t.reshape(half, width) for t in terms_a + terms_b] + [own_input, grad_res, gain_one],
        [out((2, half, width), F32), out((8, width), F32)],
        tok_count * width,
    )

    out_sums = out_sums.reshape(chips, tok_count, width)
    ring_part, own_part = ring_sum(lambda j: out_sums[j])
    block_output = residual.reshape(tok_count, width) + (
        ring_part.astype(F32) + own_part.astype(F32)
    )

    output_piece = expert_sum(output_total, chip)
    grad_w_output = expert_spread(output_piece, core, chip)[0].astype(F32)
    qkv_total = got[4] + swap_core(got[5]).astype(F32)
    qkv_piece = expert_sum(qkv_total, chip)
    sent = [lax.dynamic_index_in_dim(qkv_piece, me ^ d, 0, keepdims=False) for d in range(4)]
    low = sent[3].shape[0] // 2
    arrived = exchange_blocks(
        jnp.concatenate([sent[1], sent[3][:low]], axis=0),
        jnp.concatenate([sent[2], sent[3][low:]], axis=0),
    )
    qkv_rows = expert_spread(jnp.stack([sent[0]] + arrived), core, chip)
    shares = [lax.dynamic_index_in_dim(qkv_rows, me ^ p, 0, keepdims=False) for p in range(4)]
    grad_w_query, grad_w_key, grad_w_value = (
        jnp.concatenate([share[:, n * part : (n + 1) * part] for share in shares], axis=1).astype(
            F32
        )
        for n in range(3)
    )

    span = min(chips, 4)
    sets = [groups[low : low + span] for low in range(0, chips, span)]
    grad_w_gate = add_up([row_grad_call(some, 0) for some in sets])
    grad_w_up = add_up([row_grad_call(some, 1) for some in sets])
    grad_w_down = add_up(
        [down_grad_call(scaled_all, cots, low, span) for low in range(0, chips, span)]
    )

    packed = jnp.concatenate([grad_gain_one[:1], grad_gain_two[:1], grad_router], axis=0)
    rows_used = packed.shape[0]
    packed = jnp.pad(packed, ((0, (-rows_used) % 16), (0, 0)))
    quarters = jnp.stack(
        [lax.dynamic_slice_in_dim(packed, (me ^ d) * part, part, 1) for d in range(4)]
    )
    quarters = quarters[:2] + swap_y(quarters[2:])
    packed = (quarters[0] + swap_x(quarters[1]))[:rows_used]
    packed = jnp.concatenate([packed, gain_grads[:2]], axis=0)
    bit = 1
    while bit < expert_count:
        packed = packed + flip_expert(packed, bit)
        bit *= 2
    return (
        block_output.reshape(1, tok_count, width),
        grad_input.reshape(1, tok_count, width),
        packed[0],
        grad_w_query,
        grad_w_key,
        grad_w_value,
        packed[rows_used],
        packed[rows_used + 1],
        grad_w_output,
        packed[1],
        packed[2 : 2 + experts_all].T,
        grad_w_gate,
        grad_w_up,
        grad_w_down,
    )


def solution(mesh):
    placed = (
        P("expert", "shard", None),
        P("expert", None),
        P("expert", "shard", None),
        P("shard"),
        P("shard", None),
        P("shard", None),
        P("shard", None),
        P("shard"),
        P("shard"),
        P("shard", None),
        P("shard"),
        P("shard", None),
        P("expert", None, "shard"),
        P("expert", None, "shard"),
        P("expert", "shard", None),
        P("expert", "shard", None),
    )
    return jax.shard_map(
        on_device,
        mesh=mesh,
        in_specs=placed,
        out_specs=(
            P("expert", "shard", None),
            P("expert", "shard", None),
            P("shard"),
            P("shard", None),
            P("shard", None),
            P("shard", None),
            P("shard"),
            P("shard"),
            P("shard", None),
            P("shard"),
            P("shard", None),
            P("expert", None, "shard"),
            P("expert", None, "shard"),
            P("expert", "shard", None),
        ),
        check_vma=False,
    )
```

time: 2070 us -> 863 us (0.42)
  waiting for transfers between devices: 1500 us -> 380 us
  Pallas kernels: 0 us -> 247 us
  matrix products: 212 us -> 0 us
  local copies, waits for them, and re-layouts: 163 us -> 55.1 us
  blocking collectives: 82.6 us -> 0 us
  starting transfers between devices: 21 us -> 93.2 us
    reduce_scatter x9 -> x1, waiting for transfers between devices: 551 us -> 0.01 us  [on_device(): lax.psum_scatter(out_total, 'shard', scatter_dimension=0, tiled=True)]
    all_gather x9 -> x1, waiting for transfers between devices: 400 us -> 6.07 us  [on_device(): cot = lax.all_gather(after(cot_pieces, direct), 'shard', axis=0, tiled=True)]
    ppermute x0 -> x123, waiting for transfers between devices: none -> 374 us  [the longest x67 191 us: flip_shard(): return lax.ppermute(values, 'shard', [(i, i ^ bit) for i in range(count)])]
    all_to_all x4 -> x0, waiting for transfers between devices: 366 us -> none  [the longest x1 113 us: on_device(): lax.all_to_all(back_part.astype(jnp.bfloat16), 'expert', split_axis=1, co...]
    pallas_call x0 -> x21, Pallas kernels: none -> 247 us  [the longest x4 83.4 us: expert_call(): pl.pallas_call(lambda *refs: expert_kernel(m, experts_all, *refs), grid_s...]
    dot_general x30 -> x0, matrix products: 212 us -> none  [the longest x1 20.4 us: expert_back(): jnp.einsum('erd,efd->erf', grad_arrived, down_w, preferred_element_type=j...]
    psum x1 -> x0, waiting for transfers between devices: 175 us -> none  [on_device(): lax.psum(shared_grads[1].astype(jnp.bfloat16), 'expert').astype(jnp.float32)]
    ppermute x0 -> x123, starting transfers between devices: none -> 93.1 us  [the longest x67 74.5 us: flip_shard(): return lax.ppermute(values, 'shard', [(i, i ^ bit) for i in range(count)])]
  transfers between devices with their start and end apart: 24 -> 125, of which waited for: 20 -> 57; matrix products, arithmetic and copies ran while one was open for 16% -> 12% of each run, Pallas kernels for 0% -> 27%
where the time goes in v1:
time: 863 us; the launch traced here: 857 us
  waiting for transfers between devices  380 us (44%)
  Pallas kernels  247 us (29%)
  starting transfers between devices  93.2 us (11%)
  other arithmetic  65.8 us (8%)
  local copies, waits for them, and re-layouts  55.1 us (6%)
  between operations  15.9 us (2%)
    ppermute x67, waiting for transfers between devices, flip_shard(): return lax.ppermute(values, 'shard', [(i, i ^ bit) for i in range(count)])  191 us
    ppermute x24, waiting for transfers between devices, ring_up(): lax.ppermute(values, 'expert', [(i, (i + 2) % count) for i in range(count)])  183 us
    pallas_call x4, Pallas kernels, expert_call(): pl.pallas_call(lambda *refs: expert_kernel(m, experts_all, *refs), grid_s...  83.4 us
    ppermute x67, starting transfers between devices, flip_shard(): return lax.ppermute(values, 'shard', [(i, i ^ bit) for i in range(count)])  74.5 us
    pallas_call x8, Pallas kernels, call(): pl.pallas_call(kernel, in_specs=[scalars() if n in smem else whole(a.shap...  67 us
    pallas_call x2, Pallas kernels, row_grad_call(): pl.pallas_call(lambda *refs: row_grad_kernel(plan, which, *refs), grid=(w...  31.4 us
    pallas_call x2, Pallas kernels, mix_call(): pl.pallas_call(mix_kernel, grid=(chips,), in_specs=[pl.BlockSpec((1, coun...  19.4 us
    pallas_call x2, Pallas kernels, lead_call(): pl.pallas_call(lead_kernel, grid=(chips,), in_specs=[pl.BlockSpec((shards...  18.4 us
  transfers between devices with their start and end apart: 125, of which 57 were waited for; matrix products, arithmetic and copies ran while one was open for 12% of the time, Pallas kernels for 27%

profile of v1, /device:TPU:0, one launch (start us, length us, event | category | flops | bytes accessed | tf_op | source)
XLA Modules:
  0.0 857.0 jit_solution(13655991216959239322)
XLA Ops:
  29.1 12.7 %collective-permute-done.29 = bf16[2,64,2176]{2,1,0:T(8,128)(2,1)S(1)} collective-permute-done((bf16[2,64,2176]{2,1,0:T(8,128)(2,1)S(1)}, bf16[2,64,2176]{2,1,0:T(8,128)(2,1)S(1)}, u32[]{:S(2)}, u32[]{:S(2)}) %collective-permute-start.29) | collective-permute-done | bytes 557088 | tf_op jit(solution)/shard_map/ppermute | solution.py:57
  41.8 10.6 %collective-permute-done.7 = bf16[384,1536]{1,0:T(8,128)(2,1)S(1)} collective-permute-done((bf16[384,1536]{1,0:T(8,128)(2,1)}, bf16[384,1536]{1,0:T(8,128)(2,1)S(1)}, u32[]{:S(2)}, u32[]{:S(2)}) %collective-permute-start.7) | collective-permute-done | bytes 1179680 | tf_op jit(solution)/shard_map/ppermute | solution.py:31
  63.4 5.3 collective-permute-done.31
  70.7 6.7 flip.1
  84.9 22.9 %collective-permute-done.3 = bf16[2,1,64,2048]{3,2,0,1:T(8,128)(2,1)S(1)} collective-permute-done((bf16[2,1,64,2048]{3,2,0,1:T(8,128)(2,1)S(1)}, bf16[2,1,64,2048]{3,2,0,1:T(8,128)(2,1)S(1)}, u32[]{:S(2)}, u32[]{:S(2)}) %collective-permute-start.3) | collective-permute-done | bytes 524320 | tf_op jit(solution)/shard_map/ppermute | solution.py:31
  110.0 9.6 %project.1 = (bf16[512,2048]{1,0:T(8,128)(2,1)}, f32[512,1536]{1,0:T(8,128)}, f32[4,8,128]{2,1,0:T(8,128)}, f32[512,128]{1,0:T(8,128)}) custom-call(s32[8]{0:T(128)} %stack.217.at_ref, bf16[2,64,2048]{2,1,0:T(8,128)(2,1)} %get-tuple-element.315.r0, bf16[2,64,2048]{2,1,0:T(8,128)(2,1)} %bitcast.556, bf16[2,64,2048]{2,1,0:T(8,128)(2,1)} %get-tuple-element.309.r2, ...), custom_call_target="tpu_custom_call" | custom-call | flops 3221225472 | bytes 13918240 | tf_op jit(solution)/shard_map/project/pallas_call | solution.py:163
  127.1 9.9 %attend.1 = (bf16[512,512]{1,0:T(8,128)(2,1)}, bf16[512,512]{1,0:T(8,128)(2,1)}, bf16[512,512]{1,0:T(8,128)(2,1)}, f32[512,128]{1,0:T(8,128)}, f32[512,128]{1,0:...) custom-call(f32[512,1536]{1,0:T(8,128)} %get-tuple-element.124.refs_, ...), custom_call_target="tpu_custom_call" | custom-call | flops 1610612736 | bytes 11603968 | tf_op jit(solution)/shard_map/attend/pallas_call | solution.py:163
  142.7 19.4 %collective-permute-done.19 = bf16[2,1,64,2048]{3,2,1,0:T(8,128)(2,1)S(1)} collective-permute-done((bf16[2,1,64,2048]{3,2,1,0:T(8,128)(2,1)}, bf16[2,1,64,2048]{3,2,1,0:T(8,128)(2,1)S(1)}, u32[]{:S(2)}, u32[]{:S(2)}) %collective-permute-start.19) | collective-permute-done | bytes 524320 | tf_op jit(solution)/shard_map/ppermute | solution.py:31
  168.5 8.3 collective-permute-done.20
  183.6 6.1 all-gather.2.cloned.1.call-done
  194.8 11.8 %collective-permute-done.33 = bf16[2,64,2048]{2,1,0:T(8,128)(2,1)} collective-permute-done((bf16[2,64,2048]{2,1,0:T(8,128)(2,1)}, bf16[2,64,2048]{2,1,0:T(8,128)(2,1)}, u32[]{:S(2)}, u32[]{:S(2)}) %collective-permute-start.33) | collective-permute-done | bytes 524320 | tf_op jit(solution)/shard_map/ppermute | solution.py:57
  221.1 6.2 collective-permute-done.43
  232.8 8.1 collective-permute-done.53
  241.9 9.2 %lead.2 = f32[4,512,512]{2,1,0:T(8,128)} custom-call(bf16[4,4,2,64,2176]{4,3,2,1,0:T(8,128)(2,1)} %bitcast.476, bf16[2048,512]{1,0:T(8,128)(2,1)} %get-tuple-element.135.down_t_ref), custom_call_target="tpu_custom_call" | custom-call | flops 4294967296 | bytes 15204352 | tf_op jit(solution)/shard_map/lead/pallas_call | solution.py:315
  251.7 9.2 %lead.3 = f32[4,512,512]{2,1,0:T(8,128)} custom-call(bf16[4,4,2,64,2176]{4,3,2,1,0:T(8,128)(2,1)} %collective-permute-done.32.cot_ref.refs_10_.cot_b, bf16[2048,512]{1,0:T(8,128)(2,1)} %get-tuple-element.135.down_t_ref), custom_call_target="tpu_custom_call" | custom-call | flops 4294967296 | bytes 15204352 | tf_op jit(solution)/shard_map/lead/pallas_call | solution.py:315
  265.0 21.2 %experts.5 = (bf16[2,1,64,2176]{3,2,1,0:T(8,128)(2,1)S(1)}, bf16[2,1,64,2176]{3,2,1,0:T(8,128)(2,1)S(1)}, bf16[2,1,64,2176]{3,2,1,0:T(8,128)(2,1)}, bf16[2,1,64,...) custom-call(s32[2]{0:T(128)S(1)} %pad_add_fusion.refs_0_, ...), custom_call_target="tpu_custom_call" | custom-call | flops 8589934592 | bytes 22020096 | tf_op jit(solution)/shard_map/experts/pallas_call | solution.py:442
  294.4 20.8 %experts.4 = (bf16[2,1,64,2176]{3,2,1,0:T(8,128)(2,1)S(1)}, bf16[2,1,64,2176]{3,2,1,0:T(8,128)(2,1)S(1)}, bf16[2,1,64,2176]{3,2,1,0:T(8,128)(2,1)}, bf16[2,1,64,...) custom-call(s32[2]{0:T(128)S(1)} %pad_add_fusion.refs_0_, ...), custom_call_target="tpu_custom_call" | custom-call | flops 8589934592 | bytes 22020096 | tf_op jit(solution)/shard_map/experts/pallas_call | solution.py:442
  322.3 9.4 %collective-permute-done.55 = bf16[2,1,64,2048]{3,2,1,0:T(8,128)(2,1)S(1)} collective-permute-done((bf16[2,1,64,2048]{3,2,1,0:T(8,128)(2,1)S(1)}, bf16[2,1,64,2048]{3,2,1,0:T(8,128)(2,1)S(1)}, u32[]{:S(2)}, u32[]{:S(2)}) %collective-permute-start.55) | collective-permute-done | bytes 524320 | tf_op jit(solution)/shard_map/ppermute | solution.py:31
  335.8 20.6 %experts.7 = (bf16[2,1,64,2176]{3,2,1,0:T(8,128)(2,1)S(1)}, bf16[2,1,64,2176]{3,2,1,0:T(8,128)(2,1)S(1)}, bf16[2,1,64,2176]{3,2,1,0:T(8,128)(2,1)}, bf16[2,1,64,...) custom-call(s32[2]{0:T(128)S(1)} %pad_add_fusion.refs_0_, ...), custom_call_target="tpu_custom_call" | custom-call | flops 8589934592 | bytes 22020096 | tf_op jit(solution)/shard_map/experts/pallas_call | solution.py:442
  359.5 20.8 %experts.6 = (bf16[2,1,64,2176]{3,2,1,0:T(8,128)(2,1)S(1)}, bf16[2,1,64,2176]{3,2,1,0:T(8,128)(2,1)S(1)}, bf16[2,1,64,2176]{3,2,1,0:T(8,128)(2,1)}, bf16[2,1,64,...) custom-call(s32[2]{0:T(128)S(1)} %pad_add_fusion.refs_0_, ...), custom_call_target="tpu_custom_call" | custom-call | flops 8589934592 | bytes 22020096 | tf_op jit(solution)/shard_map/experts/pallas_call | solution.py:442
  390.3 8.5 collective-permute-done.79
  412.6 12.0 %collective-permute-done.76 = bf16[2,1,64,2176]{3,2,1,0:T(8,128)(2,1)S(1)} collective-permute-done((bf16[2,1,64,2176]{3,2,1,0:T(8,128)(2,1)S(1)}, bf16[2,1,64,2176]{3,2,1,0:T(8,128)(2,1)S(1)}, u32[]{:S(2)}, u32[]{:S(2)}) %collective-permute-start.76) | collective-permute-done | bytes 557088 | tf_op jit(solution)/shard_map/ppermute | solution.py:31
  426.8 10.7 %collective-permute-done.70 = bf16[2,1,64,2176]{3,2,1,0:T(8,128)(2,1)S(1)} collective-permute-done((bf16[2,1,64,2176]{3,2,1,0:T(8,128)(2,1)S(1)}, bf16[2,1,64,2176]{3,2,1,0:T(8,128)(2,1)S(1)}, u32[]{:S(2)}, u32[]{:S(2)}) %collective-permute-start.70) | collective-permute-done | bytes 557088 | tf_op jit(solution)/shard_map/ppermute | solution.py:31
  439.9 10.7 %collective-permute-done.71 = bf16[1,64,2176]{2,1,0:T(8,128)(2,1)S(1)} collective-permute-done((bf16[1,64,2176]{2,1,0:T(8,128)(2,1)S(1)}, bf16[1,64,2176]{2,1,0:T(8,128)(2,1)S(1)}, u32[]{:S(2)}, u32[]{:S(2)}) %collective-permute-start.71) | collective-permute-done | bytes 278560 | tf_op jit(solution)/shard_map/ppermute | solution.py:31
  451.4 6.5 collective-permute-done.69
  464.6 7.8 collective-permute-done.72
  473.3 10.6 %collective-permute-done.78.refs_0_ = bf16[2,64,2176]{2,1,0:T(8,128)(2,1)S(1)} collective-permute-done((bf16[2,64,2176]{2,1,0:T(8,128)(2,1)S(1)}, bf16[2,64,2176]{2,1,0:T(8,128)(2,1)S(1)}, u32[]{:S(2)}, u32[]{:S(2)}) %collective-permute-start.78) | collective-permute-done | bytes 557088 | tf_op jit(solution)/shard_map/ppermute | solution.py:57
  484.7 5.4 turn.1
  490.1 8.7 %mix.2 = bf16[4,4,128,2048]{3,2,1,0:T(8,128)(2,1)} custom-call(bf16[4,512,512]{2,1,0:T(8,128)(2,1)} %bitcast.509, bf16[512,2048]{1,0:T(8,128)(2,1)} %bitcast.497), custom_call_target="tpu_custom_call" | custom-call | flops 4294967296 | bytes 20971520 | tf_op jit(solution)/shard_map/mix/pallas_call | solution.py:507
  501.0 6.8 collective-permute-done.85
  511.5 10.7 %collective-permute-done.86 = bf16[2,1,64,2048]{3,2,0,1:T(8,128)(2,1)S(1)} collective-permute-done((bf16[2,1,64,2048]{3,2,0,1:T(8,128)(2,1)S(1)}, bf16[2,1,64,2048]{3,2,0,1:T(8,128)(2,1)S(1)}, u32[]{:S(2)}, u32[]{:S(2)}) %collective-permute-start.86) | collective-permute-done | bytes 524320 | tf_op jit(solution)/shard_map/ppermute | solution.py:31
  528.7 14.4 %attend_back.1 = (f32[512,512]{1,0:T(8,128)}, f32[512,512]{1,0:T(8,128)}, bf16[512,512]{1,0:T(8,128)(2,1)}, f32[4,8,128]{2,1,0:T(8,128)}, f32[8,512]{1,0:T(8,128)}, /*index=5*/bf16[512,2048]{1,0:T(8,128)(2,1)}) custom-call(bf16[2,64,2048]{2,1,0:T(8,128)(2,1)} %get-tuple-element.186.g0, bf16[2,64,2048]{2,1,0:T(8,128)(2,1)} %bitcast.520, ...), custom_call_target="tpu_custom_call" | custom-call | flops 2415919104 | bytes 16289792 | tf_op jit(solution)/shard_map/attend_back/pallas_call | solution.py:163
  550.6 16.3 %project_back.1 = (bf16[2,64,2048]{2,1,0:T(8,128)(2,1)}, bf16[2,64,2048]{2,1,0:T(8,128)(2,1)}, bf16[2,64,2048]{2,1,0:T(8,128)(2,1)}, bf16[2,64,2048]{2,1,0:T(8,1...) custom-call(s32[8]{0:T(128)} %stack.217.at_ref, s32[1]{0:T(128)} %bitcast.24.core_ref, ...), custom_call_target="tpu_custom_call" | custom-call | flops 6442450944 | bytes 27590692 | tf_op jit(solution)/shard_map/project_back/pallas_call | solution.py:163
  572.2 5.6 collective-permute-done.96
  601.5 10.7 %mix.3 = bf16[4,4,128,2048]{3,2,1,0:T(8,128)(2,1)} custom-call(bf16[4,512,512]{2,1,0:T(8,128)(2,1)} %bitcast.499, bf16[512,2048]{1,0:T(8,128)(2,1)} %bitcast.498, bf16[4,4,128,2048]{3,2,1,0:T(8,128)(2,1)} %collective-permute-done.87.refs_0_), custom_call_target="tpu_custom_call" | custom-call | flops 4294967296 | bytes 20971520 | tf_op jit(solution)/shard_map/mix/pallas_call | solution.py:507
  619.1 19.7 %collective-permute-done.104 = bf16[4,64,1536]{2,1,0:T(8,128)(2,1)S(1)} collective-permute-done((bf16[4,64,1536]{2,1,0:T(8,128)(2,1)S(1)}, bf16[4,64,1536]{2,1,0:T(8,128)(2,1)S(1)}, u32[]{:S(2)}, u32[]{:S(2)}) %collective-permute-start.104) | collective-permute-done | bytes 786464 | tf_op jit(solution)/shard_map/ppermute | solution.py:57
  639.3 5.2 collective-permute-done.116
  644.6 16.7 %collective-permute-done.105 = bf16[4,64,1536]{2,1,0:T(8,128)(2,1)S(1)} collective-permute-done((bf16[4,64,1536]{2,1,0:T(8,128)(2,1)S(1)}, bf16[4,64,1536]{2,1,0:T(8,128)(2,1)S(1)}, u32[]{:S(2)}, u32[]{:S(2)}) %collective-permute-start.105) | collective-permute-done | bytes 786464 | tf_op jit(solution)/shard_map/ppermute | solution.py:57
  662.4 15.9 %down_grads.1 = f32[2,256,2048]{2,1,0:T(8,128)} custom-call(bf16[4,512,512]{2,1,0:T(8,128)(2,1)} %bitcast.500, bf16[4,512,512]{2,1,0:T(8,128)(2,1)} %bitcast.510, bf16[4,4,2,64,2176]{4,3,2,1,0:T(8,128)(2,1)} %bitcast.481, bf16[4,4,2,64,2176]{4,3,2,1,0:T(8,128)(2,1)} %collective-permute-done.32.cot_ref.refs_10_.cot_b), custom_call_target="tpu_custom_call" | custom-call | flops 8589934592 | bytes 25165824 | tf_op jit(solution)/shard_map/down_grads/pallas_call | solution.py:601
  691.1 8.8 %collective-permute-done.108 = bf16[96,1536]{1,0:T(8,128)(2,1)S(1)} collective-permute-done((bf16[96,1536]{1,0:T(8,128)(2,1)S(1)}, bf16[96,1536]{1,0:T(8,128)(2,1)S(1)}, u32[]{:S(2)}, u32[]{:S(2)}) %collective-permute-start.108) | collective-permute-done | bytes 294944 | tf_op jit(solution)/shard_map/ppermute | solution.py:31
  708.2 15.8 %row_grads.3 = f32[2,2048,256]{2,1,0:T(8,128)} custom-call(bf16[2,512,1024]{2,1,0:T(8,128)(2,1)} %get-tuple-element.214.refs_0_, bf16[2,64,2048]{2,1,0:T(8,128)(2,1)} %copy-done.1, bf16[2,64,2048]{2,1,0:T(8,128)(2,1)} %bitcast.457, bf16[2,64,2048]{2,1,0:T(8,128)(2,1)} %copy-done.4, bf16[2,64,2048]{2,1,0:T(8,128)(2,1)} %bitcast.57.refs_4_, ...), custom_call_target="tpu_custom_call" | custom-call | flops 8589934592 | bytes 25165824 | tf_op jit(solution)/shard_map/row_grads/pallas_call | solution.py:561
  729.7 7.5 collective-permute-done.120
  738.7 15.4 %collective-permute-done.112 = bf16[4,64,1536]{2,1,0:T(8,128)(2,1)S(1)} collective-permute-done((bf16[4,64,1536]{2,1,0:T(8,128)(2,1)}, bf16[4,64,1536]{2,1,0:T(8,128)(2,1)S(1)}, u32[]{:S(2)}, u32[]{:S(2)}) %collective-permute-start.112) | collective-permute-done | bytes 786464 | tf_op jit(solution)/shard_map/ppermute | solution.py:57
  755.7 17.6 %collective-permute-done.113 = bf16[4,64,1536]{2,1,0:T(8,128)(2,1)S(1)} collective-permute-done((bf16[4,64,1536]{2,1,0:T(8,128)(2,1)S(1)}, bf16[4,64,1536]{2,1,0:T(8,128)(2,1)S(1)}, u32[]{:S(2)}, u32[]{:S(2)}) %collective-permute-start.113) | collective-permute-done | bytes 786464 | tf_op jit(solution)/shard_map/ppermute | solution.py:57
  774.6 15.6 %row_grads.2 = f32[2,2048,256]{2,1,0:T(8,128)} custom-call(bf16[2,512,1024]{2,1,0:T(8,128)(2,1)} %get-tuple-element.214.refs_0_, bf16[2,64,2048]{2,1,0:T(8,128)(2,1)} %copy-done.1, bf16[2,64,2048]{2,1,0:T(8,128)(2,1)} %bitcast.458, bf16[2,64,2048]{2,1,0:T(8,128)(2,1)} %copy-done.4, bf16[2,64,2048]{2,1,0:T(8,128)(2,1)} %bitcast.57.refs_4_, ...), custom_call_target="tpu_custom_call" | custom-call | flops 8589934592 | bytes 25165824 | tf_op jit(solution)/shard_map/row_grads/pallas_call | solution.py:561
  805.7 14.0 %collective-permute-done.88 = bf16[128,2048]{1,0:T(8,128)(2,1)S(1)} collective-permute-done((bf16[128,2048]{1,0:T(8,128)(2,1)S(1)}, bf16[128,2048]{1,0:T(8,128)(2,1)S(1)}, u32[]{:S(2)}, u32[]{:S(2)}) %collective-permute-start.88) | collective-permute-done | bytes 524320 | tf_op jit(solution)/shard_map/ppermute | solution.py:57
  822.6 12.1 %collective-permute-done.89 = bf16[128,2048]{1,0:T(8,128)(2,1)S(1)} collective-permute-done((bf16[128,2048]{1,0:T(8,128)(2,1)S(1)}, bf16[128,2048]{1,0:T(8,128)(2,1)S(1)}, u32[]{:S(2)}, u32[]{:S(2)}) %collective-permute-start.89) | collective-permute-done | bytes 524320 | tf_op jit(solution)/shard_map/ppermute | solution.py:57
  840.0 8.7 %collective-permute-done.90 = bf16[128,2048]{1,0:T(8,128)(2,1)S(1)} collective-permute-done((bf16[128,2048]{1,0:T(8,128)(2,1)S(1)}, bf16[128,2048]{1,0:T(8,128)(2,1)S(1)}, u32[]{:S(2)}, u32[]{:S(2)}) %collective-permute-start.90) | collective-permute-done | bytes 524320 | tf_op jit(solution)/shard_map/ppermute | solution.py:57
  (567 shorter events, 274.0 us)
Async XLA Ops:
  7.2 182.5 %all-gather.2.cloned.1.call-start = ((), (), s32[]{:S(2)}) async-start(), calls=%async_computation.1 | async-start | bytes 11141120 | tf_op jit(solution)/shard_map/all_gather | solution.py:903
  25.8 26.6 %collective-permute-start.7 = (bf16[384,1536]{1,0:T(8,128)(2,1)}, bf16[384,1536]{1,0:T(8,128)(2,1)S(1)}, u32[]{:S(2)}, u32[]{:S(2)}) collective-permute-start(bf16[384,1536]{1,0:T(8,128)(2,1)} %get-tuple-element.122), channel_id=1, source_target_pairs={{0,8},{8,0},{16,24},{24,16},{1,9},{9,1},{17,25},{25,17},{2,10},{10... | collective-permute-start | bytes 3538952 | tf_op jit(solution)/shard_map/ppermute | solution.py:31
  26.4 26.6 %collective-permute-start.8 = (bf16[384,1536]{1,0:T(8,128)(2,1)}, bf16[384,1536]{1,0:T(8,128)(2,1)}, u32[]{:S(2)}, u32[]{:S(2)}) collective-permute-start(bf16[384,1536]{1,0:T(8,128)(2,1)} %get-tuple-element.123), channel_id=1, source_target_pairs={{0,16},{8,24},{16,0},{24,8},{1,17},{9,25},{17,1},{25,9},{2,18},{10... | collective-permute-start | bytes 3538952 | tf_op jit(solution)/shard_map/ppermute | solution.py:31
  70.4 732.4 %reduce-scatter.2.cloned.1.call-start = ((), (), s32[]{:S(2)}) async-start(), calls=%async_computation.2 | async-start | bytes 10485760 | tf_op jit(solution)/shard_map/reduce_scatter | solution.py:1049
  81.2 27.2 %collective-permute-start.11 = (bf16[256,1536]{1,0:T(8,128)(2,1)S(1)}, bf16[256,1536]{1,0:T(8,128)(2,1)S(1)}, u32[]{:S(2)}, u32[]{:S(2)}) collective-permute-start(bf16[256,1536]{1,0:T(8,128)(2,1)S(1)} %slice.523.refs_2_), channel_id=1, source_target_pairs={{0,1},{1,0},{2,3},{3,2},{4,5},{5,4},{6,7},{7,6},{8,9},{9,8},{10,11... | collective-permute-start | bytes 2359304 | tf_op jit(solution)/shard_map/ppermute | solution.py:48
  81.2 27.2 %collective-permute-start.12 = (bf16[256,1536]{1,0:T(8,128)(2,1)S(1)}, bf16[256,1536]{1,0:T(8,128)(2,1)S(1)}, u32[]{:S(2)}, u32[]{:S(2)}) collective-permute-start(bf16[256,1536]{1,0:T(8,128)(2,1)S(1)} %slice.524.refs_3_), channel_id=1, source_target_pairs={{0,1},{1,0},{2,3},{3,2},{4,5},{5,4},{6,7},{7,6},{8,9},{9,8},{10,11... | collective-permute-start | bytes 2359304 | tf_op jit(solution)/shard_map/ppermute | solution.py:48
  81.7 26.7 %collective-permute-start.13 = (bf16[256,1536]{1,0:T(8,128)(2,1)}, bf16[256,1536]{1,0:T(8,128)(2,1)S(1)}, u32[]{:S(2)}, u32[]{:S(2)}) collective-permute-start(bf16[256,1536]{1,0:T(8,128)(2,1)} %copy-done.68), channel_id=1, source_target_pairs={{0,1},{1,0},{2,3},{3,2},{4,5},{5,4},{6,7},{7,6},{8,9},{9,8},{10,11... | collective-permute-start | bytes 2359304 | tf_op jit(solution)/shard_map/ppermute | solution.py:48
  81.8 25.9 %collective-permute-start.3 = (bf16[2,1,64,2048]{3,2,0,1:T(8,128)(2,1)S(1)}, bf16[2,1,64,2048]{3,2,0,1:T(8,128)(2,1)S(1)}, u32[]{:S(2)}, u32[]{:S(2)}) collective-permute-start(bf16[2,1,64,2048]{3,2,0,1:T(8,128)(2,1)S(1)} %copy-done.57), channel_id=1, source_target_pairs={{0,8},{8,0},{16,24},{24,16},{1,9},{9,1},{17,25},{25,17},{2,10},{10... | collective-permute-start | bytes 1572872 | tf_op jit(solution)/shard_map/ppermute | solution.py:31
  82.7 25.7 %collective-permute-start.1 = (bf16[2,1,64,2048]{3,2,0,1:T(8,128)(2,1)S(1)}, bf16[2,1,64,2048]{3,2,0,1:T(8,128)(2,1)S(1)}, u32[]{:S(2)}, u32[]{:S(2)}) collective-permute-start(bf16[2,1,64,2048]{3,2,0,1:T(8,128)(2,1)S(1)} %get-tuple-element.314), channel_id=1, source_target_pairs={{0,16},{8,24},{16,0},{24,8},{1,17},{9,25},{17,1},{25,9},{2,18},{10... | collective-permute-start | bytes 1572872 | tf_op jit(solution)/shard_map/ppermute | solution.py:31
  137.0 25.1 %collective-permute-start.19 = (bf16[2,1,64,2048]{3,2,1,0:T(8,128)(2,1)}, bf16[2,1,64,2048]{3,2,1,0:T(8,128)(2,1)S(1)}, u32[]{:S(2)}, u32[]{:S(2)}) collective-permute-start(bf16[2,1,64,2048]{3,2,1,0:T(8,128)(2,1)} %bitcast.558), channel_id=1, source_target_pairs={{0,8},{8,0},{16,24},{24,16},{1,9},{9,1},{17,25},{25,17},{2,10},{10... | collective-permute-start | bytes 1572872 | tf_op jit(solution)/shard_map/ppermute | solution.py:31
  139.6 26.0 %collective-permute-start.17 = (bf16[2,1,64,2048]{3,2,1,0:T(8,128)(2,1)}, bf16[2,1,64,2048]{3,2,1,0:T(8,128)(2,1)S(1)}, u32[]{:S(2)}, u32[]{:S(2)}) collective-permute-start(bf16[2,1,64,2048]{3,2,1,0:T(8,128)(2,1)} %bitcast.557), channel_id=1, source_target_pairs={{0,16},{8,24},{16,0},{24,8},{1,17},{9,25},{17,1},{25,9},{2,18},{10... | collective-permute-start | bytes 1572872 | tf_op jit(solution)/shard_map/ppermute | solution.py:31
  189.7 61.3 %collective-permute-start.32 = (bf16[4,4,2,64,2176]{4,3,2,1,0:T(8,128)(2,1)}, bf16[4,4,2,64,2176]{4,3,2,1,0:T(8,128)(2,1)}, u32[]{:S(2)}, u32[]{:S(2)}) collective-permute-start(bf16[4,4,2,64,2176]{4,3,2,1,0:T(8,128)(2,1)} %bitcast.475), channel_id=1, source_target_pairs={{0,1},{1,0},{2,3},{3,2},{4,5},{5,4},{6,7},{7,6},{8,9},{9,8},{10,11... | collective-permute-start | bytes 26738696 | tf_op jit(solution)/shard_map/ppermute | solution.py:48
  228.1 32.7 %collective-permute-start.40 = (bf16[2,64,2048]{2,1,0:T(8,128)(2,1)S(1)}, bf16[2,64,2048]{2,1,0:T(8,128)(2,1)}, u32[]{:S(2)}, u32[]{:S(2)}) collective-permute-start(bf16[2,64,2048]{2,1,0:T(8,128)(2,1)S(1)} %get-tuple-element.301.refs_3_.refs_12_), channel_id=1, source_target_pairs={{0,1},{1,0},{2,3},{3,2},{4,5},{5,4},{6,7},{7,6},{8,9},{9,8},{10,11... | collective-permute-start | bytes 1572872 | tf_op jit(solution)/shard_map/ppermute | solution.py:48
  230.3 32.0 %collective-permute-start.38 = (bf16[2,64,2048]{2,1,0:T(8,128)(2,1)S(1)}, bf16[2,64,2048]{2,1,0:T(8,128)(2,1)}, u32[]{:S(2)}, u32[]{:S(2)}) collective-permute-start(bf16[2,64,2048]{2,1,0:T(8,128)(2,1)S(1)} %get-tuple-element.307.refs_1_.refs_10_), channel_id=1, source_target_pairs={{0,1},{1,0},{2,3},{3,2},{4,5},{5,4},{6,7},{7,6},{8,9},{9,8},{10,11... | collective-permute-start | bytes 1572872 | tf_op jit(solution)/shard_map/ppermute | solution.py:48
  232.8 30.1 %collective-permute-start.41 = (bf16[2,64,2048]{2,1,0:T(8,128)(2,1)S(1)}, bf16[2,64,2048]{2,1,0:T(8,128)(2,1)}, u32[]{:S(2)}, u32[]{:S(2)}) collective-permute-start(bf16[2,64,2048]{2,1,0:T(8,128)(2,1)S(1)} %bitcast.451), channel_id=1, source_target_pairs={{0,1},{1,0},{2,3},{3,2},{4,5},{5,4},{6,7},{7,6},{8,9},{9,8},{10,11... | collective-permute-start | bytes 1572872 | tf_op jit(solution)/shard_map/ppermute | solution.py:48
  240.9 23.4 %collective-permute-start.39 = (bf16[2,64,2048]{2,1,0:T(8,128)(2,1)}, bf16[2,64,2048]{2,1,0:T(8,128)(2,1)}, u32[]{:S(2)}, u32[]{:S(2)}) collective-permute-start(bf16[2,64,2048]{2,1,0:T(8,128)(2,1)} %bitcast.68.refs_2_.refs_11_), channel_id=1, source_target_pairs={{0,1},{1,0},{2,3},{3,2},{4,5},{5,4},{6,7},{7,6},{8,9},{9,8},{10,11... | collective-permute-start | bytes 1572872 | tf_op jit(solution)/shard_map/ppermute | solution.py:48
  251.0 35.2 %collective-permute-start.24 = (bf16[2,1,64,2048]{3,2,0,1:T(8,128)(2,1)}, bf16[2,1,64,2048]{3,2,0,1:T(8,128)(2,1)}, u32[]{:S(2)}, u32[]{:S(2)}) collective-permute-start(bf16[2,1,64,2048]{3,2,0,1:T(8,128)(2,1)} %get-tuple-element.284), channel_id=1, source_target_pairs={{0,8},{8,0},{16,24},{24,16},{1,9},{9,1},{17,25},{25,17},{2,10},{10... | collective-permute-start | bytes 1572872 | tf_op jit(solution)/shard_map/ppermute | solution.py:31
  260.9 25.4 %collective-permute-start.22 = (bf16[2,1,64,2048]{3,2,0,1:T(8,128)(2,1)}, bf16[2,1,64,2048]{3,2,0,1:T(8,128)(2,1)S(1)}, u32[]{:S(2)}, u32[]{:S(2)}) collective-permute-start(bf16[2,1,64,2048]{3,2,0,1:T(8,128)(2,1)} %get-tuple-element.290), channel_id=1, source_target_pairs={{0,16},{8,24},{16,0},{24,8},{1,17},{9,25},{17,1},{25,9},{2,18},{10... | collective-permute-start | bytes 1572872 | tf_op jit(solution)/shard_map/ppermute | solution.py:31
  262.2 24.5 %collective-permute-start.46 = (bf16[1,64,2048]{2,1,0:T(8,128)(2,1)}, bf16[1,64,2048]{2,1,0:T(8,128)(2,1)S(1)}, u32[]{:S(2)}, u32[]{:S(2)}) collective-permute-start(bf16[1,64,2048]{2,1,0:T(8,128)(2,1)} %get-tuple-element.280), channel_id=1, source_target_pairs={{0,16},{8,24},{16,0},{24,8},{1,17},{9,25},{17,1},{25,9},{2,18},{10... | collective-permute-start | bytes 786440 | tf_op jit(solution)/shard_map/ppermute | solution.py:31
  262.9 24.0 %collective-permute-start.44 = (bf16[1,64,2048]{2,1,0:T(8,128)(2,1)}, bf16[1,64,2048]{2,1,0:T(8,128)(2,1)S(1)}, u32[]{:S(2)}, u32[]{:S(2)}) collective-permute-start(bf16[1,64,2048]{2,1,0:T(8,128)(2,1)} %get-tuple-element.281), channel_id=1, source_target_pairs={{0,8},{8,0},{16,24},{24,16},{1,9},{9,1},{17,25},{25,17},{2,10},{10... | collective-permute-start | bytes 786440 | tf_op jit(solution)/shard_map/ppermute | solution.py:31
  264.3 23.0 %collective-permute-start.56 = (bf16[1,64,2048]{2,1,0:T(8,128)(2,1)}, bf16[1,64,2048]{2,1,0:T(8,128)(2,1)S(1)}, u32[]{:S(2)}, u32[]{:S(2)}) collective-permute-start(bf16[1,64,2048]{2,1,0:T(8,128)(2,1)} %get-tuple-element.296), channel_id=1, source_target_pairs={{0,16},{8,24},{16,0},{24,8},{1,17},{9,25},{17,1},{25,9},{2,18},{10... | collective-permute-start | bytes 786440 | tf_op jit(solution)/shard_map/ppermute | solution.py:31
  287.3 31.3 %collective-permute-start.52 = (bf16[4,2,1,64,2176]{4,3,1,2,0:T(8,128)(2,1)}, bf16[4,2,1,64,2176]{4,3,1,2,0:T(8,128)(2,1)S(1)}, u32[]{:S(2)}, u32[]{:S(2)}) collective-permute-start(bf16[4,2,1,64,2176]{4,3,1,2,0:T(8,128)(2,1)} %bitcast.549), channel_id=1, source_target_pairs={{0,1},{1,0},{2,3},{3,2},{4,5},{5,4},{6,7},{7,6},{8,9},{9,8},{10,11... | collective-permute-start | bytes 6684680 | tf_op jit(solution)/shard_map/ppermute | solution.py:48
  290.3 31.4 %collective-permute-start.47 = (bf16[2,1,64,2048]{3,2,1,0:T(8,128)(2,1)}, bf16[2,1,64,2048]{3,2,1,0:T(8,128)(2,1)S(1)}, u32[]{:S(2)}, u32[]{:S(2)}) collective-permute-start(bf16[2,1,64,2048]{3,2,1,0:T(8,128)(2,1)} %get-tuple-element.276), channel_id=1, source_target_pairs={{0,8},{8,0},{16,24},{24,16},{1,9},{9,1},{17,25},{25,17},{2,10},{10... | collective-permute-start | bytes 1572872 | tf_op jit(solution)/shard_map/ppermute | solution.py:31
  291.6 30.1 %collective-permute-start.45 = (bf16[2,1,64,2048]{3,2,1,0:T(8,128)(2,1)}, bf16[2,1,64,2048]{3,2,1,0:T(8,128)(2,1)S(1)}, u32[]{:S(2)}, u32[]{:S(2)}) collective-permute-start(bf16[2,1,64,2048]{3,2,1,0:T(8,128)(2,1)} %get-tuple-element.282), channel_id=1, source_target_pairs={{0,16},{8,24},{16,0},{24,8},{1,17},{9,25},{17,1},{25,9},{2,18},{10... | collective-permute-start | bytes 1572872 | tf_op jit(solution)/shard_map/ppermute | solution.py:31
  293.8 28.5 %collective-permute-start.57 = (bf16[2,1,64,2048]{3,2,0,1:T(8,128)(2,1)}, bf16[2,1,64,2048]{3,2,0,1:T(8,128)(2,1)S(1)}, u32[]{:S(2)}, u32[]{:S(2)}) collective-permute-start(bf16[2,1,64,2048]{3,2,0,1:T(8,128)(2,1)} %get-tuple-element.292), channel_id=1, source_target_pairs={{0,8},{8,0},{16,24},{24,16},{1,9},{9,1},{17,25},{25,17},{2,10},{10... | collective-permute-start | bytes 1572872 | tf_op jit(solution)/shard_map/ppermute | solution.py:31
  321.7 37.1 %collective-permute-start.50 = (bf16[2,64,2048]{2,1,0:T(8,128)(2,1)S(1)}, bf16[2,64,2048]{2,1,0:T(8,128)(2,1)S(1)}, u32[]{:S(2)}, u32[]{:S(2)}) collective-permute-start(bf16[2,64,2048]{2,1,0:T(8,128)(2,1)S(1)} %get-tuple-element.277.refs_3_.refs_21_), channel_id=1, source_target_pairs={{0,1},{1,0},{2,3},{3,2},{4,5},{5,4},{6,7},{7,6},{8,9},{9,8},{10,11... | collective-permute-start | bytes 1572872 | tf_op jit(solution)/shard_map/ppermute | solution.py:48
  333.5 25.9 %collective-permute-start.48 = (bf16[2,64,2048]{2,1,0:T(8,128)(2,1)S(1)}, bf16[2,64,2048]{2,1,0:T(8,128)(2,1)S(1)}, u32[]{:S(2)}, u32[]{:S(2)}) collective-permute-start(bf16[2,64,2048]{2,1,0:T(8,128)(2,1)S(1)} %get-tuple-element.283.refs_1_.refs_19_), channel_id=1, source_target_pairs={{0,1},{1,0},{2,3},{3,2},{4,5},{5,4},{6,7},{7,6},{8,9},{9,8},{10,11... | collective-permute-start | bytes 1572872 | tf_op jit(solution)/shard_map/ppermute | solution.py:48
  333.6 25.9 %collective-permute-start.51 = (bf16[2,64,2048]{2,1,0:T(8,128)(2,1)S(1)}, bf16[2,64,2048]{2,1,0:T(8,128)(2,1)S(1)}, u32[]{:S(2)}, u32[]{:S(2)}) collective-permute-start(bf16[2,64,2048]{2,1,0:T(8,128)(2,1)S(1)} %bitcast.459), channel_id=1, source_target_pairs={{0,1},{1,0},{2,3},{3,2},{4,5},{5,4},{6,7},{7,6},{8,9},{9,8},{10,11... | collective-permute-start | bytes 1572872 | tf_op jit(solution)/shard_map/ppermute | solution.py:48
  334.0 25.4 %collective-permute-start.49 = (bf16[2,64,2048]{2,1,0:T(8,128)(2,1)S(1)}, bf16[2,64,2048]{2,1,0:T(8,128)(2,1)S(1)}, u32[]{:S(2)}, u32[]{:S(2)}) collective-permute-start(bf16[2,64,2048]{2,1,0:T(8,128)(2,1)S(1)} %bitcast.463), channel_id=1, source_target_pairs={{0,1},{1,0},{2,3},{3,2},{4,5},{5,4},{6,7},{7,6},{8,9},{9,8},{10,11... | collective-permute-start | bytes 1572872 | tf_op jit(solution)/shard_map/ppermute | solution.py:48
  334.4 53.3 %collective-permute-start.64 = (bf16[2,1,64,2176]{3,2,1,0:T(8,128)(2,1)}, bf16[2,1,64,2176]{3,2,1,0:T(8,128)(2,1)}, u32[]{:S(2)}, u32[]{:S(2)}) collective-permute-start(bf16[2,1,64,2176]{3,2,1,0:T(8,128)(2,1)} %bitcast.110), channel_id=1, source_target_pairs={{0,8},{8,0},{16,24},{24,16},{1,9},{9,1},{17,25},{25,17},{2,10},{10... | collective-permute-start | bytes 1671176 | tf_op jit(solution)/shard_map/ppermute | solution.py:31
  358.8 30.0 %collective-permute-start.62 = (bf16[2,1,64,2176]{3,2,0,1:T(8,128)(2,1)}, bf16[2,1,64,2176]{3,2,0,1:T(8,128)(2,1)S(1)}, u32[]{:S(2)}, u32[]{:S(2)}) collective-permute-start(bf16[2,1,64,2176]{3,2,0,1:T(8,128)(2,1)} %get-tuple-element.153), channel_id=1, source_target_pairs={{0,16},{8,24},{16,0},{24,8},{1,17},{9,25},{17,1},{25,9},{2,18},{10... | collective-permute-start | bytes 1671176 | tf_op jit(solution)/shard_map/ppermute | solution.py:31
  359.4 49.2 %collective-permute-start.73 = (bf16[4,2,1,64,2176]{4,3,1,2,0:T(8,128)(2,1)}, bf16[4,2,1,64,2176]{4,3,1,2,0:T(8,128)(2,1)S(1)}, u32[]{:S(2)}, u32[]{:S(2)}) collective-permute-start(bf16[4,2,1,64,2176]{4,3,1,2,0:T(8,128)(2,1)} %bitcast.127), channel_id=1, source_target_pairs={{0,1},{1,0},{2,3},{3,2},{4,5},{5,4},{6,7},{7,6},{8,9},{9,8},{10,11... | collective-permute-start | bytes 6684680 | tf_op jit(solution)/shard_map/ppermute | solution.py:48
  387.8 23.5 %collective-permute-start.67 = (bf16[4,2,1,64,2176]{4,3,1,2,0:T(8,128)(2,1)S(1)}, bf16[4,2,1,64,2176]{4,3,1,2,0:T(8,128)(2,1)S(1)}, u32[]{:S(2)}, u32[]{:S(2)}) collective-permute-start(bf16[4,2,1,64,2176]{4,3,1,2,0:T(8,128)(2,1)S(1)} %bitcast.550), channel_id=1, source_target_pairs={{0,1},{1,0},{2,3},{3,2},{4,5},{5,4},{6,7},{7,6},{8,9},{9,8},{10,11... | collective-permute-start | bytes 6684680 | tf_op jit(solution)/shard_map/ppermute | solution.py:48
  400.2 73.1 %collective-permute-start.80 = (bf16[1,64,2176]{2,1,0:T(8,128)(2,1)S(1)}, bf16[1,64,2176]{2,1,0:T(8,128)(2,1)S(1)}, u32[]{:S(2)}, u32[]{:S(2)}) collective-permute-start(bf16[1,64,2176]{2,1,0:T(8,128)(2,1)S(1)} %fusion.38), channel_id=1, source_target_pairs={{0,8},{8,0},{16,24},{24,16},{1,9},{9,1},{17,25},{25,17},{2,10},{10... | collective-permute-start | bytes 835592 | tf_op jit(solution)/shard_map/ppermute | solution.py:31
  404.3 69.0 %collective-permute-start.82 = (bf16[1,64,2176]{2,1,0:T(8,128)(2,1)S(1)}, bf16[1,64,2176]{2,1,0:T(8,128)(2,1)S(1)}, u32[]{:S(2)}, u32[]{:S(2)}) collective-permute-start(bf16[1,64,2176]{2,1,0:T(8,128)(2,1)S(1)} %fusion.42), channel_id=1, source_target_pairs={{0,16},{8,24},{16,0},{24,8},{1,17},{9,25},{17,1},{25,9},{2,18},{10... | collective-permute-start | bytes 835592 | tf_op jit(solution)/shard_map/ppermute | solution.py:31
  408.6 50.5 %collective-permute-start.66 = (bf16[2,64,2176]{2,1,0:T(8,128)(2,1)S(1)}, bf16[2,64,2176]{2,1,0:T(8,128)(2,1)S(1)}, u32[]{:S(2)}, u32[]{:S(2)}) collective-permute-start(bf16[2,64,2176]{2,1,0:T(8,128)(2,1)S(1)} %pad_maximum_fusion.6), channel_id=1, source_target_pairs={{0,2},{1,3},{2,4},{3,5},{4,6},{5,7},{6,0},{7,1},{8,10},{9,11},{10,... | collective-permute-start | bytes 1671176 | tf_op jit(solution)/shard_map/ppermute | solution.py:57
  498.8 102.7 %collective-permute-start.87 = (bf16[4,4,128,2048]{3,2,1,0:T(8,128)(2,1)}, bf16[4,4,128,2048]{3,2,1,0:T(8,128)(2,1)}, u32[]{:S(2)}, u32[]{:S(2)}) collective-permute-start(bf16[4,4,128,2048]{3,2,1,0:T(8,128)(2,1)} %mix.2), channel_id=1, source_target_pairs={{0,1},{1,0},{2,3},{3,2},{4,5},{5,4},{6,7},{7,6},{8,9},{9,8},{10,11... | collective-permute-start | bytes 25165832 | tf_op jit(solution)/shard_map/ppermute | solution.py:48
  572.2 40.1 %collective-permute-start.103 = (bf16[4,256,1536]{2,1,0:T(8,128)(2,1)}, bf16[4,256,1536]{2,1,0:T(8,128)(2,1)S(1)}, u32[]{:S(2)}, u32[]{:S(2)}) collective-permute-start(bf16[4,256,1536]{2,1,0:T(8,128)(2,1)} %get-tuple-element.212), channel_id=1, source_target_pairs={{0,1},{1,0},{2,3},{3,2},{4,5},{5,4},{6,7},{7,6},{8,9},{9,8},{10,11... | collective-permute-start | bytes 9437192 | tf_op jit(solution)/shard_map/ppermute | solution.py:48
  600.2 38.9 %collective-permute-start.99 = (f32[32,512]{1,0:T(8,128)S(1)}, f32[32,512]{1,0:T(8,128)S(1)}, u32[]{:S(2)}, u32[]{:S(2)}) collective-permute-start(f32[32,512]{1,0:T(8,128)S(1)} %get-tuple-element.321), channel_id=1, source_target_pairs={{0,8},{8,0},{16,24},{24,16},{1,9},{9,1},{17,25},{25,17},{2,10},{10... | collective-permute-start | bytes 196616 | tf_op jit(solution)/shard_map/ppermute | solution.py:31
  619.1 25.4 %collective-permute-start.116 = (bf16[1,64,2048]{2,1,0:T(8,128)(2,1)S(1)}, bf16[1,64,2048]{2,1,0:T(8,128)(2,1)S(1)}, u32[]{:S(2)}, u32[]{:S(2)}) collective-permute-start(bf16[1,64,2048]{2,1,0:T(8,128)(2,1)S(1)} %fusion.43), channel_id=1, source_target_pairs={{0,2},{1,3},{2,4},{3,5},{4,6},{5,7},{6,0},{7,1},{8,10},{9,11},{10,... | collective-permute-start | bytes 786440 | tf_op jit(solution)/shard_map/ppermute | solution.py:57
  639.2 39.1 %collective-permute-start.100 = (f32[20,512]{1,0:T(8,128)S(1)}, f32[20,512]{1,0:T(8,128)S(1)}, u32[]{:S(2)}, u32[]{:S(2)}) collective-permute-start(f32[20,512]{1,0:T(8,128)S(1)} %pad_maximum_fusion.24), channel_id=1, source_target_pairs={{0,1},{1,0},{2,3},{3,2},{4,5},{5,4},{6,7},{7,6},{8,9},{9,8},{10,11... | collective-permute-start | bytes 122888 | tf_op jit(solution)/shard_map/ppermute | solution.py:48
  644.5 35.1 %collective-permute-start.117 = (bf16[1,64,2048]{2,1,0:T(8,128)(2,1)S(1)}, bf16[1,64,2048]{2,1,0:T(8,128)(2,1)S(1)}, u32[]{:S(2)}, u32[]{:S(2)}) collective-permute-start(bf16[1,64,2048]{2,1,0:T(8,128)(2,1)S(1)} %fusion.34), channel_id=1, source_target_pairs={{0,2},{1,3},{2,4},{3,5},{4,6},{5,7},{6,0},{7,1},{8,10},{9,11},{10,... | collective-permute-start | bytes 786440 | tf_op jit(solution)/shard_map/ppermute | solution.py:57
  679.6 44.4 %collective-permute-start.101 = (f32[20,512]{1,0:T(8,128)}, f32[20,512]{1,0:T(8,128)}, u32[]{:S(2)}, u32[]{:S(2)}) collective-permute-start(f32[20,512]{1,0:T(8,128)} %fusion.81), channel_id=1, source_target_pairs={{0,2},{1,3},{2,0},{3,1},{4,6},{5,7},{6,4},{7,5},{8,10},{9,11},{10,... | collective-permute-start | bytes 122888 | tf_op jit(solution)/shard_map/ppermute | solution.py:48
  690.6 35.0 %collective-permute-start.119 = (bf16[1,64,2048]{2,1,0:T(8,128)(2,1)S(1)}, bf16[1,64,2048]{2,1,0:T(8,128)(2,1)S(1)}, u32[]{:S(2)}, u32[]{:S(2)}) collective-permute-start(bf16[1,64,2048]{2,1,0:T(8,128)(2,1)S(1)} %get-tuple-element.219), channel_id=1, source_target_pairs={{0,2},{1,3},{2,4},{3,5},{4,6},{5,7},{6,0},{7,1},{8,10},{9,11},{10,... | collective-permute-start | bytes 786440 | tf_op jit(solution)/shard_map/ppermute | solution.py:57
  725.5 64.7 %collective-permute-start.102 = (f32[20,512]{1,0:T(8,128)}, f32[20,512]{1,0:T(8,128)}, u32[]{:S(2)}, u32[]{:S(2)}) collective-permute-start(f32[20,512]{1,0:T(8,128)} %add.646), channel_id=1, source_target_pairs={{0,4},{1,5},{2,6},{3,7},{4,0},{5,1},{6,2},{7,3},{8,12},{9,13},{10,... | collective-permute-start | bytes 122888 | tf_op jit(solution)/shard_map/ppermute | solution.py:48
  728.3 25.7 %collective-permute-start.112 = (bf16[4,64,1536]{2,1,0:T(8,128)(2,1)}, bf16[4,64,1536]{2,1,0:T(8,128)(2,1)S(1)}, u32[]{:S(2)}, u32[]{:S(2)}) collective-permute-start(bf16[4,64,1536]{2,1,0:T(8,128)(2,1)} %collective-permute-done.111), channel_id=1, source_target_pairs={{0,2},{1,3},{2,4},{3,5},{4,6},{5,7},{6,0},{7,1},{8,10},{9,11},{10,... | collective-permute-start | bytes 2359304 | tf_op jit(solution)/shard_map/ppermute | solution.py:57
  737.2 36.2 %collective-permute-start.121 = (bf16[1,64,2048]{2,1,0:T(8,128)(2,1)S(1)}, bf16[1,64,2048]{2,1,0:T(8,128)(2,1)S(1)}, u32[]{:S(2)}, u32[]{:S(2)}) collective-permute-start(bf16[1,64,2048]{2,1,0:T(8,128)(2,1)S(1)} %collective-permute-done.120), channel_id=1, source_target_pairs={{0,2},{1,3},{2,4},{3,5},{4,6},{5,7},{6,0},{7,1},{8,10},{9,11},{10,... | collective-permute-start | bytes 786440 | tf_op jit(solution)/shard_map/ppermute | solution.py:57
  773.3 23.5 %collective-permute-start.114 = (bf16[4,1,256,1536]{3,2,0,1:T(8,128)(2,1)S(1)}, bf16[4,1,256,1536]{3,2,0,1:T(8,128)(2,1)}, u32[]{:S(2)}, u32[]{:S(2)}) collective-permute-start(bf16[4,1,256,1536]{3,2,0,1:T(8,128)(2,1)S(1)} %bitcast.496), channel_id=1, source_target_pairs={{0,1},{1,0},{2,3},{3,2},{4,5},{5,4},{6,7},{7,6},{8,9},{9,8},{10,11... | collective-permute-start | bytes 9437192 | tf_op jit(solution)/shard_map/ppermute | solution.py:48
  (164 other events, 2340.8 us)
Sparse Core Ops, SparseCore 0:
  70.6 119.0 all-gather.1
  612.4 90.1 reduce-scatter.1

commit v2 on v1

--- a/solution.py
+++ b/solution.py
@@ -67,9 +67,9 @@
     return [pair_a, swap_y(pair_a), pair_b, swap_x(pair_b)]
 
 
-def reduce_xy(blocks):
+def reduce_xy(blocks, *others):
     keep_a, send_a, keep_b, send_b = blocks
-    got_a, got_b = swap_y(send_a), swap_x(send_b)
+    got_a, got_b = after((swap_y(send_a), swap_x(send_b)), *others)
     far_a = swap_x((keep_a[1].astype(F32) + got_a[1].astype(F32)).astype(BF16))
     far_b = swap_y((keep_b[1].astype(F32) + got_b[1].astype(F32)).astype(BF16))
     return (keep_a[0], got_a[0], far_a), (keep_b[0], got_b[0], far_b)
@@ -82,8 +82,8 @@
     return total
 
 
-def exchange_blocks(for_x, for_y):
-    got_x, got_y = swap_x(for_x), swap_y(for_y)
+def exchange_blocks(for_x, for_y, *others):
+    got_x, got_y = after((swap_x(for_x), swap_y(for_y)), *others)
     depth = 2 * for_x.shape[0] // 3
     far = jnp.concatenate([swap_y(got_x[depth:]), swap_x(got_y[depth:])], axis=0)
     return [got_x[:depth], got_y[:depth], far]
@@ -100,32 +100,17 @@
     return pieces
 
 
-def ring_sum(pieces):
+def ring_sum(total, pieces):
+    for piece in pieces:
+        total = (ring_up(total).astype(F32) + piece).astype(BF16)
+    return total
+
+
+def expert_spread(pieces, core, chip):
     chips = lax.axis_size("expert") // 2
-    total = pieces(1).astype(BF16)
-    for j in range(2, chips):
-        total = (ring_up(total).astype(F32) + pieces(j).astype(F32)).astype(BF16)
-    return ring_up(total), pieces(0)
-
-
-def expert_sum(own, chip):
-    chips = lax.axis_size("expert") // 2
-    parts, rows, columns = own.shape
-    split = own.reshape(parts, chips, rows // chips, columns)
-
-    def piece(j):
-        at = lax.rem(chip + chips - j, chips)
-        return lax.dynamic_index_in_dim(split, at, 1, keepdims=False)
-
-    total, mine = ring_sum(piece)
-    return (total.astype(F32) + mine).astype(BF16)
-
-
-def expert_spread(piece, core, chip):
-    chips = lax.axis_size("expert") // 2
-    parts, rows, columns = piece.shape
-    spread = jnp.zeros((parts, chips, rows, columns), piece.dtype)
-    for j, got in enumerate(ring_gather(piece)):
+    parts, rows, columns = pieces[0].shape
+    spread = jnp.zeros((parts, chips, rows, columns), pieces[0].dtype)
+    for j, got in enumerate(pieces):
         spread = lax.dynamic_update_slice_in_dim(
             spread, got[:, None], lax.rem(chip + chips - j, chips), 1
         )
@@ -303,71 +288,85 @@
 
 def lead_kernel(cot_ref, down_t_ref, lead_ref):
     width = down_t_ref.shape[0]
-    count = lead_ref.shape[1]
-    cot = cot_ref[...].reshape(count, cot_ref.shape[4])[:, :width]
-    lead_ref[0] = dot(cot, down_t_ref[...])
+    cot = cot_ref[...].reshape(-1, cot_ref.shape[5])[:, :width]
+    lead_ref[0, 0] = dot(cot, down_t_ref[...]).reshape(lead_ref.shape[2:])
 
 
 def lead_call(cot, down_t):
-    shards, chips, two, rows, columns = cot.shape
+    shards, chips, cores, two, rows, columns = cot.shape
     width, units = down_t.shape
     count = shards * two * rows
     return pl.pallas_call(
         lead_kernel,
-        grid=(chips,),
+        grid=(chips, cores),
         in_specs=[
-            pl.BlockSpec((shards, 1, two, rows, columns), lambda i: (0, i, 0, 0, 0)),
+            pl.BlockSpec((shards, 1, 1, two, rows, columns), lambda i, c: (0, i, c, 0, 0, 0)),
             whole(down_t.shape),
         ],
-        out_specs=pl.BlockSpec((1, count, units), lambda i: (i, 0, 0)),
-        out_shape=out((chips, count, units), F32),
+        out_specs=pl.BlockSpec((1, 1, shards * two, rows, units), lambda i, c: (i, c, 0, 0, 0)),
+        out_shape=out((chips, cores, shards * two, rows, units), F32),
         cost_estimate=pl.CostEstimate(
-            flops=2 * chips * count * down_t.size,
-            bytes_accessed=2 * cot.size + 4 * chips * count * units + 2 * down_t.size,
+            flops=2 * chips * cores * count * down_t.size,
+            bytes_accessed=2 * cot.size + 4 * chips * cores * count * units,
             transcendentals=0,
         ),
         name="lead",
     )(cot, down_t)
 
 
-def expert_kernel(m, experts_all, at_ref, *refs):
-    row_refs = refs[: 8 * m]
-    routed_refs, lead_refs = refs[8 * m : 8 * m + 2], refs[8 * m + 2 : 8 * m + 4]
-    gate_ref, up_ref, gate_up_t_ref, router_ref = refs[8 * m + 4 : 8 * m + 8]
-    own_refs, other_ref, grads_ref, scaled_out = (
-        refs[8 * m + 8 : 8 * m + 12],
-        refs[8 * m + 12],
-        refs[8 * m + 13],
-        refs[8 * m + 14],
-    )
-    rows_ref, routed_ref, lead_ref, scaled_ref = refs[8 * m + 15 :]
+def join_kernel(a_ref, b_ref, c_ref, d_ref, out_ref):
+    for n, ref in enumerate((a_ref, b_ref, c_ref, d_ref)):
+        out_ref[2 * n : 2 * n + 2] = ref[:, 0]
+
+
+def join_call(parts, j):
+    two, _, rows, width = parts[0].shape
+    step = rows // 2
+    return pl.pallas_call(
+        join_kernel,
+        grid=(2,),
+        in_specs=[pl.BlockSpec((two, 1, step, width), lambda i: (0, j, i, 0))] * 4,
+        out_specs=pl.BlockSpec((4 * two, step, width), lambda i: (0, i, 0)),
+        out_shape=out((4 * two, rows, width), BF16),
+        cost_estimate=pl.CostEstimate(
+            flops=0, bytes_accessed=16 * two * rows * width, transcendentals=0
+        ),
+        name="join",
+    )(*parts)
+
+
+def expert_kernel(experts_all, at_ref, *refs):
+    row_refs, routed_ref, lead_ref = refs[:2], refs[2], refs[3]
+    gate_ref, up_ref, gate_up_t_ref, router_ref = refs[4:8]
+    own_refs, other_ref, grads_ref, scaled_out, scaled_ref = (
+        refs[8:12],
+        refs[12],
+        refs[13],
+        refs[14],
+        refs[15],
+    )
+    rows_ref, mask_ref, lead_here_ref = refs[16:]
     width = router_ref.shape[0]
-    units = lead_ref.shape[1]
+    units = lead_here_ref.shape[1]
     unit_part = units // 2
     half = LANES // 2
     me = at_ref[1]
     now = pl.program_id(0)
     blocks = [block for pair in ORDER for block in pair]
     for side in range(2):
-        for j in range(m):
-
-            @pl.when(now == side * m + j)
-            def _():
-                for n in range(4):
-                    ref = row_refs[(side * m + j) * 4 + n]
-                    rows_ref[n * LANES : (n + 1) * LANES, :] = ref[...].reshape(LANES, width)
-
-        @pl.when(now // m == side)
+
+        @pl.when(now == side)
         def _():
-            for n, (part, d) in enumerate(blocks):
-                to = slice(n * half, (n + 1) * half)
-                routed_ref[to, :] = routed_refs[side][me ^ d, 0, part]
-                lead_ref[to, :] = lead_refs[side][0, 2 * (me ^ d) + part]
-
+            rows_ref[...] = row_refs[side][...].reshape(rows_ref.shape)
+
+    for n, (part, d) in enumerate(blocks):
+        to = slice(n * half, (n + 1) * half)
+        mask_ref[to, :] = routed_ref[me ^ d, 0, 0, part]
+        lead_here_ref[to, :] = lead_ref[0, 0, 2 * (me ^ d) + part]
     rows = rows_ref[...]
     count = rows.shape[0]
     lane = lax.broadcasted_iota(jnp.int32, (count, LANES), 1)
-    routed = routed_ref[...].astype(F32)
+    routed = mask_ref[...].astype(F32)
     powers = jnp.where(lane < experts_all, jnp.exp(dot(rows, router_ref[...])), 0.0)
     weights = powers * routed / jnp.sum(powers, axis=-1, keepdims=True)
     spot = jnp.zeros((count, LANES), F32)
@@ -377,7 +376,7 @@
         low = e * unit_part
         gate_pre = dot(rows, gate_ref[e])
         up_pre = dot(rows, up_ref[e])
-        lead = lead_ref[:, low : low + unit_part]
+        lead = lead_here_ref[:, low : low + unit_part]
         sigmoid_gate = 1.0 / (1.0 + jnp.exp(-gate_pre))
         silu_gate = gate_pre * sigmoid_gate
         hidden = (silu_gate * up_pre).astype(BF16).astype(F32)
@@ -388,129 +387,127 @@
         grads_ref[0, :, units + low : units + low + unit_part] = (grad_hidden * silu_gate).astype(
             BF16
         )
-        scaled_ref[:, low : low + unit_part] = (hidden * chosen).astype(BF16)
+        scaled_ref[0, :, low : low + unit_part] = (hidden * chosen).astype(BF16)
     for n, (part, d) in enumerate(blocks):
-        scaled_out[0, 2 * (me ^ d) + part] = scaled_ref[n * half : (n + 1) * half, :]
-    spot = spot.astype(BF16)
+        scaled_out[0, 2 * (me ^ d) + part] = scaled_ref[0, n * half : (n + 1) * half, :]
+    mask_ref[...] = spot.astype(BF16)
     step = 512
-    parts = [
-        dot(grads_ref[0], gate_up_t_ref[:, c * step : (c + 1) * step]).astype(BF16)
-        for c in range(width // step)
-    ]
-
-    @pl.when(now < m)
+
+    @pl.when(now == 0)
     def _():
         for n, ref in enumerate(own_refs):
             at = slice(n * LANES, (n + 1) * LANES)
-            ref[:, 0, :, width:] = spot[at].reshape(2, half, LANES)
-            for c in range(width // step):
-                ref[:, 0, :, c * step : (c + 1) * step] = parts[c][at].reshape(2, half, step)
-
-    @pl.when(now >= m)
+            ref[:, 0, :, width:] = mask_ref[at, :].reshape(2, half, LANES)
+        for c in range(width // step):
+            cols = slice(c * step, (c + 1) * step)
+            part = dot(grads_ref[0], gate_up_t_ref[:, cols]).astype(BF16)
+            for n, ref in enumerate(own_refs):
+                at = slice(n * LANES, (n + 1) * LANES)
+                ref[:, 0, :, cols] = part[at].reshape(2, half, step)
+
+    @pl.when(now == 1)
     def _():
         for n in range(4):
             at = slice(n * LANES, (n + 1) * LANES)
-            other_ref[n, :, 0, :, width:] = spot[at].reshape(2, half, LANES)
-            for c in range(width // step):
-                other_ref[n, :, 0, :, c * step : (c + 1) * step] = parts[c][at].reshape(
-                    2, half, step
-                )
-
-
-def expert_call(at, rows, cots, first, leads, w_gate, w_up, gate_up_t, router, experts_all):
-    m = len(rows[0])
-    two, half, width = rows[0][0][0].shape
-    shards, _, _, _, columns = cots[0].shape
-    units = leads[0].shape[2]
-    count = 8 * half
-    leads = [v.reshape(v.shape[0], 8, half, units) for v in leads]
-    own_shape = (two, m, half, width + LANES)
-    flat = [array for side in rows for chip_rows in side for array in chip_rows]
-
-    def where(side, i):
-        return jnp.minimum(i, m - 1) if side == 0 else jnp.maximum(i - m, 0)
-
-    def routed_spec(side):
-        return pl.BlockSpec(
-            (shards, 1, two, half, LANES),
-            lambda i, _: (0, where(side, i) + first, 0, 0, width // LANES),
-        )
-
-    def lead_spec(side):
-        return pl.BlockSpec((1, 8, half, units), lambda i, _: (where(side, i) + first, 0, 0, 0))
+            other_ref[n, :, 0, :, width:] = mask_ref[at, :].reshape(2, half, LANES)
+        for c in range(width // step):
+            cols = slice(c * step, (c + 1) * step)
+            part = dot(grads_ref[0], gate_up_t_ref[:, cols]).astype(BF16)
+            for n in range(4):
+                at = slice(n * LANES, (n + 1) * LANES)
+                other_ref[n, :, 0, :, cols] = part[at].reshape(2, half, step)
+
+
+def expert_call(at, rows, cot, lead, w_gate, w_up, gate_up_t, router, experts_all):
+    eight, half, width = rows[0].shape
+    shards, units = cot.shape[0], lead.shape[4]
+    count = eight * half
+    own_shape = (2, 1, half, width + LANES)
+
+    def core_of(i, at):
+        return lax.rem(at[3] + i, 2)
 
     return pl.pallas_call(
-        lambda *refs: expert_kernel(m, experts_all, *refs),
+        lambda *refs: expert_kernel(experts_all, *refs),
         grid_spec=pltpu.PrefetchScalarGridSpec(
             num_scalar_prefetch=1,
-            grid=(2 * m,),
+            grid=(2,),
             in_specs=[
-                pl.BlockSpec(a.shape, lambda i, _: (0, 0, 0), pipeline_mode=pl.Buffered(1))
-                for a in flat
-            ]
-            + [routed_spec(0), routed_spec(1), lead_spec(0), lead_spec(1)]
-            + [whole(w_gate.shape), whole(w_up.shape), whole(gate_up_t.shape), whole(router.shape)],
-            out_specs=[
-                pl.BlockSpec(
-                    (two, 1, half, width + LANES), lambda i, _: (0, where(0, i), 0, 0)
-                )
-                for _ in range(4)
+                pl.BlockSpec(r.shape, lambda i, _: (0, 0, 0), pipeline_mode=pl.Buffered(1))
+                for r in rows
             ]
             + [
                 pl.BlockSpec(
-                    (4, two, 1, half, width + LANES), lambda i, _: (0, 0, where(1, i), 0, 0)
+                    (shards, 1, 1, 2, half, LANES),
+                    lambda i, at: (0, at[2], core_of(i, at), 0, 0, width // LANES),
                 ),
+                pl.BlockSpec(
+                    (1, 1, eight, half, units), lambda i, at: (at[2], core_of(i, at), 0, 0, 0)
+                ),
+            ]
+            + [whole(w_gate.shape), whole(w_up.shape), whole(gate_up_t.shape), whole(router.shape)],
+            out_specs=[whole(own_shape) for _ in range(4)]
+            + [
+                whole((4,) + own_shape),
                 pl.BlockSpec((1, count, 2 * units), lambda i, _: (i, 0, 0)),
-                pl.BlockSpec((1, 8, half, units), lambda i, _: (i, 0, 0, 0)),
+                pl.BlockSpec((1, eight, half, units), lambda i, _: (i, 0, 0, 0)),
+                pl.BlockSpec((1, count, units), lambda i, _: (i, 0, 0)),
             ],
             scratch_shapes=[
                 pltpu.VMEM((count, width), BF16),
                 pltpu.VMEM((count, LANES), BF16),
                 pltpu.VMEM((count, units), F32),
-                pltpu.VMEM((count, units), BF16),
             ],
         ),
         out_shape=[out(own_shape, BF16)] * 4
         + [
             out((4,) + own_shape, BF16),
-            out((2 * m, count, 2 * units), BF16),
-            out((2 * m, 8, half, units), BF16),
+            out((2, count, 2 * units), BF16),
+            out((2, eight, half, units), BF16),
+            out((2, count, units), BF16),
         ],
         compiler_params=pltpu.CompilerParams(vmem_limit_bytes=48 << 20),
         cost_estimate=pl.CostEstimate(
-            flops=8 * m * count * gate_up_t.size,
-            bytes_accessed=8 * m * count * width + 4 * gate_up_t.size + 20 * m * count * units,
-            transcendentals=2 * m * count * units,
+            flops=8 * count * gate_up_t.size,
+            bytes_accessed=8 * count * width + 4 * gate_up_t.size + 20 * count * units,
+            transcendentals=2 * count * units,
         ),
         name="experts",
-    )(at, *flat, *cots, *leads, w_gate, w_up, gate_up_t, router)
+    )(at, *rows, cot, lead, w_gate, w_up, gate_up_t, router)
 
 
 def mix_kernel(scaled_ref, down_ref, *refs):
-    out_ref = refs[-1]
     width = down_ref.shape[1]
-    shards, _, rows, _ = out_ref.shape
+    half = LANES // 2
     step = 512
     for c in range(width // step):
         cols = slice(c * step, (c + 1) * step)
-        part = dot(scaled_ref[0], down_ref[:, cols]).reshape(shards, rows, step)
-        if len(refs) == 2:
-            part = part + refs[0][:, 0, :, cols].astype(F32)
-        out_ref[:, 0, :, cols] = part.astype(BF16)
-
-
-def mix_call(scaled, down, shards, *others):
+        part = dot(scaled_ref[0], down_ref[:, cols])
+        for n in range(4):
+            some = part[n * LANES : (n + 1) * LANES].reshape(2, half, step)
+            if len(refs) == 1:
+                refs[0][n, :, 0, :, cols] = some.astype(BF16)
+            else:
+                more = refs[0][n, :, 0, :, cols].astype(F32)
+                refs[1 + n][:, 0, :, cols] = (some + more).astype(BF16)
+
+
+def mix_call(scaled, down, *others):
     chips, count, units = scaled.shape
     width = down.shape[1]
-    rows = count // shards
-    result = pl.BlockSpec((shards, 1, rows, width), lambda i: (0, i, 0, 0))
+    shape = (2, chips, LANES // 2, width)
+    quad = pl.BlockSpec((2, 1, LANES // 2, width), lambda i: (0, i, 0, 0))
+    quads = pl.BlockSpec((4, 2, 1, LANES // 2, width), lambda i: (0, 0, i, 0, 0))
     return pl.pallas_call(
         mix_kernel,
         grid=(chips,),
-        in_specs=[pl.BlockSpec((1, count, units), lambda i: (i, 0, 0)), whole(down.shape)]
-        + [result] * len(others),
-        out_specs=result,
-        out_shape=out((shards, chips, rows, width), BF16),
+        in_specs=[
+            pl.BlockSpec((1, count, units), lambda i: (i, 0, 0)),
+            whole(down.shape),
+        ]
+        + [quads] * len(others),
+        out_specs=[quad] * 4 if others else quads,
+        out_shape=[out(shape, BF16)] * 4 if others else out((4,) + shape, BF16),
         cost_estimate=pl.CostEstimate(
             flops=2 * scaled.size * width,
             bytes_accessed=2 * scaled.size + 2 * down.size + 4 * chips * count * width,
@@ -520,97 +517,86 @@
     )(scaled, down, *others)
 
 
-def row_grad_kernel(plan, grad_columns, *refs):
-    out_ref = refs[-1]
+def row_grad_kernel(count, *refs):
+    rows_refs, grads_refs, out_ref = refs[:count], refs[count:-1], refs[-1]
     _, step, unit_part = out_ref.shape
     total = jnp.zeros((step, 2 * unit_part), F32)
-    for row_at, grads_at, k in plan:
-        rows = jnp.concatenate([refs[n][...].reshape(LANES, step) for n in row_at], axis=0)
-        total = total + t_dot(rows, refs[grads_at][k])
+    for n, ref in enumerate(rows_refs):
+        total = total + t_dot(ref[...].reshape(-1, step), grads_refs[n // 2][n % 2])
     for e in range(2):
         out_ref[e] = total[:, e * unit_part : (e + 1) * unit_part]
 
 
 def row_grad_call(groups, which):
     step = 256
-    half, width = groups[0][0][0][0][0].shape[1:]
-    count, four = groups[0][2].shape[1:]
+    rows = [r for pair, _ in groups for r in pair]
+    eight, half, width = rows[0].shape
+    _, count, four = groups[0][1].shape
     units = four // 2
-    args, specs, plan = [], [], []
-
-    def add(array, spec):
-        args.append(array)
-        specs.append(spec)
-        return len(args) - 1
-
-    for rows, _, grads, _ in groups:
-        m = len(rows[0])
-        held = add(
-            grads,
-            pl.BlockSpec(
-                (2 * m, count, units), lambda i: (0, 0, which), pipeline_mode=pl.Buffered(1)
-            ),
-        )
-        for side in range(2):
-            for j in range(m):
-                tiles = [
-                    add(r, pl.BlockSpec((2, half, step), lambda i: (0, 0, i)))
-                    for r in rows[side][j]
-                ]
-                plan.append((tiles, held, side * m + j))
+    held = pl.BlockSpec((2, count, units), lambda i: (0, 0, which), pipeline_mode=pl.Buffered(1))
     return pl.pallas_call(
-        lambda *refs: row_grad_kernel(plan, which, *refs),
+        lambda *refs: row_grad_kernel(len(rows), *refs),
         grid=(width // step,),
-        in_specs=specs,
+        in_specs=[pl.BlockSpec((eight, half, step), lambda i: (0, 0, i))] * len(rows)
+        + [held] * len(groups),
         out_specs=pl.BlockSpec((2, step, units // 2), lambda i: (0, i, 0)),
         out_shape=out((2, width, units // 2), F32),
         cost_estimate=pl.CostEstimate(
-            flops=2 * len(plan) * count * width * units,
-            bytes_accessed=2 * len(plan) * count * (width + units) + 4 * width * units,
+            flops=2 * len(rows) * count * width * units,
+            bytes_accessed=2 * len(rows) * count * (width + units) + 4 * width * units,
             transcendentals=0,
         ),
         name="row_grads",
-    )(*args)
-
-
-def down_grad_kernel(scaled_a, scaled_b, cot_a, cot_b, out_ref):
+    )(*rows, *[g for _, g in groups])
+
+
+def down_grad_kernel(count, at_ref, *refs):
+    scaled_refs, cot_refs, out_ref = refs[:count], refs[count:-1], refs[-1]
     _, unit_part, step = out_ref.shape
-    shards, chips, two, half, _ = cot_a.shape
-    count = shards * two * half
     total = jnp.zeros((2 * unit_part, step), F32)
-    for scaled_ref, cot_ref in ((scaled_a, cot_a), (scaled_b, cot_b)):
-        for j in range(chips):
-            total = total + t_dot(scaled_ref[j], cot_ref[:, j].reshape(count, step))
+    for n, scaled_ref in enumerate(scaled_refs):
+        for side in range(2):
+            cot = cot_refs[2 * n + side][...].reshape(-1, step)
+            total = total + t_dot(scaled_ref[side].reshape(-1, 2 * unit_part), cot)
     for e in range(2):
         out_ref[e] = total[e * unit_part : (e + 1) * unit_part]
 
 
-def down_grad_call(scaled, cots, first, chips_now):
+def down_grad_call(at, scaled, cot):
     step = 256
-    shards, _, two, half, _ = cots[0].shape
-    _, count, units = scaled[0].shape
-    width = (cots[0].shape[4] // step) * step
-    held = pl.BlockSpec(
-        (chips_now, count, units),
-        lambda i: (first // chips_now, 0, 0),
-        pipeline_mode=pl.Buffered(1),
-    )
-    tile = pl.BlockSpec(
-        (shards, chips_now, two, half, step), lambda i: (0, first // chips_now, 0, 0, i)
-    )
+    shards, _, _, two, half, columns = cot.shape
+    _, eight, _, units = scaled[0].shape
+    width = (columns // step) * step
+    count = len(scaled)
+
+    def tile(n, side):
+        return pl.BlockSpec(
+            (shards, 1, 1, two, half, step),
+            lambda i, at: (0, at[1 + n], lax.rem(at[0] + side, 2), 0, 0, i),
+        )
+
     return pl.pallas_call(
-        down_grad_kernel,
-        grid=(width // step,),
-        in_specs=[held, held, tile, tile],
-        out_specs=pl.BlockSpec((2, units // 2, step), lambda i: (0, 0, i)),
+        lambda *refs: down_grad_kernel(count, *refs),
+        grid_spec=pltpu.PrefetchScalarGridSpec(
+            num_scalar_prefetch=1,
+            grid=(width // step,),
+            in_specs=[
+                pl.BlockSpec(
+                    s.shape, lambda i, _: (0, 0, 0, 0), pipeline_mode=pl.Buffered(1)
+                )
+                for s in scaled
+            ]
+            + [tile(n, side) for n in range(count) for side in range(2)],
+            out_specs=pl.BlockSpec((2, units // 2, step), lambda i, _: (0, 0, i)),
+        ),
         out_shape=out((2, units // 2, width), F32),
         cost_estimate=pl.CostEstimate(
-            flops=4 * chips_now * count * width * units,
-            bytes_accessed=4 * chips_now * count * (width + units) + 4 * width * units,
+            flops=4 * count * eight * half * width * units,
+            bytes_accessed=4 * count * eight * half * (width + units) + 4 * width * units,
             transcendentals=0,
         ),
         name="down_grads",
-    )(*scaled, *cots)
+    )(at, *scaled, *([cot] * (2 * count)))
 
 
 def add_up(parts):
@@ -667,18 +653,16 @@
 
 
 def output_grad_kernel(core_ref, g0, g1, g2, g3, attended_ref, own_ref, other_ref):
-    part, width = attended_ref.shape[1], g0.shape[2]
-    half = part // 2
-    step = 512
+    blocks, half, step = own_ref.shape
     own_cols = pl.ds(pl.multiple_of(core_ref[0] * half, half), half)
     other_cols = pl.ds(pl.multiple_of((1 - core_ref[0]) * half, half), half)
-    for c in range(width // step):
+    for c in range(blocks):
         cols = slice(c * step, (c + 1) * step)
         grads = jnp.concatenate(
             [g[:, :, cols].reshape(LANES, step) for g in (g0, g1, g2, g3)], axis=0
         )
-        own_ref[0, :, cols] = t_dot(attended_ref[:, own_cols], grads)
-        other_ref[0, :, cols] = t_dot(attended_ref[:, other_cols], grads).astype(BF16)
+        own_ref[c] = t_dot(attended_ref[:, own_cols], grads)
+        other_ref[c] = t_dot(attended_ref[:, other_cols], grads).astype(BF16)
 
 
 def attend_back_kernel(
@@ -746,10 +730,10 @@
 
 
 def project_back_kernel(
-    at_ref, core_ref, s0, s1, s2, s3, query_ref, key_ref, value_ref, proj_ref, scales_ref, normed_ref, *refs
+    at_ref, s0, s1, s2, s3, query_ref, key_ref, value_ref, proj_ref, scales_ref, normed_ref, *refs
 ):
     weight_refs = refs[:8]
-    part_refs, own_ref, other_ref, all_ref = refs[8:12], refs[12], refs[13], refs[14]
+    part_refs, pair_ref, all_ref = refs[8:12], refs[12], refs[13]
     width = normed_ref.shape[1]
     part = query_ref.shape[1]
     inner = sum_stats(s0, s1, s2, s3) / width
@@ -766,12 +750,21 @@
         got = dot_t(all_ref[...], ref[...]).astype(BF16)
         for k, part_ref in enumerate(part_refs):
             part_ref[:, :, at] = got[k * LANES : (k + 1) * LANES].reshape(2, LANES // 2, depth)
-    for p in range(width // (2 * depth)):
+    members, parts, rows, _ = pair_ref.shape
+    for p in range(parts):
+        for third in range(2):
+            cols = slice(third * part, (third + 1) * part)
+            got = t_dot(normed_ref[:, p * part : (p + 1) * part], all_ref[:, cols]).astype(BF16)
+            for e in range(members):
+                pair_ref[e, p, :, cols] = got[e * rows : (e + 1) * rows]
+
+
+def value_back_kernel(core_ref, value_ref, normed_ref, own_ref, other_ref):
+    parts, depth, _ = own_ref.shape
+    for p in range(parts):
         for ref, side in ((own_ref, core_ref[0]), (other_ref, 1 - core_ref[0])):
             at = pl.ds(pl.multiple_of((2 * p + side) * depth, depth), depth)
-            for third in range(3):
-                cols = slice(third * part, (third + 1) * part)
-                ref[p, :, cols] = t_dot(normed_ref[:, at], all_ref[:, cols]).astype(ref.dtype)
+            ref[p] = t_dot(normed_ref[:, at], value_ref[...]).astype(ref.dtype)
 
 
 def finish_kernel(a0, a1, a2, b0, b1, b2, x_ref, grad_ref, gain_ref, out_ref, gain_grad_ref):
@@ -877,7 +870,10 @@
     depth = part // 2
     at = jnp.stack([me, me ^ 1, me ^ 2, me ^ 3, core, 1 - core])
     cuts = cut_call(at, w_query, w_key, w_value)
-    direct = exchange_blocks(*after(cuts[2:], group_input[0], group_input[2], small_parts))
+    gate_up_t, down_t = flip_call(w_gate, w_up, w_down)
+    direct = exchange_blocks(
+        *after(cuts[2:], group_input[0], group_input[2], small_parts), group_input, gate_up_t
+    )
     passed = [swap_core(block) for block in direct]
     weight_blocks = list(cuts[:2]) + direct + passed
     weight_at = jnp.stack(
@@ -896,14 +892,10 @@
             [cotangent, routed, jnp.zeros((tok_count, LANES - experts_all), F32)], axis=1
         )
         .astype(BF16)
-        .reshape(2, half, width + LANES)
-    )
-    cot_block = after(cot_block, group_input[0], group_input[2])
-    cot_pieces = jnp.concatenate(ring_gather(cot_block), axis=0)
-    cot = lax.all_gather(after(cot_pieces, direct), "shard", axis=0, tiled=True)
+    )
+    cot = lax.all_gather(cot_block, ("shard", "expert"), axis=0, tiled=True)
 
     down_w = w_down.reshape(units, width)
-    gate_up_t, down_t = flip_call(w_gate, w_up, w_down)
 
     starts = [(me ^ d) * tok_count + side * half for pair in ORDER for side, d in pair]
     position = jnp.concatenate([p + jnp.arange(half) for p in starts])
@@ -921,7 +913,7 @@
     normed, proj, squares, scale_one = call(
         project_kernel,
         "project",
-        [weight_at] + group_input + [after(gain_one, gate_up_t)] + weight_blocks,
+        [weight_at] + group_input + [gain_one] + weight_blocks,
         [
             out((group_count, width), BF16),
             out((group_count, 3 * part), F32),
@@ -955,44 +947,79 @@
         tok_count * width,
     )
 
-    pieces = ring_gather(mixed_in)
-    cot = after(cot, mixed_in).reshape(shard_count, chips, 2, half, width + LANES)
-    cots = (cot, swap_core(cot))
-    leads = [lead_call(c, down_t) for c in cots]
-    size = 1
-    at = jnp.stack([place, me])
-    all_rows = []
-    for piece in pieces:
-        own = [b.reshape(2, half, width) for b in spread_xy(piece[:1], piece[1:])]
-        all_rows.append((own, [swap_core(r) for r in own]))
-    groups, back_terms, scaled_all, totals_all = [], [None] * chips, ([], []), []
-    for low in range(0, chips, size):
-        rows = [[all_rows[j][side] for j in range(low, low + size)] for side in range(2)]
-        at_now = after(at, totals_all[low - 2]) if low > 1 else at
+    pieces = [mixed_in, ring_up(mixed_in)]
+    cot = after(cot, mixed_in).reshape(shard_count, chips, 2, 2, half, width + LANES)
+    lead = lead_call(cot, down_t)
+    pieces[1] = after(pieces[1], lead)
+    while len(pieces) < chips:
+        pieces.append(ring_up(pieces[-1]))
+    chip_at = [lax.rem(chip + chips - j, chips) for j in range(chips)]
+    lows, low = [0, 1], 2
+    while low < chips:
+        lows.append(low)
+        low *= 2
+    lows.append(chips)
+    all_rows, firsts = [], []
+    for low, high in zip(lows[:-1], lows[1:]):
+        sides = [jnp.stack([p[s] for p in pieces[low:high]]) for s in range(2)]
+        pair_a = jnp.stack([sides[0], swap_x(sides[0])])
+        pair_b = jnp.stack([sides[1], swap_y(sides[1])])
+        firsts.append((pair_a, pair_b))
+        if low > 1:
+            pair_a, pair_b = after((pair_a, pair_b), all_rows[1][0])
+        parts = [pair_a, swap_y(pair_a), pair_b, swap_x(pair_b)]
+        for j in range(high - low):
+            own = join_call(parts, j)
+            all_rows.append((own, swap_core(own)))
+    groups, totals_all = [], []
+    for j in range(chips):
+        at = jnp.stack([place, me, chip_at[j], core])
+        at = after(at, totals_all[j - 2] if j > 1 else firsts[:3])
         got = expert_call(
-            at_now, rows, cots, low, leads, w_gate, w_up, gate_up_t, router_t, experts_all
+            at, all_rows[j], cot, lead, w_gate, w_up, gate_up_t, router_t, experts_all
         )
-        groups.append((rows, low, got[5], got[6]))
-        for side in range(2):
-            scaled_all[side].append(got[6][side * size : (side + 1) * size])
-        passed_back = swap_core(got[4])
+        groups.append((all_rows[j], got[5], got[6], got[7]))
+        if 0 < j < chips - 1:
+            passed_back = swap_core(after(got[4], all_rows[j + 1][1]))
+        else:
+            passed_back = swap_core(got[4])
         totals_all.append(
             [
                 (a.astype(F32) + passed_back[n].astype(F32)).astype(BF16)
                 for n, a in enumerate(got[:4])
             ]
         )
-    for n, low in enumerate(range(0, chips, size)):
-        terms_a, terms_b = reduce_xy(after(totals_all[n], [r[0] for r in all_rows]))
-        for j in range(low, low + size):
-            back_terms[j] = [[t[j - low] for t in terms] for terms in (terms_a, terms_b)]
+    back_terms = [None] * chips
 
     def back_piece(j):
         return jnp.stack([total_of(terms) for terms in back_terms[j]])
 
-    ring_total = back_piece(1).astype(BF16)
-    for j in range(2, chips):
-        ring_total = (ring_up(ring_total).astype(F32) + back_piece(j)).astype(BF16)
+    back_pieces, arrived = [], []
+    for j in list(range(1, chips)) + [0]:
+        totals = totals_all[j]
+        if j == 0:
+            totals = after(totals, totals_all[-1], arrived[0])
+        back_terms[j] = [
+            [t[0] for t in terms]
+            for terms in reduce_xy(
+                after(totals, [r[0] for r in all_rows]),
+                totals_all[min(j + 2, chips - 1)],
+                back_pieces[-1:],
+                arrived[-1:],
+            )
+        ]
+        if j:
+            back_pieces.append(back_piece(j))
+        if j == 1:
+            ring_total = back_pieces[0].astype(BF16)
+        elif j:
+            arrived.append(ring_up(ring_total))
+            ring_total = (arrived[-1].astype(F32) + back_pieces[-1]).astype(BF16)
+    scaled_sides = [
+        jnp.concatenate([g[3][side : side + 1] for g in groups]) for side in range(2)
+    ]
+    mix_passed = swap_core(mix_call(after(scaled_sides[1], arrived[0], back_pieces[1]), down_w))
+
     ring_total = ring_up(ring_total)
     grad_res, grad_res_b, grad_gain_two, grad_router = call(
         lambda *refs: turn_kernel(experts_all, *refs),
@@ -1011,18 +1038,15 @@
         8 * tok_count * width * LANES,
     )
 
-    scaled_all = [
-        jnp.concatenate(s, axis=0).reshape(chips, group_count, units) for s in scaled_all
-    ]
-    mix_other = mix_call(after(scaled_all[1], grad_res_b), down_w, shard_count)
-    mix_passed = swap_core(mix_other)
-
     group_grad = [b.reshape(2, half, width) for b in spread_xy(grad_res_b[:1], grad_res_b[1:])]
+    out_totals = mix_call(
+        after(scaled_sides[0], group_grad[0], group_grad[2]), down_w, mix_passed
+    )
     output_own, output_other = call(
         output_grad_kernel,
         "output_grad",
-        [core_at] + after(group_grad, mix_other) + [attended],
-        [out((1, part // 2, width), F32), out((1, part // 2, width), BF16)],
+        [core_at] + after(group_grad, out_totals) + [attended],
+        [out((4, part // 2, width // 4), F32), out((4, part // 2, width // 4), BF16)],
         2 * group_count * part * width,
         smem=(0,),
     )
@@ -1042,69 +1066,155 @@
         ],
         10 * group_count * group_count * part + 2 * group_count * part * width,
     )
-    output_total = output_own + swap_core(output_other).astype(F32)
-    out_total = mix_call(
-        after(scaled_all[0], query_pre), down_w, shard_count, mix_passed
-    ).reshape(-1, width)
-    out_sums = lax.psum_scatter(out_total, "shard", scatter_dimension=0, tiled=True)
+    def split_rows(own):
+        parts, rows, columns = own.shape
+        split = own.reshape(parts, chips, rows // chips, columns)
+        return [lax.dynamic_index_in_dim(split, at, 1, keepdims=False) for at in chip_at]
+
+    inner_parts = gather_parts(inner)
+    keep_a, send_a, keep_b, send_b = after(out_totals, inner_parts)
+    got_a, got_b = swap_y(send_a), swap_x(send_b)
+    out_far = (
+        (keep_a[1].astype(F32) + got_a[1].astype(F32)).astype(BF16),
+        (keep_b[1].astype(F32) + got_b[1].astype(F32)).astype(BF16),
+    )
+    out_terms = (
+        (keep_a[0], got_a[0], swap_x(out_far[0])),
+        (keep_b[0], got_b[0], swap_y(out_far[1])),
+    )
+
+    def out_piece(j):
+        return jnp.stack([total_of([t[j] for t in side]) for side in out_terms])
+
+    def ring_add(total, pieces, *others):
+        moved = after(ring_up(total), *others)
+        return (moved.astype(F32) + pieces.pop(0)).astype(BF16)
+
+    output_passed = after(swap_core(output_other), query_pre)
+    output_pieces = split_rows(output_own + output_passed.astype(F32))
+    output_pieces = output_pieces[1:] + output_pieces[:1]
+    output_total = output_pieces.pop(0).astype(BF16)
+    value_own, value_other = call(
+        value_back_kernel,
+        "value_back",
+        [core_at] + after([value_grad], inner, output_total) + [normed],
+        [out((4, depth, part), F32), out((4, depth, part), BF16)],
+        2 * group_count * width * part,
+        smem=(0,),
+    )
+    value_passed = swap_core(value_other)
+    output_total = ring_add(output_total, output_pieces, value_other)
     got = call(
         project_back_kernel,
         "project_back",
-        [weight_at, core_at]
-        + gather_parts(inner)
-        + [query_pre, key_pre, value_grad, proj, scales, normed]
+        [weight_at]
+        + inner_parts
+        + after([query_pre, key_pre, value_grad, proj, scales, normed], output_total)
         + weight_blocks,
         [quad] * 4
         + [
-            out((4, depth, 3 * part), F32),
-            out((4, depth, 3 * part), BF16),
+            out((expert_count, 4, part // expert_count, 2 * part), BF16),
             out((group_count, 3 * part), BF16),
         ],
         4 * group_count * width * 3 * part,
-        smem=(0, 1),
-    )
-    terms_a, terms_b = reduce_xy([b.reshape(2, 1, half, width) for b in got[:4]])
-    grad_input, grad_gain_one = call(
-        finish_kernel,
-        "finish",
-        [t.reshape(half, width) for t in terms_a + terms_b] + [own_input, grad_res, gain_one],
-        [out((2, half, width), F32), out((8, width), F32)],
-        tok_count * width,
-    )
-
-    out_sums = out_sums.reshape(chips, tok_count, width)
-    ring_part, own_part = ring_sum(lambda j: out_sums[j])
-    block_output = residual.reshape(tok_count, width) + (
-        ring_part.astype(F32) + own_part.astype(F32)
-    )
-
-    output_piece = expert_sum(output_total, chip)
-    grad_w_output = expert_spread(output_piece, core, chip)[0].astype(F32)
-    qkv_total = got[4] + swap_core(got[5]).astype(F32)
-    qkv_piece = expert_sum(qkv_total, chip)
-    sent = [lax.dynamic_index_in_dim(qkv_piece, me ^ d, 0, keepdims=False) for d in range(4)]
-    low = sent[3].shape[0] // 2
-    arrived = exchange_blocks(
-        jnp.concatenate([sent[1], sent[3][:low]], axis=0),
-        jnp.concatenate([sent[2], sent[3][low:]], axis=0),
-    )
-    qkv_rows = expert_spread(jnp.stack([sent[0]] + arrived), core, chip)
-    shares = [lax.dynamic_index_in_dim(qkv_rows, me ^ p, 0, keepdims=False) for p in range(4)]
-    grad_w_query, grad_w_key, grad_w_value = (
-        jnp.concatenate([share[:, n * part : (n + 1) * part] for share in shares], axis=1).astype(
-            F32
+        smem=(0,),
+    )
+    def exchange_grads(piece):
+        sent = [lax.dynamic_index_in_dim(piece, me ^ d, 0, keepdims=False) for d in range(4)]
+        low = sent[3].shape[0] // 2
+        arrived = exchange_blocks(
+            jnp.concatenate([sent[1], sent[3][:low]], axis=0),
+            jnp.concatenate([sent[2], sent[3][low:]], axis=0),
         )
-        for n in range(3)
-    )
-
+        return jnp.stack([sent[0]] + arrived)
+
+    def whole_grads(rows):
+        shares = [lax.dynamic_index_in_dim(rows, me ^ p, 0, keepdims=False) for p in range(4)]
+        return [
+            jnp.concatenate(
+                [share[:, n * part : (n + 1) * part] for share in shares], axis=1
+            ).astype(F32)
+            for n in range(rows.shape[2] // part)
+        ]
+
+    pair_sums = lax.psum_scatter(got[4], "expert", scatter_dimension=0, tiled=True)[0]
+
+    output_total = ring_add(output_total, output_pieces, got[0])
+    value_pieces = split_rows(after(value_own + value_passed.astype(F32), output_total))
+    value_pieces = value_pieces[1:] + value_pieces[:1]
+    total = value_pieces.pop(0).astype(BF16)
     span = min(chips, 4)
-    sets = [groups[low : low + span] for low in range(0, chips, span)]
-    grad_w_gate = add_up([row_grad_call(some, 0) for some in sets])
-    grad_w_up = add_up([row_grad_call(some, 1) for some in sets])
-    grad_w_down = add_up(
-        [down_grad_call(scaled_all, cots, low, span) for low in range(0, chips, span)]
-    )
-
+    starts = range(0, chips, span)
+
+    def row_grads(which, *others):
+        late = after([g[1] for g in groups], *others)
+        return add_up(
+            [
+                row_grad_call([(g[0], v) for g, v in zip(groups, late)][low : low + span], which)
+                for low in starts
+            ]
+        )
+
+    def down_grads(*others):
+        late = after([g[2] for g in groups], *others)
+        return add_up(
+            [
+                down_grad_call(
+                    jnp.stack([core] + chip_at[low : low + span]), late[low : low + span], cot
+                )
+                for low in starts
+            ]
+        )
+
+    expert_grads = []
+    out_spread = []
+    while len(value_pieces) > 1:
+        if not expert_grads:
+            expert_grads.append(down_grads(total))
+            terms_a, terms_b = reduce_xy(
+                [b.reshape(2, 1, half, width) for b in got[:4]], expert_grads[0]
+            )
+        elif len(expert_grads) == 1:
+            expert_grads.append(row_grads(0, total, out_far, output_total))
+            grad_input, grad_gain_one = call(
+                finish_kernel,
+                "finish",
+                [t.reshape(half, width) for t in terms_a + terms_b]
+                + [own_input, grad_res, after(gain_one, expert_grads[1])],
+                [out((2, half, width), F32), out((8, width), F32)],
+                tok_count * width,
+            )
+        total = ring_add(total, value_pieces, expert_grads[-1])
+        if output_pieces:
+            output_total = ring_add(output_total, output_pieces, total)
+        if not output_pieces:
+            out_spread.append(
+                after(ring_up(out_spread[-1]), total) if out_spread else output_total
+            )
+    out_now = out_piece(1).astype(BF16)
+    pair_mine = exchange_grads(after(pair_sums, grad_gain_one, out_spread[-1], out_now))
+    pair_rows = lax.all_gather(pair_mine, "expert", axis=0)
+    total = ring_add(total, value_pieces, pair_mine)
+    spread = [exchange_grads(total)]
+    expert_grads.append(row_grads(1, spread[0], out_now))
+    grad_w_down, grad_w_gate, grad_w_up = expert_grads
+    for j in range(1, chips):
+        moved = after(ring_up(out_now), grad_w_up)
+        if j + 1 < chips:
+            out_now = (moved.astype(F32) + out_piece(j + 1)).astype(BF16)
+        spread.append(after(ring_up(spread[-1]), out_now if j + 1 < chips else moved))
+        if len(out_spread) < chips:
+            out_spread.append(after(ring_up(out_spread[-1]), spread[-1]))
+    while len(out_spread) < chips:
+        out_spread.append(ring_up(out_spread[-1]))
+    block_output = residual + (moved.astype(F32) + out_piece(0))
+    early_rows = expert_spread(out_spread, core, chip)
+    grad_w_output = jnp.concatenate([early_rows[c] for c in range(4)], axis=1).astype(F32)
+    (grad_w_value,) = whole_grads(expert_spread(spread, core, chip))
+    pair_rows = jnp.transpose(pair_rows, (1, 0, 2, 3)).reshape(4, part, 2 * part)
+    grad_w_query, grad_w_key = whole_grads(pair_rows)
+
+    grad_gain_one = after(grad_gain_one, spread[0])
     packed = jnp.concatenate([grad_gain_one[:1], grad_gain_two[:1], grad_router], axis=0)
     rows_used = packed.shape[0]
     packed = jnp.pad(packed, ((0, (-rows_used) % 16), (0, 0)))
@@ -1113,7 +1223,7 @@
     )
     quarters = quarters[:2] + swap_y(quarters[2:])
     packed = (quarters[0] + swap_x(quarters[1]))[:rows_used]
-    packed = jnp.concatenate([packed, gain_grads[:2]], axis=0)
+    packed = after(jnp.concatenate([packed, gain_grads[:2]], axis=0), spread[-1])
     bit = 1
     while bit < expert_count:
         packed = packed + flip_expert(packed, bit)

time: 863 us -> 770 us (0.89)
  waiting for transfers between devices: 380 us -> 267 us
  other arithmetic: 65.8 us -> 79.5 us
    ppermute x24 -> x21, waiting for transfers between devices: 183 us -> 95.5 us  [ring_up(): lax.ppermute(values, 'expert', [(i, (i + 2) % count) for i in range(count)])]
    ppermute x67 -> x71, waiting for transfers between devices: 191 us -> 163 us  [flip_shard(): return lax.ppermute(values, 'shard', [(i, i ^ bit) for i in range(count)])]
    another operation x7 -> x17, other arithmetic: 1.48 us -> 15.5 us
    convert_element_type x13 -> x16, other arithmetic: 13.8 us -> 22.6 us  [the longest x3 7.67 us: whole_grads(): return [jnp.concatenate([share[:, n * part:(n + 1) * part] for share in s...]
    ppermute x67 -> x71, starting transfers between devices: 74.5 us -> 67.6 us  [flip_shard(): return lax.ppermute(values, 'shard', [(i, i ^ bit) for i in range(count)])]
    ppermute x24 -> x21, starting transfers between devices: 14.1 us -> 20.5 us  [ring_up(): lax.ppermute(values, 'expert', [(i, (i + 2) % count) for i in range(count)])]
    pallas_call x9 -> x12, Pallas kernels: 149 us -> 152 us  [the longest x4 77.2 us: expert_call(): pl.pallas_call(lambda *refs: expert_kernel(experts_all, *refs), grid_spec...]
    pallas_call x8 -> x9, Pallas kernels: 67 us -> 68.7 us  [call(): pl.pallas_call(kernel, in_specs=[scalars() if n in smem else whole(a.shap...]
  transfers between devices with their start and end apart: 125 -> 114, of which waited for: 57 -> 46; matrix products, arithmetic and copies ran while one was open for 12% -> 15% of each run, Pallas kernels for 27% -> 31%
where the time goes in v2:
time: 770 us; the launch traced here: 764 us
  waiting for transfers between devices  267 us (35%)
  Pallas kernels  251 us (33%)
  starting transfers between devices  90.8 us (12%)
  other arithmetic  79.5 us (10%)
  local copies, waits for them, and re-layouts  60.4 us (8%)
  between operations  15.7 us (2%)
    ppermute x71, waiting for transfers between devices, flip_shard(): return lax.ppermute(values, 'shard', [(i, i ^ bit) for i in range(count)])  163 us
    ppermute x21, waiting for transfers between devices, ring_up(): lax.ppermute(values, 'expert', [(i, (i + 2) % count) for i in range(count)])  95.5 us
    pallas_call x4, Pallas kernels, expert_call(): pl.pallas_call(lambda *refs: expert_kernel(experts_all, *refs), grid_spec...  77.2 us
    pallas_call x9, Pallas kernels, call(): pl.pallas_call(kernel, in_specs=[scalars() if n in smem else whole(a.shap...  68.7 us
    ppermute x71, starting transfers between devices, flip_shard(): return lax.ppermute(values, 'shard', [(i, i ^ bit) for i in range(count)])  67.6 us
    pallas_call x2, Pallas kernels, row_grad_call(): pl.pallas_call(lambda *refs: row_grad_kernel(len(rows), *refs), grid=(wid...  31.7 us
    ppermute x21, starting transfers between devices, ring_up(): lax.ppermute(values, 'expert', [(i, (i + 2) % count) for i in range(count)])  20.5 us
    pallas_call x2, Pallas kernels, mix_call(): pl.pallas_call(mix_kernel, grid=(chips,), in_specs=[pl.BlockSpec((1, coun...  19.2 us
  transfers between devices with their start and end apart: 114, of which 46 were waited for; matrix products, arithmetic and copies ran while one was open for 15% of the time, Pallas kernels for 31%

profile of v2, /device:TPU:0, one launch (start us, length us, event | category | flops | bytes accessed | tf_op | source)
XLA Modules:
  0.0 764.3 jit_solution(13714279644516396436)
XLA Ops:
  10.6 3.0 collective-permute-start
  20.6 5.0 cut.1
  32.2 6.5 flip.1
  40.1 41.9 %collective-permute-done.3 = bf16[2,1,64,2048]{3,2,0,1:T(8,128)(2,1)} collective-permute-done((bf16[2,1,64,2048]{3,2,0,1:T(8,128)(2,1)S(1)}, bf16[2,1,64,2048]{3,2,0,1:T(8,128)(2,1)}, u32[]{:S(2)}, u32[]{:S(2)}) %collective-permute-start.3) | collective-permute-done | bytes 524320 | tf_op jit(solution)/shard_map/ppermute | solution.py:31
  89.0 3.7 collective-permute-done.9
  101.2 9.7 %project.1 = (bf16[512,2048]{1,0:T(8,128)(2,1)}, f32[512,1536]{1,0:T(8,128)}, f32[4,8,128]{2,1,0:T(8,128)}, f32[512,128]{1,0:T(8,128)}) custom-call(s32[8]{0:T(128)} %stack.265.at_ref, bf16[2,64,2048]{2,1,0:T(8,128)(2,1)} %get-tuple-element.471.r0, bf16[2,64,2048]{2,1,0:T(8,128)(2,1)} %bitcast.13.r1, bf16[2,64,2048]{2,1,0:T(8,128)(2,1)} %get-tuple-element.465.r2, ...), custom_call_target="tpu_custom_call" | custom-call | flops 3221225472 | bytes 13918240 | tf_op jit(solution)/shard_map/project/pallas_call | solution.py:148
  118.2 9.9 %attend.1 = (bf16[512,512]{1,0:T(8,128)(2,1)}, bf16[512,512]{1,0:T(8,128)(2,1)}, bf16[512,512]{1,0:T(8,128)(2,1)}, f32[512,128]{1,0:T(8,128)}, f32[512,128]{1,0:...) custom-call(f32[512,1536]{1,0:T(8,128)} %get-tuple-element.321.refs_, ...), custom_call_target="tpu_custom_call" | custom-call | flops 1610612736 | bytes 11603968 | tf_op jit(solution)/shard_map/attend/pallas_call | solution.py:148
  132.8 8.3 %collective-permute-done.18 = bf16[2,1,64,2048]{3,2,1,0:T(8,128)(2,1)S(1)} collective-permute-done((bf16[2,1,64,2048]{3,2,1,0:T(8,128)(2,1)}, bf16[2,1,64,2048]{3,2,1,0:T(8,128)(2,1)S(1)}, u32[]{:S(2)}, u32[]{:S(2)}) %collective-permute-start.18) | collective-permute-done | bytes 524320 | tf_op jit(solution)/shard_map/ppermute | solution.py:31
  152.2 3.0 settle.1
  159.5 3.9 collective-permute-done.21
  163.6 3.0 collective-permute-done.22
  167.4 16.1 %lead.1.refs_4_ = f32[4,2,8,64,512]{4,3,2,1,0:T(8,128)} custom-call(bf16[4,4,2,2,64,2176]{5,4,3,2,1,0:T(8,128)(2,1)} %bitcast.460, bf16[2048,512]{1,0:T(8,128)(2,1)} %get-tuple-element.215.down_t_ref), custom_call_target="tpu_custom_call" | custom-call | flops 8589934592 | bytes 26214400 | tf_op jit(solution)/shard_map/lead/pallas_call | solution.py:299
  197.4 12.1 %collective-permute-done.27 = bf16[2,64,2048]{2,1,0:T(8,128)(2,1)S(1)} collective-permute-done((bf16[2,64,2048]{2,1,0:T(8,128)(2,1)S(1)}, bf16[2,64,2048]{2,1,0:T(8,128)(2,1)S(1)}, u32[]{:S(2)}, u32[]{:S(2)}) %collective-permute-start.27) | collective-permute-done | bytes 524320 | tf_op jit(solution)/shard_map/ppermute | solution.py:57
  214.3 7.8 %collective-permute-done.29 = bf16[2,64,2048]{2,1,0:T(8,128)(2,1)} collective-permute-done((bf16[2,64,2048]{2,1,0:T(8,128)(2,1)S(1)}, bf16[2,64,2048]{2,1,0:T(8,128)(2,1)}, u32[]{:S(2)}, u32[]{:S(2)}) %collective-permute-start.29) | collective-permute-done | bytes 524320 | tf_op jit(solution)/shard_map/ppermute | solution.py:31
  227.8 19.2 %experts.4 = (bf16[2,1,64,2176]{3,2,1,0:T(8,128)(2,1)S(1)}, bf16[2,1,64,2176]{3,2,1,0:T(8,128)(2,1)S(1)}, bf16[2,1,64,2176]{3,2,1,0:T(8,128)(2,1)S(1)}, bf16[2,1...) custom-call(s32[4]{0:T(128)S(1)} %get-tuple-element.217.refs_0_, ...), custom_call_target="tpu_custom_call" | custom-call | flops 8589934592 | bytes 22020096 | tf_op jit(solution)/shard_map/experts/pallas_call | solution.py:430
  256.1 19.3 %experts.5 = (bf16[2,1,64,2176]{3,2,1,0:T(8,128)(2,1)S(1)}, bf16[2,1,64,2176]{3,2,1,0:T(8,128)(2,1)S(1)}, bf16[2,1,64,2176]{3,2,1,0:T(8,128)(2,1)S(1)}, bf16[2,1...) custom-call(s32[4]{0:T(128)S(1)} %get-tuple-element.219.refs_0_, ...), custom_call_target="tpu_custom_call" | custom-call | flops 8589934592 | bytes 22020096 | tf_op jit(solution)/shard_map/experts/pallas_call | solution.py:430
  281.6 19.2 %experts.6 = (bf16[2,1,64,2176]{3,2,1,0:T(8,128)(2,1)S(1)}, bf16[2,1,64,2176]{3,2,1,0:T(8,128)(2,1)S(1)}, bf16[2,1,64,2176]{3,2,1,0:T(8,128)(2,1)S(1)}, bf16[2,1...) custom-call(s32[4]{0:T(128)S(1)} %get-tuple-element.226.refs_0_, ...), custom_call_target="tpu_custom_call" | custom-call | flops 8589934592 | bytes 22020096 | tf_op jit(solution)/shard_map/experts/pallas_call | solution.py:430
  302.9 19.5 %experts.7 = (bf16[2,1,64,2176]{3,2,1,0:T(8,128)(2,1)S(1)}, bf16[2,1,64,2176]{3,2,1,0:T(8,128)(2,1)S(1)}, bf16[2,1,64,2176]{3,2,1,0:T(8,128)(2,1)S(1)}, bf16[2,1...) custom-call(s32[4]{0:T(128)S(1)} %get-tuple-element.236.refs_0_, ...), custom_call_target="tpu_custom_call" | custom-call | flops 8589934592 | bytes 22020096 | tf_op jit(solution)/shard_map/experts/pallas_call | solution.py:430
  331.8 7.5 collective-permute-done.43
  345.3 6.0 collective-permute-done.50
  355.1 4.0 collective-permute-done.46
  360.6 15.3 %collective-permute-done.52 = bf16[1,64,2176]{2,1,0:T(8,128)(2,1)S(1)} collective-permute-done((bf16[1,64,2176]{2,1,0:T(8,128)(2,1)S(1)}, bf16[1,64,2176]{2,1,0:T(8,128)(2,1)S(1)}, u32[]{:S(2)}, u32[]{:S(2)}) %collective-permute-start.52) | collective-permute-done | bytes 278560 | tf_op jit(solution)/shard_map/ppermute | solution.py:31
  382.7 8.5 %mix.2 = bf16[4,2,4,64,2048]{4,3,2,1,0:T(8,128)(2,1)} custom-call(bf16[4,512,512]{2,1,0:T(8,128)(2,1)} %pad_maximum_fusion.1.scaled_ref, bf16[512,2048]{1,0:T(8,128)(2,1)} %bitcast.491), custom_call_target="tpu_custom_call" | custom-call | flops 4294967296 | bytes 20971520 | tf_op jit(solution)/shard_map/mix/pallas_call | solution.py:501
  398.3 13.0 %collective-permute-done.53 = bf16[2,64,2176]{2,1,0:T(8,128)(2,1)S(1)} collective-permute-done((bf16[2,64,2176]{2,1,0:T(8,128)(2,1)S(1)}, bf16[2,64,2176]{2,1,0:T(8,128)(2,1)S(1)}, u32[]{:S(2)}, u32[]{:S(2)}) %collective-permute-start.53) | collective-permute-done | bytes 557088 | tf_op jit(solution)/shard_map/ppermute | solution.py:57
  421.8 8.3 %collective-permute-done.58.refs_0_ = bf16[2,64,2176]{2,1,0:T(8,128)(2,1)S(1)} collective-permute-done((bf16[2,64,2176]{2,1,0:T(8,128)(2,1)S(1)}, bf16[2,64,2176]{2,1,0:T(8,128)(2,1)S(1)}, u32[]{:S(2)}, u32[]{:S(2)}) %collective-permute-start.58) | collective-permute-done | bytes 557088 | tf_op jit(solution)/shard_map/ppermute | solution.py:57
  430.9 5.4 turn.1
  438.5 6.3 collective-permute-done.64
  451.4 10.7 %mix.3 = (bf16[2,4,64,2048]{3,2,1,0:T(8,128)(2,1)}, bf16[2,4,64,2048]{3,2,1,0:T(8,128)(2,1)}, bf16[2,4,64,2048]{3,2,1,0:T(8,128)(2,1)}, bf16[2,4,64,2048]{3,2,1,0:T(8,128)(2,1)}) custom-call(bf16[4,512,512]{2,1,0:T(8,128)(2,1)} %pad_maximum_fusion.scaled_ref, bf16[512,2048]{1,0:T(8,128)(2,1)} %bitcast.492, ...), custom_call_target="tpu_custom_call" | custom-call | flops 4294967296 | bytes 20971520 | tf_op jit(solution)/shard_map/mix/pallas_call | solution.py:501
  463.0 4.5 output_grad.1
  467.5 14.4 %attend_back.1 = (f32[512,512]{1,0:T(8,128)}, f32[512,512]{1,0:T(8,128)}, bf16[512,512]{1,0:T(8,128)(2,1)}, f32[4,8,128]{2,1,0:T(8,128)}, f32[8,512]{1,0:T(8,128)}, /*index=5*/bf16[512,2048]{1,0:T(8,128)(2,1)}) custom-call(bf16[2,64,2048]{2,1,0:T(8,128)(2,1)} %get-tuple-element.290.g0, bf16[2,64,2048]{2,1,0:T(8,128)(2,1)} %bitcast.509, ...), custom_call_target="tpu_custom_call" | custom-call | flops 2415919104 | bytes 16289792 | tf_op jit(solution)/shard_map/attend_back/pallas_call | solution.py:148
  487.9 4.6 value_back.1
  496.1 13.1 %project_back.1 = (bf16[2,64,2048]{2,1,0:T(8,128)(2,1)}, bf16[2,64,2048]{2,1,0:T(8,128)(2,1)}, bf16[2,64,2048]{2,1,0:T(8,128)(2,1)}, bf16[2,64,2048]{2,1,0:T(8,1...) custom-call(s32[8]{0:T(128)} %stack.265.at_ref, f32[4,8,128]{2,1,0:T(8,128)} %get-tuple-element.299.s0, ...), custom_call_target="tpu_custom_call" | custom-call | flops 6442450944 | bytes 22347808 | tf_op jit(solution)/shard_map/project_back/pallas_call | solution.py:148
  513.9 12.9 %collective-permute-done.79 = bf16[4,64,512]{2,1,0:T(8,128)(2,1)S(1)} collective-permute-done((bf16[4,64,512]{2,1,0:T(8,128)(2,1)S(1)}, bf16[4,64,512]{2,1,0:T(8,128)(2,1)S(1)}, u32[]{:S(2)}, u32[]{:S(2)}) %collective-permute-start.79) | collective-permute-done | bytes 262176 | tf_op jit(solution)/shard_map/ppermute | solution.py:57
  530.8 16.5 %down_grads.1 = f32[2,256,2048]{2,1,0:T(8,128)} custom-call(s32[5]{0:T(128)} %stack.314.refs_0_, bf16[2,8,64,512]{3,2,1,0:T(8,128)(2,1)} %copy-done.1, bf16[2,8,64,512]{3,2,1,0:T(8,128)(2,1)} %copy-done.2, bf16[2,8,64,512]{3,2,1,0:T(8,128)(2,1)} %copy-done.3, bf16[2,8,64,512]{3,2,1,0:T(8,128)(2,1)} %copy-done.4, bf16[4,4,2,2,64,2176]{5,4,3,2,1,0:T(8,128)(2,1)} %bitcast.465, ...), custom_call_target="tpu_custom_call" | custom-call | flops 8589934592 | bytes 25165824 | tf_op jit(solution)/shard_map/down_grads/pallas_call | solution.py:578
  547.4 21.4 %collective-permute-done.84 = bf16[2,1,64,2048]{3,2,1,0:T(8,128)(2,1)} collective-permute-done((bf16[2,1,64,2048]{3,2,1,0:T(8,128)(2,1)}, bf16[2,1,64,2048]{3,2,1,0:T(8,128)(2,1)}, u32[]{:S(2)}, u32[]{:S(2)}) %collective-permute-start.84) | collective-permute-done | bytes 524320 | tf_op jit(solution)/shard_map/ppermute | solution.py:31
  589.6 15.8 %row_grads.2 = f32[2,2048,256]{2,1,0:T(8,128)} custom-call(bf16[8,64,2048]{2,1,0:T(8,128)(2,1)} %join.4.refs_1_.refs_0_, bf16[8,64,2048]{2,1,0:T(8,128)(2,1)} %collective-permute-done.32.refs_2_.refs_1_, bf16[8,64,2048]{2,1,0:T(8,128)(2,1)} %join.5.refs_1_.refs_2_, bf16[8,64,2048]{2,1,0:T(8,128)(2,1)} %collective-permute-done.35.refs_2_.refs_3_, ...), custom_call_target="tpu_custom_call" | custom-call | flops 8589934592 | bytes 25165824 | tf_op jit(solution)/shard_map/row_grads/pallas_call | solution.py:537
  605.4 4.0 finish.1
  611.1 3.5 fusion.39
  614.6 2.9 fusion.38
  654.3 15.9 %row_grads.3 = f32[2,2048,256]{2,1,0:T(8,128)} custom-call(bf16[8,64,2048]{2,1,0:T(8,128)(2,1)} %join.4.refs_1_.refs_0_, bf16[8,64,2048]{2,1,0:T(8,128)(2,1)} %collective-permute-done.32.refs_2_.refs_1_, bf16[8,64,2048]{2,1,0:T(8,128)(2,1)} %join.5.refs_1_.refs_2_, bf16[8,64,2048]{2,1,0:T(8,128)(2,1)} %collective-permute-done.35.refs_2_.refs_3_, ...), custom_call_target="tpu_custom_call" | custom-call | flops 8589934592 | bytes 25165824 | tf_op jit(solution)/shard_map/row_grads/pallas_call | solution.py:537
  672.4 3.0 collective-permute-done.99
  675.7 4.1 collective-permute-done.100
  681.0 17.4 %collective-permute-done.97 = bf16[2,64,2048]{2,1,0:T(8,128)(2,1)S(1)} collective-permute-done((bf16[2,64,2048]{2,1,0:T(8,128)(2,1)S(1)}, bf16[2,64,2048]{2,1,0:T(8,128)(2,1)S(1)}, u32[]{:S(2)}, u32[]{:S(2)}) %collective-permute-start.97) | collective-permute-done | bytes 524320 | tf_op jit(solution)/shard_map/ppermute | solution.py:57
  701.4 8.3 %collective-permute-done.102 = bf16[4,64,512]{2,1,0:T(8,128)(2,1)S(1)} collective-permute-done((bf16[4,64,512]{2,1,0:T(8,128)(2,1)}, bf16[4,64,512]{2,1,0:T(8,128)(2,1)S(1)}, u32[]{:S(2)}, u32[]{:S(2)}) %collective-permute-start.102) | collective-permute-done | bytes 262176 | tf_op jit(solution)/shard_map/ppermute | solution.py:57
  710.7 6.7 collective-permute-done.109
  717.4 10.9 %collective-permute-done.98 = bf16[2,64,2048]{2,1,0:T(8,128)(2,1)S(1)} collective-permute-done((bf16[2,64,2048]{2,1,0:T(8,128)(2,1)S(1)}, bf16[2,64,2048]{2,1,0:T(8,128)(2,1)S(1)}, u32[]{:S(2)}, u32[]{:S(2)}) %collective-permute-start.98) | collective-permute-done | bytes 524320 | tf_op jit(solution)/shard_map/ppermute | solution.py:57
  732.7 3.8 collective-permute-done.105
  738.1 3.5 collective-permute-done.106
  (546 shorter events, 265.1 us)
Async XLA Ops:
  7.2 160.2 %all-gather.4.cloned.1.call-start = ((), (), s32[]{:S(2)}) async-start(), calls=%async_computation.1 | async-start | bytes 18382848 | tf_op jit(solution)/shard_map/all_gather | solution.py:896
  10.4 607.9 %reduce-scatter.2.cloned.1.call-start = ((), (), s32[]{:S(2)}) async-start(), calls=%async_computation.2 | async-start | bytes 4718592 | tf_op jit(solution)/shard_map/reduce_scatter | solution.py:1140
  28.0 54.0 %collective-permute-start.7 = (bf16[384,1536]{1,0:T(8,128)(2,1)}, bf16[384,1536]{1,0:T(8,128)(2,1)S(1)}, u32[]{:S(2)}, u32[]{:S(2)}) collective-permute-start(bf16[384,1536]{1,0:T(8,128)(2,1)} %get-tuple-element.199), channel_id=1, source_target_pairs={{0,8},{8,0},{16,24},{24,16},{1,9},{9,1},{17,25},{25,17},{2,10},{10... | collective-permute-start | bytes 3538952 | tf_op jit(solution)/shard_map/ppermute | solution.py:31
  28.3 53.7 %collective-permute-start.8 = (bf16[384,1536]{1,0:T(8,128)(2,1)}, bf16[384,1536]{1,0:T(8,128)(2,1)S(1)}, u32[]{:S(2)}, u32[]{:S(2)}) collective-permute-start(bf16[384,1536]{1,0:T(8,128)(2,1)} %get-tuple-element.200), channel_id=1, source_target_pairs={{0,16},{8,24},{16,0},{24,8},{1,17},{9,25},{17,1},{25,9},{2,18},{10... | collective-permute-start | bytes 3538952 | tf_op jit(solution)/shard_map/ppermute | solution.py:31
  28.4 53.6 %collective-permute-start.3 = (bf16[2,1,64,2048]{3,2,0,1:T(8,128)(2,1)S(1)}, bf16[2,1,64,2048]{3,2,0,1:T(8,128)(2,1)}, u32[]{:S(2)}, u32[]{:S(2)}) collective-permute-start(bf16[2,1,64,2048]{3,2,0,1:T(8,128)(2,1)S(1)} %get-tuple-element.464), channel_id=1, source_target_pairs={{0,8},{8,0},{16,24},{24,16},{1,9},{9,1},{17,25},{25,17},{2,10},{10... | collective-permute-start | bytes 1572872 | tf_op jit(solution)/shard_map/ppermute | solution.py:31
  30.4 51.6 %collective-permute-start.1 = (bf16[2,1,64,2048]{3,2,0,1:T(8,128)(2,1)S(1)}, bf16[2,1,64,2048]{3,2,0,1:T(8,128)(2,1)}, u32[]{:S(2)}, u32[]{:S(2)}) collective-permute-start(bf16[2,1,64,2048]{3,2,0,1:T(8,128)(2,1)S(1)} %get-tuple-element.470), channel_id=1, source_target_pairs={{0,16},{8,24},{16,0},{24,8},{1,17},{9,25},{17,1},{25,9},{2,18},{10... | collective-permute-start | bytes 1572872 | tf_op jit(solution)/shard_map/ppermute | solution.py:31
  157.8 25.6 %collective-permute-start.23 = (bf16[2,64,2048]{2,1,0:T(8,128)(2,1)}, bf16[2,64,2048]{2,1,0:T(8,128)(2,1)S(1)}, u32[]{:S(2)}, u32[]{:S(2)}) collective-permute-start(bf16[2,64,2048]{2,1,0:T(8,128)(2,1)} %get-tuple-element.213.refs_9_), channel_id=1, source_target_pairs={{0,2},{1,3},{2,4},{3,5},{4,6},{5,7},{6,0},{7,1},{8,10},{9,11},{10,... | collective-permute-start | bytes 1572872 | tf_op jit(solution)/shard_map/ppermute | solution.py:57
  163.5 23.7 %collective-permute-start.30 = (bf16[2,1,64,2048]{3,2,1,0:T(8,128)(2,1)S(1)}, bf16[2,1,64,2048]{3,2,1,0:T(8,128)(2,1)S(1)}, u32[]{:S(2)}, u32[]{:S(2)}) collective-permute-start(bf16[2,1,64,2048]{3,2,1,0:T(8,128)(2,1)S(1)} %pad_maximum_fusion.11.a_ref), channel_id=1, source_target_pairs={{0,16},{8,24},{16,0},{24,8},{1,17},{9,25},{17,1},{25,9},{2,18},{10... | collective-permute-start | bytes 1572872 | tf_op jit(solution)/shard_map/ppermute | solution.py:31
  166.6 20.5 %collective-permute-start.31 = (bf16[2,1,64,2048]{3,2,1,0:T(8,128)(2,1)S(1)}, bf16[2,1,64,2048]{3,2,1,0:T(8,128)(2,1)}, u32[]{:S(2)}, u32[]{:S(2)}) collective-permute-start(bf16[2,1,64,2048]{3,2,1,0:T(8,128)(2,1)S(1)} %pad_maximum_fusion.12.c_ref), channel_id=1, source_target_pairs={{0,8},{8,0},{16,24},{24,16},{1,9},{9,1},{17,25},{25,17},{2,10},{10... | collective-permute-start | bytes 1572872 | tf_op jit(solution)/shard_map/ppermute | solution.py:31
  190.5 37.3 %collective-permute-start.32 = (bf16[8,64,2048]{2,1,0:T(8,128)(2,1)}, bf16[8,64,2048]{2,1,0:T(8,128)(2,1)}, u32[]{:S(2)}, u32[]{:S(2)}) collective-permute-start(bf16[8,64,2048]{2,1,0:T(8,128)(2,1)} %join.4.refs_1_.refs_0_), channel_id=1, source_target_pairs={{0,1},{1,0},{2,3},{3,2},{4,5},{5,4},{6,7},{7,6},{8,9},{9,8},{10,11... | collective-permute-start | bytes 6291464 | tf_op jit(solution)/shard_map/ppermute | solution.py:48
  193.2 18.5 %collective-permute-start.33 = (bf16[2,1,64,2048]{3,2,1,0:T(8,128)(2,1)S(1)}, bf16[2,1,64,2048]{3,2,1,0:T(8,128)(2,1)}, u32[]{:S(2)}, u32[]{:S(2)}) collective-permute-start(bf16[2,1,64,2048]{3,2,1,0:T(8,128)(2,1)S(1)} %pad_maximum_fusion.13.a_ref), channel_id=1, source_target_pairs={{0,16},{8,24},{16,0},{24,8},{1,17},{9,25},{17,1},{25,9},{2,18},{10... | collective-permute-start | bytes 1572872 | tf_op jit(solution)/shard_map/ppermute | solution.py:31
  214.3 41.8 %collective-permute-start.35 = (bf16[8,64,2048]{2,1,0:T(8,128)(2,1)}, bf16[8,64,2048]{2,1,0:T(8,128)(2,1)}, u32[]{:S(2)}, u32[]{:S(2)}) collective-permute-start(bf16[8,64,2048]{2,1,0:T(8,128)(2,1)} %join.5.refs_1_.refs_2_), channel_id=1, source_target_pairs={{0,1},{1,0},{2,3},{3,2},{4,5},{5,4},{6,7},{7,6},{8,9},{9,8},{10,11... | collective-permute-start | bytes 6291464 | tf_op jit(solution)/shard_map/ppermute | solution.py:48
  226.3 22.9 %collective-permute-start.37 = (bf16[2,2,64,2048]{3,2,1,0:T(8,128)(2,1)}, bf16[2,2,64,2048]{3,2,1,0:T(8,128)(2,1)}, u32[]{:S(2)}, u32[]{:S(2)}) collective-permute-start(bf16[2,2,64,2048]{3,2,1,0:T(8,128)(2,1)} %pad_maximum_fusion.6.a_ref), channel_id=1, source_target_pairs={{0,16},{8,24},{16,0},{24,8},{1,17},{9,25},{17,1},{25,9},{2,18},{10... | collective-permute-start | bytes 3145736 | tf_op jit(solution)/shard_map/ppermute | solution.py:31
  226.6 22.6 %collective-permute-start.38 = (bf16[2,2,64,2048]{3,2,1,0:T(8,128)(2,1)}, bf16[2,2,64,2048]{3,2,1,0:T(8,128)(2,1)}, u32[]{:S(2)}, u32[]{:S(2)}) collective-permute-start(bf16[2,2,64,2048]{3,2,1,0:T(8,128)(2,1)} %pad_maximum_fusion.7.c_ref), channel_id=1, source_target_pairs={{0,8},{8,0},{16,24},{24,16},{1,9},{9,1},{17,25},{25,17},{2,10},{10... | collective-permute-start | bytes 3145736 | tf_op jit(solution)/shard_map/ppermute | solution.py:31
  248.8 27.5 %collective-permute-start.36 = (bf16[4,2,1,64,2176]{4,3,1,2,0:T(8,128)(2,1)}, bf16[4,2,1,64,2176]{4,3,1,2,0:T(8,128)(2,1)}, u32[]{:S(2)}, u32[]{:S(2)}) collective-permute-start(bf16[4,2,1,64,2176]{4,3,1,2,0:T(8,128)(2,1)} %bitcast.530), channel_id=1, source_target_pairs={{0,1},{1,0},{2,3},{3,2},{4,5},{5,4},{6,7},{7,6},{8,9},{9,8},{10,11... | collective-permute-start | bytes 6684680 | tf_op jit(solution)/shard_map/ppermute | solution.py:48
  251.8 24.4 %collective-permute-start.39 = (bf16[8,64,2048]{2,1,0:T(8,128)(2,1)}, bf16[8,64,2048]{2,1,0:T(8,128)(2,1)}, u32[]{:S(2)}, u32[]{:S(2)}) collective-permute-start(bf16[8,64,2048]{2,1,0:T(8,128)(2,1)} %join.6.refs_1_.refs_4_), channel_id=1, source_target_pairs={{0,1},{1,0},{2,3},{3,2},{4,5},{5,4},{6,7},{7,6},{8,9},{9,8},{10,11... | collective-permute-start | bytes 6291464 | tf_op jit(solution)/shard_map/ppermute | solution.py:48
  255.6 45.1 %collective-permute-start.41 = (bf16[8,64,2048]{2,1,0:T(8,128)(2,1)}, bf16[8,64,2048]{2,1,0:T(8,128)(2,1)S(1)}, u32[]{:S(2)}, u32[]{:S(2)}) collective-permute-start(bf16[8,64,2048]{2,1,0:T(8,128)(2,1)} %join.7.refs_1_.refs_6_), channel_id=1, source_target_pairs={{0,1},{1,0},{2,3},{3,2},{4,5},{5,4},{6,7},{7,6},{8,9},{9,8},{10,11... | collective-permute-start | bytes 6291464 | tf_op jit(solution)/shard_map/ppermute | solution.py:48
  276.2 24.7 %collective-permute-start.40 = (bf16[4,2,1,64,2176]{4,3,1,2,0:T(8,128)(2,1)}, bf16[4,2,1,64,2176]{4,3,1,2,0:T(8,128)(2,1)S(1)}, u32[]{:S(2)}, u32[]{:S(2)}) collective-permute-start(bf16[4,2,1,64,2176]{4,3,1,2,0:T(8,128)(2,1)} %bitcast.533), channel_id=1, source_target_pairs={{0,1},{1,0},{2,3},{3,2},{4,5},{5,4},{6,7},{7,6},{8,9},{9,8},{10,11... | collective-permute-start | bytes 6684680 | tf_op jit(solution)/shard_map/ppermute | solution.py:48
  300.8 26.7 %collective-permute-start.48 = (bf16[4,2,1,64,2176]{4,3,1,2,0:T(8,128)(2,1)}, bf16[4,2,1,64,2176]{4,3,1,2,0:T(8,128)(2,1)S(1)}, u32[]{:S(2)}, u32[]{:S(2)}) collective-permute-start(bf16[4,2,1,64,2176]{4,3,1,2,0:T(8,128)(2,1)} %bitcast.531), channel_id=1, source_target_pairs={{0,1},{1,0},{2,3},{3,2},{4,5},{5,4},{6,7},{7,6},{8,9},{9,8},{10,11... | collective-permute-start | bytes 6684680 | tf_op jit(solution)/shard_map/ppermute | solution.py:48
  328.1 23.2 %collective-permute-start.50 = (bf16[2,1,64,2176]{3,2,1,0:T(8,128)(2,1)S(1)}, bf16[2,1,64,2176]{3,2,1,0:T(8,128)(2,1)S(1)}, u32[]{:S(2)}, u32[]{:S(2)}) collective-permute-start(bf16[2,1,64,2176]{3,2,1,0:T(8,128)(2,1)S(1)} %bitcast.500), channel_id=1, source_target_pairs={{0,8},{8,0},{16,24},{24,16},{1,9},{9,1},{17,25},{25,17},{2,10},{10... | collective-permute-start | bytes 1671176 | tf_op jit(solution)/shard_map/ppermute | solution.py:31
  328.5 24.7 %collective-permute-start.49 = (bf16[2,1,64,2176]{3,2,0,1:T(8,128)(2,1)S(1)}, bf16[2,1,64,2176]{3,2,0,1:T(8,128)(2,1)S(1)}, u32[]{:S(2)}, u32[]{:S(2)}) collective-permute-start(bf16[2,1,64,2176]{3,2,0,1:T(8,128)(2,1)S(1)} %get-tuple-element.256), channel_id=1, source_target_pairs={{0,16},{8,24},{16,0},{24,8},{1,17},{9,25},{17,1},{25,9},{2,18},{10... | collective-permute-start | bytes 1671176 | tf_op jit(solution)/shard_map/ppermute | solution.py:31
  341.3 17.8 %collective-permute-start.46 = (bf16[1,64,2176]{2,1,0:T(8,128)(2,1)S(1)}, bf16[1,64,2176]{2,1,0:T(8,128)(2,1)S(1)}, u32[]{:S(2)}, u32[]{:S(2)}) collective-permute-start(bf16[1,64,2176]{2,1,0:T(8,128)(2,1)S(1)} %fusion.40), channel_id=1, source_target_pairs={{0,16},{8,24},{16,0},{24,8},{1,17},{9,25},{17,1},{25,9},{2,18},{10... | collective-permute-start | bytes 835592 | tf_op jit(solution)/shard_map/ppermute | solution.py:31
  343.5 35.8 %collective-permute-start.55 = (bf16[2,1,64,2176]{3,2,1,0:T(8,128)(2,1)S(1)}, bf16[2,1,64,2176]{3,2,1,0:T(8,128)(2,1)S(1)}, u32[]{:S(2)}, u32[]{:S(2)}) collective-permute-start(bf16[2,1,64,2176]{3,2,1,0:T(8,128)(2,1)S(1)} %bitcast.498), channel_id=1, source_target_pairs={{0,8},{8,0},{16,24},{24,16},{1,9},{9,1},{17,25},{25,17},{2,10},{10... | collective-permute-start | bytes 1671176 | tf_op jit(solution)/shard_map/ppermute | solution.py:31
  351.2 28.1 %collective-permute-start.54 = (bf16[2,1,64,2176]{3,2,0,1:T(8,128)(2,1)S(1)}, bf16[2,1,64,2176]{3,2,0,1:T(8,128)(2,1)S(1)}, u32[]{:S(2)}, u32[]{:S(2)}) collective-permute-start(bf16[2,1,64,2176]{3,2,0,1:T(8,128)(2,1)S(1)} %get-tuple-element.262), channel_id=1, source_target_pairs={{0,16},{8,24},{16,0},{24,8},{1,17},{9,25},{17,1},{25,9},{2,18},{10... | collective-permute-start | bytes 1671176 | tf_op jit(solution)/shard_map/ppermute | solution.py:31
  353.2 22.7 %collective-permute-start.52 = (bf16[1,64,2176]{2,1,0:T(8,128)(2,1)S(1)}, bf16[1,64,2176]{2,1,0:T(8,128)(2,1)S(1)}, u32[]{:S(2)}, u32[]{:S(2)}) collective-permute-start(bf16[1,64,2176]{2,1,0:T(8,128)(2,1)S(1)} %fusion.41), channel_id=1, source_target_pairs={{0,16},{8,24},{16,0},{24,8},{1,17},{9,25},{17,1},{25,9},{2,18},{10... | collective-permute-start | bytes 835592 | tf_op jit(solution)/shard_map/ppermute | solution.py:31
  377.0 21.3 %collective-permute-start.59 = (bf16[2,1,64,2176]{3,2,0,1:T(8,128)(2,1)}, bf16[2,1,64,2176]{3,2,0,1:T(8,128)(2,1)}, u32[]{:S(2)}, u32[]{:S(2)}) collective-permute-start(bf16[2,1,64,2176]{3,2,0,1:T(8,128)(2,1)} %get-tuple-element.272), channel_id=1, source_target_pairs={{0,16},{8,24},{16,0},{24,8},{1,17},{9,25},{17,1},{25,9},{2,18},{10... | collective-permute-start | bytes 1671176 | tf_op jit(solution)/shard_map/ppermute | solution.py:31
  378.7 19.6 %collective-permute-start.60 = (bf16[2,1,64,2176]{3,2,1,0:T(8,128)(2,1)}, bf16[2,1,64,2176]{3,2,1,0:T(8,128)(2,1)}, u32[]{:S(2)}, u32[]{:S(2)}) collective-permute-start(bf16[2,1,64,2176]{3,2,1,0:T(8,128)(2,1)} %fusion.12), channel_id=1, source_target_pairs={{0,8},{8,0},{16,24},{24,16},{1,9},{9,1},{17,25},{25,17},{2,10},{10... | collective-permute-start | bytes 1671176 | tf_op jit(solution)/shard_map/ppermute | solution.py:31
  391.2 60.2 %collective-permute-start.65 = (bf16[4,2,4,64,2048]{4,3,2,1,0:T(8,128)(2,1)}, bf16[4,2,4,64,2048]{4,3,2,1,0:T(8,128)(2,1)}, u32[]{:S(2)}, u32[]{:S(2)}) collective-permute-start(bf16[4,2,4,64,2048]{4,3,2,1,0:T(8,128)(2,1)} %mix.2), channel_id=1, source_target_pairs={{0,1},{1,0},{2,3},{3,2},{4,5},{5,4},{6,7},{7,6},{8,9},{9,8},{10,11... | collective-permute-start | bytes 25165832 | tf_op jit(solution)/shard_map/ppermute | solution.py:48
  509.3 239.5 %all-gather.6.cloned.1.call-start = ((), (), s32[]{:S(2)}) async-start(), calls=%async_computation.3 | async-start | bytes 4718592 | tf_op jit(solution)/shard_map/all_gather | solution.py:1196
  510.0 65.7 %collective-permute-start.71 = (bf16[2,4,64,2048]{3,2,1,0:T(8,128)(2,1)}, bf16[2,4,64,2048]{3,2,1,0:T(8,128)(2,1)}, u32[]{:S(2)}, u32[]{:S(2)}) collective-permute-start(bf16[2,4,64,2048]{3,2,1,0:T(8,128)(2,1)} %get-tuple-element.301), channel_id=1, source_target_pairs={{0,16},{8,24},{16,0},{24,8},{1,17},{9,25},{17,1},{25,9},{2,18},{10... | collective-permute-start | bytes 6291464 | tf_op jit(solution)/shard_map/ppermute | solution.py:31
  510.0 69.9 %collective-permute-start.73 = (bf16[2,4,64,2048]{3,2,1,0:T(8,128)(2,1)}, bf16[2,4,64,2048]{3,2,1,0:T(8,128)(2,1)}, u32[]{:S(2)}, u32[]{:S(2)}) collective-permute-start(bf16[2,4,64,2048]{3,2,1,0:T(8,128)(2,1)} %get-tuple-element.303), channel_id=1, source_target_pairs={{0,8},{8,0},{16,24},{24,16},{1,9},{9,1},{17,25},{25,17},{2,10},{10... | collective-permute-start | bytes 6291464 | tf_op jit(solution)/shard_map/ppermute | solution.py:31
  510.9 17.5 %collective-permute-start.77 = (bf16[4,256,512]{2,1,0:T(8,128)(2,1)}, bf16[4,256,512]{2,1,0:T(8,128)(2,1)S(1)}, u32[]{:S(2)}, u32[]{:S(2)}) collective-permute-start(bf16[4,256,512]{2,1,0:T(8,128)(2,1)} %get-tuple-element.315), channel_id=1, source_target_pairs={{0,1},{1,0},{2,3},{3,2},{4,5},{5,4},{6,7},{7,6},{8,9},{9,8},{10,11... | collective-permute-start | bytes 3145736 | tf_op jit(solution)/shard_map/ppermute | solution.py:48
  510.9 57.9 %collective-permute-start.84 = (bf16[2,1,64,2048]{3,2,1,0:T(8,128)(2,1)}, bf16[2,1,64,2048]{3,2,1,0:T(8,128)(2,1)}, u32[]{:S(2)}, u32[]{:S(2)}) collective-permute-start(bf16[2,1,64,2048]{3,2,1,0:T(8,128)(2,1)} %bitcast.536), channel_id=1, source_target_pairs={{0,16},{8,24},{16,0},{24,8},{1,17},{9,25},{17,1},{25,9},{2,18},{10... | collective-permute-start | bytes 1572872 | tf_op jit(solution)/shard_map/ppermute | solution.py:31
  526.8 42.0 %collective-permute-start.85 = (bf16[2,1,64,2048]{3,2,1,0:T(8,128)(2,1)}, bf16[2,1,64,2048]{3,2,1,0:T(8,128)(2,1)}, u32[]{:S(2)}, u32[]{:S(2)}) collective-permute-start(bf16[2,1,64,2048]{3,2,1,0:T(8,128)(2,1)} %bitcast.535), channel_id=1, source_target_pairs={{0,8},{8,0},{16,24},{24,16},{1,9},{9,1},{17,25},{25,17},{2,10},{10... | collective-permute-start | bytes 1572872 | tf_op jit(solution)/shard_map/ppermute | solution.py:31
  528.4 57.8 %collective-permute-start.82 = (bf16[4,64,512]{2,1,0:T(8,128)(2,1)}, bf16[4,64,512]{2,1,0:T(8,128)(2,1)S(1)}, u32[]{:S(2)}, u32[]{:S(2)}) collective-permute-start(bf16[4,64,512]{2,1,0:T(8,128)(2,1)} %fusion.36), channel_id=1, source_target_pairs={{0,2},{1,3},{2,4},{3,5},{4,6},{5,7},{6,0},{7,1},{8,10},{9,11},{10,... | collective-permute-start | bytes 786440 | tf_op jit(solution)/shard_map/ppermute | solution.py:57
  575.7 29.6 %collective-permute-start.87 = (bf16[1,64,2048]{2,1,0:T(8,128)(2,1)}, bf16[1,64,2048]{2,1,0:T(8,128)(2,1)}, u32[]{:S(2)}, u32[]{:S(2)}) collective-permute-start(bf16[1,64,2048]{2,1,0:T(8,128)(2,1)} %fusion.28), channel_id=1, source_target_pairs={{0,16},{8,24},{16,0},{24,8},{1,17},{9,25},{17,1},{25,9},{2,18},{10... | collective-permute-start | bytes 786440 | tf_op jit(solution)/shard_map/ppermute | solution.py:31
  580.0 31.1 %collective-permute-start.72 = (bf16[4,64,2048]{2,1,0:T(8,128)(2,1)}, bf16[4,64,2048]{2,1,0:T(8,128)(2,1)}, u32[]{:S(2)}, u32[]{:S(2)}) collective-permute-start(bf16[4,64,2048]{2,1,0:T(8,128)(2,1)} %fusion.16), channel_id=1, source_target_pairs={{0,8},{8,0},{16,24},{24,16},{1,9},{9,1},{17,25},{25,17},{2,10},{10... | collective-permute-start | bytes 3145736 | tf_op jit(solution)/shard_map/ppermute | solution.py:31
  584.1 30.5 %collective-permute-start.74 = (bf16[4,64,2048]{2,1,0:T(8,128)(2,1)}, bf16[4,64,2048]{2,1,0:T(8,128)(2,1)}, u32[]{:S(2)}, u32[]{:S(2)}) collective-permute-start(bf16[4,64,2048]{2,1,0:T(8,128)(2,1)} %fusion.17), channel_id=1, source_target_pairs={{0,16},{8,24},{16,0},{24,8},{1,17},{9,25},{17,1},{25,9},{2,18},{10... | collective-permute-start | bytes 3145736 | tf_op jit(solution)/shard_map/ppermute | solution.py:31
  587.1 24.0 %collective-permute-start.88 = (bf16[4,64,512]{2,1,0:T(8,128)(2,1)}, bf16[4,64,512]{2,1,0:T(8,128)(2,1)S(1)}, u32[]{:S(2)}, u32[]{:S(2)}) collective-permute-start(bf16[4,64,512]{2,1,0:T(8,128)(2,1)} %get-tuple-element.377), channel_id=1, source_target_pairs={{0,2},{1,3},{2,4},{3,5},{4,6},{5,7},{6,0},{7,1},{8,10},{9,11},{10,... | collective-permute-start | bytes 786440 | tf_op jit(solution)/shard_map/ppermute | solution.py:57
  587.1 22.2 %collective-permute-start.81 = (bf16[4,64,512]{2,1,0:T(8,128)(2,1)}, bf16[4,64,512]{2,1,0:T(8,128)(2,1)}, u32[]{:S(2)}, u32[]{:S(2)}) collective-permute-start(bf16[4,64,512]{2,1,0:T(8,128)(2,1)} %fusion.35), channel_id=1, source_target_pairs={{0,2},{1,3},{2,4},{3,5},{4,6},{5,7},{6,0},{7,1},{8,10},{9,11},{10,... | collective-permute-start | bytes 786440 | tf_op jit(solution)/shard_map/ppermute | solution.py:57
  624.8 55.2 %collective-permute-start.108 = (bf16[4,64,512]{2,1,0:T(8,128)(2,1)S(1)}, bf16[4,64,512]{2,1,0:T(8,128)(2,1)}, u32[]{:S(2)}, u32[]{:S(2)}) collective-permute-start(bf16[4,64,512]{2,1,0:T(8,128)(2,1)S(1)} %collective-permute-done.88), channel_id=1, source_target_pairs={{0,2},{1,3},{2,4},{3,5},{4,6},{5,7},{6,0},{7,1},{8,10},{9,11},{10,... | collective-permute-start | bytes 786440 | tf_op jit(solution)/shard_map/ppermute | solution.py:57
  641.1 29.1 %collective-permute-start.75 = (bf16[2,64,2048]{2,1,0:T(8,128)(2,1)}, bf16[2,64,2048]{2,1,0:T(8,128)(2,1)S(1)}, u32[]{:S(2)}, u32[]{:S(2)}) collective-permute-start(bf16[2,64,2048]{2,1,0:T(8,128)(2,1)} %pad_maximum_fusion.19), channel_id=1, source_target_pairs={{0,2},{1,3},{2,4},{3,5},{4,6},{5,7},{6,0},{7,1},{8,10},{9,11},{10,... | collective-permute-start | bytes 1572872 | tf_op jit(solution)/shard_map/ppermute | solution.py:57
  650.8 29.0 %collective-permute-start.101 = (bf16[4,64,512]{2,1,0:T(8,128)(2,1)}, bf16[4,64,512]{2,1,0:T(8,128)(2,1)}, u32[]{:S(2)}, u32[]{:S(2)}) collective-permute-start(bf16[4,64,512]{2,1,0:T(8,128)(2,1)} %pad_maximum_fusion.23), channel_id=1, source_target_pairs={{0,2},{1,3},{2,4},{3,5},{4,6},{5,7},{6,0},{7,1},{8,10},{9,11},{10,... | collective-permute-start | bytes 786440 | tf_op jit(solution)/shard_map/ppermute | solution.py:57
  670.6 27.8 %collective-permute-start.97 = (bf16[2,64,2048]{2,1,0:T(8,128)(2,1)S(1)}, bf16[2,64,2048]{2,1,0:T(8,128)(2,1)S(1)}, u32[]{:S(2)}, u32[]{:S(2)}) collective-permute-start(bf16[2,64,2048]{2,1,0:T(8,128)(2,1)S(1)} %fusion.18), channel_id=1, source_target_pairs={{0,2},{1,3},{2,4},{3,5},{4,6},{5,7},{6,0},{7,1},{8,10},{9,11},{10,... | collective-permute-start | bytes 1572872 | tf_op jit(solution)/shard_map/ppermute | solution.py:57
  679.8 29.9 %collective-permute-start.102 = (bf16[4,64,512]{2,1,0:T(8,128)(2,1)}, bf16[4,64,512]{2,1,0:T(8,128)(2,1)S(1)}, u32[]{:S(2)}, u32[]{:S(2)}) collective-permute-start(bf16[4,64,512]{2,1,0:T(8,128)(2,1)} %collective-permute-done.101), channel_id=1, source_target_pairs={{0,2},{1,3},{2,4},{3,5},{4,6},{5,7},{6,0},{7,1},{8,10},{9,11},{10,... | collective-permute-start | bytes 786440 | tf_op jit(solution)/shard_map/ppermute | solution.py:57
  679.9 37.5 %collective-permute-start.109 = (bf16[4,64,512]{2,1,0:T(8,128)(2,1)}, bf16[4,64,512]{2,1,0:T(8,128)(2,1)S(1)}, u32[]{:S(2)}, u32[]{:S(2)}) collective-permute-start(bf16[4,64,512]{2,1,0:T(8,128)(2,1)} %collective-permute-done.108), channel_id=1, source_target_pairs={{0,2},{1,3},{2,4},{3,5},{4,6},{5,7},{6,0},{7,1},{8,10},{9,11},{10,... | collective-permute-start | bytes 786440 | tf_op jit(solution)/shard_map/ppermute | solution.py:57
  698.6 29.7 %collective-permute-start.98 = (bf16[2,64,2048]{2,1,0:T(8,128)(2,1)S(1)}, bf16[2,64,2048]{2,1,0:T(8,128)(2,1)S(1)}, u32[]{:S(2)}, u32[]{:S(2)}) collective-permute-start(bf16[2,64,2048]{2,1,0:T(8,128)(2,1)S(1)} %fusion.19), channel_id=1, source_target_pairs={{0,2},{1,3},{2,4},{3,5},{4,6},{5,7},{6,0},{7,1},{8,10},{9,11},{10,... | collective-permute-start | bytes 1572872 | tf_op jit(solution)/shard_map/ppermute | solution.py:57
  709.7 21.4 %collective-permute-start.103 = (bf16[4,64,512]{2,1,0:T(8,128)(2,1)S(1)}, bf16[4,64,512]{2,1,0:T(8,128)(2,1)S(1)}, u32[]{:S(2)}, u32[]{:S(2)}) collective-permute-start(bf16[4,64,512]{2,1,0:T(8,128)(2,1)S(1)} %collective-permute-done.102), channel_id=1, source_target_pairs={{0,2},{1,3},{2,4},{3,5},{4,6},{5,7},{6,0},{7,1},{8,10},{9,11},{10,... | collective-permute-start | bytes 786440 | tf_op jit(solution)/shard_map/ppermute | solution.py:57
  (143 other events, 1371.3 us)
Sparse Core Ops, SparseCore 0:
  11.4 139.4 all-gather.3
  509.4 57.9 reduce-scatter.1
  642.6 72.6 all-gather.5

commit v3 on v2

--- a/solution.py
+++ b/solution.py
@@ -67,12 +67,20 @@
     return [pair_a, swap_y(pair_a), pair_b, swap_x(pair_b)]
 
 
-def reduce_xy(blocks, *others):
+def reduce_first(blocks, *others):
     keep_a, send_a, keep_b, send_b = blocks
     got_a, got_b = after((swap_y(send_a), swap_x(send_b)), *others)
-    far_a = swap_x((keep_a[1].astype(F32) + got_a[1].astype(F32)).astype(BF16))
-    far_b = swap_y((keep_b[1].astype(F32) + got_b[1].astype(F32)).astype(BF16))
-    return (keep_a[0], got_a[0], far_a), (keep_b[0], got_b[0], far_b)
+    on_a = (keep_a[1].astype(F32) + got_a[1].astype(F32)).astype(BF16)
+    on_b = (keep_b[1].astype(F32) + got_b[1].astype(F32)).astype(BF16)
+    return ((keep_a[0], got_a[0]), (keep_b[0], got_b[0])), (on_a, on_b)
+
+
+def reduce_last(kept, on):
+    return kept[0] + (swap_x(on[0]),), kept[1] + (swap_y(on[1]),)
+
+
+def reduce_xy(blocks, *others):
+    return reduce_last(*reduce_first(blocks, *others))
 
 
 def total_of(terms):
@@ -445,7 +453,12 @@
                     (1, 1, eight, half, units), lambda i, at: (at[2], core_of(i, at), 0, 0, 0)
                 ),
             ]
-            + [whole(w_gate.shape), whole(w_up.shape), whole(gate_up_t.shape), whole(router.shape)],
+            + [
+                pl.BlockSpec(
+                    w.shape, lambda i, _, n=w.ndim: (0,) * n, pipeline_mode=pl.Buffered(1)
+                )
+                for w in (w_gate, w_up, gate_up_t, router)
+            ],
             out_specs=[whole(own_shape) for _ in range(4)]
             + [
                 whole((4,) + own_shape),
@@ -466,7 +479,7 @@
             out((2, eight, half, units), BF16),
             out((2, count, units), BF16),
         ],
-        compiler_params=pltpu.CompilerParams(vmem_limit_bytes=48 << 20),
+        compiler_params=pltpu.CompilerParams(vmem_limit_bytes=38 << 20),
         cost_estimate=pl.CostEstimate(
             flops=8 * count * gate_up_t.size,
             bytes_accessed=8 * count * width + 4 * gate_up_t.size + 20 * count * units,
@@ -1003,7 +1016,7 @@
             [t[0] for t in terms]
             for terms in reduce_xy(
                 after(totals, [r[0] for r in all_rows]),
-                totals_all[min(j + 2, chips - 1)],
+                totals_all[-1] if j != 1 else (),
                 back_pieces[-1:],
                 arrived[-1:],
             )
@@ -1139,10 +1152,6 @@
 
     pair_sums = lax.psum_scatter(got[4], "expert", scatter_dimension=0, tiled=True)[0]
 
-    output_total = ring_add(output_total, output_pieces, got[0])
-    value_pieces = split_rows(after(value_own + value_passed.astype(F32), output_total))
-    value_pieces = value_pieces[1:] + value_pieces[:1]
-    total = value_pieces.pop(0).astype(BF16)
     span = min(chips, 4)
     starts = range(0, chips, span)
 
@@ -1166,40 +1175,42 @@
             ]
         )
 
-    expert_grads = []
-    out_spread = []
+    expert_grads = [down_grads(got[0])]
+    output_total = ring_add(output_total, output_pieces, expert_grads[0])
+    value_pieces = split_rows(
+        value_own + after(value_passed, expert_grads[0]).astype(F32)
+    )
+    value_pieces = value_pieces[1:] + value_pieces[:1]
+    total = value_pieces.pop(0).astype(BF16)
+    expert_grads.append(row_grads(0, total, output_total))
+    total = ring_add(total, value_pieces, expert_grads[1])
+    output_total = ring_add(output_total, output_pieces, expert_grads[1])
+    first_kept, first_on = reduce_first(
+        [b.reshape(2, 1, half, width) for b in got[:4]], total, output_total
+    )
+    expert_grads.append(row_grads(1, total, output_total, first_on, out_far))
+    while output_pieces:
+        output_total = ring_add(output_total, output_pieces, expert_grads[2])
+    out_spread = [output_total]
     while len(value_pieces) > 1:
-        if not expert_grads:
-            expert_grads.append(down_grads(total))
-            terms_a, terms_b = reduce_xy(
-                [b.reshape(2, 1, half, width) for b in got[:4]], expert_grads[0]
-            )
-        elif len(expert_grads) == 1:
-            expert_grads.append(row_grads(0, total, out_far, output_total))
-            grad_input, grad_gain_one = call(
-                finish_kernel,
-                "finish",
-                [t.reshape(half, width) for t in terms_a + terms_b]
-                + [own_input, grad_res, after(gain_one, expert_grads[1])],
-                [out((2, half, width), F32), out((8, width), F32)],
-                tok_count * width,
-            )
-        total = ring_add(total, value_pieces, expert_grads[-1])
-        if output_pieces:
-            output_total = ring_add(output_total, output_pieces, total)
-        if not output_pieces:
-            out_spread.append(
-                after(ring_up(out_spread[-1]), total) if out_spread else output_total
-            )
-    out_now = out_piece(1).astype(BF16)
-    pair_mine = exchange_grads(after(pair_sums, grad_gain_one, out_spread[-1], out_now))
+        total = ring_add(total, value_pieces, expert_grads[2])
+    terms_a, terms_b = reduce_last(first_kept, first_on)
+    grad_input, grad_gain_one = call(
+        finish_kernel,
+        "finish",
+        [t.reshape(half, width) for t in terms_a + terms_b]
+        + [own_input, grad_res, after(gain_one, total)],
+        [out((2, half, width), F32), out((8, width), F32)],
+        tok_count * width,
+    )
+    out_now = after(out_piece(1), total).astype(BF16)
+    pair_mine = exchange_grads(after(pair_sums, grad_gain_one, out_now))
     pair_rows = lax.all_gather(pair_mine, "expert", axis=0)
     total = ring_add(total, value_pieces, pair_mine)
     spread = [exchange_grads(total)]
-    expert_grads.append(row_grads(1, spread[0], out_now))
     grad_w_down, grad_w_gate, grad_w_up = expert_grads
     for j in range(1, chips):
-        moved = after(ring_up(out_now), grad_w_up)
+        moved = after(ring_up(out_now), spread[0])
         if j + 1 < chips:
             out_now = (moved.astype(F32) + out_piece(j + 1)).astype(BF16)
         spread.append(after(ring_up(spread[-1]), out_now if j + 1 < chips else moved))

time: 770 us -> 773 us (level)
  waiting for transfers between devices: 267 us -> 250 us
  starting transfers between devices: 90.8 us -> 102 us
  other arithmetic: 79.5 us -> 90 us
  Pallas kernels: 251 us -> 242 us
    ppermute x71, waiting for transfers between devices: 163 us -> 136 us  [flip_shard(): return lax.ppermute(values, 'shard', [(i, i ^ bit) for i in range(count)])]
    ppermute x21, waiting for transfers between devices: 95.5 us -> 106 us  [ring_up(): lax.ppermute(values, 'expert', [(i, (i + 2) % count) for i in range(count)])]
    pallas_call x4, Pallas kernels: 77.2 us -> 67.7 us  [expert_call(): pl.pallas_call(lambda *refs: expert_kernel(experts_all, *refs), grid_spec...]
    add x6 -> x10, other arithmetic: 2.35 us -> 11.7 us  [total_of(): total = total + term.astype(F32)]
    unnamed x155 -> x173, local copies, waits for them, and re-layouts: 11.7 us -> 20 us
    ppermute x21, starting transfers between devices: 20.5 us -> 28.7 us  [ring_up(): lax.ppermute(values, 'expert', [(i, (i + 2) % count) for i in range(count)])]
  transfers between devices with their start and end apart: 114 -> 114, of which waited for: 46 -> 44; matrix products, arithmetic and copies ran while one was open for 15% -> 16% of each run, Pallas kernels for 31% -> 31%
where the time goes in v3:
time: 773 us; the launch traced here: 767 us
  waiting for transfers between devices  250 us (32%)
  Pallas kernels  242 us (31%)
  starting transfers between devices  102 us (13%)
  other arithmetic  90 us (12%)
  local copies, waits for them, and re-layouts  67.4 us (9%)
  between operations  15.6 us (2%)
    ppermute x71, waiting for transfers between devices, flip_shard(): return lax.ppermute(values, 'shard', [(i, i ^ bit) for i in range(count)])  136 us
    ppermute x21, waiting for transfers between devices, ring_up(): lax.ppermute(values, 'expert', [(i, (i + 2) % count) for i in range(count)])  106 us
    ppermute x71, starting transfers between devices, flip_shard(): return lax.ppermute(values, 'shard', [(i, i ^ bit) for i in range(count)])  70.7 us
    pallas_call x9, Pallas kernels, call(): pl.pallas_call(kernel, in_specs=[scalars() if n in smem else whole(a.shap...  68.5 us
    pallas_call x4, Pallas kernels, expert_call(): pl.pallas_call(lambda *refs: expert_kernel(experts_all, *refs), grid_spec...  67.7 us
    pallas_call x2, Pallas kernels, row_grad_call(): pl.pallas_call(lambda *refs: row_grad_kernel(len(rows), *refs), grid=(wid...  31.7 us
    ppermute x21, starting transfers between devices, ring_up(): lax.ppermute(values, 'expert', [(i, (i + 2) % count) for i in range(count)])  28.7 us
    unnamed x173, local copies, waits for them, and re-layouts  20 us
  transfers between devices with their start and end apart: 114, of which 44 were waited for; matrix products, arithmetic and copies ran while one was open for 16% of the time, Pallas kernels for 31%

profile of v3, /device:TPU:0, one launch (start us, length us, event | category | flops | bytes accessed | tf_op | source)
XLA Modules:
  0.0 767.0 jit_solution(3830093373637749625)
XLA Ops:
  10.6 3.0 collective-permute-start
  20.5 5.0 cut.1
  32.1 6.5 flip.1
  40.0 42.0 %collective-permute-done.3 = bf16[2,1,64,2048]{3,2,0,1:T(8,128)(2,1)} collective-permute-done((bf16[2,1,64,2048]{3,2,0,1:T(8,128)(2,1)S(1)}, bf16[2,1,64,2048]{3,2,0,1:T(8,128)(2,1)}, u32[]{:S(2)}, u32[]{:S(2)}) %collective-permute-start.3) | collective-permute-done | bytes 524320 | tf_op jit(solution)/shard_map/ppermute | solution.py:31
  89.1 3.6 collective-permute-done.9
  101.2 9.7 %project.1 = (bf16[512,2048]{1,0:T(8,128)(2,1)}, f32[512,1536]{1,0:T(8,128)}, f32[4,8,128]{2,1,0:T(8,128)}, f32[512,128]{1,0:T(8,128)}) custom-call(s32[8]{0:T(128)} %stack.264.at_ref, bf16[2,64,2048]{2,1,0:T(8,128)(2,1)} %get-tuple-element.471.r0, bf16[2,64,2048]{2,1,0:T(8,128)(2,1)} %bitcast.13.r1, bf16[2,64,2048]{2,1,0:T(8,128)(2,1)} %get-tuple-element.465.r2, ...), custom_call_target="tpu_custom_call" | custom-call | flops 3221225472 | bytes 13918240 | tf_op jit(solution)/shard_map/project/pallas_call | solution.py:156
  118.2 9.9 %attend.1 = (bf16[512,512]{1,0:T(8,128)(2,1)}, bf16[512,512]{1,0:T(8,128)(2,1)}, bf16[512,512]{1,0:T(8,128)(2,1)}, f32[512,128]{1,0:T(8,128)}, f32[512,128]{1,0:...) custom-call(f32[512,1536]{1,0:T(8,128)} %get-tuple-element.322.refs_, ...), custom_call_target="tpu_custom_call" | custom-call | flops 1610612736 | bytes 11603968 | tf_op jit(solution)/shard_map/attend/pallas_call | solution.py:156
  132.9 8.3 %collective-permute-done.18 = bf16[2,1,64,2048]{3,2,1,0:T(8,128)(2,1)S(1)} collective-permute-done((bf16[2,1,64,2048]{3,2,1,0:T(8,128)(2,1)}, bf16[2,1,64,2048]{3,2,1,0:T(8,128)(2,1)S(1)}, u32[]{:S(2)}, u32[]{:S(2)}) %collective-permute-start.18) | collective-permute-done | bytes 524320 | tf_op jit(solution)/shard_map/ppermute | solution.py:31
  159.5 3.9 collective-permute-done.21
  167.5 16.1 %lead.1.refs_4_ = f32[4,2,8,64,512]{4,3,2,1,0:T(8,128)} custom-call(bf16[4,4,2,2,64,2176]{5,4,3,2,1,0:T(8,128)(2,1)} %bitcast.456, bf16[2048,512]{1,0:T(8,128)(2,1)} %get-tuple-element.216.down_t_ref), custom_call_target="tpu_custom_call" | custom-call | flops 8589934592 | bytes 26214400 | tf_op jit(solution)/shard_map/lead/pallas_call | solution.py:307
  197.5 12.0 %collective-permute-done.27 = bf16[2,64,2048]{2,1,0:T(8,128)(2,1)S(1)} collective-permute-done((bf16[2,64,2048]{2,1,0:T(8,128)(2,1)S(1)}, bf16[2,64,2048]{2,1,0:T(8,128)(2,1)S(1)}, u32[]{:S(2)}, u32[]{:S(2)}) %collective-permute-start.27) | collective-permute-done | bytes 524320 | tf_op jit(solution)/shard_map/ppermute | solution.py:57
  215.0 7.9 %collective-permute-done.29 = bf16[2,64,2048]{2,1,0:T(8,128)(2,1)} collective-permute-done((bf16[2,64,2048]{2,1,0:T(8,128)(2,1)}, bf16[2,64,2048]{2,1,0:T(8,128)(2,1)}, u32[]{:S(2)}, u32[]{:S(2)}) %collective-permute-start.29) | collective-permute-done | bytes 524320 | tf_op jit(solution)/shard_map/ppermute | solution.py:31
  233.0 16.9 %experts.4 = (bf16[2,1,64,2176]{3,2,1,0:T(8,128)(2,1)S(1)}, bf16[2,1,64,2176]{3,2,1,0:T(8,128)(2,1)S(1)}, bf16[2,1,64,2176]{3,2,1,0:T(8,128)(2,1)S(1)}, bf16[2,1...) custom-call(s32[4]{0:T(128)S(1)} %get-tuple-element.218.refs_0_, ...), custom_call_target="tpu_custom_call" | custom-call | flops 8589934592 | bytes 22020096 | tf_op jit(solution)/shard_map/experts/pallas_call | solution.py:438
  267.0 17.1 %experts.5 = (bf16[2,1,64,2176]{3,2,1,0:T(8,128)(2,1)S(1)}, bf16[2,1,64,2176]{3,2,1,0:T(8,128)(2,1)S(1)}, bf16[2,1,64,2176]{3,2,1,0:T(8,128)(2,1)S(1)}, bf16[2,1...) custom-call(s32[4]{0:T(128)S(1)} %get-tuple-element.220.refs_0_, ...), custom_call_target="tpu_custom_call" | custom-call | flops 8589934592 | bytes 22020096 | tf_op jit(solution)/shard_map/experts/pallas_call | solution.py:438
  290.7 16.9 %experts.6 = (bf16[2,1,64,2176]{3,2,1,0:T(8,128)(2,1)S(1)}, bf16[2,1,64,2176]{3,2,1,0:T(8,128)(2,1)S(1)}, bf16[2,1,64,2176]{3,2,1,0:T(8,128)(2,1)S(1)}, bf16[2,1...) custom-call(s32[4]{0:T(128)S(1)} %get-tuple-element.227.refs_0_, ...), custom_call_target="tpu_custom_call" | custom-call | flops 8589934592 | bytes 22020096 | tf_op jit(solution)/shard_map/experts/pallas_call | solution.py:438
  315.0 16.7 %experts.7 = (bf16[2,1,64,2176]{3,2,1,0:T(8,128)(2,1)S(1)}, bf16[2,1,64,2176]{3,2,1,0:T(8,128)(2,1)S(1)}, bf16[2,1,64,2176]{3,2,1,0:T(8,128)(2,1)S(1)}, bf16[2,1...) custom-call(s32[4]{0:T(128)S(1)} %get-tuple-element.237.refs_0_, ...), custom_call_target="tpu_custom_call" | custom-call | flops 8589934592 | bytes 22020096 | tf_op jit(solution)/shard_map/experts/pallas_call | solution.py:438
  344.5 11.5 %collective-permute-done.45 = bf16[1,64,2176]{2,1,0:T(8,128)(2,1)S(1)} collective-permute-done((bf16[1,64,2176]{2,1,0:T(8,128)(2,1)S(1)}, bf16[1,64,2176]{2,1,0:T(8,128)(2,1)S(1)}, u32[]{:S(2)}, u32[]{:S(2)}) %collective-permute-start.45) | collective-permute-done | bytes 278560 | tf_op jit(solution)/shard_map/ppermute | solution.py:31
  361.5 11.9 %collective-permute-done.46 = bf16[2,64,2176]{2,1,0:T(8,128)(2,1)S(1)} collective-permute-done((bf16[2,64,2176]{2,1,0:T(8,128)(2,1)S(1)}, bf16[2,64,2176]{2,1,0:T(8,128)(2,1)S(1)}, u32[]{:S(2)}, u32[]{:S(2)}) %collective-permute-start.46) | collective-permute-done | bytes 557088 | tf_op jit(solution)/shard_map/ppermute | solution.py:57
  378.5 15.0 %collective-permute-done.52 = bf16[1,64,2176]{2,1,0:T(8,128)(2,1)S(1)} collective-permute-done((bf16[1,64,2176]{2,1,0:T(8,128)(2,1)S(1)}, bf16[1,64,2176]{2,1,0:T(8,128)(2,1)S(1)}, u32[]{:S(2)}, u32[]{:S(2)}) %collective-permute-start.52) | collective-permute-done | bytes 278560 | tf_op jit(solution)/shard_map/ppermute | solution.py:31
  393.8 6.2 collective-permute-done.51
  400.1 8.4 %mix.2 = bf16[4,2,4,64,2048]{4,3,2,1,0:T(8,128)(2,1)} custom-call(bf16[4,512,512]{2,1,0:T(8,128)(2,1)} %pad_maximum_fusion.1.scaled_ref, bf16[512,2048]{1,0:T(8,128)(2,1)} %bitcast.487), custom_call_target="tpu_custom_call" | custom-call | flops 4294967296 | bytes 20971520 | tf_op jit(solution)/shard_map/mix/pallas_call | solution.py:514
  414.1 12.4 %collective-permute-done.53 = bf16[2,64,2176]{2,1,0:T(8,128)(2,1)S(1)} collective-permute-done((bf16[2,64,2176]{2,1,0:T(8,128)(2,1)S(1)}, bf16[2,64,2176]{2,1,0:T(8,128)(2,1)S(1)}, u32[]{:S(2)}, u32[]{:S(2)}) %collective-permute-start.53) | collective-permute-done | bytes 557088 | tf_op jit(solution)/shard_map/ppermute | solution.py:57
  438.4 10.2 %collective-permute-done.58.refs_0_ = bf16[2,64,2176]{2,1,0:T(8,128)(2,1)S(1)} collective-permute-done((bf16[2,64,2176]{2,1,0:T(8,128)(2,1)S(1)}, bf16[2,64,2176]{2,1,0:T(8,128)(2,1)S(1)}, u32[]{:S(2)}, u32[]{:S(2)}) %collective-permute-start.58) | collective-permute-done | bytes 557088 | tf_op jit(solution)/shard_map/ppermute | solution.py:57
  449.4 5.5 turn.1
  458.4 4.5 collective-permute-done.64
  468.1 10.7 %mix.3 = (bf16[2,4,64,2048]{3,2,1,0:T(8,128)(2,1)}, bf16[2,4,64,2048]{3,2,1,0:T(8,128)(2,1)}, bf16[2,4,64,2048]{3,2,1,0:T(8,128)(2,1)}, bf16[2,4,64,2048]{3,2,1,0:T(8,128)(2,1)}) custom-call(bf16[4,512,512]{2,1,0:T(8,128)(2,1)} %pad_maximum_fusion.scaled_ref, bf16[512,2048]{1,0:T(8,128)(2,1)} %bitcast.488, ...), custom_call_target="tpu_custom_call" | custom-call | flops 4294967296 | bytes 20971520 | tf_op jit(solution)/shard_map/mix/pallas_call | solution.py:514
  479.9 4.5 output_grad.1
  484.3 14.4 %attend_back.1 = (f32[512,512]{1,0:T(8,128)}, f32[512,512]{1,0:T(8,128)}, bf16[512,512]{1,0:T(8,128)(2,1)}, f32[4,8,128]{2,1,0:T(8,128)}, f32[8,512]{1,0:T(8,128)}, /*index=5*/bf16[512,2048]{1,0:T(8,128)(2,1)}) custom-call(bf16[2,64,2048]{2,1,0:T(8,128)(2,1)} %get-tuple-element.291.g0, bf16[2,64,2048]{2,1,0:T(8,128)(2,1)} %bitcast.503, ...), custom_call_target="tpu_custom_call" | custom-call | flops 2415919104 | bytes 16289792 | tf_op jit(solution)/shard_map/attend_back/pallas_call | solution.py:156
  510.0 4.6 value_back.1
  516.5 13.2 %project_back.1 = (bf16[2,64,2048]{2,1,0:T(8,128)(2,1)}, bf16[2,64,2048]{2,1,0:T(8,128)(2,1)}, bf16[2,64,2048]{2,1,0:T(8,128)(2,1)}, bf16[2,64,2048]{2,1,0:T(8,1...) custom-call(s32[8]{0:T(128)} %stack.264.at_ref, f32[4,8,128]{2,1,0:T(8,128)} %get-tuple-element.300.s0, ...), custom_call_target="tpu_custom_call" | custom-call | flops 6442450944 | bytes 22347808 | tf_op jit(solution)/shard_map/project_back/pallas_call | solution.py:156
  530.3 16.6 %down_grads.1 = f32[2,256,2048]{2,1,0:T(8,128)} custom-call(s32[5]{0:T(128)} %stack.313.refs_0_, bf16[2,8,64,512]{3,2,1,0:T(8,128)(2,1)} %copy-done.10, bf16[2,8,64,512]{3,2,1,0:T(8,128)(2,1)} %copy-done.11, bf16[2,8,64,512]{3,2,1,0:T(8,128)(2,1)} %copy-done.12, bf16[2,8,64,512]{3,2,1,0:T(8,128)(2,1)} %copy-done.13, ...), custom_call_target="tpu_custom_call" | custom-call | flops 8589934592 | bytes 25165824 | tf_op jit(solution)/shard_map/down_grads/pallas_call | solution.py:591
  554.7 15.9 %row_grads.2 = f32[2,2048,256]{2,1,0:T(8,128)} custom-call(bf16[8,64,2048]{2,1,0:T(8,128)(2,1)} %join.4.refs_1_.refs_0_, bf16[8,64,2048]{2,1,0:T(8,128)(2,1)} %collective-permute-done.32.refs_2_.refs_1_, bf16[8,64,2048]{2,1,0:T(8,128)(2,1)} %join.5.refs_1_.refs_2_, bf16[8,64,2048]{2,1,0:T(8,128)(2,1)} %collective-permute-done.35.refs_2_.refs_3_, ...), custom_call_target="tpu_custom_call" | custom-call | flops 8589934592 | bytes 25165824 | tf_op jit(solution)/shard_map/row_grads/pallas_call | solution.py:550
  570.6 4.0 collective-permute-start.78
  583.2 4.0 collective-permute-done.78
  595.6 15.8 %row_grads.3 = f32[2,2048,256]{2,1,0:T(8,128)} custom-call(bf16[8,64,2048]{2,1,0:T(8,128)(2,1)} %join.4.refs_1_.refs_0_, bf16[8,64,2048]{2,1,0:T(8,128)(2,1)} %collective-permute-done.32.refs_2_.refs_1_, bf16[8,64,2048]{2,1,0:T(8,128)(2,1)} %join.5.refs_1_.refs_2_, bf16[8,64,2048]{2,1,0:T(8,128)(2,1)} %collective-permute-done.35.refs_2_.refs_3_, ...), custom_call_target="tpu_custom_call" | custom-call | flops 8589934592 | bytes 25165824 | tf_op jit(solution)/shard_map/row_grads/pallas_call | solution.py:550
  617.4 3.8 finish.1
  659.2 3.1 collective-permute-done.98
  662.7 4.1 collective-permute-done.99
  666.7 4.0 collective-permute-done.100
  671.3 3.7 collective-permute-start.108
  675.0 18.3 %collective-permute-done.96 = bf16[2,64,2048]{2,1,0:T(8,128)(2,1)S(1)} collective-permute-done((bf16[2,64,2048]{2,1,0:T(8,128)(2,1)S(1)}, bf16[2,64,2048]{2,1,0:T(8,128)(2,1)S(1)}, u32[]{:S(2)}, u32[]{:S(2)}) %collective-permute-start.96) | collective-permute-done | bytes 524320 | tf_op jit(solution)/shard_map/ppermute | solution.py:57
  693.4 5.3 collective-permute-start.97
  699.7 4.8 collective-permute-done.101
  706.5 9.2 %collective-permute-done.108 = bf16[4,64,512]{2,1,0:T(8,128)(2,1)S(1)} collective-permute-done((bf16[4,64,512]{2,1,0:T(8,128)(2,1)}, bf16[4,64,512]{2,1,0:T(8,128)(2,1)S(1)}, u32[]{:S(2)}, u32[]{:S(2)}) %collective-permute-start.108) | collective-permute-done | bytes 262176 | tf_op jit(solution)/shard_map/ppermute | solution.py:57
  716.1 11.5 %collective-permute-done.97 = bf16[2,64,2048]{2,1,0:T(8,128)(2,1)S(1)} collective-permute-done((bf16[2,64,2048]{2,1,0:T(8,128)(2,1)S(1)}, bf16[2,64,2048]{2,1,0:T(8,128)(2,1)S(1)}, u32[]{:S(2)}, u32[]{:S(2)}) %collective-permute-start.97) | collective-permute-done | bytes 524320 | tf_op jit(solution)/shard_map/ppermute | solution.py:57
  727.6 4.2 collective-permute-done.102
  735.4 3.5 collective-permute-done.104
  740.6 3.6 collective-permute-done.105
  (566 shorter events, 287.0 us)
Async XLA Ops:
  7.2 160.3 %all-gather.4.cloned.1.call-start = ((), (), s32[]{:S(2)}) async-start(), calls=%async_computation.1 | async-start | bytes 18382848 | tf_op jit(solution)/shard_map/all_gather | solution.py:909
  10.4 615.9 %reduce-scatter.2.cloned.1.call-start = ((), (), s32[]{:S(2)}) async-start(), calls=%async_computation.2 | async-start | bytes 4718592 | tf_op jit(solution)/shard_map/reduce_scatter | solution.py:1153
  27.9 54.0 %collective-permute-start.7 = (bf16[384,1536]{1,0:T(8,128)(2,1)}, bf16[384,1536]{1,0:T(8,128)(2,1)S(1)}, u32[]{:S(2)}, u32[]{:S(2)}) collective-permute-start(bf16[384,1536]{1,0:T(8,128)(2,1)} %get-tuple-element.200), channel_id=1, source_target_pairs={{0,8},{8,0},{16,24},{24,16},{1,9},{9,1},{17,25},{25,17},{2,10},{10... | collective-permute-start | bytes 3538952 | tf_op jit(solution)/shard_map/ppermute | solution.py:31
  28.3 53.7 %collective-permute-start.8 = (bf16[384,1536]{1,0:T(8,128)(2,1)}, bf16[384,1536]{1,0:T(8,128)(2,1)S(1)}, u32[]{:S(2)}, u32[]{:S(2)}) collective-permute-start(bf16[384,1536]{1,0:T(8,128)(2,1)} %get-tuple-element.201), channel_id=1, source_target_pairs={{0,16},{8,24},{16,0},{24,8},{1,17},{9,25},{17,1},{25,9},{2,18},{10... | collective-permute-start | bytes 3538952 | tf_op jit(solution)/shard_map/ppermute | solution.py:31
  28.4 53.6 %collective-permute-start.3 = (bf16[2,1,64,2048]{3,2,0,1:T(8,128)(2,1)S(1)}, bf16[2,1,64,2048]{3,2,0,1:T(8,128)(2,1)}, u32[]{:S(2)}, u32[]{:S(2)}) collective-permute-start(bf16[2,1,64,2048]{3,2,0,1:T(8,128)(2,1)S(1)} %get-tuple-element.464), channel_id=1, source_target_pairs={{0,8},{8,0},{16,24},{24,16},{1,9},{9,1},{17,25},{25,17},{2,10},{10... | collective-permute-start | bytes 1572872 | tf_op jit(solution)/shard_map/ppermute | solution.py:31
  30.4 51.6 %collective-permute-start.1 = (bf16[2,1,64,2048]{3,2,0,1:T(8,128)(2,1)S(1)}, bf16[2,1,64,2048]{3,2,0,1:T(8,128)(2,1)}, u32[]{:S(2)}, u32[]{:S(2)}) collective-permute-start(bf16[2,1,64,2048]{3,2,0,1:T(8,128)(2,1)S(1)} %get-tuple-element.470), channel_id=1, source_target_pairs={{0,16},{8,24},{16,0},{24,8},{1,17},{9,25},{17,1},{25,9},{2,18},{10... | collective-permute-start | bytes 1572872 | tf_op jit(solution)/shard_map/ppermute | solution.py:31
  157.9 25.7 %collective-permute-start.23 = (bf16[2,64,2048]{2,1,0:T(8,128)(2,1)}, bf16[2,64,2048]{2,1,0:T(8,128)(2,1)S(1)}, u32[]{:S(2)}, u32[]{:S(2)}) collective-permute-start(bf16[2,64,2048]{2,1,0:T(8,128)(2,1)} %get-tuple-element.214.refs_9_), channel_id=1, source_target_pairs={{0,2},{1,3},{2,4},{3,5},{4,6},{5,7},{6,0},{7,1},{8,10},{9,11},{10,... | collective-permute-start | bytes 1572872 | tf_op jit(solution)/shard_map/ppermute | solution.py:57
  163.5 23.7 %collective-permute-start.30 = (bf16[2,1,64,2048]{3,2,1,0:T(8,128)(2,1)S(1)}, bf16[2,1,64,2048]{3,2,1,0:T(8,128)(2,1)S(1)}, u32[]{:S(2)}, u32[]{:S(2)}) collective-permute-start(bf16[2,1,64,2048]{3,2,1,0:T(8,128)(2,1)S(1)} %pad_maximum_fusion.12.a_ref), channel_id=1, source_target_pairs={{0,16},{8,24},{16,0},{24,8},{1,17},{9,25},{17,1},{25,9},{2,18},{10... | collective-permute-start | bytes 1572872 | tf_op jit(solution)/shard_map/ppermute | solution.py:31
  166.6 20.6 %collective-permute-start.31 = (bf16[2,1,64,2048]{3,2,1,0:T(8,128)(2,1)S(1)}, bf16[2,1,64,2048]{3,2,1,0:T(8,128)(2,1)}, u32[]{:S(2)}, u32[]{:S(2)}) collective-permute-start(bf16[2,1,64,2048]{3,2,1,0:T(8,128)(2,1)S(1)} %pad_maximum_fusion.13.c_ref), channel_id=1, source_target_pairs={{0,8},{8,0},{16,24},{24,16},{1,9},{9,1},{17,25},{25,17},{2,10},{10... | collective-permute-start | bytes 1572872 | tf_op jit(solution)/shard_map/ppermute | solution.py:31
  190.6 39.1 %collective-permute-start.32 = (bf16[8,64,2048]{2,1,0:T(8,128)(2,1)}, bf16[8,64,2048]{2,1,0:T(8,128)(2,1)}, u32[]{:S(2)}, u32[]{:S(2)}) collective-permute-start(bf16[8,64,2048]{2,1,0:T(8,128)(2,1)} %join.4.refs_1_.refs_0_), channel_id=1, source_target_pairs={{0,1},{1,0},{2,3},{3,2},{4,5},{5,4},{6,7},{7,6},{8,9},{9,8},{10,11... | collective-permute-start | bytes 6291464 | tf_op jit(solution)/shard_map/ppermute | solution.py:48
  215.0 48.8 %collective-permute-start.35 = (bf16[8,64,2048]{2,1,0:T(8,128)(2,1)}, bf16[8,64,2048]{2,1,0:T(8,128)(2,1)}, u32[]{:S(2)}, u32[]{:S(2)}) collective-permute-start(bf16[8,64,2048]{2,1,0:T(8,128)(2,1)} %join.5.refs_1_.refs_2_), channel_id=1, source_target_pairs={{0,1},{1,0},{2,3},{3,2},{4,5},{5,4},{6,7},{7,6},{8,9},{9,8},{10,11... | collective-permute-start | bytes 6291464 | tf_op jit(solution)/shard_map/ppermute | solution.py:48
  228.1 27.6 %collective-permute-start.37 = (bf16[2,2,64,2048]{3,2,1,0:T(8,128)(2,1)}, bf16[2,2,64,2048]{3,2,1,0:T(8,128)(2,1)}, u32[]{:S(2)}, u32[]{:S(2)}) collective-permute-start(bf16[2,2,64,2048]{3,2,1,0:T(8,128)(2,1)} %pad_maximum_fusion.6.a_ref), channel_id=1, source_target_pairs={{0,16},{8,24},{16,0},{24,8},{1,17},{9,25},{17,1},{25,9},{2,18},{10... | collective-permute-start | bytes 3145736 | tf_op jit(solution)/shard_map/ppermute | solution.py:31
  228.4 27.3 %collective-permute-start.38 = (bf16[2,2,64,2048]{3,2,1,0:T(8,128)(2,1)}, bf16[2,2,64,2048]{3,2,1,0:T(8,128)(2,1)}, u32[]{:S(2)}, u32[]{:S(2)}) collective-permute-start(bf16[2,2,64,2048]{3,2,1,0:T(8,128)(2,1)} %pad_maximum_fusion.7.c_ref), channel_id=1, source_target_pairs={{0,8},{8,0},{16,24},{24,16},{1,9},{9,1},{17,25},{25,17},{2,10},{10... | collective-permute-start | bytes 3145736 | tf_op jit(solution)/shard_map/ppermute | solution.py:31
  255.7 29.8 %collective-permute-start.36 = (bf16[4,2,1,64,2176]{4,3,1,2,0:T(8,128)(2,1)}, bf16[4,2,1,64,2176]{4,3,1,2,0:T(8,128)(2,1)}, u32[]{:S(2)}, u32[]{:S(2)}) collective-permute-start(bf16[4,2,1,64,2176]{4,3,1,2,0:T(8,128)(2,1)} %bitcast.524), channel_id=1, source_target_pairs={{0,1},{1,0},{2,3},{3,2},{4,5},{5,4},{6,7},{7,6},{8,9},{9,8},{10,11... | collective-permute-start | bytes 6684680 | tf_op jit(solution)/shard_map/ppermute | solution.py:48
  258.3 26.7 %collective-permute-start.39 = (bf16[8,64,2048]{2,1,0:T(8,128)(2,1)}, bf16[8,64,2048]{2,1,0:T(8,128)(2,1)}, u32[]{:S(2)}, u32[]{:S(2)}) collective-permute-start(bf16[8,64,2048]{2,1,0:T(8,128)(2,1)} %join.6.refs_1_.refs_4_), channel_id=1, source_target_pairs={{0,1},{1,0},{2,3},{3,2},{4,5},{5,4},{6,7},{7,6},{8,9},{9,8},{10,11... | collective-permute-start | bytes 6291464 | tf_op jit(solution)/shard_map/ppermute | solution.py:48
  263.8 43.9 %collective-permute-start.41 = (bf16[8,64,2048]{2,1,0:T(8,128)(2,1)}, bf16[8,64,2048]{2,1,0:T(8,128)(2,1)S(1)}, u32[]{:S(2)}, u32[]{:S(2)}) collective-permute-start(bf16[8,64,2048]{2,1,0:T(8,128)(2,1)} %join.7.refs_1_.refs_6_), channel_id=1, source_target_pairs={{0,1},{1,0},{2,3},{3,2},{4,5},{5,4},{6,7},{7,6},{8,9},{9,8},{10,11... | collective-permute-start | bytes 6291464 | tf_op jit(solution)/shard_map/ppermute | solution.py:48
  285.0 24.6 %collective-permute-start.40 = (bf16[4,2,1,64,2176]{4,3,1,2,0:T(8,128)(2,1)}, bf16[4,2,1,64,2176]{4,3,1,2,0:T(8,128)(2,1)S(1)}, u32[]{:S(2)}, u32[]{:S(2)}) collective-permute-start(bf16[4,2,1,64,2176]{4,3,1,2,0:T(8,128)(2,1)} %bitcast.527), channel_id=1, source_target_pairs={{0,1},{1,0},{2,3},{3,2},{4,5},{5,4},{6,7},{7,6},{8,9},{9,8},{10,11... | collective-permute-start | bytes 6684680 | tf_op jit(solution)/shard_map/ppermute | solution.py:48
  307.7 24.1 %collective-permute-start.47 = (bf16[4,2,1,64,2176]{4,3,1,2,0:T(8,128)(2,1)}, bf16[4,2,1,64,2176]{4,3,1,2,0:T(8,128)(2,1)}, u32[]{:S(2)}, u32[]{:S(2)}) collective-permute-start(bf16[4,2,1,64,2176]{4,3,1,2,0:T(8,128)(2,1)} %bitcast.526), channel_id=1, source_target_pairs={{0,1},{1,0},{2,3},{3,2},{4,5},{5,4},{6,7},{7,6},{8,9},{9,8},{10,11... | collective-permute-start | bytes 6684680 | tf_op jit(solution)/shard_map/ppermute | solution.py:48
  311.2 28.6 %collective-permute-start.43 = (bf16[2,1,64,2176]{3,2,1,0:T(8,128)(2,1)}, bf16[2,1,64,2176]{3,2,1,0:T(8,128)(2,1)}, u32[]{:S(2)}, u32[]{:S(2)}) collective-permute-start(bf16[2,1,64,2176]{3,2,1,0:T(8,128)(2,1)} %bitcast.82), channel_id=1, source_target_pairs={{0,8},{8,0},{16,24},{24,16},{1,9},{9,1},{17,25},{25,17},{2,10},{10... | collective-permute-start | bytes 1671176 | tf_op jit(solution)/shard_map/ppermute | solution.py:31
  313.3 26.5 %collective-permute-start.42 = (bf16[2,1,64,2176]{3,2,0,1:T(8,128)(2,1)}, bf16[2,1,64,2176]{3,2,0,1:T(8,128)(2,1)}, u32[]{:S(2)}, u32[]{:S(2)}) collective-permute-start(bf16[2,1,64,2176]{3,2,0,1:T(8,128)(2,1)} %get-tuple-element.240), channel_id=1, source_target_pairs={{0,16},{8,24},{16,0},{24,8},{1,17},{9,25},{17,1},{25,9},{2,18},{10... | collective-permute-start | bytes 1671176 | tf_op jit(solution)/shard_map/ppermute | solution.py:31
  331.7 27.0 %collective-permute-start.50 = (bf16[4,2,1,64,2176]{4,3,1,2,0:T(8,128)(2,1)}, bf16[4,2,1,64,2176]{4,3,1,2,0:T(8,128)(2,1)S(1)}, u32[]{:S(2)}, u32[]{:S(2)}) collective-permute-start(bf16[4,2,1,64,2176]{4,3,1,2,0:T(8,128)(2,1)} %bitcast.525), channel_id=1, source_target_pairs={{0,1},{1,0},{2,3},{3,2},{4,5},{5,4},{6,7},{7,6},{8,9},{9,8},{10,11... | collective-permute-start | bytes 6684680 | tf_op jit(solution)/shard_map/ppermute | solution.py:48
  335.7 41.3 %collective-permute-start.49 = (bf16[2,1,64,2176]{3,2,1,0:T(8,128)(2,1)S(1)}, bf16[2,1,64,2176]{3,2,1,0:T(8,128)(2,1)S(1)}, u32[]{:S(2)}, u32[]{:S(2)}) collective-permute-start(bf16[2,1,64,2176]{3,2,1,0:T(8,128)(2,1)S(1)} %bitcast.494), channel_id=1, source_target_pairs={{0,8},{8,0},{16,24},{24,16},{1,9},{9,1},{17,25},{25,17},{2,10},{10... | collective-permute-start | bytes 1671176 | tf_op jit(solution)/shard_map/ppermute | solution.py:31
  335.9 41.1 %collective-permute-start.48 = (bf16[2,1,64,2176]{3,2,0,1:T(8,128)(2,1)S(1)}, bf16[2,1,64,2176]{3,2,0,1:T(8,128)(2,1)S(1)}, u32[]{:S(2)}, u32[]{:S(2)}) collective-permute-start(bf16[2,1,64,2176]{3,2,0,1:T(8,128)(2,1)S(1)} %get-tuple-element.252), channel_id=1, source_target_pairs={{0,16},{8,24},{16,0},{24,8},{1,17},{9,25},{17,1},{25,9},{2,18},{10... | collective-permute-start | bytes 1671176 | tf_op jit(solution)/shard_map/ppermute | solution.py:31
  359.3 50.4 %collective-permute-start.55 = (bf16[2,1,64,2176]{3,2,1,0:T(8,128)(2,1)S(1)}, bf16[2,1,64,2176]{3,2,1,0:T(8,128)(2,1)}, u32[]{:S(2)}, u32[]{:S(2)}) collective-permute-start(bf16[2,1,64,2176]{3,2,1,0:T(8,128)(2,1)S(1)} %bitcast.495), channel_id=1, source_target_pairs={{0,8},{8,0},{16,24},{24,16},{1,9},{9,1},{17,25},{25,17},{2,10},{10... | collective-permute-start | bytes 1671176 | tf_op jit(solution)/shard_map/ppermute | solution.py:31
  361.1 48.8 %collective-permute-start.54 = (bf16[2,1,64,2176]{3,2,0,1:T(8,128)(2,1)S(1)}, bf16[2,1,64,2176]{3,2,0,1:T(8,128)(2,1)}, u32[]{:S(2)}, u32[]{:S(2)}) collective-permute-start(bf16[2,1,64,2176]{3,2,0,1:T(8,128)(2,1)S(1)} %get-tuple-element.263), channel_id=1, source_target_pairs={{0,16},{8,24},{16,0},{24,8},{1,17},{9,25},{17,1},{25,9},{2,18},{10... | collective-permute-start | bytes 1671176 | tf_op jit(solution)/shard_map/ppermute | solution.py:31
  374.2 39.5 %collective-permute-start.59 = (bf16[2,1,64,2176]{3,2,0,1:T(8,128)(2,1)}, bf16[2,1,64,2176]{3,2,0,1:T(8,128)(2,1)}, u32[]{:S(2)}, u32[]{:S(2)}) collective-permute-start(bf16[2,1,64,2176]{3,2,0,1:T(8,128)(2,1)} %get-tuple-element.273), channel_id=1, source_target_pairs={{0,16},{8,24},{16,0},{24,8},{1,17},{9,25},{17,1},{25,9},{2,18},{10... | collective-permute-start | bytes 1671176 | tf_op jit(solution)/shard_map/ppermute | solution.py:31
  377.0 37.1 %collective-permute-start.60 = (bf16[2,1,64,2176]{3,2,1,0:T(8,128)(2,1)}, bf16[2,1,64,2176]{3,2,1,0:T(8,128)(2,1)}, u32[]{:S(2)}, u32[]{:S(2)}) collective-permute-start(bf16[2,1,64,2176]{3,2,1,0:T(8,128)(2,1)} %fusion.12), channel_id=1, source_target_pairs={{0,8},{8,0},{16,24},{24,16},{1,9},{9,1},{17,25},{25,17},{2,10},{10... | collective-permute-start | bytes 1671176 | tf_op jit(solution)/shard_map/ppermute | solution.py:31
  408.5 59.6 %collective-permute-start.65 = (bf16[4,2,4,64,2048]{4,3,2,1,0:T(8,128)(2,1)}, bf16[4,2,4,64,2048]{4,3,2,1,0:T(8,128)(2,1)}, u32[]{:S(2)}, u32[]{:S(2)}) collective-permute-start(bf16[4,2,4,64,2048]{4,3,2,1,0:T(8,128)(2,1)} %mix.2), channel_id=1, source_target_pairs={{0,1},{1,0},{2,3},{3,2},{4,5},{5,4},{6,7},{7,6},{8,9},{9,8},{10,11... | collective-permute-start | bytes 25165832 | tf_op jit(solution)/shard_map/ppermute | solution.py:48
  508.2 67.9 %collective-permute-start.71 = (bf16[2,4,64,2048]{3,2,1,0:T(8,128)(2,1)}, bf16[2,4,64,2048]{3,2,1,0:T(8,128)(2,1)}, u32[]{:S(2)}, u32[]{:S(2)}) collective-permute-start(bf16[2,4,64,2048]{3,2,1,0:T(8,128)(2,1)} %get-tuple-element.302), channel_id=1, source_target_pairs={{0,16},{8,24},{16,0},{24,8},{1,17},{9,25},{17,1},{25,9},{2,18},{10... | collective-permute-start | bytes 6291464 | tf_op jit(solution)/shard_map/ppermute | solution.py:31
  508.6 70.9 %collective-permute-start.73 = (bf16[2,4,64,2048]{3,2,1,0:T(8,128)(2,1)}, bf16[2,4,64,2048]{3,2,1,0:T(8,128)(2,1)}, u32[]{:S(2)}, u32[]{:S(2)}) collective-permute-start(bf16[2,4,64,2048]{3,2,1,0:T(8,128)(2,1)} %get-tuple-element.304), channel_id=1, source_target_pairs={{0,8},{8,0},{16,24},{24,16},{1,9},{9,1},{17,25},{25,17},{2,10},{10... | collective-permute-start | bytes 6291464 | tf_op jit(solution)/shard_map/ppermute | solution.py:31
  514.7 38.1 %collective-permute-start.76 = (bf16[4,256,512]{2,1,0:T(8,128)(2,1)}, bf16[4,256,512]{2,1,0:T(8,128)(2,1)S(1)}, u32[]{:S(2)}, u32[]{:S(2)}) collective-permute-start(bf16[4,256,512]{2,1,0:T(8,128)(2,1)} %get-tuple-element.312), channel_id=1, source_target_pairs={{0,1},{1,0},{2,3},{3,2},{4,5},{5,4},{6,7},{7,6},{8,9},{9,8},{10,11... | collective-permute-start | bytes 3145736 | tf_op jit(solution)/shard_map/ppermute | solution.py:48
  516.4 34.1 %collective-permute-start.79 = (bf16[4,64,512]{2,1,0:T(8,128)(2,1)}, bf16[4,64,512]{2,1,0:T(8,128)(2,1)S(1)}, u32[]{:S(2)}, u32[]{:S(2)}) collective-permute-start(bf16[4,64,512]{2,1,0:T(8,128)(2,1)} %fusion.37), channel_id=1, source_target_pairs={{0,2},{1,3},{2,4},{3,5},{4,6},{5,7},{6,0},{7,1},{8,10},{9,11},{10,... | collective-permute-start | bytes 786440 | tf_op jit(solution)/shard_map/ppermute | solution.py:57
  529.7 221.8 %all-gather.6.cloned.1.call-start = ((), (), s32[]{:S(2)}) async-start(), calls=%async_computation.3 | async-start | bytes 4718592 | tf_op jit(solution)/shard_map/all_gather | solution.py:1208
  529.7 58.2 %collective-permute-start.83 = (bf16[2,1,64,2048]{3,2,1,0:T(8,128)(2,1)}, bf16[2,1,64,2048]{3,2,1,0:T(8,128)(2,1)}, u32[]{:S(2)}, u32[]{:S(2)}) collective-permute-start(bf16[2,1,64,2048]{3,2,1,0:T(8,128)(2,1)} %bitcast.530), channel_id=1, source_target_pairs={{0,8},{8,0},{16,24},{24,16},{1,9},{9,1},{17,25},{25,17},{2,10},{10... | collective-permute-start | bytes 1572872 | tf_op jit(solution)/shard_map/ppermute | solution.py:31
  550.5 37.5 %collective-permute-start.82 = (bf16[2,1,64,2048]{3,2,1,0:T(8,128)(2,1)}, bf16[2,1,64,2048]{3,2,1,0:T(8,128)(2,1)}, u32[]{:S(2)}, u32[]{:S(2)}) collective-permute-start(bf16[2,1,64,2048]{3,2,1,0:T(8,128)(2,1)} %bitcast.529), channel_id=1, source_target_pairs={{0,16},{8,24},{16,0},{24,8},{1,17},{9,25},{17,1},{25,9},{2,18},{10... | collective-permute-start | bytes 1572872 | tf_op jit(solution)/shard_map/ppermute | solution.py:31
  578.7 42.5 %collective-permute-start.72 = (bf16[4,64,2048]{2,1,0:T(8,128)(2,1)}, bf16[4,64,2048]{2,1,0:T(8,128)(2,1)}, u32[]{:S(2)}, u32[]{:S(2)}) collective-permute-start(bf16[4,64,2048]{2,1,0:T(8,128)(2,1)} %fusion.16), channel_id=1, source_target_pairs={{0,8},{8,0},{16,24},{24,16},{1,9},{9,1},{17,25},{25,17},{2,10},{10... | collective-permute-start | bytes 3145736 | tf_op jit(solution)/shard_map/ppermute | solution.py:31
  582.1 40.3 %collective-permute-start.74 = (bf16[4,64,2048]{2,1,0:T(8,128)(2,1)}, bf16[4,64,2048]{2,1,0:T(8,128)(2,1)}, u32[]{:S(2)}, u32[]{:S(2)}) collective-permute-start(bf16[4,64,2048]{2,1,0:T(8,128)(2,1)} %fusion.17), channel_id=1, source_target_pairs={{0,16},{8,24},{16,0},{24,8},{1,17},{9,25},{17,1},{25,9},{2,18},{10... | collective-permute-start | bytes 3145736 | tf_op jit(solution)/shard_map/ppermute | solution.py:31
  589.7 27.2 %collective-permute-start.86 = (bf16[1,64,2048]{2,1,0:T(8,128)(2,1)}, bf16[1,64,2048]{2,1,0:T(8,128)(2,1)}, u32[]{:S(2)}, u32[]{:S(2)}) collective-permute-start(bf16[1,64,2048]{2,1,0:T(8,128)(2,1)} %fusion.29), channel_id=1, source_target_pairs={{0,8},{8,0},{16,24},{24,16},{1,9},{9,1},{17,25},{25,17},{2,10},{10... | collective-permute-start | bytes 786440 | tf_op jit(solution)/shard_map/ppermute | solution.py:31
  591.9 25.5 %collective-permute-start.87 = (bf16[1,64,2048]{2,1,0:T(8,128)(2,1)}, bf16[1,64,2048]{2,1,0:T(8,128)(2,1)}, u32[]{:S(2)}, u32[]{:S(2)}) collective-permute-start(bf16[1,64,2048]{2,1,0:T(8,128)(2,1)} %fusion.28), channel_id=1, source_target_pairs={{0,16},{8,24},{16,0},{24,8},{1,17},{9,25},{17,1},{25,9},{2,18},{10... | collective-permute-start | bytes 786440 | tf_op jit(solution)/shard_map/ppermute | solution.py:31
  593.2 21.5 %collective-permute-start.80 = (bf16[4,64,512]{2,1,0:T(8,128)(2,1)}, bf16[4,64,512]{2,1,0:T(8,128)(2,1)}, u32[]{:S(2)}, u32[]{:S(2)}) collective-permute-start(bf16[4,64,512]{2,1,0:T(8,128)(2,1)} %fusion.35), channel_id=1, source_target_pairs={{0,2},{1,3},{2,4},{3,5},{4,6},{5,7},{6,0},{7,1},{8,10},{9,11},{10,... | collective-permute-start | bytes 786440 | tf_op jit(solution)/shard_map/ppermute | solution.py:57
  614.7 56.6 %collective-permute-start.107 = (bf16[4,64,512]{2,1,0:T(8,128)(2,1)S(1)}, bf16[4,64,512]{2,1,0:T(8,128)(2,1)}, u32[]{:S(2)}, u32[]{:S(2)}) collective-permute-start(bf16[4,64,512]{2,1,0:T(8,128)(2,1)S(1)} %get-tuple-element.379), channel_id=1, source_target_pairs={{0,2},{1,3},{2,4},{3,5},{4,6},{5,7},{6,0},{7,1},{8,10},{9,11},{10,... | collective-permute-start | bytes 786440 | tf_op jit(solution)/shard_map/ppermute | solution.py:57
  616.9 25.3 %collective-permute-start.85 = (bf16[4,64,512]{2,1,0:T(8,128)(2,1)}, bf16[4,64,512]{2,1,0:T(8,128)(2,1)}, u32[]{:S(2)}, u32[]{:S(2)}) collective-permute-start(bf16[4,64,512]{2,1,0:T(8,128)(2,1)} %fusion.33), channel_id=1, source_target_pairs={{0,2},{1,3},{2,4},{3,5},{4,6},{5,7},{6,0},{7,1},{8,10},{9,11},{10,... | collective-permute-start | bytes 786440 | tf_op jit(solution)/shard_map/ppermute | solution.py:57
  624.5 33.4 %collective-permute-start.84 = (bf16[2,64,2048]{2,1,0:T(8,128)(2,1)}, bf16[2,64,2048]{2,1,0:T(8,128)(2,1)}, u32[]{:S(2)}, u32[]{:S(2)}) collective-permute-start(bf16[2,64,2048]{2,1,0:T(8,128)(2,1)} %pad_maximum_fusion.8), channel_id=1, source_target_pairs={{0,2},{1,3},{2,4},{3,5},{4,6},{5,7},{6,0},{7,1},{8,10},{9,11},{10,... | collective-permute-start | bytes 1572872 | tf_op jit(solution)/shard_map/ppermute | solution.py:57
  659.1 34.1 %collective-permute-start.96 = (bf16[2,64,2048]{2,1,0:T(8,128)(2,1)S(1)}, bf16[2,64,2048]{2,1,0:T(8,128)(2,1)S(1)}, u32[]{:S(2)}, u32[]{:S(2)}) collective-permute-start(bf16[2,64,2048]{2,1,0:T(8,128)(2,1)S(1)} %fusion.18), channel_id=1, source_target_pairs={{0,2},{1,3},{2,4},{3,5},{4,6},{5,7},{6,0},{7,1},{8,10},{9,11},{10,... | collective-permute-start | bytes 1572872 | tf_op jit(solution)/shard_map/ppermute | solution.py:57
  670.8 33.7 %collective-permute-start.101 = (bf16[4,64,512]{2,1,0:T(8,128)(2,1)S(1)}, bf16[4,64,512]{2,1,0:T(8,128)(2,1)S(1)}, u32[]{:S(2)}, u32[]{:S(2)}) collective-permute-start(bf16[4,64,512]{2,1,0:T(8,128)(2,1)S(1)} %collective-permute-done.100), channel_id=1, source_target_pairs={{0,2},{1,3},{2,4},{3,5},{4,6},{5,7},{6,0},{7,1},{8,10},{9,11},{10,... | collective-permute-start | bytes 786440 | tf_op jit(solution)/shard_map/ppermute | solution.py:57
  671.3 44.4 %collective-permute-start.108 = (bf16[4,64,512]{2,1,0:T(8,128)(2,1)}, bf16[4,64,512]{2,1,0:T(8,128)(2,1)S(1)}, u32[]{:S(2)}, u32[]{:S(2)}) collective-permute-start(bf16[4,64,512]{2,1,0:T(8,128)(2,1)} %collective-permute-done.107), channel_id=1, source_target_pairs={{0,2},{1,3},{2,4},{3,5},{4,6},{5,7},{6,0},{7,1},{8,10},{9,11},{10,... | collective-permute-start | bytes 786440 | tf_op jit(solution)/shard_map/ppermute | solution.py:57
  693.4 34.2 %collective-permute-start.97 = (bf16[2,64,2048]{2,1,0:T(8,128)(2,1)S(1)}, bf16[2,64,2048]{2,1,0:T(8,128)(2,1)S(1)}, u32[]{:S(2)}, u32[]{:S(2)}) collective-permute-start(bf16[2,64,2048]{2,1,0:T(8,128)(2,1)S(1)} %fusion.19), channel_id=1, source_target_pairs={{0,2},{1,3},{2,4},{3,5},{4,6},{5,7},{6,0},{7,1},{8,10},{9,11},{10,... | collective-permute-start | bytes 1572872 | tf_op jit(solution)/shard_map/ppermute | solution.py:57
  704.5 27.4 %collective-permute-start.102 = (bf16[4,64,512]{2,1,0:T(8,128)(2,1)S(1)}, bf16[4,64,512]{2,1,0:T(8,128)(2,1)S(1)}, u32[]{:S(2)}, u32[]{:S(2)}) collective-permute-start(bf16[4,64,512]{2,1,0:T(8,128)(2,1)S(1)} %collective-permute-done.101), channel_id=1, source_target_pairs={{0,2},{1,3},{2,4},{3,5},{4,6},{5,7},{6,0},{7,1},{8,10},{9,11},{10,... | collective-permute-start | bytes 786440 | tf_op jit(solution)/shard_map/ppermute | solution.py:57
  (152 other events, 1589.2 us)
Sparse Core Ops, SparseCore 0:
  11.4 139.4 all-gather.3
  529.8 62.3 reduce-scatter.1
  642.3 75.8 all-gather.5

commit v4 on v3

--- a/solution.py
+++ b/solution.py
@@ -453,12 +453,7 @@
                     (1, 1, eight, half, units), lambda i, at: (at[2], core_of(i, at), 0, 0, 0)
                 ),
             ]
-            + [
-                pl.BlockSpec(
-                    w.shape, lambda i, _, n=w.ndim: (0,) * n, pipeline_mode=pl.Buffered(1)
-                )
-                for w in (w_gate, w_up, gate_up_t, router)
-            ],
+            + [whole(w_gate.shape), whole(w_up.shape), whole(gate_up_t.shape), whole(router.shape)],
             out_specs=[whole(own_shape) for _ in range(4)]
             + [
                 whole((4,) + own_shape),
@@ -479,7 +474,7 @@
             out((2, eight, half, units), BF16),
             out((2, count, units), BF16),
         ],
-        compiler_params=pltpu.CompilerParams(vmem_limit_bytes=38 << 20),
+        compiler_params=pltpu.CompilerParams(vmem_limit_bytes=48 << 20),
         cost_estimate=pl.CostEstimate(
             flops=8 * count * gate_up_t.size,
             bytes_accessed=8 * count * width + 4 * gate_up_t.size + 20 * count * units,
@@ -1011,7 +1006,7 @@
     for j in list(range(1, chips)) + [0]:
         totals = totals_all[j]
         if j == 0:
-            totals = after(totals, totals_all[-1], arrived[0])
+            totals = after(totals, totals_all[-1], back_pieces[min(1, chips - 2)])
         back_terms[j] = [
             [t[0] for t in terms]
             for terms in reduce_xy(
@@ -1194,12 +1189,13 @@
     out_spread = [output_total]
     while len(value_pieces) > 1:
         total = ring_add(total, value_pieces, expert_grads[2])
+    out_spread.append(after(ring_up(out_spread[-1]), total))
     terms_a, terms_b = reduce_last(first_kept, first_on)
     grad_input, grad_gain_one = call(
         finish_kernel,
         "finish",
         [t.reshape(half, width) for t in terms_a + terms_b]
-        + [own_input, grad_res, after(gain_one, total)],
+        + [own_input, grad_res, after(gain_one, out_spread[-1])],
         [out((2, half, width), F32), out((8, width), F32)],
         tok_count * width,
     )

time: 773 us -> 750 us (0.970)
  waiting for transfers between devices: 250 us -> 230 us
  local copies, waits for them, and re-layouts: 67.4 us -> 55.8 us
  Pallas kernels: 242 us -> 251 us
    ppermute x21, waiting for transfers between devices: 106 us -> 87.4 us  [ring_up(): lax.ppermute(values, 'expert', [(i, (i + 2) % count) for i in range(count)])]
    pallas_call x4, Pallas kernels: 67.7 us -> 77.2 us  [expert_call(): pl.pallas_call(lambda *refs: expert_kernel(experts_all, *refs), grid_spec...]
    unnamed x173 -> x133, local copies, waits for them, and re-layouts: 20 us -> 10.7 us
  transfers between devices with their start and end apart: 114 -> 114, of which waited for: 44 -> 44; matrix products, arithmetic and copies ran while one was open for 16% -> 16% of each run, Pallas kernels for 31% -> 33%
where the time goes in v4:
time: 750 us; the launch traced here: 744 us
  Pallas kernels  251 us (33%)
  waiting for transfers between devices  230 us (31%)
  starting transfers between devices  106 us (14%)
  other arithmetic  86.1 us (11%)
  local copies, waits for them, and re-layouts  55.8 us (7%)
  between operations  15.6 us (2%)
    ppermute x71, waiting for transfers between devices, flip_shard(): return lax.ppermute(values, 'shard', [(i, i ^ bit) for i in range(count)])  134 us
    ppermute x21, waiting for transfers between devices, ring_up(): lax.ppermute(values, 'expert', [(i, (i + 2) % count) for i in range(count)])  87.4 us
    pallas_call x4, Pallas kernels, expert_call(): pl.pallas_call(lambda *refs: expert_kernel(experts_all, *refs), grid_spec...  77.2 us
    ppermute x71, starting transfers between devices, flip_shard(): return lax.ppermute(values, 'shard', [(i, i ^ bit) for i in range(count)])  70.2 us
    pallas_call x9, Pallas kernels, call(): pl.pallas_call(kernel, in_specs=[scalars() if n in smem else whole(a.shap...  68.5 us
    ppermute x21, starting transfers between devices, ring_up(): lax.ppermute(values, 'expert', [(i, (i + 2) % count) for i in range(count)])  33.9 us
    pallas_call x2, Pallas kernels, row_grad_call(): pl.pallas_call(lambda *refs: row_grad_kernel(len(rows), *refs), grid=(wid...  31.7 us
    pallas_call x2, Pallas kernels, mix_call(): pl.pallas_call(mix_kernel, grid=(chips,), in_specs=[pl.BlockSpec((1, coun...  19 us
  transfers between devices with their start and end apart: 114, of which 44 were waited for; matrix products, arithmetic and copies ran while one was open for 16% of the time, Pallas kernels for 33%

profile of v4, /device:TPU:0, one launch (start us, length us, event | category | flops | bytes accessed | tf_op | source)
XLA Modules:
  0.0 744.2 jit_solution(11468681710589700605)
XLA Ops:
  10.6 3.0 collective-permute-start
  17.1 2.9 collective-permute-start.6
  20.5 5.0 cut.1
  32.1 6.5 flip.1
  40.0 42.0 %collective-permute-done.3 = bf16[2,1,64,2048]{3,2,0,1:T(8,128)(2,1)} collective-permute-done((bf16[2,1,64,2048]{3,2,0,1:T(8,128)(2,1)S(1)}, bf16[2,1,64,2048]{3,2,0,1:T(8,128)(2,1)}, u32[]{:S(2)}, u32[]{:S(2)}) %collective-permute-start.3) | collective-permute-done | bytes 524320 | tf_op jit(solution)/shard_map/ppermute | solution.py:31
  89.1 3.6 collective-permute-done.9
  101.2 9.7 %project.1 = (bf16[512,2048]{1,0:T(8,128)(2,1)}, f32[512,1536]{1,0:T(8,128)}, f32[4,8,128]{2,1,0:T(8,128)}, f32[512,128]{1,0:T(8,128)}) custom-call(s32[8]{0:T(128)} %stack.264.at_ref, bf16[2,64,2048]{2,1,0:T(8,128)(2,1)} %get-tuple-element.471.r0, bf16[2,64,2048]{2,1,0:T(8,128)(2,1)} %bitcast.13.r1, bf16[2,64,2048]{2,1,0:T(8,128)(2,1)} %get-tuple-element.465.r2, ...), custom_call_target="tpu_custom_call" | custom-call | flops 3221225472 | bytes 13918240 | tf_op jit(solution)/shard_map/project/pallas_call | solution.py:156
  118.2 9.9 %attend.1 = (bf16[512,512]{1,0:T(8,128)(2,1)}, bf16[512,512]{1,0:T(8,128)(2,1)}, bf16[512,512]{1,0:T(8,128)(2,1)}, f32[512,128]{1,0:T(8,128)}, f32[512,128]{1,0:...) custom-call(f32[512,1536]{1,0:T(8,128)} %get-tuple-element.322.refs_, ...), custom_call_target="tpu_custom_call" | custom-call | flops 1610612736 | bytes 11603968 | tf_op jit(solution)/shard_map/attend/pallas_call | solution.py:156
  132.9 8.3 %collective-permute-done.18 = bf16[2,1,64,2048]{3,2,1,0:T(8,128)(2,1)S(1)} collective-permute-done((bf16[2,1,64,2048]{3,2,1,0:T(8,128)(2,1)}, bf16[2,1,64,2048]{3,2,1,0:T(8,128)(2,1)S(1)}, u32[]{:S(2)}, u32[]{:S(2)}) %collective-permute-start.18) | collective-permute-done | bytes 524320 | tf_op jit(solution)/shard_map/ppermute | solution.py:31
  152.2 3.0 settle.1
  159.5 3.9 collective-permute-done.21
  163.6 3.0 collective-permute-done.22
  167.4 16.1 %lead.1.refs_4_ = f32[4,2,8,64,512]{4,3,2,1,0:T(8,128)} custom-call(bf16[4,4,2,2,64,2176]{5,4,3,2,1,0:T(8,128)(2,1)} %bitcast.456, bf16[2048,512]{1,0:T(8,128)(2,1)} %get-tuple-element.216.down_t_ref), custom_call_target="tpu_custom_call" | custom-call | flops 8589934592 | bytes 26214400 | tf_op jit(solution)/shard_map/lead/pallas_call | solution.py:307
  197.4 12.1 %collective-permute-done.27 = bf16[2,64,2048]{2,1,0:T(8,128)(2,1)S(1)} collective-permute-done((bf16[2,64,2048]{2,1,0:T(8,128)(2,1)S(1)}, bf16[2,64,2048]{2,1,0:T(8,128)(2,1)S(1)}, u32[]{:S(2)}, u32[]{:S(2)}) %collective-permute-start.27) | collective-permute-done | bytes 524320 | tf_op jit(solution)/shard_map/ppermute | solution.py:57
  214.3 7.7 %collective-permute-done.29 = bf16[2,64,2048]{2,1,0:T(8,128)(2,1)} collective-permute-done((bf16[2,64,2048]{2,1,0:T(8,128)(2,1)S(1)}, bf16[2,64,2048]{2,1,0:T(8,128)(2,1)}, u32[]{:S(2)}, u32[]{:S(2)}) %collective-permute-start.29) | collective-permute-done | bytes 524320 | tf_op jit(solution)/shard_map/ppermute | solution.py:31
  227.7 19.1 %experts.4 = (bf16[2,1,64,2176]{3,2,1,0:T(8,128)(2,1)S(1)}, bf16[2,1,64,2176]{3,2,1,0:T(8,128)(2,1)S(1)}, bf16[2,1,64,2176]{3,2,1,0:T(8,128)(2,1)S(1)}, bf16[2,1...) custom-call(s32[4]{0:T(128)S(1)} %get-tuple-element.218.refs_0_, ...), custom_call_target="tpu_custom_call" | custom-call | flops 8589934592 | bytes 22020096 | tf_op jit(solution)/shard_map/experts/pallas_call | solution.py:438
  256.0 19.3 %experts.5 = (bf16[2,1,64,2176]{3,2,1,0:T(8,128)(2,1)S(1)}, bf16[2,1,64,2176]{3,2,1,0:T(8,128)(2,1)S(1)}, bf16[2,1,64,2176]{3,2,1,0:T(8,128)(2,1)S(1)}, bf16[2,1...) custom-call(s32[4]{0:T(128)S(1)} %get-tuple-element.220.refs_0_, ...), custom_call_target="tpu_custom_call" | custom-call | flops 8589934592 | bytes 22020096 | tf_op jit(solution)/shard_map/experts/pallas_call | solution.py:438
  281.5 19.2 %experts.6 = (bf16[2,1,64,2176]{3,2,1,0:T(8,128)(2,1)S(1)}, bf16[2,1,64,2176]{3,2,1,0:T(8,128)(2,1)S(1)}, bf16[2,1,64,2176]{3,2,1,0:T(8,128)(2,1)S(1)}, bf16[2,1...) custom-call(s32[4]{0:T(128)S(1)} %get-tuple-element.227.refs_0_, ...), custom_call_target="tpu_custom_call" | custom-call | flops 8589934592 | bytes 22020096 | tf_op jit(solution)/shard_map/experts/pallas_call | solution.py:438
  308.4 19.5 %experts.7 = (bf16[2,1,64,2176]{3,2,1,0:T(8,128)(2,1)S(1)}, bf16[2,1,64,2176]{3,2,1,0:T(8,128)(2,1)S(1)}, bf16[2,1,64,2176]{3,2,1,0:T(8,128)(2,1)S(1)}, bf16[2,1...) custom-call(s32[4]{0:T(128)S(1)} %get-tuple-element.237.refs_0_, ...), custom_call_target="tpu_custom_call" | custom-call | flops 8589934592 | bytes 22020096 | tf_op jit(solution)/shard_map/experts/pallas_call | solution.py:438
  336.8 12.9 %collective-permute-done.45 = bf16[1,64,2176]{2,1,0:T(8,128)(2,1)S(1)} collective-permute-done((bf16[1,64,2176]{2,1,0:T(8,128)(2,1)S(1)}, bf16[1,64,2176]{2,1,0:T(8,128)(2,1)S(1)}, u32[]{:S(2)}, u32[]{:S(2)}) %collective-permute-start.45) | collective-permute-done | bytes 278560 | tf_op jit(solution)/shard_map/ppermute | solution.py:31
  358.7 16.1 %collective-permute-done.52 = bf16[1,64,2176]{2,1,0:T(8,128)(2,1)S(1)} collective-permute-done((bf16[1,64,2176]{2,1,0:T(8,128)(2,1)S(1)}, bf16[1,64,2176]{2,1,0:T(8,128)(2,1)S(1)}, u32[]{:S(2)}, u32[]{:S(2)}) %collective-permute-start.52) | collective-permute-done | bytes 278560 | tf_op jit(solution)/shard_map/ppermute | solution.py:31
  377.1 8.3 %mix.2 = bf16[4,2,4,64,2048]{4,3,2,1,0:T(8,128)(2,1)} custom-call(bf16[4,512,512]{2,1,0:T(8,128)(2,1)} %pad_maximum_fusion.1.scaled_ref, bf16[512,2048]{1,0:T(8,128)(2,1)} %bitcast.487), custom_call_target="tpu_custom_call" | custom-call | flops 4294967296 | bytes 20971520 | tf_op jit(solution)/shard_map/mix/pallas_call | solution.py:509
  394.0 10.2 %collective-permute-done.53 = bf16[2,64,2176]{2,1,0:T(8,128)(2,1)S(1)} collective-permute-done((bf16[2,64,2176]{2,1,0:T(8,128)(2,1)S(1)}, bf16[2,64,2176]{2,1,0:T(8,128)(2,1)S(1)}, u32[]{:S(2)}, u32[]{:S(2)}) %collective-permute-start.53) | collective-permute-done | bytes 557088 | tf_op jit(solution)/shard_map/ppermute | solution.py:57
  415.9 11.2 %collective-permute-done.58.refs_0_ = bf16[2,64,2176]{2,1,0:T(8,128)(2,1)S(1)} collective-permute-done((bf16[2,64,2176]{2,1,0:T(8,128)(2,1)S(1)}, bf16[2,64,2176]{2,1,0:T(8,128)(2,1)S(1)}, u32[]{:S(2)}, u32[]{:S(2)}) %collective-permute-start.58) | collective-permute-done | bytes 557088 | tf_op jit(solution)/shard_map/ppermute | solution.py:57
  427.9 5.4 turn.1
  435.9 5.2 collective-permute-done.64
  446.6 10.7 %mix.3 = (bf16[2,4,64,2048]{3,2,1,0:T(8,128)(2,1)}, bf16[2,4,64,2048]{3,2,1,0:T(8,128)(2,1)}, bf16[2,4,64,2048]{3,2,1,0:T(8,128)(2,1)}, bf16[2,4,64,2048]{3,2,1,0:T(8,128)(2,1)}) custom-call(bf16[4,512,512]{2,1,0:T(8,128)(2,1)} %pad_maximum_fusion.scaled_ref, bf16[512,2048]{1,0:T(8,128)(2,1)} %bitcast.488, ...), custom_call_target="tpu_custom_call" | custom-call | flops 4294967296 | bytes 20971520 | tf_op jit(solution)/shard_map/mix/pallas_call | solution.py:509
  458.3 4.5 output_grad.1
  462.8 14.4 %attend_back.1 = (f32[512,512]{1,0:T(8,128)}, f32[512,512]{1,0:T(8,128)}, bf16[512,512]{1,0:T(8,128)(2,1)}, f32[4,8,128]{2,1,0:T(8,128)}, f32[8,512]{1,0:T(8,128)}, /*index=5*/bf16[512,2048]{1,0:T(8,128)(2,1)}) custom-call(bf16[2,64,2048]{2,1,0:T(8,128)(2,1)} %get-tuple-element.291.g0, bf16[2,64,2048]{2,1,0:T(8,128)(2,1)} %bitcast.501, ...), custom_call_target="tpu_custom_call" | custom-call | flops 2415919104 | bytes 16289792 | tf_op jit(solution)/shard_map/attend_back/pallas_call | solution.py:156
  487.5 4.6 value_back.1
  493.9 13.2 %project_back.1 = (bf16[2,64,2048]{2,1,0:T(8,128)(2,1)}, bf16[2,64,2048]{2,1,0:T(8,128)(2,1)}, bf16[2,64,2048]{2,1,0:T(8,128)(2,1)}, bf16[2,64,2048]{2,1,0:T(8,1...) custom-call(s32[8]{0:T(128)} %stack.264.at_ref, f32[4,8,128]{2,1,0:T(8,128)} %get-tuple-element.300.s0, ...), custom_call_target="tpu_custom_call" | custom-call | flops 6442450944 | bytes 22347808 | tf_op jit(solution)/shard_map/project_back/pallas_call | solution.py:156
  508.4 16.7 %down_grads.1 = f32[2,256,2048]{2,1,0:T(8,128)} custom-call(s32[5]{0:T(128)} %stack.313.refs_0_, bf16[2,8,64,512]{3,2,1,0:T(8,128)(2,1)} %copy-done.1, bf16[2,8,64,512]{3,2,1,0:T(8,128)(2,1)} %copy-done.2, bf16[2,8,64,512]{3,2,1,0:T(8,128)(2,1)} %copy-done.3, bf16[2,8,64,512]{3,2,1,0:T(8,128)(2,1)} %copy-done.4, bf16[4,4,2,2,64,2176]{5,4,3,2,1,0:T(8,128)(2,1)} %bitcast.461, ...), custom_call_target="tpu_custom_call" | custom-call | flops 8589934592 | bytes 25165824 | tf_op jit(solution)/shard_map/down_grads/pallas_call | solution.py:586
  532.3 15.9 %row_grads.2 = f32[2,2048,256]{2,1,0:T(8,128)} custom-call(bf16[8,64,2048]{2,1,0:T(8,128)(2,1)} %join.4.refs_1_.refs_0_, bf16[8,64,2048]{2,1,0:T(8,128)(2,1)} %collective-permute-done.32.refs_2_.refs_1_, bf16[8,64,2048]{2,1,0:T(8,128)(2,1)} %join.5.refs_1_.refs_2_, bf16[8,64,2048]{2,1,0:T(8,128)(2,1)} %collective-permute-done.35.refs_2_.refs_3_, ...), custom_call_target="tpu_custom_call" | custom-call | flops 8589934592 | bytes 25165824 | tf_op jit(solution)/shard_map/row_grads/pallas_call | solution.py:545
  548.2 3.9 collective-permute-start.78
  560.7 4.6 collective-permute-done.78
  572.7 15.8 %row_grads.3 = f32[2,2048,256]{2,1,0:T(8,128)} custom-call(bf16[8,64,2048]{2,1,0:T(8,128)(2,1)} %join.4.refs_1_.refs_0_, bf16[8,64,2048]{2,1,0:T(8,128)(2,1)} %collective-permute-done.32.refs_2_.refs_1_, bf16[8,64,2048]{2,1,0:T(8,128)(2,1)} %join.5.refs_1_.refs_2_, bf16[8,64,2048]{2,1,0:T(8,128)(2,1)} %collective-permute-done.35.refs_2_.refs_3_, ...), custom_call_target="tpu_custom_call" | custom-call | flops 8589934592 | bytes 25165824 | tf_op jit(solution)/shard_map/row_grads/pallas_call | solution.py:545
  597.8 3.8 finish.1
  643.5 4.0 collective-permute-done.100
  647.5 4.0 collective-permute-done.101
  653.5 3.6 collective-permute-start.109
  657.2 16.9 %collective-permute-done.97 = bf16[2,64,2048]{2,1,0:T(8,128)(2,1)S(1)} collective-permute-done((bf16[2,64,2048]{2,1,0:T(8,128)(2,1)S(1)}, bf16[2,64,2048]{2,1,0:T(8,128)(2,1)S(1)}, u32[]{:S(2)}, u32[]{:S(2)}) %collective-permute-start.97) | collective-permute-done | bytes 524320 | tf_op jit(solution)/shard_map/ppermute | solution.py:57
  674.2 6.1 collective-permute-start.98
  680.3 5.0 collective-permute-done.102
  685.3 3.0 collective-permute-start.103
  688.3 8.2 %collective-permute-done.109 = bf16[4,64,512]{2,1,0:T(8,128)(2,1)S(1)} collective-permute-done((bf16[4,64,512]{2,1,0:T(8,128)(2,1)S(1)}, bf16[4,64,512]{2,1,0:T(8,128)(2,1)S(1)}, u32[]{:S(2)}, u32[]{:S(2)}) %collective-permute-start.109) | collective-permute-done | bytes 262176 | tf_op jit(solution)/shard_map/ppermute | solution.py:57
  696.5 11.6 %collective-permute-done.98 = bf16[2,64,2048]{2,1,0:T(8,128)(2,1)S(1)} collective-permute-done((bf16[2,64,2048]{2,1,0:T(8,128)(2,1)S(1)}, bf16[2,64,2048]{2,1,0:T(8,128)(2,1)S(1)}, u32[]{:S(2)}, u32[]{:S(2)}) %collective-permute-start.98) | collective-permute-done | bytes 524320 | tf_op jit(solution)/shard_map/ppermute | solution.py:57
  712.5 3.8 collective-permute-done.105
  717.7 3.8 collective-permute-done.106
  (526 shorter events, 267.3 us)
Async XLA Ops:
  7.2 160.2 %all-gather.4.cloned.1.call-start = ((), (), s32[]{:S(2)}) async-start(), calls=%async_computation.1 | async-start | bytes 18382848 | tf_op jit(solution)/shard_map/all_gather | solution.py:904
  10.4 596.3 %reduce-scatter.2.cloned.1.call-start = ((), (), s32[]{:S(2)}) async-start(), calls=%async_computation.2 | async-start | bytes 4718592 | tf_op jit(solution)/shard_map/reduce_scatter | solution.py:1148
  27.9 54.0 %collective-permute-start.7 = (bf16[384,1536]{1,0:T(8,128)(2,1)}, bf16[384,1536]{1,0:T(8,128)(2,1)S(1)}, u32[]{:S(2)}, u32[]{:S(2)}) collective-permute-start(bf16[384,1536]{1,0:T(8,128)(2,1)} %get-tuple-element.200), channel_id=1, source_target_pairs={{0,8},{8,0},{16,24},{24,16},{1,9},{9,1},{17,25},{25,17},{2,10},{10... | collective-permute-start | bytes 3538952 | tf_op jit(solution)/shard_map/ppermute | solution.py:31
  28.3 53.7 %collective-permute-start.8 = (bf16[384,1536]{1,0:T(8,128)(2,1)}, bf16[384,1536]{1,0:T(8,128)(2,1)S(1)}, u32[]{:S(2)}, u32[]{:S(2)}) collective-permute-start(bf16[384,1536]{1,0:T(8,128)(2,1)} %get-tuple-element.201), channel_id=1, source_target_pairs={{0,16},{8,24},{16,0},{24,8},{1,17},{9,25},{17,1},{25,9},{2,18},{10... | collective-permute-start | bytes 3538952 | tf_op jit(solution)/shard_map/ppermute | solution.py:31
  28.4 53.6 %collective-permute-start.3 = (bf16[2,1,64,2048]{3,2,0,1:T(8,128)(2,1)S(1)}, bf16[2,1,64,2048]{3,2,0,1:T(8,128)(2,1)}, u32[]{:S(2)}, u32[]{:S(2)}) collective-permute-start(bf16[2,1,64,2048]{3,2,0,1:T(8,128)(2,1)S(1)} %get-tuple-element.464), channel_id=1, source_target_pairs={{0,8},{8,0},{16,24},{24,16},{1,9},{9,1},{17,25},{25,17},{2,10},{10... | collective-permute-start | bytes 1572872 | tf_op jit(solution)/shard_map/ppermute | solution.py:31
  30.4 51.6 %collective-permute-start.1 = (bf16[2,1,64,2048]{3,2,0,1:T(8,128)(2,1)S(1)}, bf16[2,1,64,2048]{3,2,0,1:T(8,128)(2,1)}, u32[]{:S(2)}, u32[]{:S(2)}) collective-permute-start(bf16[2,1,64,2048]{3,2,0,1:T(8,128)(2,1)S(1)} %get-tuple-element.470), channel_id=1, source_target_pairs={{0,16},{8,24},{16,0},{24,8},{1,17},{9,25},{17,1},{25,9},{2,18},{10... | collective-permute-start | bytes 1572872 | tf_op jit(solution)/shard_map/ppermute | solution.py:31
  157.8 25.7 %collective-permute-start.23 = (bf16[2,64,2048]{2,1,0:T(8,128)(2,1)}, bf16[2,64,2048]{2,1,0:T(8,128)(2,1)S(1)}, u32[]{:S(2)}, u32[]{:S(2)}) collective-permute-start(bf16[2,64,2048]{2,1,0:T(8,128)(2,1)} %get-tuple-element.214.refs_9_), channel_id=1, source_target_pairs={{0,2},{1,3},{2,4},{3,5},{4,6},{5,7},{6,0},{7,1},{8,10},{9,11},{10,... | collective-permute-start | bytes 1572872 | tf_op jit(solution)/shard_map/ppermute | solution.py:57
  163.5 23.7 %collective-permute-start.30 = (bf16[2,1,64,2048]{3,2,1,0:T(8,128)(2,1)S(1)}, bf16[2,1,64,2048]{3,2,1,0:T(8,128)(2,1)S(1)}, u32[]{:S(2)}, u32[]{:S(2)}) collective-permute-start(bf16[2,1,64,2048]{3,2,1,0:T(8,128)(2,1)S(1)} %pad_maximum_fusion.12.a_ref), channel_id=1, source_target_pairs={{0,16},{8,24},{16,0},{24,8},{1,17},{9,25},{17,1},{25,9},{2,18},{10... | collective-permute-start | bytes 1572872 | tf_op jit(solution)/shard_map/ppermute | solution.py:31
  166.6 20.6 %collective-permute-start.31 = (bf16[2,1,64,2048]{3,2,1,0:T(8,128)(2,1)S(1)}, bf16[2,1,64,2048]{3,2,1,0:T(8,128)(2,1)}, u32[]{:S(2)}, u32[]{:S(2)}) collective-permute-start(bf16[2,1,64,2048]{3,2,1,0:T(8,128)(2,1)S(1)} %pad_maximum_fusion.13.c_ref), channel_id=1, source_target_pairs={{0,8},{8,0},{16,24},{24,16},{1,9},{9,1},{17,25},{25,17},{2,10},{10... | collective-permute-start | bytes 1572872 | tf_op jit(solution)/shard_map/ppermute | solution.py:31
  190.5 37.2 %collective-permute-start.32 = (bf16[8,64,2048]{2,1,0:T(8,128)(2,1)}, bf16[8,64,2048]{2,1,0:T(8,128)(2,1)}, u32[]{:S(2)}, u32[]{:S(2)}) collective-permute-start(bf16[8,64,2048]{2,1,0:T(8,128)(2,1)} %join.4.refs_1_.refs_0_), channel_id=1, source_target_pairs={{0,1},{1,0},{2,3},{3,2},{4,5},{5,4},{6,7},{7,6},{8,9},{9,8},{10,11... | collective-permute-start | bytes 6291464 | tf_op jit(solution)/shard_map/ppermute | solution.py:48
  214.3 41.7 %collective-permute-start.35 = (bf16[8,64,2048]{2,1,0:T(8,128)(2,1)}, bf16[8,64,2048]{2,1,0:T(8,128)(2,1)}, u32[]{:S(2)}, u32[]{:S(2)}) collective-permute-start(bf16[8,64,2048]{2,1,0:T(8,128)(2,1)} %join.5.refs_1_.refs_2_), channel_id=1, source_target_pairs={{0,1},{1,0},{2,3},{3,2},{4,5},{5,4},{6,7},{7,6},{8,9},{9,8},{10,11... | collective-permute-start | bytes 6291464 | tf_op jit(solution)/shard_map/ppermute | solution.py:48
  226.2 22.9 %collective-permute-start.37 = (bf16[2,2,64,2048]{3,2,1,0:T(8,128)(2,1)}, bf16[2,2,64,2048]{3,2,1,0:T(8,128)(2,1)}, u32[]{:S(2)}, u32[]{:S(2)}) collective-permute-start(bf16[2,2,64,2048]{3,2,1,0:T(8,128)(2,1)} %pad_maximum_fusion.6.a_ref), channel_id=1, source_target_pairs={{0,16},{8,24},{16,0},{24,8},{1,17},{9,25},{17,1},{25,9},{2,18},{10... | collective-permute-start | bytes 3145736 | tf_op jit(solution)/shard_map/ppermute | solution.py:31
  226.5 22.6 %collective-permute-start.38 = (bf16[2,2,64,2048]{3,2,1,0:T(8,128)(2,1)}, bf16[2,2,64,2048]{3,2,1,0:T(8,128)(2,1)}, u32[]{:S(2)}, u32[]{:S(2)}) collective-permute-start(bf16[2,2,64,2048]{3,2,1,0:T(8,128)(2,1)} %pad_maximum_fusion.7.c_ref), channel_id=1, source_target_pairs={{0,8},{8,0},{16,24},{24,16},{1,9},{9,1},{17,25},{25,17},{2,10},{10... | collective-permute-start | bytes 3145736 | tf_op jit(solution)/shard_map/ppermute | solution.py:31
  248.7 27.6 %collective-permute-start.36 = (bf16[4,2,1,64,2176]{4,3,1,2,0:T(8,128)(2,1)}, bf16[4,2,1,64,2176]{4,3,1,2,0:T(8,128)(2,1)}, u32[]{:S(2)}, u32[]{:S(2)}) collective-permute-start(bf16[4,2,1,64,2176]{4,3,1,2,0:T(8,128)(2,1)} %bitcast.522), channel_id=1, source_target_pairs={{0,1},{1,0},{2,3},{3,2},{4,5},{5,4},{6,7},{7,6},{8,9},{9,8},{10,11... | collective-permute-start | bytes 6684680 | tf_op jit(solution)/shard_map/ppermute | solution.py:48
  251.7 24.5 %collective-permute-start.39 = (bf16[8,64,2048]{2,1,0:T(8,128)(2,1)}, bf16[8,64,2048]{2,1,0:T(8,128)(2,1)}, u32[]{:S(2)}, u32[]{:S(2)}) collective-permute-start(bf16[8,64,2048]{2,1,0:T(8,128)(2,1)} %join.6.refs_1_.refs_4_), channel_id=1, source_target_pairs={{0,1},{1,0},{2,3},{3,2},{4,5},{5,4},{6,7},{7,6},{8,9},{9,8},{10,11... | collective-permute-start | bytes 6291464 | tf_op jit(solution)/shard_map/ppermute | solution.py:48
  255.5 45.1 %collective-permute-start.41 = (bf16[8,64,2048]{2,1,0:T(8,128)(2,1)}, bf16[8,64,2048]{2,1,0:T(8,128)(2,1)S(1)}, u32[]{:S(2)}, u32[]{:S(2)}) collective-permute-start(bf16[8,64,2048]{2,1,0:T(8,128)(2,1)} %join.7.refs_1_.refs_6_), channel_id=1, source_target_pairs={{0,1},{1,0},{2,3},{3,2},{4,5},{5,4},{6,7},{7,6},{8,9},{9,8},{10,11... | collective-permute-start | bytes 6291464 | tf_op jit(solution)/shard_map/ppermute | solution.py:48
  276.2 26.8 %collective-permute-start.40 = (bf16[4,2,1,64,2176]{4,3,1,2,0:T(8,128)(2,1)}, bf16[4,2,1,64,2176]{4,3,1,2,0:T(8,128)(2,1)S(1)}, u32[]{:S(2)}, u32[]{:S(2)}) collective-permute-start(bf16[4,2,1,64,2176]{4,3,1,2,0:T(8,128)(2,1)} %bitcast.525), channel_id=1, source_target_pairs={{0,1},{1,0},{2,3},{3,2},{4,5},{5,4},{6,7},{7,6},{8,9},{9,8},{10,11... | collective-permute-start | bytes 6684680 | tf_op jit(solution)/shard_map/ppermute | solution.py:48
  302.0 25.9 %collective-permute-start.47 = (bf16[4,2,1,64,2176]{4,3,1,2,0:T(8,128)(2,1)}, bf16[4,2,1,64,2176]{4,3,1,2,0:T(8,128)(2,1)S(1)}, u32[]{:S(2)}, u32[]{:S(2)}) collective-permute-start(bf16[4,2,1,64,2176]{4,3,1,2,0:T(8,128)(2,1)} %bitcast.524), channel_id=1, source_target_pairs={{0,1},{1,0},{2,3},{3,2},{4,5},{5,4},{6,7},{7,6},{8,9},{9,8},{10,11... | collective-permute-start | bytes 6684680 | tf_op jit(solution)/shard_map/ppermute | solution.py:48
  304.5 26.4 %collective-permute-start.43 = (bf16[2,1,64,2176]{3,2,1,0:T(8,128)(2,1)}, bf16[2,1,64,2176]{3,2,1,0:T(8,128)(2,1)}, u32[]{:S(2)}, u32[]{:S(2)}) collective-permute-start(bf16[2,1,64,2176]{3,2,1,0:T(8,128)(2,1)} %bitcast.82), channel_id=1, source_target_pairs={{0,8},{8,0},{16,24},{24,16},{1,9},{9,1},{17,25},{25,17},{2,10},{10... | collective-permute-start | bytes 1671176 | tf_op jit(solution)/shard_map/ppermute | solution.py:31
  306.6 24.3 %collective-permute-start.42 = (bf16[2,1,64,2176]{3,2,0,1:T(8,128)(2,1)}, bf16[2,1,64,2176]{3,2,0,1:T(8,128)(2,1)}, u32[]{:S(2)}, u32[]{:S(2)}) collective-permute-start(bf16[2,1,64,2176]{3,2,0,1:T(8,128)(2,1)} %get-tuple-element.240), channel_id=1, source_target_pairs={{0,16},{8,24},{16,0},{24,8},{1,17},{9,25},{17,1},{25,9},{2,18},{10... | collective-permute-start | bytes 1671176 | tf_op jit(solution)/shard_map/ppermute | solution.py:31
  327.9 24.8 %collective-permute-start.50 = (bf16[4,2,1,64,2176]{4,3,1,2,0:T(8,128)(2,1)}, bf16[4,2,1,64,2176]{4,3,1,2,0:T(8,128)(2,1)S(1)}, u32[]{:S(2)}, u32[]{:S(2)}) collective-permute-start(bf16[4,2,1,64,2176]{4,3,1,2,0:T(8,128)(2,1)} %bitcast.523), channel_id=1, source_target_pairs={{0,1},{1,0},{2,3},{3,2},{4,5},{5,4},{6,7},{7,6},{8,9},{9,8},{10,11... | collective-permute-start | bytes 6684680 | tf_op jit(solution)/shard_map/ppermute | solution.py:48
  328.9 27.0 %collective-permute-start.49 = (bf16[2,1,64,2176]{3,2,1,0:T(8,128)(2,1)S(1)}, bf16[2,1,64,2176]{3,2,1,0:T(8,128)(2,1)S(1)}, u32[]{:S(2)}, u32[]{:S(2)}) collective-permute-start(bf16[2,1,64,2176]{3,2,1,0:T(8,128)(2,1)S(1)} %bitcast.494), channel_id=1, source_target_pairs={{0,8},{8,0},{16,24},{24,16},{1,9},{9,1},{17,25},{25,17},{2,10},{10... | collective-permute-start | bytes 1671176 | tf_op jit(solution)/shard_map/ppermute | solution.py:31
  329.0 26.9 %collective-permute-start.48 = (bf16[2,1,64,2176]{3,2,0,1:T(8,128)(2,1)S(1)}, bf16[2,1,64,2176]{3,2,0,1:T(8,128)(2,1)S(1)}, u32[]{:S(2)}, u32[]{:S(2)}) collective-permute-start(bf16[2,1,64,2176]{3,2,0,1:T(8,128)(2,1)S(1)} %get-tuple-element.252), channel_id=1, source_target_pairs={{0,16},{8,24},{16,0},{24,8},{1,17},{9,25},{17,1},{25,9},{2,18},{10... | collective-permute-start | bytes 1671176 | tf_op jit(solution)/shard_map/ppermute | solution.py:31
  351.9 23.1 %collective-permute-start.46 = (bf16[2,64,2176]{2,1,0:T(8,128)(2,1)S(1)}, bf16[2,64,2176]{2,1,0:T(8,128)(2,1)S(1)}, u32[]{:S(2)}, u32[]{:S(2)}) collective-permute-start(bf16[2,64,2176]{2,1,0:T(8,128)(2,1)S(1)} %fusion.68), channel_id=1, source_target_pairs={{0,2},{1,3},{2,4},{3,5},{4,6},{5,7},{6,0},{7,1},{8,10},{9,11},{10,... | collective-permute-start | bytes 1671176 | tf_op jit(solution)/shard_map/ppermute | solution.py:57
  354.3 33.1 %collective-permute-start.55 = (bf16[2,1,64,2176]{3,2,1,0:T(8,128)(2,1)}, bf16[2,1,64,2176]{3,2,1,0:T(8,128)(2,1)}, u32[]{:S(2)}, u32[]{:S(2)}) collective-permute-start(bf16[2,1,64,2176]{3,2,1,0:T(8,128)(2,1)} %bitcast.110), channel_id=1, source_target_pairs={{0,8},{8,0},{16,24},{24,16},{1,9},{9,1},{17,25},{25,17},{2,10},{10... | collective-permute-start | bytes 1671176 | tf_op jit(solution)/shard_map/ppermute | solution.py:31
  355.6 33.3 %collective-permute-start.54 = (bf16[2,1,64,2176]{3,2,0,1:T(8,128)(2,1)}, bf16[2,1,64,2176]{3,2,0,1:T(8,128)(2,1)}, u32[]{:S(2)}, u32[]{:S(2)}) collective-permute-start(bf16[2,1,64,2176]{3,2,0,1:T(8,128)(2,1)} %get-tuple-element.263), channel_id=1, source_target_pairs={{0,16},{8,24},{16,0},{24,8},{1,17},{9,25},{17,1},{25,9},{2,18},{10... | collective-permute-start | bytes 1671176 | tf_op jit(solution)/shard_map/ppermute | solution.py:31
  356.0 18.8 %collective-permute-start.52 = (bf16[1,64,2176]{2,1,0:T(8,128)(2,1)S(1)}, bf16[1,64,2176]{2,1,0:T(8,128)(2,1)S(1)}, u32[]{:S(2)}, u32[]{:S(2)}) collective-permute-start(bf16[1,64,2176]{2,1,0:T(8,128)(2,1)S(1)} %fusion.39), channel_id=1, source_target_pairs={{0,16},{8,24},{16,0},{24,8},{1,17},{9,25},{17,1},{25,9},{2,18},{10... | collective-permute-start | bytes 835592 | tf_op jit(solution)/shard_map/ppermute | solution.py:31
  385.4 61.2 %collective-permute-start.65 = (bf16[4,2,4,64,2048]{4,3,2,1,0:T(8,128)(2,1)}, bf16[4,2,4,64,2048]{4,3,2,1,0:T(8,128)(2,1)}, u32[]{:S(2)}, u32[]{:S(2)}) collective-permute-start(bf16[4,2,4,64,2048]{4,3,2,1,0:T(8,128)(2,1)} %mix.2), channel_id=1, source_target_pairs={{0,1},{1,0},{2,3},{3,2},{4,5},{5,4},{6,7},{7,6},{8,9},{9,8},{10,11... | collective-permute-start | bytes 25165832 | tf_op jit(solution)/shard_map/ppermute | solution.py:48
  389.9 19.3 %collective-permute-start.57 = (bf16[1,64,2176]{2,1,0:T(8,128)(2,1)S(1)}, bf16[1,64,2176]{2,1,0:T(8,128)(2,1)S(1)}, u32[]{:S(2)}, u32[]{:S(2)}) collective-permute-start(bf16[1,64,2176]{2,1,0:T(8,128)(2,1)S(1)} %fusion.40), channel_id=1, source_target_pairs={{0,16},{8,24},{16,0},{24,8},{1,17},{9,25},{17,1},{25,9},{2,18},{10... | collective-permute-start | bytes 835592 | tf_op jit(solution)/shard_map/ppermute | solution.py:31
  485.7 67.9 %collective-permute-start.71 = (bf16[2,4,64,2048]{3,2,1,0:T(8,128)(2,1)}, bf16[2,4,64,2048]{3,2,1,0:T(8,128)(2,1)}, u32[]{:S(2)}, u32[]{:S(2)}) collective-permute-start(bf16[2,4,64,2048]{3,2,1,0:T(8,128)(2,1)} %get-tuple-element.302), channel_id=1, source_target_pairs={{0,16},{8,24},{16,0},{24,8},{1,17},{9,25},{17,1},{25,9},{2,18},{10... | collective-permute-start | bytes 6291464 | tf_op jit(solution)/shard_map/ppermute | solution.py:31
  486.7 70.2 %collective-permute-start.73 = (bf16[2,4,64,2048]{3,2,1,0:T(8,128)(2,1)}, bf16[2,4,64,2048]{3,2,1,0:T(8,128)(2,1)}, u32[]{:S(2)}, u32[]{:S(2)}) collective-permute-start(bf16[2,4,64,2048]{3,2,1,0:T(8,128)(2,1)} %get-tuple-element.304), channel_id=1, source_target_pairs={{0,8},{8,0},{16,24},{24,16},{1,9},{9,1},{17,25},{25,17},{2,10},{10... | collective-permute-start | bytes 6291464 | tf_op jit(solution)/shard_map/ppermute | solution.py:31
  492.1 38.2 %collective-permute-start.76 = (bf16[4,256,512]{2,1,0:T(8,128)(2,1)}, bf16[4,256,512]{2,1,0:T(8,128)(2,1)S(1)}, u32[]{:S(2)}, u32[]{:S(2)}) collective-permute-start(bf16[4,256,512]{2,1,0:T(8,128)(2,1)} %get-tuple-element.312), channel_id=1, source_target_pairs={{0,1},{1,0},{2,3},{3,2},{4,5},{5,4},{6,7},{7,6},{8,9},{9,8},{10,11... | collective-permute-start | bytes 3145736 | tf_op jit(solution)/shard_map/ppermute | solution.py:48
  493.8 34.8 %collective-permute-start.79 = (bf16[4,64,512]{2,1,0:T(8,128)(2,1)}, bf16[4,64,512]{2,1,0:T(8,128)(2,1)S(1)}, u32[]{:S(2)}, u32[]{:S(2)}) collective-permute-start(bf16[4,64,512]{2,1,0:T(8,128)(2,1)} %fusion.37), channel_id=1, source_target_pairs={{0,2},{1,3},{2,4},{3,5},{4,6},{5,7},{6,0},{7,1},{8,10},{9,11},{10,... | collective-permute-start | bytes 786440 | tf_op jit(solution)/shard_map/ppermute | solution.py:57
  507.1 221.6 %all-gather.6.cloned.1.call-start = ((), (), s32[]{:S(2)}) async-start(), calls=%async_computation.3 | async-start | bytes 4718592 | tf_op jit(solution)/shard_map/all_gather | solution.py:1204
  507.1 59.8 %collective-permute-start.83 = (bf16[2,1,64,2048]{3,2,1,0:T(8,128)(2,1)}, bf16[2,1,64,2048]{3,2,1,0:T(8,128)(2,1)}, u32[]{:S(2)}, u32[]{:S(2)}) collective-permute-start(bf16[2,1,64,2048]{3,2,1,0:T(8,128)(2,1)} %bitcast.528), channel_id=1, source_target_pairs={{0,8},{8,0},{16,24},{24,16},{1,9},{9,1},{17,25},{25,17},{2,10},{10... | collective-permute-start | bytes 1572872 | tf_op jit(solution)/shard_map/ppermute | solution.py:31
  528.7 40.6 %collective-permute-start.82 = (bf16[2,1,64,2048]{3,2,1,0:T(8,128)(2,1)}, bf16[2,1,64,2048]{3,2,1,0:T(8,128)(2,1)}, u32[]{:S(2)}, u32[]{:S(2)}) collective-permute-start(bf16[2,1,64,2048]{3,2,1,0:T(8,128)(2,1)} %bitcast.527), channel_id=1, source_target_pairs={{0,16},{8,24},{16,0},{24,8},{1,17},{9,25},{17,1},{25,9},{2,18},{10... | collective-permute-start | bytes 1572872 | tf_op jit(solution)/shard_map/ppermute | solution.py:31
  553.6 42.2 %collective-permute-start.88 = (bf16[4,64,512]{2,1,0:T(8,128)(2,1)S(1)}, bf16[4,64,512]{2,1,0:T(8,128)(2,1)}, u32[]{:S(2)}, u32[]{:S(2)}) collective-permute-start(bf16[4,64,512]{2,1,0:T(8,128)(2,1)S(1)} %get-tuple-element.379), channel_id=1, source_target_pairs={{0,2},{1,3},{2,4},{3,5},{4,6},{5,7},{6,0},{7,1},{8,10},{9,11},{10,... | collective-permute-start | bytes 786440 | tf_op jit(solution)/shard_map/ppermute | solution.py:57
  556.9 45.6 %collective-permute-start.72 = (bf16[4,64,2048]{2,1,0:T(8,128)(2,1)}, bf16[4,64,2048]{2,1,0:T(8,128)(2,1)}, u32[]{:S(2)}, u32[]{:S(2)}) collective-permute-start(bf16[4,64,2048]{2,1,0:T(8,128)(2,1)} %fusion.16), channel_id=1, source_target_pairs={{0,8},{8,0},{16,24},{24,16},{1,9},{9,1},{17,25},{25,17},{2,10},{10... | collective-permute-start | bytes 3145736 | tf_op jit(solution)/shard_map/ppermute | solution.py:31
  565.3 38.5 %collective-permute-start.74 = (bf16[4,64,2048]{2,1,0:T(8,128)(2,1)}, bf16[4,64,2048]{2,1,0:T(8,128)(2,1)}, u32[]{:S(2)}, u32[]{:S(2)}) collective-permute-start(bf16[4,64,2048]{2,1,0:T(8,128)(2,1)} %fusion.17), channel_id=1, source_target_pairs={{0,16},{8,24},{16,0},{24,8},{1,17},{9,25},{17,1},{25,9},{2,18},{10... | collective-permute-start | bytes 3145736 | tf_op jit(solution)/shard_map/ppermute | solution.py:31
  567.0 24.1 %collective-permute-start.80 = (bf16[4,64,512]{2,1,0:T(8,128)(2,1)}, bf16[4,64,512]{2,1,0:T(8,128)(2,1)}, u32[]{:S(2)}, u32[]{:S(2)}) collective-permute-start(bf16[4,64,512]{2,1,0:T(8,128)(2,1)} %fusion.35), channel_id=1, source_target_pairs={{0,2},{1,3},{2,4},{3,5},{4,6},{5,7},{6,0},{7,1},{8,10},{9,11},{10,... | collective-permute-start | bytes 786440 | tf_op jit(solution)/shard_map/ppermute | solution.py:57
  595.8 27.2 %collective-permute-start.85 = (bf16[4,64,512]{2,1,0:T(8,128)(2,1)}, bf16[4,64,512]{2,1,0:T(8,128)(2,1)}, u32[]{:S(2)}, u32[]{:S(2)}) collective-permute-start(bf16[4,64,512]{2,1,0:T(8,128)(2,1)} %fusion.33), channel_id=1, source_target_pairs={{0,2},{1,3},{2,4},{3,5},{4,6},{5,7},{6,0},{7,1},{8,10},{9,11},{10,... | collective-permute-start | bytes 786440 | tf_op jit(solution)/shard_map/ppermute | solution.py:57
  596.9 56.6 %collective-permute-start.108 = (bf16[4,64,512]{2,1,0:T(8,128)(2,1)}, bf16[4,64,512]{2,1,0:T(8,128)(2,1)S(1)}, u32[]{:S(2)}, u32[]{:S(2)}) collective-permute-start(bf16[4,64,512]{2,1,0:T(8,128)(2,1)} %collective-permute-done.88), channel_id=1, source_target_pairs={{0,2},{1,3},{2,4},{3,5},{4,6},{5,7},{6,0},{7,1},{8,10},{9,11},{10,... | collective-permute-start | bytes 786440 | tf_op jit(solution)/shard_map/ppermute | solution.py:57
  605.8 33.0 %collective-permute-start.84 = (bf16[2,64,2048]{2,1,0:T(8,128)(2,1)}, bf16[2,64,2048]{2,1,0:T(8,128)(2,1)}, u32[]{:S(2)}, u32[]{:S(2)}) collective-permute-start(bf16[2,64,2048]{2,1,0:T(8,128)(2,1)} %pad_maximum_fusion.8), channel_id=1, source_target_pairs={{0,2},{1,3},{2,4},{3,5},{4,6},{5,7},{6,0},{7,1},{8,10},{9,11},{10,... | collective-permute-start | bytes 1572872 | tf_op jit(solution)/shard_map/ppermute | solution.py:57
  640.0 34.0 %collective-permute-start.97 = (bf16[2,64,2048]{2,1,0:T(8,128)(2,1)S(1)}, bf16[2,64,2048]{2,1,0:T(8,128)(2,1)S(1)}, u32[]{:S(2)}, u32[]{:S(2)}) collective-permute-start(bf16[2,64,2048]{2,1,0:T(8,128)(2,1)S(1)} %fusion.18), channel_id=1, source_target_pairs={{0,2},{1,3},{2,4},{3,5},{4,6},{5,7},{6,0},{7,1},{8,10},{9,11},{10,... | collective-permute-start | bytes 1572872 | tf_op jit(solution)/shard_map/ppermute | solution.py:57
  651.6 33.7 %collective-permute-start.102 = (bf16[4,64,512]{2,1,0:T(8,128)(2,1)S(1)}, bf16[4,64,512]{2,1,0:T(8,128)(2,1)S(1)}, u32[]{:S(2)}, u32[]{:S(2)}) collective-permute-start(bf16[4,64,512]{2,1,0:T(8,128)(2,1)S(1)} %collective-permute-done.101), channel_id=1, source_target_pairs={{0,2},{1,3},{2,4},{3,5},{4,6},{5,7},{6,0},{7,1},{8,10},{9,11},{10,... | collective-permute-start | bytes 786440 | tf_op jit(solution)/shard_map/ppermute | solution.py:57
  653.5 43.0 %collective-permute-start.109 = (bf16[4,64,512]{2,1,0:T(8,128)(2,1)S(1)}, bf16[4,64,512]{2,1,0:T(8,128)(2,1)S(1)}, u32[]{:S(2)}, u32[]{:S(2)}) collective-permute-start(bf16[4,64,512]{2,1,0:T(8,128)(2,1)S(1)} %collective-permute-done.108), channel_id=1, source_target_pairs={{0,2},{1,3},{2,4},{3,5},{4,6},{5,7},{6,0},{7,1},{8,10},{9,11},{10,... | collective-permute-start | bytes 786440 | tf_op jit(solution)/shard_map/ppermute | solution.py:57
  674.2 34.0 %collective-permute-start.98 = (bf16[2,64,2048]{2,1,0:T(8,128)(2,1)S(1)}, bf16[2,64,2048]{2,1,0:T(8,128)(2,1)S(1)}, u32[]{:S(2)}, u32[]{:S(2)}) collective-permute-start(bf16[2,64,2048]{2,1,0:T(8,128)(2,1)S(1)} %fusion.19), channel_id=1, source_target_pairs={{0,2},{1,3},{2,4},{3,5},{4,6},{5,7},{6,0},{7,1},{8,10},{9,11},{10,... | collective-permute-start | bytes 1572872 | tf_op jit(solution)/shard_map/ppermute | solution.py:57
  685.3 25.7 %collective-permute-start.103 = (bf16[4,64,512]{2,1,0:T(8,128)(2,1)S(1)}, bf16[4,64,512]{2,1,0:T(8,128)(2,1)S(1)}, u32[]{:S(2)}, u32[]{:S(2)}) collective-permute-start(bf16[4,64,512]{2,1,0:T(8,128)(2,1)S(1)} %collective-permute-done.102), channel_id=1, source_target_pairs={{0,2},{1,3},{2,4},{3,5},{4,6},{5,7},{6,0},{7,1},{8,10},{9,11},{10,... | collective-permute-start | bytes 786440 | tf_op jit(solution)/shard_map/ppermute | solution.py:57
  (132 other events, 1383.3 us)
Sparse Core Ops, SparseCore 0:
  11.4 139.4 all-gather.3
  507.2 66.6 reduce-scatter.1
  623.1 77.7 all-gather.5

commit v5 on v4

--- a/solution.py
+++ b/solution.py
@@ -81,6 +81,10 @@
 
 def reduce_xy(blocks, *others):
     return reduce_last(*reduce_first(blocks, *others))
+
+
+def reduce_late(gate, *args):
+    return after(reduce_xy(*args), gate)
 
 
 def total_of(terms):
@@ -1009,7 +1013,8 @@
             totals = after(totals, totals_all[-1], back_pieces[min(1, chips - 2)])
         back_terms[j] = [
             [t[0] for t in terms]
-            for terms in reduce_xy(
+            for terms in reduce_late(
+                totals_all[-1] if j == 1 else (),
                 after(totals, [r[0] for r in all_rows]),
                 totals_all[-1] if j != 1 else (),
                 back_pieces[-1:],
@@ -1026,7 +1031,7 @@
     scaled_sides = [
         jnp.concatenate([g[3][side : side + 1] for g in groups]) for side in range(2)
     ]
-    mix_passed = swap_core(mix_call(after(scaled_sides[1], arrived[0], back_pieces[1]), down_w))
+    mix_passed = swap_core(mix_call(after(scaled_sides[1], ring_total), down_w))
 
     ring_total = ring_up(ring_total)
     grad_res, grad_res_b, grad_gain_two, grad_router = call(

time: 750 us -> 743 us (level)
  waiting for transfers between devices: 230 us -> 241 us
  other arithmetic: 86.1 us -> 76 us
    ppermute x71, waiting for transfers between devices: 134 us -> 152 us  [flip_shard(): return lax.ppermute(values, 'shard', [(i, i ^ bit) for i in range(count)])]
  transfers between devices with their start and end apart: 114 -> 114, of which waited for: 44 -> 53; matrix products, arithmetic and copies ran while one was open for 16% -> 14% of each run, Pallas kernels for 33% -> 32%
where the time goes in v5:
time: 743 us; the launch traced here: 738 us
  Pallas kernels  251 us (34%)
  waiting for transfers between devices  241 us (32%)
  starting transfers between devices  98.7 us (13%)
  other arithmetic  76 us (10%)
  local copies, waits for them, and re-layouts  55 us (7%)
  between operations  15.6 us (2%)
    ppermute x71, waiting for transfers between devices, flip_shard(): return lax.ppermute(values, 'shard', [(i, i ^ bit) for i in range(count)])  152 us
    ppermute x21, waiting for transfers between devices, ring_up(): lax.ppermute(values, 'expert', [(i, (i + 2) % count) for i in range(count)])  81.4 us
    pallas_call x4, Pallas kernels, expert_call(): pl.pallas_call(lambda *refs: expert_kernel(experts_all, *refs), grid_spec...  77.2 us
    ppermute x71, starting transfers between devices, flip_shard(): return lax.ppermute(values, 'shard', [(i, i ^ bit) for i in range(count)])  70 us
    pallas_call x9, Pallas kernels, call(): pl.pallas_call(kernel, in_specs=[scalars() if n in smem else whole(a.shap...  68.5 us
    pallas_call x2, Pallas kernels, row_grad_call(): pl.pallas_call(lambda *refs: row_grad_kernel(len(rows), *refs), grid=(wid...  31.8 us
    ppermute x21, starting transfers between devices, ring_up(): lax.ppermute(values, 'expert', [(i, (i + 2) % count) for i in range(count)])  26.6 us
    pallas_call x2, Pallas kernels, mix_call(): pl.pallas_call(mix_kernel, grid=(chips,), in_specs=[pl.BlockSpec((1, coun...  19.2 us
  transfers between devices with their start and end apart: 114, of which 53 were waited for; matrix products, arithmetic and copies ran while one was open for 14% of the time, Pallas kernels for 32%

profile of v5, /device:TPU:0, one launch (start us, length us, event | category | flops | bytes accessed | tf_op | source)
XLA Modules:
  0.0 738.1 jit_solution(4938015327724313873)
XLA Ops:
  10.6 3.0 collective-permute-start
  20.6 5.0 cut.1
  32.2 6.5 flip.1
  40.1 41.9 %collective-permute-done.3 = bf16[2,1,64,2048]{3,2,0,1:T(8,128)(2,1)} collective-permute-done((bf16[2,1,64,2048]{3,2,0,1:T(8,128)(2,1)S(1)}, bf16[2,1,64,2048]{3,2,0,1:T(8,128)(2,1)}, u32[]{:S(2)}, u32[]{:S(2)}) %collective-permute-start.3) | collective-permute-done | bytes 524320 | tf_op jit(solution)/shard_map/ppermute | solution.py:31
  89.2 3.6 collective-permute-done.9
  101.2 9.7 %project.1 = (bf16[512,2048]{1,0:T(8,128)(2,1)}, f32[512,1536]{1,0:T(8,128)}, f32[4,8,128]{2,1,0:T(8,128)}, f32[512,128]{1,0:T(8,128)}) custom-call(s32[8]{0:T(128)} %stack.264.at_ref, bf16[2,64,2048]{2,1,0:T(8,128)(2,1)} %get-tuple-element.519.r0, bf16[2,64,2048]{2,1,0:T(8,128)(2,1)} %bitcast.13.r1, bf16[2,64,2048]{2,1,0:T(8,128)(2,1)} %get-tuple-element.513.r2, ...), custom_call_target="tpu_custom_call" | custom-call | flops 3221225472 | bytes 13918240 | tf_op jit(solution)/shard_map/project/pallas_call | solution.py:160
  118.2 9.9 %attend.1 = (bf16[512,512]{1,0:T(8,128)(2,1)}, bf16[512,512]{1,0:T(8,128)(2,1)}, bf16[512,512]{1,0:T(8,128)(2,1)}, f32[512,128]{1,0:T(8,128)}, f32[512,128]{1,0:...) custom-call(f32[512,1536]{1,0:T(8,128)} %get-tuple-element.370.refs_, ...), custom_call_target="tpu_custom_call" | custom-call | flops 1610612736 | bytes 11603968 | tf_op jit(solution)/shard_map/attend/pallas_call | solution.py:160
  132.9 8.3 %collective-permute-done.18 = bf16[2,1,64,2048]{3,2,1,0:T(8,128)(2,1)S(1)} collective-permute-done((bf16[2,1,64,2048]{3,2,1,0:T(8,128)(2,1)}, bf16[2,1,64,2048]{3,2,1,0:T(8,128)(2,1)S(1)}, u32[]{:S(2)}, u32[]{:S(2)}) %collective-permute-start.18) | collective-permute-done | bytes 524320 | tf_op jit(solution)/shard_map/ppermute | solution.py:31
  152.2 3.0 settle.1
  159.5 4.0 collective-permute-done.21
  163.6 2.9 collective-permute-done.22
  167.4 16.1 %lead.1.refs_4_ = f32[4,2,8,64,512]{4,3,2,1,0:T(8,128)} custom-call(bf16[4,4,2,2,64,2176]{5,4,3,2,1,0:T(8,128)(2,1)} %bitcast.472, bf16[2048,512]{1,0:T(8,128)(2,1)} %get-tuple-element.240.down_t_ref), custom_call_target="tpu_custom_call" | custom-call | flops 8589934592 | bytes 26214400 | tf_op jit(solution)/shard_map/lead/pallas_call | solution.py:311
  197.4 12.1 %collective-permute-done.27 = bf16[2,64,2048]{2,1,0:T(8,128)(2,1)S(1)} collective-permute-done((bf16[2,64,2048]{2,1,0:T(8,128)(2,1)S(1)}, bf16[2,64,2048]{2,1,0:T(8,128)(2,1)S(1)}, u32[]{:S(2)}, u32[]{:S(2)}) %collective-permute-start.27) | collective-permute-done | bytes 524320 | tf_op jit(solution)/shard_map/ppermute | solution.py:57
  214.3 7.7 %collective-permute-done.29 = bf16[2,64,2048]{2,1,0:T(8,128)(2,1)} collective-permute-done((bf16[2,64,2048]{2,1,0:T(8,128)(2,1)S(1)}, bf16[2,64,2048]{2,1,0:T(8,128)(2,1)}, u32[]{:S(2)}, u32[]{:S(2)}) %collective-permute-start.29) | collective-permute-done | bytes 524320 | tf_op jit(solution)/shard_map/ppermute | solution.py:31
  227.7 19.1 %experts.4 = (bf16[2,1,64,2176]{3,2,1,0:T(8,128)(2,1)S(1)}, bf16[2,1,64,2176]{3,2,1,0:T(8,128)(2,1)S(1)}, bf16[2,1,64,2176]{3,2,1,0:T(8,128)(2,1)S(1)}, bf16[2,1...) custom-call(s32[4]{0:T(128)S(1)} %get-tuple-element.242.refs_0_, ...), custom_call_target="tpu_custom_call" | custom-call | flops 8589934592 | bytes 22020096 | tf_op jit(solution)/shard_map/experts/pallas_call | solution.py:442
  255.9 19.3 %experts.5 = (bf16[2,1,64,2176]{3,2,1,0:T(8,128)(2,1)S(1)}, bf16[2,1,64,2176]{3,2,1,0:T(8,128)(2,1)S(1)}, bf16[2,1,64,2176]{3,2,1,0:T(8,128)(2,1)S(1)}, bf16[2,1...) custom-call(s32[4]{0:T(128)S(1)} %get-tuple-element.244.refs_0_, ...), custom_call_target="tpu_custom_call" | custom-call | flops 8589934592 | bytes 22020096 | tf_op jit(solution)/shard_map/experts/pallas_call | solution.py:442
  281.4 19.2 %experts.6 = (bf16[2,1,64,2176]{3,2,1,0:T(8,128)(2,1)S(1)}, bf16[2,1,64,2176]{3,2,1,0:T(8,128)(2,1)S(1)}, bf16[2,1,64,2176]{3,2,1,0:T(8,128)(2,1)S(1)}, bf16[2,1...) custom-call(s32[4]{0:T(128)S(1)} %get-tuple-element.251.refs_0_, ...), custom_call_target="tpu_custom_call" | custom-call | flops 8589934592 | bytes 22020096 | tf_op jit(solution)/shard_map/experts/pallas_call | solution.py:442
  307.7 19.6 %experts.7 = (bf16[2,1,64,2176]{3,2,1,0:T(8,128)(2,1)S(1)}, bf16[2,1,64,2176]{3,2,1,0:T(8,128)(2,1)S(1)}, bf16[2,1,64,2176]{3,2,1,0:T(8,128)(2,1)S(1)}, bf16[2,1...) custom-call(s32[4]{0:T(128)S(1)} %get-tuple-element.261.refs_0_, ...), custom_call_target="tpu_custom_call" | custom-call | flops 8589934592 | bytes 22020096 | tf_op jit(solution)/shard_map/experts/pallas_call | solution.py:442
  337.1 7.0 collective-permute-done.50
  344.6 4.5 collective-permute-done.44
  355.2 14.8 %collective-permute-done.51 = bf16[1,64,2176]{2,1,0:T(8,128)(2,1)S(1)} collective-permute-done((bf16[1,64,2176]{2,1,0:T(8,128)(2,1)S(1)}, bf16[1,64,2176]{2,1,0:T(8,128)(2,1)S(1)}, u32[]{:S(2)}, u32[]{:S(2)}) %collective-permute-start.51) | collective-permute-done | bytes 278560 | tf_op jit(solution)/shard_map/ppermute | solution.py:31
  374.5 3.0 collective-permute-done.57
  377.9 7.9 %collective-permute-done.53 = bf16[2,64,2176]{2,1,0:T(8,128)(2,1)S(1)} collective-permute-done((bf16[2,64,2176]{2,1,0:T(8,128)(2,1)S(1)}, bf16[2,64,2176]{2,1,0:T(8,128)(2,1)S(1)}, u32[]{:S(2)}, u32[]{:S(2)}) %collective-permute-start.53) | collective-permute-done | bytes 557088 | tf_op jit(solution)/shard_map/ppermute | solution.py:57
  386.7 8.5 %mix.2 = bf16[4,2,4,64,2048]{4,3,2,1,0:T(8,128)(2,1)} custom-call(bf16[4,512,512]{2,1,0:T(8,128)(2,1)} %pad_maximum_fusion.1.scaled_ref, bf16[512,2048]{1,0:T(8,128)(2,1)} %bitcast.503), custom_call_target="tpu_custom_call" | custom-call | flops 4294967296 | bytes 20971520 | tf_op jit(solution)/shard_map/mix/pallas_call | solution.py:513
  399.3 10.9 %collective-permute-done.59 = bf16[2,1,64,2176]{3,2,0,1:T(8,128)(2,1)S(1)} collective-permute-done((bf16[2,1,64,2176]{3,2,0,1:T(8,128)(2,1)S(1)}, bf16[2,1,64,2176]{3,2,0,1:T(8,128)(2,1)S(1)}, u32[]{:S(2)}, u32[]{:S(2)}) %collective-permute-start.59) | collective-permute-done | bytes 557088 | tf_op jit(solution)/shard_map/ppermute | solution.py:31
  414.7 5.2 collective-permute-done.62
  421.1 5.4 turn.1
  430.2 4.1 collective-permute-done.64
  440.0 10.7 %mix.3 = (bf16[2,4,64,2048]{3,2,1,0:T(8,128)(2,1)}, bf16[2,4,64,2048]{3,2,1,0:T(8,128)(2,1)}, bf16[2,4,64,2048]{3,2,1,0:T(8,128)(2,1)}, bf16[2,4,64,2048]{3,2,1,0:T(8,128)(2,1)}) custom-call(bf16[4,512,512]{2,1,0:T(8,128)(2,1)} %pad_maximum_fusion.scaled_ref, bf16[512,2048]{1,0:T(8,128)(2,1)} %bitcast.504, ...), custom_call_target="tpu_custom_call" | custom-call | flops 4294967296 | bytes 20971520 | tf_op jit(solution)/shard_map/mix/pallas_call | solution.py:513
  451.7 4.5 output_grad.1
  456.2 14.4 %attend_back.1 = (f32[512,512]{1,0:T(8,128)}, f32[512,512]{1,0:T(8,128)}, bf16[512,512]{1,0:T(8,128)(2,1)}, f32[4,8,128]{2,1,0:T(8,128)}, f32[8,512]{1,0:T(8,128)}, /*index=5*/bf16[512,2048]{1,0:T(8,128)(2,1)}) custom-call(bf16[2,64,2048]{2,1,0:T(8,128)(2,1)} %get-tuple-element.339.g0, bf16[2,64,2048]{2,1,0:T(8,128)(2,1)} %bitcast.523, ...), custom_call_target="tpu_custom_call" | custom-call | flops 2415919104 | bytes 16289792 | tf_op jit(solution)/shard_map/attend_back/pallas_call | solution.py:160
  481.2 4.6 value_back.1
  488.3 13.1 %project_back.1 = (bf16[2,64,2048]{2,1,0:T(8,128)(2,1)}, bf16[2,64,2048]{2,1,0:T(8,128)(2,1)}, bf16[2,64,2048]{2,1,0:T(8,128)(2,1)}, bf16[2,64,2048]{2,1,0:T(8,1...) custom-call(s32[8]{0:T(128)} %stack.264.at_ref, f32[4,8,128]{2,1,0:T(8,128)} %get-tuple-element.348.s0, ...), custom_call_target="tpu_custom_call" | custom-call | flops 6442450944 | bytes 22347808 | tf_op jit(solution)/shard_map/project_back/pallas_call | solution.py:160
  502.2 16.7 %down_grads.1 = f32[2,256,2048]{2,1,0:T(8,128)} custom-call(s32[5]{0:T(128)} %stack.313.refs_0_, bf16[2,8,64,512]{3,2,1,0:T(8,128)(2,1)} %copy-done.1, bf16[2,8,64,512]{3,2,1,0:T(8,128)(2,1)} %copy-done.2, bf16[2,8,64,512]{3,2,1,0:T(8,128)(2,1)} %copy-done.3, bf16[2,8,64,512]{3,2,1,0:T(8,128)(2,1)} %copy-done.4, bf16[4,4,2,2,64,2176]{5,4,3,2,1,0:T(8,128)(2,1)} %bitcast.477, ...), custom_call_target="tpu_custom_call" | custom-call | flops 8589934592 | bytes 25165824 | tf_op jit(solution)/shard_map/down_grads/pallas_call | solution.py:590
  527.6 16.0 %row_grads.2 = f32[2,2048,256]{2,1,0:T(8,128)} custom-call(bf16[8,64,2048]{2,1,0:T(8,128)(2,1)} %join.4.refs_1_.refs_0_, bf16[8,64,2048]{2,1,0:T(8,128)(2,1)} %collective-permute-done.32.refs_2_.refs_1_, bf16[8,64,2048]{2,1,0:T(8,128)(2,1)} %join.5.refs_1_.refs_2_, bf16[8,64,2048]{2,1,0:T(8,128)(2,1)} %collective-permute-done.35.refs_2_.refs_3_, ...), custom_call_target="tpu_custom_call" | custom-call | flops 8589934592 | bytes 25165824 | tf_op jit(solution)/shard_map/row_grads/pallas_call | solution.py:549
  554.2 6.4 collective-permute-done.78
  565.9 15.8 %row_grads.3 = f32[2,2048,256]{2,1,0:T(8,128)} custom-call(bf16[8,64,2048]{2,1,0:T(8,128)(2,1)} %join.4.refs_1_.refs_0_, bf16[8,64,2048]{2,1,0:T(8,128)(2,1)} %collective-permute-done.32.refs_2_.refs_1_, bf16[8,64,2048]{2,1,0:T(8,128)(2,1)} %join.5.refs_1_.refs_2_, bf16[8,64,2048]{2,1,0:T(8,128)(2,1)} %collective-permute-done.35.refs_2_.refs_3_, ...), custom_call_target="tpu_custom_call" | custom-call | flops 8589934592 | bytes 25165824 | tf_op jit(solution)/shard_map/row_grads/pallas_call | solution.py:549
  591.4 3.8 finish.1
  638.8 3.0 collective-permute-done.100
  641.8 5.3 collective-permute-done.101
  647.2 3.0 collective-permute-start.109
  650.2 19.5 %collective-permute-done.97 = bf16[2,64,2048]{2,1,0:T(8,128)(2,1)S(1)} collective-permute-done((bf16[2,64,2048]{2,1,0:T(8,128)(2,1)S(1)}, bf16[2,64,2048]{2,1,0:T(8,128)(2,1)S(1)}, u32[]{:S(2)}, u32[]{:S(2)}) %collective-permute-start.97) | collective-permute-done | bytes 524320 | tf_op jit(solution)/shard_map/ppermute | solution.py:57
  669.8 4.7 collective-permute-start.98
  674.4 6.4 collective-permute-done.102
  681.9 10.2 %collective-permute-done.109 = bf16[4,64,512]{2,1,0:T(8,128)(2,1)S(1)} collective-permute-done((bf16[4,64,512]{2,1,0:T(8,128)(2,1)S(1)}, bf16[4,64,512]{2,1,0:T(8,128)(2,1)S(1)}, u32[]{:S(2)}, u32[]{:S(2)}) %collective-permute-start.109) | collective-permute-done | bytes 262176 | tf_op jit(solution)/shard_map/ppermute | solution.py:57
  692.1 10.0 %collective-permute-done.98 = bf16[2,64,2048]{2,1,0:T(8,128)(2,1)S(1)} collective-permute-done((bf16[2,64,2048]{2,1,0:T(8,128)(2,1)S(1)}, bf16[2,64,2048]{2,1,0:T(8,128)(2,1)S(1)}, u32[]{:S(2)}, u32[]{:S(2)}) %collective-permute-start.98) | collective-permute-done | bytes 524320 | tf_op jit(solution)/shard_map/ppermute | solution.py:57
  706.5 3.8 collective-permute-done.105
  711.6 3.8 collective-permute-done.106
  (536 shorter events, 264.6 us)
Async XLA Ops:
  7.2 160.2 %all-gather.4.cloned.1.call-start = ((), (), s32[]{:S(2)}) async-start(), calls=%async_computation.1 | async-start | bytes 18382848 | tf_op jit(solution)/shard_map/all_gather | solution.py:908
  10.4 591.6 %reduce-scatter.2.cloned.1.call-start = ((), (), s32[]{:S(2)}) async-start(), calls=%async_computation.2 | async-start | bytes 4718592 | tf_op jit(solution)/shard_map/reduce_scatter | solution.py:1153
  28.0 54.0 %collective-permute-start.7 = (bf16[384,1536]{1,0:T(8,128)(2,1)}, bf16[384,1536]{1,0:T(8,128)(2,1)S(1)}, u32[]{:S(2)}, u32[]{:S(2)}) collective-permute-start(bf16[384,1536]{1,0:T(8,128)(2,1)} %get-tuple-element.224), channel_id=1, source_target_pairs={{0,8},{8,0},{16,24},{24,16},{1,9},{9,1},{17,25},{25,17},{2,10},{10... | collective-permute-start | bytes 3538952 | tf_op jit(solution)/shard_map/ppermute | solution.py:31
  28.3 53.7 %collective-permute-start.8 = (bf16[384,1536]{1,0:T(8,128)(2,1)}, bf16[384,1536]{1,0:T(8,128)(2,1)S(1)}, u32[]{:S(2)}, u32[]{:S(2)}) collective-permute-start(bf16[384,1536]{1,0:T(8,128)(2,1)} %get-tuple-element.225), channel_id=1, source_target_pairs={{0,16},{8,24},{16,0},{24,8},{1,17},{9,25},{17,1},{25,9},{2,18},{10... | collective-permute-start | bytes 3538952 | tf_op jit(solution)/shard_map/ppermute | solution.py:31
  28.4 53.6 %collective-permute-start.3 = (bf16[2,1,64,2048]{3,2,0,1:T(8,128)(2,1)S(1)}, bf16[2,1,64,2048]{3,2,0,1:T(8,128)(2,1)}, u32[]{:S(2)}, u32[]{:S(2)}) collective-permute-start(bf16[2,1,64,2048]{3,2,0,1:T(8,128)(2,1)S(1)} %get-tuple-element.512), channel_id=1, source_target_pairs={{0,8},{8,0},{16,24},{24,16},{1,9},{9,1},{17,25},{25,17},{2,10},{10... | collective-permute-start | bytes 1572872 | tf_op jit(solution)/shard_map/ppermute | solution.py:31
  30.4 51.6 %collective-permute-start.1 = (bf16[2,1,64,2048]{3,2,0,1:T(8,128)(2,1)S(1)}, bf16[2,1,64,2048]{3,2,0,1:T(8,128)(2,1)}, u32[]{:S(2)}, u32[]{:S(2)}) collective-permute-start(bf16[2,1,64,2048]{3,2,0,1:T(8,128)(2,1)S(1)} %get-tuple-element.518), channel_id=1, source_target_pairs={{0,16},{8,24},{16,0},{24,8},{1,17},{9,25},{17,1},{25,9},{2,18},{10... | collective-permute-start | bytes 1572872 | tf_op jit(solution)/shard_map/ppermute | solution.py:31
  157.8 25.7 %collective-permute-start.23 = (bf16[2,64,2048]{2,1,0:T(8,128)(2,1)}, bf16[2,64,2048]{2,1,0:T(8,128)(2,1)S(1)}, u32[]{:S(2)}, u32[]{:S(2)}) collective-permute-start(bf16[2,64,2048]{2,1,0:T(8,128)(2,1)} %get-tuple-element.238.refs_9_), channel_id=1, source_target_pairs={{0,2},{1,3},{2,4},{3,5},{4,6},{5,7},{6,0},{7,1},{8,10},{9,11},{10,... | collective-permute-start | bytes 1572872 | tf_op jit(solution)/shard_map/ppermute | solution.py:57
  163.5 23.6 %collective-permute-start.30 = (bf16[2,1,64,2048]{3,2,1,0:T(8,128)(2,1)S(1)}, bf16[2,1,64,2048]{3,2,1,0:T(8,128)(2,1)S(1)}, u32[]{:S(2)}, u32[]{:S(2)}) collective-permute-start(bf16[2,1,64,2048]{3,2,1,0:T(8,128)(2,1)S(1)} %pad_maximum_fusion.12.a_ref), channel_id=1, source_target_pairs={{0,16},{8,24},{16,0},{24,8},{1,17},{9,25},{17,1},{25,9},{2,18},{10... | collective-permute-start | bytes 1572872 | tf_op jit(solution)/shard_map/ppermute | solution.py:31
  166.6 20.6 %collective-permute-start.31 = (bf16[2,1,64,2048]{3,2,1,0:T(8,128)(2,1)S(1)}, bf16[2,1,64,2048]{3,2,1,0:T(8,128)(2,1)}, u32[]{:S(2)}, u32[]{:S(2)}) collective-permute-start(bf16[2,1,64,2048]{3,2,1,0:T(8,128)(2,1)S(1)} %pad_maximum_fusion.13.c_ref), channel_id=1, source_target_pairs={{0,8},{8,0},{16,24},{24,16},{1,9},{9,1},{17,25},{25,17},{2,10},{10... | collective-permute-start | bytes 1572872 | tf_op jit(solution)/shard_map/ppermute | solution.py:31
  190.5 37.2 %collective-permute-start.32 = (bf16[8,64,2048]{2,1,0:T(8,128)(2,1)}, bf16[8,64,2048]{2,1,0:T(8,128)(2,1)}, u32[]{:S(2)}, u32[]{:S(2)}) collective-permute-start(bf16[8,64,2048]{2,1,0:T(8,128)(2,1)} %join.4.refs_1_.refs_0_), channel_id=1, source_target_pairs={{0,1},{1,0},{2,3},{3,2},{4,5},{5,4},{6,7},{7,6},{8,9},{9,8},{10,11... | collective-permute-start | bytes 6291464 | tf_op jit(solution)/shard_map/ppermute | solution.py:48
  193.2 18.5 %collective-permute-start.33 = (bf16[2,1,64,2048]{3,2,1,0:T(8,128)(2,1)S(1)}, bf16[2,1,64,2048]{3,2,1,0:T(8,128)(2,1)}, u32[]{:S(2)}, u32[]{:S(2)}) collective-permute-start(bf16[2,1,64,2048]{3,2,1,0:T(8,128)(2,1)S(1)} %pad_maximum_fusion.14.a_ref), channel_id=1, source_target_pairs={{0,16},{8,24},{16,0},{24,8},{1,17},{9,25},{17,1},{25,9},{2,18},{10... | collective-permute-start | bytes 1572872 | tf_op jit(solution)/shard_map/ppermute | solution.py:31
  214.3 41.6 %collective-permute-start.35 = (bf16[8,64,2048]{2,1,0:T(8,128)(2,1)}, bf16[8,64,2048]{2,1,0:T(8,128)(2,1)}, u32[]{:S(2)}, u32[]{:S(2)}) collective-permute-start(bf16[8,64,2048]{2,1,0:T(8,128)(2,1)} %join.5.refs_1_.refs_2_), channel_id=1, source_target_pairs={{0,1},{1,0},{2,3},{3,2},{4,5},{5,4},{6,7},{7,6},{8,9},{9,8},{10,11... | collective-permute-start | bytes 6291464 | tf_op jit(solution)/shard_map/ppermute | solution.py:48
  226.2 22.8 %collective-permute-start.37 = (bf16[2,2,64,2048]{3,2,1,0:T(8,128)(2,1)}, bf16[2,2,64,2048]{3,2,1,0:T(8,128)(2,1)}, u32[]{:S(2)}, u32[]{:S(2)}) collective-permute-start(bf16[2,2,64,2048]{3,2,1,0:T(8,128)(2,1)} %pad_maximum_fusion.6.a_ref), channel_id=1, source_target_pairs={{0,16},{8,24},{16,0},{24,8},{1,17},{9,25},{17,1},{25,9},{2,18},{10... | collective-permute-start | bytes 3145736 | tf_op jit(solution)/shard_map/ppermute | solution.py:31
  226.5 22.5 %collective-permute-start.38 = (bf16[2,2,64,2048]{3,2,1,0:T(8,128)(2,1)}, bf16[2,2,64,2048]{3,2,1,0:T(8,128)(2,1)}, u32[]{:S(2)}, u32[]{:S(2)}) collective-permute-start(bf16[2,2,64,2048]{3,2,1,0:T(8,128)(2,1)} %pad_maximum_fusion.7.c_ref), channel_id=1, source_target_pairs={{0,8},{8,0},{16,24},{24,16},{1,9},{9,1},{17,25},{25,17},{2,10},{10... | collective-permute-start | bytes 3145736 | tf_op jit(solution)/shard_map/ppermute | solution.py:31
  248.6 27.5 %collective-permute-start.36 = (bf16[4,2,1,64,2176]{4,3,1,2,0:T(8,128)(2,1)}, bf16[4,2,1,64,2176]{4,3,1,2,0:T(8,128)(2,1)}, u32[]{:S(2)}, u32[]{:S(2)}) collective-permute-start(bf16[4,2,1,64,2176]{4,3,1,2,0:T(8,128)(2,1)} %bitcast.544), channel_id=1, source_target_pairs={{0,1},{1,0},{2,3},{3,2},{4,5},{5,4},{6,7},{7,6},{8,9},{9,8},{10,11... | collective-permute-start | bytes 6684680 | tf_op jit(solution)/shard_map/ppermute | solution.py:48
  251.6 24.4 %collective-permute-start.39 = (bf16[8,64,2048]{2,1,0:T(8,128)(2,1)}, bf16[8,64,2048]{2,1,0:T(8,128)(2,1)}, u32[]{:S(2)}, u32[]{:S(2)}) collective-permute-start(bf16[8,64,2048]{2,1,0:T(8,128)(2,1)} %join.6.refs_1_.refs_4_), channel_id=1, source_target_pairs={{0,1},{1,0},{2,3},{3,2},{4,5},{5,4},{6,7},{7,6},{8,9},{9,8},{10,11... | collective-permute-start | bytes 6291464 | tf_op jit(solution)/shard_map/ppermute | solution.py:48
  255.5 45.1 %collective-permute-start.41 = (bf16[8,64,2048]{2,1,0:T(8,128)(2,1)}, bf16[8,64,2048]{2,1,0:T(8,128)(2,1)S(1)}, u32[]{:S(2)}, u32[]{:S(2)}) collective-permute-start(bf16[8,64,2048]{2,1,0:T(8,128)(2,1)} %join.7.refs_1_.refs_6_), channel_id=1, source_target_pairs={{0,1},{1,0},{2,3},{3,2},{4,5},{5,4},{6,7},{7,6},{8,9},{9,8},{10,11... | collective-permute-start | bytes 6291464 | tf_op jit(solution)/shard_map/ppermute | solution.py:48
  276.0 26.8 %collective-permute-start.40 = (bf16[4,2,1,64,2176]{4,3,1,2,0:T(8,128)(2,1)}, bf16[4,2,1,64,2176]{4,3,1,2,0:T(8,128)(2,1)S(1)}, u32[]{:S(2)}, u32[]{:S(2)}) collective-permute-start(bf16[4,2,1,64,2176]{4,3,1,2,0:T(8,128)(2,1)} %bitcast.547), channel_id=1, source_target_pairs={{0,1},{1,0},{2,3},{3,2},{4,5},{5,4},{6,7},{7,6},{8,9},{9,8},{10,11... | collective-permute-start | bytes 6684680 | tf_op jit(solution)/shard_map/ppermute | solution.py:48
  300.6 26.8 %collective-permute-start.48 = (bf16[4,2,1,64,2176]{4,3,1,2,0:T(8,128)(2,1)}, bf16[4,2,1,64,2176]{4,3,1,2,0:T(8,128)(2,1)S(1)}, u32[]{:S(2)}, u32[]{:S(2)}) collective-permute-start(bf16[4,2,1,64,2176]{4,3,1,2,0:T(8,128)(2,1)} %bitcast.546), channel_id=1, source_target_pairs={{0,1},{1,0},{2,3},{3,2},{4,5},{5,4},{6,7},{7,6},{8,9},{9,8},{10,11... | collective-permute-start | bytes 6684680 | tf_op jit(solution)/shard_map/ppermute | solution.py:48
  304.2 26.7 %collective-permute-start.43 = (bf16[2,1,64,2176]{3,2,1,0:T(8,128)(2,1)}, bf16[2,1,64,2176]{3,2,1,0:T(8,128)(2,1)S(1)}, u32[]{:S(2)}, u32[]{:S(2)}) collective-permute-start(bf16[2,1,64,2176]{3,2,1,0:T(8,128)(2,1)} %bitcast.83), channel_id=1, source_target_pairs={{0,8},{8,0},{16,24},{24,16},{1,9},{9,1},{17,25},{25,17},{2,10},{10... | collective-permute-start | bytes 1671176 | tf_op jit(solution)/shard_map/ppermute | solution.py:31
  305.9 25.0 %collective-permute-start.42 = (bf16[2,1,64,2176]{3,2,0,1:T(8,128)(2,1)S(1)}, bf16[2,1,64,2176]{3,2,0,1:T(8,128)(2,1)}, u32[]{:S(2)}, u32[]{:S(2)}) collective-permute-start(bf16[2,1,64,2176]{3,2,0,1:T(8,128)(2,1)S(1)} %get-tuple-element.264), channel_id=1, source_target_pairs={{0,16},{8,24},{16,0},{24,8},{1,17},{9,25},{17,1},{25,9},{2,18},{10... | collective-permute-start | bytes 1671176 | tf_op jit(solution)/shard_map/ppermute | solution.py:31
  331.9 17.2 %collective-permute-start.44 = (bf16[1,64,2176]{2,1,0:T(8,128)(2,1)S(1)}, bf16[1,64,2176]{2,1,0:T(8,128)(2,1)S(1)}, u32[]{:S(2)}, u32[]{:S(2)}) collective-permute-start(bf16[1,64,2176]{2,1,0:T(8,128)(2,1)S(1)} %fusion.42), channel_id=1, source_target_pairs={{0,8},{8,0},{16,24},{24,16},{1,9},{9,1},{17,25},{25,17},{2,10},{10... | collective-permute-start | bytes 835592 | tf_op jit(solution)/shard_map/ppermute | solution.py:31
  349.5 21.1 %collective-permute-start.47 = (bf16[2,64,2176]{2,1,0:T(8,128)(2,1)S(1)}, bf16[2,64,2176]{2,1,0:T(8,128)(2,1)S(1)}, u32[]{:S(2)}, u32[]{:S(2)}) collective-permute-start(bf16[2,64,2176]{2,1,0:T(8,128)(2,1)S(1)} %fusion.68), channel_id=1, source_target_pairs={{0,2},{1,3},{2,4},{3,5},{4,6},{5,7},{6,0},{7,1},{8,10},{9,11},{10,... | collective-permute-start | bytes 1671176 | tf_op jit(solution)/shard_map/ppermute | solution.py:57
  351.0 19.7 %collective-permute-start.55 = (bf16[2,1,64,2176]{3,2,1,0:T(8,128)(2,1)S(1)}, bf16[2,1,64,2176]{3,2,1,0:T(8,128)(2,1)S(1)}, u32[]{:S(2)}, u32[]{:S(2)}) collective-permute-start(bf16[2,1,64,2176]{3,2,1,0:T(8,128)(2,1)S(1)} %bitcast.514), channel_id=1, source_target_pairs={{0,8},{8,0},{16,24},{24,16},{1,9},{9,1},{17,25},{25,17},{2,10},{10... | collective-permute-start | bytes 1671176 | tf_op jit(solution)/shard_map/ppermute | solution.py:31
  351.7 19.0 %collective-permute-start.54 = (bf16[2,1,64,2176]{3,2,0,1:T(8,128)(2,1)S(1)}, bf16[2,1,64,2176]{3,2,0,1:T(8,128)(2,1)S(1)}, u32[]{:S(2)}, u32[]{:S(2)}) collective-permute-start(bf16[2,1,64,2176]{3,2,0,1:T(8,128)(2,1)S(1)} %get-tuple-element.299), channel_id=1, source_target_pairs={{0,16},{8,24},{16,0},{24,8},{1,17},{9,25},{17,1},{25,9},{2,18},{10... | collective-permute-start | bytes 1671176 | tf_op jit(solution)/shard_map/ppermute | solution.py:31
  352.1 17.9 %collective-permute-start.51 = (bf16[1,64,2176]{2,1,0:T(8,128)(2,1)S(1)}, bf16[1,64,2176]{2,1,0:T(8,128)(2,1)S(1)}, u32[]{:S(2)}, u32[]{:S(2)}) collective-permute-start(bf16[1,64,2176]{2,1,0:T(8,128)(2,1)S(1)} %fusion.43), channel_id=1, source_target_pairs={{0,8},{8,0},{16,24},{24,16},{1,9},{9,1},{17,25},{25,17},{2,10},{10... | collective-permute-start | bytes 835592 | tf_op jit(solution)/shard_map/ppermute | solution.py:31
  395.2 44.7 %collective-permute-start.65 = (bf16[4,2,4,64,2048]{4,3,2,1,0:T(8,128)(2,1)}, bf16[4,2,4,64,2048]{4,3,2,1,0:T(8,128)(2,1)}, u32[]{:S(2)}, u32[]{:S(2)}) collective-permute-start(bf16[4,2,4,64,2048]{4,3,2,1,0:T(8,128)(2,1)} %mix.2), channel_id=1, source_target_pairs={{0,1},{1,0},{2,3},{3,2},{4,5},{5,4},{6,7},{7,6},{8,9},{9,8},{10,11... | collective-permute-start | bytes 25165832 | tf_op jit(solution)/shard_map/ppermute | solution.py:48
  399.2 21.0 %collective-permute-start.58 = (bf16[2,64,2176]{2,1,0:T(8,128)(2,1)}, bf16[2,64,2176]{2,1,0:T(8,128)(2,1)S(1)}, u32[]{:S(2)}, u32[]{:S(2)}) collective-permute-start(bf16[2,64,2176]{2,1,0:T(8,128)(2,1)} %add_convert_fusion.2), channel_id=1, source_target_pairs={{0,2},{1,3},{2,4},{3,5},{4,6},{5,7},{6,0},{7,1},{8,10},{9,11},{10,... | collective-permute-start | bytes 1671176 | tf_op jit(solution)/shard_map/ppermute | solution.py:57
  479.3 68.1 %collective-permute-start.71 = (bf16[2,4,64,2048]{3,2,1,0:T(8,128)(2,1)}, bf16[2,4,64,2048]{3,2,1,0:T(8,128)(2,1)}, u32[]{:S(2)}, u32[]{:S(2)}) collective-permute-start(bf16[2,4,64,2048]{3,2,1,0:T(8,128)(2,1)} %get-tuple-element.350), channel_id=1, source_target_pairs={{0,16},{8,24},{16,0},{24,8},{1,17},{9,25},{17,1},{25,9},{2,18},{10... | collective-permute-start | bytes 6291464 | tf_op jit(solution)/shard_map/ppermute | solution.py:31
  479.9 70.9 %collective-permute-start.73 = (bf16[2,4,64,2048]{3,2,1,0:T(8,128)(2,1)}, bf16[2,4,64,2048]{3,2,1,0:T(8,128)(2,1)}, u32[]{:S(2)}, u32[]{:S(2)}) collective-permute-start(bf16[2,4,64,2048]{3,2,1,0:T(8,128)(2,1)} %get-tuple-element.352), channel_id=1, source_target_pairs={{0,8},{8,0},{16,24},{24,16},{1,9},{9,1},{17,25},{25,17},{2,10},{10... | collective-permute-start | bytes 6291464 | tf_op jit(solution)/shard_map/ppermute | solution.py:31
  485.8 39.1 %collective-permute-start.76 = (bf16[4,256,512]{2,1,0:T(8,128)(2,1)}, bf16[4,256,512]{2,1,0:T(8,128)(2,1)S(1)}, u32[]{:S(2)}, u32[]{:S(2)}) collective-permute-start(bf16[4,256,512]{2,1,0:T(8,128)(2,1)} %get-tuple-element.360), channel_id=1, source_target_pairs={{0,1},{1,0},{2,3},{3,2},{4,5},{5,4},{6,7},{7,6},{8,9},{9,8},{10,11... | collective-permute-start | bytes 3145736 | tf_op jit(solution)/shard_map/ppermute | solution.py:48
  487.5 35.0 %collective-permute-start.79 = (bf16[4,64,512]{2,1,0:T(8,128)(2,1)}, bf16[4,64,512]{2,1,0:T(8,128)(2,1)S(1)}, u32[]{:S(2)}, u32[]{:S(2)}) collective-permute-start(bf16[4,64,512]{2,1,0:T(8,128)(2,1)} %fusion.37), channel_id=1, source_target_pairs={{0,2},{1,3},{2,4},{3,5},{4,6},{5,7},{6,0},{7,1},{8,10},{9,11},{10,... | collective-permute-start | bytes 786440 | tf_op jit(solution)/shard_map/ppermute | solution.py:57
  501.5 221.1 %all-gather.6.cloned.1.call-start = ((), (), s32[]{:S(2)}) async-start(), calls=%async_computation.3 | async-start | bytes 4718592 | tf_op jit(solution)/shard_map/all_gather | solution.py:1209
  501.5 60.6 %collective-permute-start.83 = (bf16[2,1,64,2048]{3,2,1,0:T(8,128)(2,1)}, bf16[2,1,64,2048]{3,2,1,0:T(8,128)(2,1)}, u32[]{:S(2)}, u32[]{:S(2)}) collective-permute-start(bf16[2,1,64,2048]{3,2,1,0:T(8,128)(2,1)} %bitcast.550), channel_id=1, source_target_pairs={{0,8},{8,0},{16,24},{24,16},{1,9},{9,1},{17,25},{25,17},{2,10},{10... | collective-permute-start | bytes 1572872 | tf_op jit(solution)/shard_map/ppermute | solution.py:31
  522.5 40.0 %collective-permute-start.82 = (bf16[2,1,64,2048]{3,2,1,0:T(8,128)(2,1)}, bf16[2,1,64,2048]{3,2,1,0:T(8,128)(2,1)}, u32[]{:S(2)}, u32[]{:S(2)}) collective-permute-start(bf16[2,1,64,2048]{3,2,1,0:T(8,128)(2,1)} %bitcast.549), channel_id=1, source_target_pairs={{0,16},{8,24},{16,0},{24,8},{1,17},{9,25},{17,1},{25,9},{2,18},{10... | collective-permute-start | bytes 1572872 | tf_op jit(solution)/shard_map/ppermute | solution.py:31
  524.8 18.7 %collective-permute-start.81 = (bf16[4,64,512]{2,1,0:T(8,128)(2,1)}, bf16[4,64,512]{2,1,0:T(8,128)(2,1)S(1)}, u32[]{:S(2)}, u32[]{:S(2)}) collective-permute-start(bf16[4,64,512]{2,1,0:T(8,128)(2,1)} %fusion.36), channel_id=1, source_target_pairs={{0,2},{1,3},{2,4},{3,5},{4,6},{5,7},{6,0},{7,1},{8,10},{9,11},{10,... | collective-permute-start | bytes 786440 | tf_op jit(solution)/shard_map/ppermute | solution.py:57
  547.4 41.6 %collective-permute-start.88 = (bf16[4,64,512]{2,1,0:T(8,128)(2,1)S(1)}, bf16[4,64,512]{2,1,0:T(8,128)(2,1)}, u32[]{:S(2)}, u32[]{:S(2)}) collective-permute-start(bf16[4,64,512]{2,1,0:T(8,128)(2,1)S(1)} %get-tuple-element.427), channel_id=1, source_target_pairs={{0,2},{1,3},{2,4},{3,5},{4,6},{5,7},{6,0},{7,1},{8,10},{9,11},{10,... | collective-permute-start | bytes 786440 | tf_op jit(solution)/shard_map/ppermute | solution.py:57
  550.8 45.4 %collective-permute-start.72 = (bf16[4,64,2048]{2,1,0:T(8,128)(2,1)}, bf16[4,64,2048]{2,1,0:T(8,128)(2,1)}, u32[]{:S(2)}, u32[]{:S(2)}) collective-permute-start(bf16[4,64,2048]{2,1,0:T(8,128)(2,1)} %fusion.16), channel_id=1, source_target_pairs={{0,8},{8,0},{16,24},{24,16},{1,9},{9,1},{17,25},{25,17},{2,10},{10... | collective-permute-start | bytes 3145736 | tf_op jit(solution)/shard_map/ppermute | solution.py:31
  560.6 36.8 %collective-permute-start.74 = (bf16[4,64,2048]{2,1,0:T(8,128)(2,1)}, bf16[4,64,2048]{2,1,0:T(8,128)(2,1)}, u32[]{:S(2)}, u32[]{:S(2)}) collective-permute-start(bf16[4,64,2048]{2,1,0:T(8,128)(2,1)} %fusion.17), channel_id=1, source_target_pairs={{0,16},{8,24},{16,0},{24,8},{1,17},{9,25},{17,1},{25,9},{2,18},{10... | collective-permute-start | bytes 3145736 | tf_op jit(solution)/shard_map/ppermute | solution.py:31
  562.1 22.6 %collective-permute-start.80 = (bf16[4,64,512]{2,1,0:T(8,128)(2,1)}, bf16[4,64,512]{2,1,0:T(8,128)(2,1)}, u32[]{:S(2)}, u32[]{:S(2)}) collective-permute-start(bf16[4,64,512]{2,1,0:T(8,128)(2,1)} %fusion.35), channel_id=1, source_target_pairs={{0,2},{1,3},{2,4},{3,5},{4,6},{5,7},{6,0},{7,1},{8,10},{9,11},{10,... | collective-permute-start | bytes 786440 | tf_op jit(solution)/shard_map/ppermute | solution.py:57
  589.1 29.5 %collective-permute-start.85 = (bf16[4,64,512]{2,1,0:T(8,128)(2,1)}, bf16[4,64,512]{2,1,0:T(8,128)(2,1)}, u32[]{:S(2)}, u32[]{:S(2)}) collective-permute-start(bf16[4,64,512]{2,1,0:T(8,128)(2,1)} %fusion.33), channel_id=1, source_target_pairs={{0,2},{1,3},{2,4},{3,5},{4,6},{5,7},{6,0},{7,1},{8,10},{9,11},{10,... | collective-permute-start | bytes 786440 | tf_op jit(solution)/shard_map/ppermute | solution.py:57
  590.0 57.1 %collective-permute-start.108 = (bf16[4,64,512]{2,1,0:T(8,128)(2,1)}, bf16[4,64,512]{2,1,0:T(8,128)(2,1)S(1)}, u32[]{:S(2)}, u32[]{:S(2)}) collective-permute-start(bf16[4,64,512]{2,1,0:T(8,128)(2,1)} %collective-permute-done.88), channel_id=1, source_target_pairs={{0,2},{1,3},{2,4},{3,5},{4,6},{5,7},{6,0},{7,1},{8,10},{9,11},{10,... | collective-permute-start | bytes 786440 | tf_op jit(solution)/shard_map/ppermute | solution.py:57
  599.4 34.3 %collective-permute-start.84 = (bf16[2,64,2048]{2,1,0:T(8,128)(2,1)}, bf16[2,64,2048]{2,1,0:T(8,128)(2,1)}, u32[]{:S(2)}, u32[]{:S(2)}) collective-permute-start(bf16[2,64,2048]{2,1,0:T(8,128)(2,1)} %pad_maximum_fusion.8), channel_id=1, source_target_pairs={{0,2},{1,3},{2,4},{3,5},{4,6},{5,7},{6,0},{7,1},{8,10},{9,11},{10,... | collective-permute-start | bytes 1572872 | tf_op jit(solution)/shard_map/ppermute | solution.py:57
  635.0 34.6 %collective-permute-start.97 = (bf16[2,64,2048]{2,1,0:T(8,128)(2,1)S(1)}, bf16[2,64,2048]{2,1,0:T(8,128)(2,1)S(1)}, u32[]{:S(2)}, u32[]{:S(2)}) collective-permute-start(bf16[2,64,2048]{2,1,0:T(8,128)(2,1)S(1)} %fusion.18), channel_id=1, source_target_pairs={{0,2},{1,3},{2,4},{3,5},{4,6},{5,7},{6,0},{7,1},{8,10},{9,11},{10,... | collective-permute-start | bytes 1572872 | tf_op jit(solution)/shard_map/ppermute | solution.py:57
  647.1 33.7 %collective-permute-start.102 = (bf16[4,64,512]{2,1,0:T(8,128)(2,1)S(1)}, bf16[4,64,512]{2,1,0:T(8,128)(2,1)S(1)}, u32[]{:S(2)}, u32[]{:S(2)}) collective-permute-start(bf16[4,64,512]{2,1,0:T(8,128)(2,1)S(1)} %collective-permute-done.101), channel_id=1, source_target_pairs={{0,2},{1,3},{2,4},{3,5},{4,6},{5,7},{6,0},{7,1},{8,10},{9,11},{10,... | collective-permute-start | bytes 786440 | tf_op jit(solution)/shard_map/ppermute | solution.py:57
  647.2 44.9 %collective-permute-start.109 = (bf16[4,64,512]{2,1,0:T(8,128)(2,1)S(1)}, bf16[4,64,512]{2,1,0:T(8,128)(2,1)S(1)}, u32[]{:S(2)}, u32[]{:S(2)}) collective-permute-start(bf16[4,64,512]{2,1,0:T(8,128)(2,1)S(1)} %collective-permute-done.108), channel_id=1, source_target_pairs={{0,2},{1,3},{2,4},{3,5},{4,6},{5,7},{6,0},{7,1},{8,10},{9,11},{10,... | collective-permute-start | bytes 786440 | tf_op jit(solution)/shard_map/ppermute | solution.py:57
  669.8 32.3 %collective-permute-start.98 = (bf16[2,64,2048]{2,1,0:T(8,128)(2,1)S(1)}, bf16[2,64,2048]{2,1,0:T(8,128)(2,1)S(1)}, u32[]{:S(2)}, u32[]{:S(2)}) collective-permute-start(bf16[2,64,2048]{2,1,0:T(8,128)(2,1)S(1)} %fusion.19), channel_id=1, source_target_pairs={{0,2},{1,3},{2,4},{3,5},{4,6},{5,7},{6,0},{7,1},{8,10},{9,11},{10,... | collective-permute-start | bytes 1572872 | tf_op jit(solution)/shard_map/ppermute | solution.py:57
  680.9 24.0 %collective-permute-start.103 = (bf16[4,64,512]{2,1,0:T(8,128)(2,1)S(1)}, bf16[4,64,512]{2,1,0:T(8,128)(2,1)S(1)}, u32[]{:S(2)}, u32[]{:S(2)}) collective-permute-start(bf16[4,64,512]{2,1,0:T(8,128)(2,1)S(1)} %collective-permute-done.102), channel_id=1, source_target_pairs={{0,2},{1,3},{2,4},{3,5},{4,6},{5,7},{6,0},{7,1},{8,10},{9,11},{10,... | collective-permute-start | bytes 786440 | tf_op jit(solution)/shard_map/ppermute | solution.py:57
  (131 other events, 1228.4 us)
Sparse Core Ops, SparseCore 0:
  11.4 139.4 all-gather.3
  501.6 64.7 reduce-scatter.1
  618.7 75.9 all-gather.5

commit v6 on v5

--- a/solution.py
+++ b/solution.py
@@ -1031,7 +1031,7 @@
     scaled_sides = [
         jnp.concatenate([g[3][side : side + 1] for g in groups]) for side in range(2)
     ]
-    mix_passed = swap_core(mix_call(after(scaled_sides[1], ring_total), down_w))
+    mix_passed = swap_core(mix_call(after(scaled_sides[1], ring_total, back_terms[0]), down_w))
 
     ring_total = ring_up(ring_total)
     grad_res, grad_res_b, grad_gain_two, grad_router = call(

time: 743 us -> 748 us (level)
  transfers between devices with their start and end apart: 114 -> 114, of which waited for: 53 -> 50; matrix products, arithmetic and copies ran while one was open for 14% -> 14% of each run, Pallas kernels for 32% -> 32%
where the time goes in v6:
time: 748 us; the launch traced here: 743 us
  Pallas kernels  251 us (34%)
  waiting for transfers between devices  242 us (32%)
  starting transfers between devices  106 us (14%)
  other arithmetic  74.4 us (10%)
  local copies, waits for them, and re-layouts  54.4 us (7%)
  between operations  15.5 us (2%)
    ppermute x71, waiting for transfers between devices, flip_shard(): return lax.ppermute(values, 'shard', [(i, i ^ bit) for i in range(count)])  149 us
    ppermute x21, waiting for transfers between devices, ring_up(): lax.ppermute(values, 'expert', [(i, (i + 2) % count) for i in range(count)])  84.5 us
    pallas_call x4, Pallas kernels, expert_call(): pl.pallas_call(lambda *refs: expert_kernel(experts_all, *refs), grid_spec...  77.2 us
    ppermute x71, starting transfers between devices, flip_shard(): return lax.ppermute(values, 'shard', [(i, i ^ bit) for i in range(count)])  72 us
    pallas_call x9, Pallas kernels, call(): pl.pallas_call(kernel, in_specs=[scalars() if n in smem else whole(a.shap...  68.4 us
    ppermute x21, starting transfers between devices, ring_up(): lax.ppermute(values, 'expert', [(i, (i + 2) % count) for i in range(count)])  31.8 us
    pallas_call x2, Pallas kernels, row_grad_call(): pl.pallas_call(lambda *refs: row_grad_kernel(len(rows), *refs), grid=(wid...  31.7 us
    pallas_call x2, Pallas kernels, mix_call(): pl.pallas_call(mix_kernel, grid=(chips,), in_specs=[pl.BlockSpec((1, coun...  19.4 us
  transfers between devices with their start and end apart: 114, of which 50 were waited for; matrix products, arithmetic and copies ran while one was open for 14% of the time, Pallas kernels for 32%

profile of v6, /device:TPU:0, one launch (start us, length us, event | category | flops | bytes accessed | tf_op | source)
XLA Modules:
  0.0 742.8 jit_solution(15494922087589108493)
XLA Ops:
  10.6 3.0 collective-permute-start
  17.0 2.9 collective-permute-start.6
  20.6 5.0 cut.1
  32.1 6.5 flip.1
  40.0 42.0 %collective-permute-done.3 = bf16[2,1,64,2048]{3,2,0,1:T(8,128)(2,1)} collective-permute-done((bf16[2,1,64,2048]{3,2,0,1:T(8,128)(2,1)S(1)}, bf16[2,1,64,2048]{3,2,0,1:T(8,128)(2,1)}, u32[]{:S(2)}, u32[]{:S(2)}) %collective-permute-start.3) | collective-permute-done | bytes 524320 | tf_op jit(solution)/shard_map/ppermute | solution.py:31
  89.1 3.7 collective-permute-done.9
  101.2 9.7 %project.1 = (bf16[512,2048]{1,0:T(8,128)(2,1)}, f32[512,1536]{1,0:T(8,128)}, f32[4,8,128]{2,1,0:T(8,128)}, f32[512,128]{1,0:T(8,128)}) custom-call(s32[8]{0:T(128)} %stack.264.at_ref, bf16[2,64,2048]{2,1,0:T(8,128)(2,1)} %get-tuple-element.519.r0, bf16[2,64,2048]{2,1,0:T(8,128)(2,1)} %bitcast.13.r1, bf16[2,64,2048]{2,1,0:T(8,128)(2,1)} %get-tuple-element.513.r2, ...), custom_call_target="tpu_custom_call" | custom-call | flops 3221225472 | bytes 13918240 | tf_op jit(solution)/shard_map/project/pallas_call | solution.py:160
  118.1 9.9 %attend.1 = (bf16[512,512]{1,0:T(8,128)(2,1)}, bf16[512,512]{1,0:T(8,128)(2,1)}, bf16[512,512]{1,0:T(8,128)(2,1)}, f32[512,128]{1,0:T(8,128)}, f32[512,128]{1,0:...) custom-call(f32[512,1536]{1,0:T(8,128)} %get-tuple-element.370.refs_, ...), custom_call_target="tpu_custom_call" | custom-call | flops 1610612736 | bytes 11603968 | tf_op jit(solution)/shard_map/attend/pallas_call | solution.py:160
  132.8 8.3 %collective-permute-done.18 = bf16[2,1,64,2048]{3,2,1,0:T(8,128)(2,1)S(1)} collective-permute-done((bf16[2,1,64,2048]{3,2,1,0:T(8,128)(2,1)}, bf16[2,1,64,2048]{3,2,1,0:T(8,128)(2,1)S(1)}, u32[]{:S(2)}, u32[]{:S(2)}) %collective-permute-start.18) | collective-permute-done | bytes 524320 | tf_op jit(solution)/shard_map/ppermute | solution.py:31
  152.1 3.0 settle.1
  159.4 4.0 collective-permute-done.21
  163.5 3.0 collective-permute-done.22
  167.3 16.1 %lead.1.refs_4_ = f32[4,2,8,64,512]{4,3,2,1,0:T(8,128)} custom-call(bf16[4,4,2,2,64,2176]{5,4,3,2,1,0:T(8,128)(2,1)} %bitcast.472, bf16[2048,512]{1,0:T(8,128)(2,1)} %get-tuple-element.240.down_t_ref), custom_call_target="tpu_custom_call" | custom-call | flops 8589934592 | bytes 26214400 | tf_op jit(solution)/shard_map/lead/pallas_call | solution.py:311
  197.4 12.1 %collective-permute-done.27 = bf16[2,64,2048]{2,1,0:T(8,128)(2,1)S(1)} collective-permute-done((bf16[2,64,2048]{2,1,0:T(8,128)(2,1)S(1)}, bf16[2,64,2048]{2,1,0:T(8,128)(2,1)S(1)}, u32[]{:S(2)}, u32[]{:S(2)}) %collective-permute-start.27) | collective-permute-done | bytes 524320 | tf_op jit(solution)/shard_map/ppermute | solution.py:57
  214.2 7.7 %collective-permute-done.29 = bf16[2,64,2048]{2,1,0:T(8,128)(2,1)} collective-permute-done((bf16[2,64,2048]{2,1,0:T(8,128)(2,1)S(1)}, bf16[2,64,2048]{2,1,0:T(8,128)(2,1)}, u32[]{:S(2)}, u32[]{:S(2)}) %collective-permute-start.29) | collective-permute-done | bytes 524320 | tf_op jit(solution)/shard_map/ppermute | solution.py:31
  227.7 19.1 %experts.4 = (bf16[2,1,64,2176]{3,2,1,0:T(8,128)(2,1)S(1)}, bf16[2,1,64,2176]{3,2,1,0:T(8,128)(2,1)S(1)}, bf16[2,1,64,2176]{3,2,1,0:T(8,128)(2,1)S(1)}, bf16[2,1...) custom-call(s32[4]{0:T(128)S(1)} %get-tuple-element.242.refs_0_, ...), custom_call_target="tpu_custom_call" | custom-call | flops 8589934592 | bytes 22020096 | tf_op jit(solution)/shard_map/experts/pallas_call | solution.py:442
  255.9 19.3 %experts.5 = (bf16[2,1,64,2176]{3,2,1,0:T(8,128)(2,1)S(1)}, bf16[2,1,64,2176]{3,2,1,0:T(8,128)(2,1)S(1)}, bf16[2,1,64,2176]{3,2,1,0:T(8,128)(2,1)S(1)}, bf16[2,1...) custom-call(s32[4]{0:T(128)S(1)} %get-tuple-element.244.refs_0_, ...), custom_call_target="tpu_custom_call" | custom-call | flops 8589934592 | bytes 22020096 | tf_op jit(solution)/shard_map/experts/pallas_call | solution.py:442
  281.3 19.2 %experts.6 = (bf16[2,1,64,2176]{3,2,1,0:T(8,128)(2,1)S(1)}, bf16[2,1,64,2176]{3,2,1,0:T(8,128)(2,1)S(1)}, bf16[2,1,64,2176]{3,2,1,0:T(8,128)(2,1)S(1)}, bf16[2,1...) custom-call(s32[4]{0:T(128)S(1)} %get-tuple-element.251.refs_0_, ...), custom_call_target="tpu_custom_call" | custom-call | flops 8589934592 | bytes 22020096 | tf_op jit(solution)/shard_map/experts/pallas_call | solution.py:442
  308.1 19.6 %experts.7 = (bf16[2,1,64,2176]{3,2,1,0:T(8,128)(2,1)S(1)}, bf16[2,1,64,2176]{3,2,1,0:T(8,128)(2,1)S(1)}, bf16[2,1,64,2176]{3,2,1,0:T(8,128)(2,1)S(1)}, bf16[2,1...) custom-call(s32[4]{0:T(128)S(1)} %get-tuple-element.261.refs_0_, ...), custom_call_target="tpu_custom_call" | custom-call | flops 8589934592 | bytes 22020096 | tf_op jit(solution)/shard_map/experts/pallas_call | solution.py:442
  335.7 8.9 %collective-permute-done.50 = bf16[2,1,64,2176]{3,2,1,0:T(8,128)(2,1)S(1)} collective-permute-done((bf16[2,1,64,2176]{3,2,1,0:T(8,128)(2,1)S(1)}, bf16[2,1,64,2176]{3,2,1,0:T(8,128)(2,1)S(1)}, u32[]{:S(2)}, u32[]{:S(2)}) %collective-permute-start.50) | collective-permute-done | bytes 557088 | tf_op jit(solution)/shard_map/ppermute | solution.py:31
  344.8 4.8 collective-permute-done.44
  355.1 14.8 %collective-permute-done.51 = bf16[1,64,2176]{2,1,0:T(8,128)(2,1)S(1)} collective-permute-done((bf16[1,64,2176]{2,1,0:T(8,128)(2,1)S(1)}, bf16[1,64,2176]{2,1,0:T(8,128)(2,1)S(1)}, u32[]{:S(2)}, u32[]{:S(2)}) %collective-permute-start.51) | collective-permute-done | bytes 278560 | tf_op jit(solution)/shard_map/ppermute | solution.py:31
  378.6 11.0 %collective-permute-done.57 = bf16[1,64,2176]{2,1,0:T(8,128)(2,1)S(1)} collective-permute-done((bf16[1,64,2176]{2,1,0:T(8,128)(2,1)S(1)}, bf16[1,64,2176]{2,1,0:T(8,128)(2,1)S(1)}, u32[]{:S(2)}, u32[]{:S(2)}) %collective-permute-start.57) | collective-permute-done | bytes 278560 | tf_op jit(solution)/shard_map/ppermute | solution.py:31
  394.2 3.2 collective-permute-done.62
  399.0 8.5 %mix.2 = bf16[4,2,4,64,2048]{4,3,2,1,0:T(8,128)(2,1)} custom-call(bf16[4,512,512]{2,1,0:T(8,128)(2,1)} %pad_maximum_fusion.1.scaled_ref, bf16[512,2048]{1,0:T(8,128)(2,1)} %bitcast.503), custom_call_target="tpu_custom_call" | custom-call | flops 4294967296 | bytes 20971520 | tf_op jit(solution)/shard_map/mix/pallas_call | solution.py:513
  409.2 15.2 %collective-permute-done.58.refs_0_ = bf16[2,64,2176]{2,1,0:T(8,128)(2,1)S(1)} collective-permute-done((bf16[2,64,2176]{2,1,0:T(8,128)(2,1)S(1)}, bf16[2,64,2176]{2,1,0:T(8,128)(2,1)S(1)}, u32[]{:S(2)}, u32[]{:S(2)}) %collective-permute-start.58) | collective-permute-done | bytes 557088 | tf_op jit(solution)/shard_map/ppermute | solution.py:57
  425.2 5.4 turn.1
  433.2 6.6 collective-permute-done.64
  444.5 10.9 %mix.3 = (bf16[2,4,64,2048]{3,2,1,0:T(8,128)(2,1)}, bf16[2,4,64,2048]{3,2,1,0:T(8,128)(2,1)}, bf16[2,4,64,2048]{3,2,1,0:T(8,128)(2,1)}, bf16[2,4,64,2048]{3,2,1,0:T(8,128)(2,1)}) custom-call(bf16[4,512,512]{2,1,0:T(8,128)(2,1)} %pad_maximum_fusion.scaled_ref, bf16[512,2048]{1,0:T(8,128)(2,1)} %bitcast.504, ...), custom_call_target="tpu_custom_call" | custom-call | flops 4294967296 | bytes 20971520 | tf_op jit(solution)/shard_map/mix/pallas_call | solution.py:513
  456.4 4.5 output_grad.1
  460.9 14.4 %attend_back.1 = (f32[512,512]{1,0:T(8,128)}, f32[512,512]{1,0:T(8,128)}, bf16[512,512]{1,0:T(8,128)(2,1)}, f32[4,8,128]{2,1,0:T(8,128)}, f32[8,512]{1,0:T(8,128)}, /*index=5*/bf16[512,2048]{1,0:T(8,128)(2,1)}) custom-call(bf16[2,64,2048]{2,1,0:T(8,128)(2,1)} %get-tuple-element.339.g0, bf16[2,64,2048]{2,1,0:T(8,128)(2,1)} %bitcast.524, ...), custom_call_target="tpu_custom_call" | custom-call | flops 2415919104 | bytes 16289792 | tf_op jit(solution)/shard_map/attend_back/pallas_call | solution.py:160
  486.5 4.6 value_back.1
  493.6 13.1 %project_back.1 = (bf16[2,64,2048]{2,1,0:T(8,128)(2,1)}, bf16[2,64,2048]{2,1,0:T(8,128)(2,1)}, bf16[2,64,2048]{2,1,0:T(8,128)(2,1)}, bf16[2,64,2048]{2,1,0:T(8,1...) custom-call(s32[8]{0:T(128)} %stack.264.at_ref, f32[4,8,128]{2,1,0:T(8,128)} %get-tuple-element.348.s0, ...), custom_call_target="tpu_custom_call" | custom-call | flops 6442450944 | bytes 22347808 | tf_op jit(solution)/shard_map/project_back/pallas_call | solution.py:160
  507.7 16.5 %down_grads.1 = f32[2,256,2048]{2,1,0:T(8,128)} custom-call(s32[5]{0:T(128)} %stack.313.refs_0_, bf16[2,8,64,512]{3,2,1,0:T(8,128)(2,1)} %copy-done.1, bf16[2,8,64,512]{3,2,1,0:T(8,128)(2,1)} %copy-done.2, bf16[2,8,64,512]{3,2,1,0:T(8,128)(2,1)} %copy-done.3, bf16[2,8,64,512]{3,2,1,0:T(8,128)(2,1)} %copy-done.4, bf16[4,4,2,2,64,2176]{5,4,3,2,1,0:T(8,128)(2,1)} %bitcast.477, ...), custom_call_target="tpu_custom_call" | custom-call | flops 8589934592 | bytes 25165824 | tf_op jit(solution)/shard_map/down_grads/pallas_call | solution.py:590
  532.5 16.0 %row_grads.2 = f32[2,2048,256]{2,1,0:T(8,128)} custom-call(bf16[8,64,2048]{2,1,0:T(8,128)(2,1)} %join.4.refs_1_.refs_0_, bf16[8,64,2048]{2,1,0:T(8,128)(2,1)} %collective-permute-done.32.refs_2_.refs_1_, bf16[8,64,2048]{2,1,0:T(8,128)(2,1)} %join.5.refs_1_.refs_2_, bf16[8,64,2048]{2,1,0:T(8,128)(2,1)} %collective-permute-done.35.refs_2_.refs_3_, ...), custom_call_target="tpu_custom_call" | custom-call | flops 8589934592 | bytes 25165824 | tf_op jit(solution)/shard_map/row_grads/pallas_call | solution.py:549
  559.0 6.6 collective-permute-done.78
  571.5 15.8 %row_grads.3 = f32[2,2048,256]{2,1,0:T(8,128)} custom-call(bf16[8,64,2048]{2,1,0:T(8,128)(2,1)} %join.4.refs_1_.refs_0_, bf16[8,64,2048]{2,1,0:T(8,128)(2,1)} %collective-permute-done.32.refs_2_.refs_1_, bf16[8,64,2048]{2,1,0:T(8,128)(2,1)} %join.5.refs_1_.refs_2_, bf16[8,64,2048]{2,1,0:T(8,128)(2,1)} %collective-permute-done.35.refs_2_.refs_3_, ...), custom_call_target="tpu_custom_call" | custom-call | flops 8589934592 | bytes 25165824 | tf_op jit(solution)/shard_map/row_grads/pallas_call | solution.py:549
  596.6 3.8 finish.1
  644.3 3.2 collective-permute-done.100
  647.5 4.3 collective-permute-done.101
  653.3 3.4 collective-permute-start.109
  656.7 17.6 %collective-permute-done.97 = bf16[2,64,2048]{2,1,0:T(8,128)(2,1)S(1)} collective-permute-done((bf16[2,64,2048]{2,1,0:T(8,128)(2,1)S(1)}, bf16[2,64,2048]{2,1,0:T(8,128)(2,1)S(1)}, u32[]{:S(2)}, u32[]{:S(2)}) %collective-permute-start.97) | collective-permute-done | bytes 524320 | tf_op jit(solution)/shard_map/ppermute | solution.py:57
  674.4 5.2 collective-permute-start.98
  679.6 5.9 collective-permute-done.102
  687.6 9.1 %collective-permute-done.109 = bf16[4,64,512]{2,1,0:T(8,128)(2,1)S(1)} collective-permute-done((bf16[4,64,512]{2,1,0:T(8,128)(2,1)S(1)}, bf16[4,64,512]{2,1,0:T(8,128)(2,1)S(1)}, u32[]{:S(2)}, u32[]{:S(2)}) %collective-permute-start.109) | collective-permute-done | bytes 262176 | tf_op jit(solution)/shard_map/ppermute | solution.py:57
  696.7 10.2 %collective-permute-done.98 = bf16[2,64,2048]{2,1,0:T(8,128)(2,1)S(1)} collective-permute-done((bf16[2,64,2048]{2,1,0:T(8,128)(2,1)S(1)}, bf16[2,64,2048]{2,1,0:T(8,128)(2,1)S(1)}, u32[]{:S(2)}, u32[]{:S(2)}) %collective-permute-start.98) | collective-permute-done | bytes 524320 | tf_op jit(solution)/shard_map/ppermute | solution.py:57
  711.3 3.8 collective-permute-done.105
  716.4 3.8 collective-permute-done.106
  (534 shorter events, 262.5 us)
Async XLA Ops:
  7.2 160.1 %all-gather.4.cloned.1.call-start = ((), (), s32[]{:S(2)}) async-start(), calls=%async_computation.1 | async-start | bytes 18382848 | tf_op jit(solution)/shard_map/all_gather | solution.py:908
  10.4 596.5 %reduce-scatter.2.cloned.1.call-start = ((), (), s32[]{:S(2)}) async-start(), calls=%async_computation.2 | async-start | bytes 4718592 | tf_op jit(solution)/shard_map/reduce_scatter | solution.py:1153
  28.0 54.0 %collective-permute-start.7 = (bf16[384,1536]{1,0:T(8,128)(2,1)}, bf16[384,1536]{1,0:T(8,128)(2,1)S(1)}, u32[]{:S(2)}, u32[]{:S(2)}) collective-permute-start(bf16[384,1536]{1,0:T(8,128)(2,1)} %get-tuple-element.224), channel_id=1, source_target_pairs={{0,8},{8,0},{16,24},{24,16},{1,9},{9,1},{17,25},{25,17},{2,10},{10... | collective-permute-start | bytes 3538952 | tf_op jit(solution)/shard_map/ppermute | solution.py:31
  28.3 53.7 %collective-permute-start.8 = (bf16[384,1536]{1,0:T(8,128)(2,1)}, bf16[384,1536]{1,0:T(8,128)(2,1)S(1)}, u32[]{:S(2)}, u32[]{:S(2)}) collective-permute-start(bf16[384,1536]{1,0:T(8,128)(2,1)} %get-tuple-element.225), channel_id=1, source_target_pairs={{0,16},{8,24},{16,0},{24,8},{1,17},{9,25},{17,1},{25,9},{2,18},{10... | collective-permute-start | bytes 3538952 | tf_op jit(solution)/shard_map/ppermute | solution.py:31
  28.4 53.6 %collective-permute-start.3 = (bf16[2,1,64,2048]{3,2,0,1:T(8,128)(2,1)S(1)}, bf16[2,1,64,2048]{3,2,0,1:T(8,128)(2,1)}, u32[]{:S(2)}, u32[]{:S(2)}) collective-permute-start(bf16[2,1,64,2048]{3,2,0,1:T(8,128)(2,1)S(1)} %get-tuple-element.512), channel_id=1, source_target_pairs={{0,8},{8,0},{16,24},{24,16},{1,9},{9,1},{17,25},{25,17},{2,10},{10... | collective-permute-start | bytes 1572872 | tf_op jit(solution)/shard_map/ppermute | solution.py:31
  30.4 51.6 %collective-permute-start.1 = (bf16[2,1,64,2048]{3,2,0,1:T(8,128)(2,1)S(1)}, bf16[2,1,64,2048]{3,2,0,1:T(8,128)(2,1)}, u32[]{:S(2)}, u32[]{:S(2)}) collective-permute-start(bf16[2,1,64,2048]{3,2,0,1:T(8,128)(2,1)S(1)} %get-tuple-element.518), channel_id=1, source_target_pairs={{0,16},{8,24},{16,0},{24,8},{1,17},{9,25},{17,1},{25,9},{2,18},{10... | collective-permute-start | bytes 1572872 | tf_op jit(solution)/shard_map/ppermute | solution.py:31
  157.8 25.7 %collective-permute-start.23 = (bf16[2,64,2048]{2,1,0:T(8,128)(2,1)}, bf16[2,64,2048]{2,1,0:T(8,128)(2,1)S(1)}, u32[]{:S(2)}, u32[]{:S(2)}) collective-permute-start(bf16[2,64,2048]{2,1,0:T(8,128)(2,1)} %get-tuple-element.238.refs_9_), channel_id=1, source_target_pairs={{0,2},{1,3},{2,4},{3,5},{4,6},{5,7},{6,0},{7,1},{8,10},{9,11},{10,... | collective-permute-start | bytes 1572872 | tf_op jit(solution)/shard_map/ppermute | solution.py:57
  163.4 23.7 %collective-permute-start.30 = (bf16[2,1,64,2048]{3,2,1,0:T(8,128)(2,1)S(1)}, bf16[2,1,64,2048]{3,2,1,0:T(8,128)(2,1)S(1)}, u32[]{:S(2)}, u32[]{:S(2)}) collective-permute-start(bf16[2,1,64,2048]{3,2,1,0:T(8,128)(2,1)S(1)} %pad_maximum_fusion.12.a_ref), channel_id=1, source_target_pairs={{0,16},{8,24},{16,0},{24,8},{1,17},{9,25},{17,1},{25,9},{2,18},{10... | collective-permute-start | bytes 1572872 | tf_op jit(solution)/shard_map/ppermute | solution.py:31
  166.5 20.5 %collective-permute-start.31 = (bf16[2,1,64,2048]{3,2,1,0:T(8,128)(2,1)S(1)}, bf16[2,1,64,2048]{3,2,1,0:T(8,128)(2,1)}, u32[]{:S(2)}, u32[]{:S(2)}) collective-permute-start(bf16[2,1,64,2048]{3,2,1,0:T(8,128)(2,1)S(1)} %pad_maximum_fusion.13.c_ref), channel_id=1, source_target_pairs={{0,8},{8,0},{16,24},{24,16},{1,9},{9,1},{17,25},{25,17},{2,10},{10... | collective-permute-start | bytes 1572872 | tf_op jit(solution)/shard_map/ppermute | solution.py:31
  190.4 37.2 %collective-permute-start.32 = (bf16[8,64,2048]{2,1,0:T(8,128)(2,1)}, bf16[8,64,2048]{2,1,0:T(8,128)(2,1)}, u32[]{:S(2)}, u32[]{:S(2)}) collective-permute-start(bf16[8,64,2048]{2,1,0:T(8,128)(2,1)} %join.4.refs_1_.refs_0_), channel_id=1, source_target_pairs={{0,1},{1,0},{2,3},{3,2},{4,5},{5,4},{6,7},{7,6},{8,9},{9,8},{10,11... | collective-permute-start | bytes 6291464 | tf_op jit(solution)/shard_map/ppermute | solution.py:48
  193.1 18.5 %collective-permute-start.33 = (bf16[2,1,64,2048]{3,2,1,0:T(8,128)(2,1)S(1)}, bf16[2,1,64,2048]{3,2,1,0:T(8,128)(2,1)}, u32[]{:S(2)}, u32[]{:S(2)}) collective-permute-start(bf16[2,1,64,2048]{3,2,1,0:T(8,128)(2,1)S(1)} %pad_maximum_fusion.14.a_ref), channel_id=1, source_target_pairs={{0,16},{8,24},{16,0},{24,8},{1,17},{9,25},{17,1},{25,9},{2,18},{10... | collective-permute-start | bytes 1572872 | tf_op jit(solution)/shard_map/ppermute | solution.py:31
  214.2 41.7 %collective-permute-start.35 = (bf16[8,64,2048]{2,1,0:T(8,128)(2,1)}, bf16[8,64,2048]{2,1,0:T(8,128)(2,1)}, u32[]{:S(2)}, u32[]{:S(2)}) collective-permute-start(bf16[8,64,2048]{2,1,0:T(8,128)(2,1)} %join.5.refs_1_.refs_2_), channel_id=1, source_target_pairs={{0,1},{1,0},{2,3},{3,2},{4,5},{5,4},{6,7},{7,6},{8,9},{9,8},{10,11... | collective-permute-start | bytes 6291464 | tf_op jit(solution)/shard_map/ppermute | solution.py:48
  226.2 22.9 %collective-permute-start.37 = (bf16[2,2,64,2048]{3,2,1,0:T(8,128)(2,1)}, bf16[2,2,64,2048]{3,2,1,0:T(8,128)(2,1)}, u32[]{:S(2)}, u32[]{:S(2)}) collective-permute-start(bf16[2,2,64,2048]{3,2,1,0:T(8,128)(2,1)} %pad_maximum_fusion.6.a_ref), channel_id=1, source_target_pairs={{0,16},{8,24},{16,0},{24,8},{1,17},{9,25},{17,1},{25,9},{2,18},{10... | collective-permute-start | bytes 3145736 | tf_op jit(solution)/shard_map/ppermute | solution.py:31
  226.5 22.6 %collective-permute-start.38 = (bf16[2,2,64,2048]{3,2,1,0:T(8,128)(2,1)}, bf16[2,2,64,2048]{3,2,1,0:T(8,128)(2,1)}, u32[]{:S(2)}, u32[]{:S(2)}) collective-permute-start(bf16[2,2,64,2048]{3,2,1,0:T(8,128)(2,1)} %pad_maximum_fusion.7.c_ref), channel_id=1, source_target_pairs={{0,8},{8,0},{16,24},{24,16},{1,9},{9,1},{17,25},{25,17},{2,10},{10... | collective-permute-start | bytes 3145736 | tf_op jit(solution)/shard_map/ppermute | solution.py:31
  248.6 27.5 %collective-permute-start.36 = (bf16[4,2,1,64,2176]{4,3,1,2,0:T(8,128)(2,1)}, bf16[4,2,1,64,2176]{4,3,1,2,0:T(8,128)(2,1)}, u32[]{:S(2)}, u32[]{:S(2)}) collective-permute-start(bf16[4,2,1,64,2176]{4,3,1,2,0:T(8,128)(2,1)} %bitcast.545), channel_id=1, source_target_pairs={{0,1},{1,0},{2,3},{3,2},{4,5},{5,4},{6,7},{7,6},{8,9},{9,8},{10,11... | collective-permute-start | bytes 6684680 | tf_op jit(solution)/shard_map/ppermute | solution.py:48
  251.7 24.4 %collective-permute-start.39 = (bf16[8,64,2048]{2,1,0:T(8,128)(2,1)}, bf16[8,64,2048]{2,1,0:T(8,128)(2,1)}, u32[]{:S(2)}, u32[]{:S(2)}) collective-permute-start(bf16[8,64,2048]{2,1,0:T(8,128)(2,1)} %join.6.refs_1_.refs_4_), channel_id=1, source_target_pairs={{0,1},{1,0},{2,3},{3,2},{4,5},{5,4},{6,7},{7,6},{8,9},{9,8},{10,11... | collective-permute-start | bytes 6291464 | tf_op jit(solution)/shard_map/ppermute | solution.py:48
  255.4 45.1 %collective-permute-start.41 = (bf16[8,64,2048]{2,1,0:T(8,128)(2,1)}, bf16[8,64,2048]{2,1,0:T(8,128)(2,1)S(1)}, u32[]{:S(2)}, u32[]{:S(2)}) collective-permute-start(bf16[8,64,2048]{2,1,0:T(8,128)(2,1)} %join.7.refs_1_.refs_6_), channel_id=1, source_target_pairs={{0,1},{1,0},{2,3},{3,2},{4,5},{5,4},{6,7},{7,6},{8,9},{9,8},{10,11... | collective-permute-start | bytes 6291464 | tf_op jit(solution)/shard_map/ppermute | solution.py:48
  276.1 26.6 %collective-permute-start.40 = (bf16[4,2,1,64,2176]{4,3,1,2,0:T(8,128)(2,1)}, bf16[4,2,1,64,2176]{4,3,1,2,0:T(8,128)(2,1)S(1)}, u32[]{:S(2)}, u32[]{:S(2)}) collective-permute-start(bf16[4,2,1,64,2176]{4,3,1,2,0:T(8,128)(2,1)} %bitcast.548), channel_id=1, source_target_pairs={{0,1},{1,0},{2,3},{3,2},{4,5},{5,4},{6,7},{7,6},{8,9},{9,8},{10,11... | collective-permute-start | bytes 6684680 | tf_op jit(solution)/shard_map/ppermute | solution.py:48
  301.8 26.0 %collective-permute-start.48 = (bf16[4,2,1,64,2176]{4,3,1,2,0:T(8,128)(2,1)}, bf16[4,2,1,64,2176]{4,3,1,2,0:T(8,128)(2,1)S(1)}, u32[]{:S(2)}, u32[]{:S(2)}) collective-permute-start(bf16[4,2,1,64,2176]{4,3,1,2,0:T(8,128)(2,1)} %bitcast.547), channel_id=1, source_target_pairs={{0,1},{1,0},{2,3},{3,2},{4,5},{5,4},{6,7},{7,6},{8,9},{9,8},{10,11... | collective-permute-start | bytes 6684680 | tf_op jit(solution)/shard_map/ppermute | solution.py:48
  304.3 27.0 %collective-permute-start.43 = (bf16[2,1,64,2176]{3,2,1,0:T(8,128)(2,1)}, bf16[2,1,64,2176]{3,2,1,0:T(8,128)(2,1)S(1)}, u32[]{:S(2)}, u32[]{:S(2)}) collective-permute-start(bf16[2,1,64,2176]{3,2,1,0:T(8,128)(2,1)} %bitcast.83), channel_id=1, source_target_pairs={{0,8},{8,0},{16,24},{24,16},{1,9},{9,1},{17,25},{25,17},{2,10},{10... | collective-permute-start | bytes 1671176 | tf_op jit(solution)/shard_map/ppermute | solution.py:31
  306.4 25.0 %collective-permute-start.42 = (bf16[2,1,64,2176]{3,2,0,1:T(8,128)(2,1)}, bf16[2,1,64,2176]{3,2,0,1:T(8,128)(2,1)S(1)}, u32[]{:S(2)}, u32[]{:S(2)}) collective-permute-start(bf16[2,1,64,2176]{3,2,0,1:T(8,128)(2,1)} %get-tuple-element.264), channel_id=1, source_target_pairs={{0,16},{8,24},{16,0},{24,8},{1,17},{9,25},{17,1},{25,9},{2,18},{10... | collective-permute-start | bytes 1671176 | tf_op jit(solution)/shard_map/ppermute | solution.py:31
  331.4 18.1 %collective-permute-start.44 = (bf16[1,64,2176]{2,1,0:T(8,128)(2,1)S(1)}, bf16[1,64,2176]{2,1,0:T(8,128)(2,1)S(1)}, u32[]{:S(2)}, u32[]{:S(2)}) collective-permute-start(bf16[1,64,2176]{2,1,0:T(8,128)(2,1)S(1)} %fusion.42), channel_id=1, source_target_pairs={{0,8},{8,0},{16,24},{24,16},{1,9},{9,1},{17,25},{25,17},{2,10},{10... | collective-permute-start | bytes 835592 | tf_op jit(solution)/shard_map/ppermute | solution.py:31
  350.0 23.6 %collective-permute-start.47 = (bf16[2,64,2176]{2,1,0:T(8,128)(2,1)S(1)}, bf16[2,64,2176]{2,1,0:T(8,128)(2,1)S(1)}, u32[]{:S(2)}, u32[]{:S(2)}) collective-permute-start(bf16[2,64,2176]{2,1,0:T(8,128)(2,1)S(1)} %fusion.68), channel_id=1, source_target_pairs={{0,2},{1,3},{2,4},{3,5},{4,6},{5,7},{6,0},{7,1},{8,10},{9,11},{10,... | collective-permute-start | bytes 1671176 | tf_op jit(solution)/shard_map/ppermute | solution.py:57
  350.9 22.8 %collective-permute-start.55 = (bf16[2,1,64,2176]{3,2,1,0:T(8,128)(2,1)S(1)}, bf16[2,1,64,2176]{3,2,1,0:T(8,128)(2,1)S(1)}, u32[]{:S(2)}, u32[]{:S(2)}) collective-permute-start(bf16[2,1,64,2176]{3,2,1,0:T(8,128)(2,1)S(1)} %bitcast.514), channel_id=1, source_target_pairs={{0,8},{8,0},{16,24},{24,16},{1,9},{9,1},{17,25},{25,17},{2,10},{10... | collective-permute-start | bytes 1671176 | tf_op jit(solution)/shard_map/ppermute | solution.py:31
  352.1 21.6 %collective-permute-start.54 = (bf16[2,1,64,2176]{3,2,0,1:T(8,128)(2,1)S(1)}, bf16[2,1,64,2176]{3,2,0,1:T(8,128)(2,1)S(1)}, u32[]{:S(2)}, u32[]{:S(2)}) collective-permute-start(bf16[2,1,64,2176]{3,2,0,1:T(8,128)(2,1)S(1)} %get-tuple-element.299), channel_id=1, source_target_pairs={{0,16},{8,24},{16,0},{24,8},{1,17},{9,25},{17,1},{25,9},{2,18},{10... | collective-permute-start | bytes 1671176 | tf_op jit(solution)/shard_map/ppermute | solution.py:31
  371.7 18.1 %collective-permute-start.59 = (bf16[2,1,64,2176]{3,2,0,1:T(8,128)(2,1)S(1)}, bf16[2,1,64,2176]{3,2,0,1:T(8,128)(2,1)S(1)}, u32[]{:S(2)}, u32[]{:S(2)}) collective-permute-start(bf16[2,1,64,2176]{3,2,0,1:T(8,128)(2,1)S(1)} %copy-done.27), channel_id=1, source_target_pairs={{0,16},{8,24},{16,0},{24,8},{1,17},{9,25},{17,1},{25,9},{2,18},{10... | collective-permute-start | bytes 1671176 | tf_op jit(solution)/shard_map/ppermute | solution.py:31
  372.0 17.8 %collective-permute-start.60 = (bf16[2,1,64,2176]{3,2,1,0:T(8,128)(2,1)S(1)}, bf16[2,1,64,2176]{3,2,1,0:T(8,128)(2,1)S(1)}, u32[]{:S(2)}, u32[]{:S(2)}) collective-permute-start(bf16[2,1,64,2176]{3,2,1,0:T(8,128)(2,1)S(1)} %copy-done.29), channel_id=1, source_target_pairs={{0,8},{8,0},{16,24},{24,16},{1,9},{9,1},{17,25},{25,17},{2,10},{10... | collective-permute-start | bytes 1671176 | tf_op jit(solution)/shard_map/ppermute | solution.py:31
  407.5 37.0 %collective-permute-start.65 = (bf16[4,2,4,64,2048]{4,3,2,1,0:T(8,128)(2,1)}, bf16[4,2,4,64,2048]{4,3,2,1,0:T(8,128)(2,1)}, u32[]{:S(2)}, u32[]{:S(2)}) collective-permute-start(bf16[4,2,4,64,2048]{4,3,2,1,0:T(8,128)(2,1)} %mix.2), channel_id=1, source_target_pairs={{0,1},{1,0},{2,3},{3,2},{4,5},{5,4},{6,7},{7,6},{8,9},{9,8},{10,11... | collective-permute-start | bytes 25165832 | tf_op jit(solution)/shard_map/ppermute | solution.py:48
  483.8 68.1 %collective-permute-start.71 = (bf16[2,4,64,2048]{3,2,1,0:T(8,128)(2,1)}, bf16[2,4,64,2048]{3,2,1,0:T(8,128)(2,1)}, u32[]{:S(2)}, u32[]{:S(2)}) collective-permute-start(bf16[2,4,64,2048]{3,2,1,0:T(8,128)(2,1)} %get-tuple-element.350), channel_id=1, source_target_pairs={{0,16},{8,24},{16,0},{24,8},{1,17},{9,25},{17,1},{25,9},{2,18},{10... | collective-permute-start | bytes 6291464 | tf_op jit(solution)/shard_map/ppermute | solution.py:31
  485.5 69.7 %collective-permute-start.73 = (bf16[2,4,64,2048]{3,2,1,0:T(8,128)(2,1)}, bf16[2,4,64,2048]{3,2,1,0:T(8,128)(2,1)}, u32[]{:S(2)}, u32[]{:S(2)}) collective-permute-start(bf16[2,4,64,2048]{3,2,1,0:T(8,128)(2,1)} %get-tuple-element.352), channel_id=1, source_target_pairs={{0,8},{8,0},{16,24},{24,16},{1,9},{9,1},{17,25},{25,17},{2,10},{10... | collective-permute-start | bytes 6291464 | tf_op jit(solution)/shard_map/ppermute | solution.py:31
  491.1 37.7 %collective-permute-start.76 = (bf16[4,256,512]{2,1,0:T(8,128)(2,1)}, bf16[4,256,512]{2,1,0:T(8,128)(2,1)S(1)}, u32[]{:S(2)}, u32[]{:S(2)}) collective-permute-start(bf16[4,256,512]{2,1,0:T(8,128)(2,1)} %get-tuple-element.360), channel_id=1, source_target_pairs={{0,1},{1,0},{2,3},{3,2},{4,5},{5,4},{6,7},{7,6},{8,9},{9,8},{10,11... | collective-permute-start | bytes 3145736 | tf_op jit(solution)/shard_map/ppermute | solution.py:48
  492.8 34.9 %collective-permute-start.79 = (bf16[4,64,512]{2,1,0:T(8,128)(2,1)}, bf16[4,64,512]{2,1,0:T(8,128)(2,1)S(1)}, u32[]{:S(2)}, u32[]{:S(2)}) collective-permute-start(bf16[4,64,512]{2,1,0:T(8,128)(2,1)} %fusion.37), channel_id=1, source_target_pairs={{0,2},{1,3},{2,4},{3,5},{4,6},{5,7},{6,0},{7,1},{8,10},{9,11},{10,... | collective-permute-start | bytes 786440 | tf_op jit(solution)/shard_map/ppermute | solution.py:57
  506.7 220.7 %all-gather.6.cloned.1.call-start = ((), (), s32[]{:S(2)}) async-start(), calls=%async_computation.3 | async-start | bytes 4718592 | tf_op jit(solution)/shard_map/all_gather | solution.py:1209
  506.8 61.0 %collective-permute-start.83 = (bf16[2,1,64,2048]{3,2,1,0:T(8,128)(2,1)}, bf16[2,1,64,2048]{3,2,1,0:T(8,128)(2,1)}, u32[]{:S(2)}, u32[]{:S(2)}) collective-permute-start(bf16[2,1,64,2048]{3,2,1,0:T(8,128)(2,1)} %bitcast.551), channel_id=1, source_target_pairs={{0,8},{8,0},{16,24},{24,16},{1,9},{9,1},{17,25},{25,17},{2,10},{10... | collective-permute-start | bytes 1572872 | tf_op jit(solution)/shard_map/ppermute | solution.py:31
  527.7 40.4 %collective-permute-start.82 = (bf16[2,1,64,2048]{3,2,1,0:T(8,128)(2,1)}, bf16[2,1,64,2048]{3,2,1,0:T(8,128)(2,1)}, u32[]{:S(2)}, u32[]{:S(2)}) collective-permute-start(bf16[2,1,64,2048]{3,2,1,0:T(8,128)(2,1)} %bitcast.550), channel_id=1, source_target_pairs={{0,16},{8,24},{16,0},{24,8},{1,17},{9,25},{17,1},{25,9},{2,18},{10... | collective-permute-start | bytes 1572872 | tf_op jit(solution)/shard_map/ppermute | solution.py:31
  528.8 19.7 %collective-permute-start.81 = (bf16[4,64,512]{2,1,0:T(8,128)(2,1)}, bf16[4,64,512]{2,1,0:T(8,128)(2,1)S(1)}, u32[]{:S(2)}, u32[]{:S(2)}) collective-permute-start(bf16[4,64,512]{2,1,0:T(8,128)(2,1)} %fusion.36), channel_id=1, source_target_pairs={{0,2},{1,3},{2,4},{3,5},{4,6},{5,7},{6,0},{7,1},{8,10},{9,11},{10,... | collective-permute-start | bytes 786440 | tf_op jit(solution)/shard_map/ppermute | solution.py:57
  551.9 41.9 %collective-permute-start.88 = (bf16[4,64,512]{2,1,0:T(8,128)(2,1)S(1)}, bf16[4,64,512]{2,1,0:T(8,128)(2,1)}, u32[]{:S(2)}, u32[]{:S(2)}) collective-permute-start(bf16[4,64,512]{2,1,0:T(8,128)(2,1)S(1)} %get-tuple-element.427), channel_id=1, source_target_pairs={{0,2},{1,3},{2,4},{3,5},{4,6},{5,7},{6,0},{7,1},{8,10},{9,11},{10,... | collective-permute-start | bytes 786440 | tf_op jit(solution)/shard_map/ppermute | solution.py:57
  555.2 46.2 %collective-permute-start.72 = (bf16[4,64,2048]{2,1,0:T(8,128)(2,1)}, bf16[4,64,2048]{2,1,0:T(8,128)(2,1)}, u32[]{:S(2)}, u32[]{:S(2)}) collective-permute-start(bf16[4,64,2048]{2,1,0:T(8,128)(2,1)} %fusion.16), channel_id=1, source_target_pairs={{0,8},{8,0},{16,24},{24,16},{1,9},{9,1},{17,25},{25,17},{2,10},{10... | collective-permute-start | bytes 3145736 | tf_op jit(solution)/shard_map/ppermute | solution.py:31
  565.5 37.1 %collective-permute-start.74 = (bf16[4,64,2048]{2,1,0:T(8,128)(2,1)}, bf16[4,64,2048]{2,1,0:T(8,128)(2,1)}, u32[]{:S(2)}, u32[]{:S(2)}) collective-permute-start(bf16[4,64,2048]{2,1,0:T(8,128)(2,1)} %fusion.17), channel_id=1, source_target_pairs={{0,16},{8,24},{16,0},{24,8},{1,17},{9,25},{17,1},{25,9},{2,18},{10... | collective-permute-start | bytes 3145736 | tf_op jit(solution)/shard_map/ppermute | solution.py:31
  567.8 22.1 %collective-permute-start.80 = (bf16[4,64,512]{2,1,0:T(8,128)(2,1)}, bf16[4,64,512]{2,1,0:T(8,128)(2,1)}, u32[]{:S(2)}, u32[]{:S(2)}) collective-permute-start(bf16[4,64,512]{2,1,0:T(8,128)(2,1)} %fusion.35), channel_id=1, source_target_pairs={{0,2},{1,3},{2,4},{3,5},{4,6},{5,7},{6,0},{7,1},{8,10},{9,11},{10,... | collective-permute-start | bytes 786440 | tf_op jit(solution)/shard_map/ppermute | solution.py:57
  593.8 29.5 %collective-permute-start.85 = (bf16[4,64,512]{2,1,0:T(8,128)(2,1)}, bf16[4,64,512]{2,1,0:T(8,128)(2,1)}, u32[]{:S(2)}, u32[]{:S(2)}) collective-permute-start(bf16[4,64,512]{2,1,0:T(8,128)(2,1)} %fusion.33), channel_id=1, source_target_pairs={{0,2},{1,3},{2,4},{3,5},{4,6},{5,7},{6,0},{7,1},{8,10},{9,11},{10,... | collective-permute-start | bytes 786440 | tf_op jit(solution)/shard_map/ppermute | solution.py:57
  595.6 57.7 %collective-permute-start.108 = (bf16[4,64,512]{2,1,0:T(8,128)(2,1)}, bf16[4,64,512]{2,1,0:T(8,128)(2,1)S(1)}, u32[]{:S(2)}, u32[]{:S(2)}) collective-permute-start(bf16[4,64,512]{2,1,0:T(8,128)(2,1)} %collective-permute-done.88), channel_id=1, source_target_pairs={{0,2},{1,3},{2,4},{3,5},{4,6},{5,7},{6,0},{7,1},{8,10},{9,11},{10,... | collective-permute-start | bytes 786440 | tf_op jit(solution)/shard_map/ppermute | solution.py:57
  604.7 34.0 %collective-permute-start.84 = (bf16[2,64,2048]{2,1,0:T(8,128)(2,1)}, bf16[2,64,2048]{2,1,0:T(8,128)(2,1)}, u32[]{:S(2)}, u32[]{:S(2)}) collective-permute-start(bf16[2,64,2048]{2,1,0:T(8,128)(2,1)} %pad_maximum_fusion.8), channel_id=1, source_target_pairs={{0,2},{1,3},{2,4},{3,5},{4,6},{5,7},{6,0},{7,1},{8,10},{9,11},{10,... | collective-permute-start | bytes 1572872 | tf_op jit(solution)/shard_map/ppermute | solution.py:57
  639.9 34.4 %collective-permute-start.97 = (bf16[2,64,2048]{2,1,0:T(8,128)(2,1)S(1)}, bf16[2,64,2048]{2,1,0:T(8,128)(2,1)S(1)}, u32[]{:S(2)}, u32[]{:S(2)}) collective-permute-start(bf16[2,64,2048]{2,1,0:T(8,128)(2,1)S(1)} %fusion.18), channel_id=1, source_target_pairs={{0,2},{1,3},{2,4},{3,5},{4,6},{5,7},{6,0},{7,1},{8,10},{9,11},{10,... | collective-permute-start | bytes 1572872 | tf_op jit(solution)/shard_map/ppermute | solution.py:57
  651.8 33.7 %collective-permute-start.102 = (bf16[4,64,512]{2,1,0:T(8,128)(2,1)S(1)}, bf16[4,64,512]{2,1,0:T(8,128)(2,1)S(1)}, u32[]{:S(2)}, u32[]{:S(2)}) collective-permute-start(bf16[4,64,512]{2,1,0:T(8,128)(2,1)S(1)} %collective-permute-done.101), channel_id=1, source_target_pairs={{0,2},{1,3},{2,4},{3,5},{4,6},{5,7},{6,0},{7,1},{8,10},{9,11},{10,... | collective-permute-start | bytes 786440 | tf_op jit(solution)/shard_map/ppermute | solution.py:57
  653.3 43.4 %collective-permute-start.109 = (bf16[4,64,512]{2,1,0:T(8,128)(2,1)S(1)}, bf16[4,64,512]{2,1,0:T(8,128)(2,1)S(1)}, u32[]{:S(2)}, u32[]{:S(2)}) collective-permute-start(bf16[4,64,512]{2,1,0:T(8,128)(2,1)S(1)} %collective-permute-done.108), channel_id=1, source_target_pairs={{0,2},{1,3},{2,4},{3,5},{4,6},{5,7},{6,0},{7,1},{8,10},{9,11},{10,... | collective-permute-start | bytes 786440 | tf_op jit(solution)/shard_map/ppermute | solution.py:57
  674.4 32.5 %collective-permute-start.98 = (bf16[2,64,2048]{2,1,0:T(8,128)(2,1)S(1)}, bf16[2,64,2048]{2,1,0:T(8,128)(2,1)S(1)}, u32[]{:S(2)}, u32[]{:S(2)}) collective-permute-start(bf16[2,64,2048]{2,1,0:T(8,128)(2,1)S(1)} %fusion.19), channel_id=1, source_target_pairs={{0,2},{1,3},{2,4},{3,5},{4,6},{5,7},{6,0},{7,1},{8,10},{9,11},{10,... | collective-permute-start | bytes 1572872 | tf_op jit(solution)/shard_map/ppermute | solution.py:57
  685.5 24.2 %collective-permute-start.103 = (bf16[4,64,512]{2,1,0:T(8,128)(2,1)S(1)}, bf16[4,64,512]{2,1,0:T(8,128)(2,1)S(1)}, u32[]{:S(2)}, u32[]{:S(2)}) collective-permute-start(bf16[4,64,512]{2,1,0:T(8,128)(2,1)S(1)} %collective-permute-done.102), channel_id=1, source_target_pairs={{0,2},{1,3},{2,4},{3,5},{4,6},{5,7},{6,0},{7,1},{8,10},{9,11},{10,... | collective-permute-start | bytes 786440 | tf_op jit(solution)/shard_map/ppermute | solution.py:57
  (130 other events, 1277.8 us)
Sparse Core Ops, SparseCore 0:
  11.4 139.4 all-gather.3
  506.9 63.9 reduce-scatter.1
  623.4 76.1 all-gather.5
